TPU v7x, 32 devices: a whole 2x2x4 slice. The times are simulated.
32 devices in a mesh: dp: 16 (over z, x, core), tensor: 2 (over y).
Axes of the slice: x: 2, y: 2, z: 4, core: 2. Of those that a mesh axis runs over, the one named last changes fastest.
Arguments:
- inputs: bfloat16 [3152, 768], P('dp'), may hold values from -6 to 6
- norm1_gain: float32 [768], replicated, may hold values from 0.5 to 1.5
- norm1_bias: float32 [768], replicated, may hold values from -4 to 4
- qkv_weight: bfloat16 [3, 768, 768], P(None, None, 'tensor'), may hold values from -0.21875 to 0.21875
- qv_bias: float32 [2, 768], P(None, 'tensor'), may hold values from -4 to 4
- proj_weight: bfloat16 [768, 768], P('tensor'), may hold values from -2 to 2
- proj_bias: float32 [768], replicated, may hold values from -4 to 4
- norm2_gain: float32 [768], replicated, may hold values from 0.5 to 1.5
- norm2_bias: float32 [768], replicated, may hold values from -4 to 4
- router: bfloat16 [768, 16], replicated, may hold values from -0.21582031 to 0.21582031
- expert_in: bfloat16 [16, 768, 3072], P('dp', None, 'tensor'), may hold values from -0.21875 to 0.21875
- expert_in_bias: float32 [16, 3072], P('dp', 'tensor'), may hold values from -4 to 4
- expert_out: bfloat16 [16, 3072, 768], P('dp', 'tensor'), may hold values from -0.109375 to 0.109375
- expert_out_bias: float32 [16, 768], replicated, may hold values from -4 to 4
- routes: int32 [3152, 2], P('dp'), may hold values from 0 to 15, all different within a row; in each aligned block of 197 rows (0 to 196, 197 to 393, ...) at most 42 rows name the same one
- cotangent: bfloat16 [3152, 768], P('dp'), may hold values from -6 to 6
Outputs:
- output: bfloat16 [3152, 768], P('dp')
- input_grad: float32 [3152, 768], P('dp')
- norm1_gain_grad: float32 [768], replicated
- norm1_bias_grad: float32 [768], replicated
- qkv_grad: float32 [3, 768, 768], P(None, None, 'tensor')
- qv_bias_grad: float32 [2, 768], P(None, 'tensor')
- proj_grad: float32 [768, 768], P('tensor')
- proj_bias_grad: float32 [768], replicated
- norm2_gain_grad: float32 [768], replicated
- norm2_bias_grad: float32 [768], replicated
- router_grad: float32 [768, 16], replicated
- expert_in_grad: float32 [16, 768, 3072], P('dp', None, 'tensor')
- expert_in_bias_grad: float32 [16, 3072], P('dp', 'tensor')
- expert_out_grad: float32 [16, 3072, 768], P('dp', 'tensor')
- expert_out_bias_grad: float32 [16, 768], replicated
Inputs may be any that keep to these rules, and one draw needn't show every extreme that they name: `routes`: each token names two different experts; among the tokens of one aligned block of 197 no expert is named more than 42 times, and in some block one expert is named exactly 42 times.
All inputs are finite; a program needn't handle non-finite values.
Results may differ from a plain program's by a relative error of at most 0.011.
Values may be sent and summed in bfloat16 or wider, within the bound.
No kernel may reach another device: no remote copies, remote signals or barrier semaphores. Data moves between devices by JAX's collectives and lax.ppermute only.
A program may use at most 192 MiB of HBM per device.

v0:
```python
import jax
import jax.numpy as jnp
from jax import lax
from jax.sharding import PartitionSpec as P

HEAD = 64
SEQ = 197


epsilon = 1e-06


def norm_parts(values):
    average = jnp.mean(values, axis=-1, keepdims=True)
    centred = values - average
    inverse = lax.rsqrt(jnp.mean(centred * centred, axis=-1, keepdims=True) + epsilon)
    return (centred * inverse, inverse)


def norm_back(inner_grad, normed, inverse):
    first_mean = jnp.mean(inner_grad, axis=-1, keepdims=True)
    second_mean = jnp.mean(inner_grad * normed, axis=-1, keepdims=True)
    return inverse * (inner_grad - first_mean - normed * second_mean)


def gelu_parts(pre_act):
    normal_cdf = 0.5 * (1.0 + lax.erf(pre_act * 0.7071067811865476))
    density = jnp.exp(-0.5 * pre_act * pre_act) * 0.3989422804014327
    return (pre_act * normal_cdf, normal_cdf + pre_act * density)


def local(
    inputs,
    norm1_gain,
    norm1_bias,
    qkv_weight,
    qv_bias,
    proj_weight,
    proj_bias,
    norm2_gain,
    norm2_bias,
    router,
    expert_in,
    expert_in_bias,
    expert_out,
    expert_out_bias,
    routes,
    cotangent,
):
    tok_count = inputs.shape[0]
    feat_dim = inputs.shape[1]
    head_cols = qkv_weight.shape[2]
    heads_here = head_cols // HEAD
    images = tok_count // SEQ
    experts = router.shape[1]
    sources = lax.axis_size("dp")
    group_size = sources // experts
    capacity = max(2, (10 * tok_count + 3 * experts - 1) // (3 * experts))
    score_scale = HEAD ** (-0.5)
    x_in = inputs.astype(jnp.float32)
    normed1, inverse1 = norm_parts(x_in)
    hidden1 = (normed1 * norm1_gain + norm1_bias).astype(jnp.bfloat16)
    projected = jnp.einsum("td,jde->jte", hidden1, qkv_weight, preferred_element_type=jnp.float32)
    bias_rows = jnp.stack([qv_bias[0], jnp.zeros_like(qv_bias[0]), qv_bias[1]])
    projected = (projected + bias_rows[:, None, :]).astype(jnp.bfloat16)
    heads_view = projected.reshape(3, images, SEQ, heads_here, HEAD)
    queries, key_vals, values_in = (heads_view[0], heads_view[1], heads_view[2])
    scores = (
        jnp.einsum("bqhd,bkhd->bhqk", queries, key_vals, preferred_element_type=jnp.float32)
        * score_scale
    )
    row_max = jnp.max(scores, axis=-1, keepdims=True)
    exp_scores = jnp.exp(scores - row_max)
    row_total = jnp.sum(exp_scores, axis=-1, keepdims=True)
    log_total = row_max + jnp.log(row_total)
    prob_low = (exp_scores / row_total).astype(jnp.bfloat16)
    attended = jnp.einsum(
        "bhqk,bkhd->bqhd", prob_low, values_in, preferred_element_type=jnp.float32
    )
    attended = attended.reshape(tok_count, head_cols).astype(jnp.bfloat16)
    attn_part = jnp.dot(attended, proj_weight, preferred_element_type=jnp.float32)
    middle = x_in + lax.psum(attn_part, "tensor") + proj_bias
    normed2, inverse2 = norm_parts(middle)
    hidden2 = (normed2 * norm2_gain + norm2_bias).astype(jnp.bfloat16)
    logits = jnp.dot(hidden2, router, preferred_element_type=jnp.float32)
    expert_ids = jnp.arange(experts, dtype=jnp.int32)
    pick_mask = (routes[:, :, None] == expert_ids[None, None, :]).astype(jnp.float32)
    chosen = jnp.sum(pick_mask * logits[:, None, :], axis=-1)
    chosen_max = jnp.max(chosen, axis=1, keepdims=True)
    chosen_exp = jnp.exp(chosen - chosen_max)
    gate_vals = chosen_exp / jnp.sum(chosen_exp, axis=1, keepdims=True)
    flat_routes = routes.reshape(-1)
    onehot = (flat_routes[:, None] == expert_ids[None, :]).astype(jnp.int32)
    rank_vals = jnp.sum(onehot * (jnp.cumsum(onehot, axis=0) - 1), axis=1)
    slot_index = flat_routes * capacity + rank_vals
    send_rows = jnp.zeros((experts * capacity, feat_dim), jnp.bfloat16)
    send_rows = send_rows.at[slot_index].set(jnp.repeat(hidden2, 2, axis=0))
    send_all = jnp.repeat(send_rows.reshape(experts, capacity, feat_dim), group_size, axis=0)
    arrived = lax.all_to_all(send_all, "dp", split_axis=0, concat_axis=0, tiled=True)
    arrived_flat = arrived.reshape(-1, feat_dim)
    pre_act = (
        jnp.dot(arrived_flat, expert_in[0], preferred_element_type=jnp.float32) + expert_in_bias[0]
    )
    activ_vals, gelu_slope = gelu_parts(pre_act)
    activ_low = activ_vals.astype(jnp.bfloat16)
    part_out = jnp.dot(activ_low, expert_out[0], preferred_element_type=jnp.float32).reshape(
        sources, capacity, feat_dim
    )
    came_back = lax.all_to_all(part_out, "dp", split_axis=0, concat_axis=0, tiled=True)
    local_rows = jnp.sum(came_back.reshape(experts, group_size, capacity, feat_dim), axis=1)
    full_rows = lax.psum(local_rows, "tensor") + expert_out_bias[:, None, :]
    result_rows = full_rows.astype(jnp.bfloat16)
    picked = (
        result_rows.reshape(-1, feat_dim)[slot_index]
        .reshape(tok_count, 2, feat_dim)
        .astype(jnp.float32)
    )
    output = (middle + jnp.sum(gate_vals[:, :, None] * picked, axis=1)).astype(jnp.bfloat16)
    grad_out = cotangent.astype(jnp.float32)
    gate_grad = jnp.sum(picked * grad_out[:, None, :], axis=-1)
    chosen_grad = gate_vals * (gate_grad - jnp.sum(gate_vals * gate_grad, axis=1, keepdims=True))
    logit_grad = jnp.sum(pick_mask * chosen_grad[:, :, None], axis=1).astype(jnp.bfloat16)
    row_grad = (
        (gate_vals[:, :, None] * grad_out[:, None, :]).astype(jnp.bfloat16).reshape(-1, feat_dim)
    )
    out_bias_grad = jnp.einsum(
        "re,rd->ed", onehot.astype(jnp.bfloat16), row_grad, preferred_element_type=jnp.float32
    )
    send_grad = jnp.zeros((experts * capacity, feat_dim), jnp.bfloat16).at[slot_index].set(row_grad)
    send_grad_all = jnp.repeat(send_grad.reshape(experts, capacity, feat_dim), group_size, axis=0)
    grad_arrived = lax.all_to_all(send_grad_all, "dp", split_axis=0, concat_axis=0, tiled=True)
    grad_arrived = grad_arrived.reshape(-1, feat_dim)
    out_weight_grad = jnp.einsum(
        "rf,rd->fd", activ_low, grad_arrived, preferred_element_type=jnp.float32
    )
    act_grad = (
        jnp.einsum("rd,fd->rf", grad_arrived, expert_out[0], preferred_element_type=jnp.float32)
        * gelu_slope
    )
    in_bias_grad = jnp.sum(act_grad, axis=0)
    act_low = act_grad.astype(jnp.bfloat16)
    in_weight_grad = jnp.einsum(
        "rd,rf->df", arrived_flat, act_low, preferred_element_type=jnp.float32
    )
    row_part = jnp.einsum("rf,df->rd", act_low, expert_in[0], preferred_element_type=jnp.float32)
    row_part = row_part.reshape(sources, capacity, feat_dim)
    home_whole = lax.all_to_all(row_part, "dp", split_axis=0, concat_axis=0, tiled=True)
    home_local = jnp.sum(home_whole.reshape(experts, group_size, capacity, feat_dim), axis=1)
    row_back = lax.psum(home_local, "tensor").astype(jnp.bfloat16)
    row_home = (
        row_back.reshape(-1, feat_dim)[slot_index]
        .reshape(tok_count, 2, feat_dim)
        .astype(jnp.float32)
    )
    hidden2_grad = jnp.sum(row_home, axis=1) + jnp.einsum(
        "te,de->td", logit_grad, router, preferred_element_type=jnp.float32
    )
    router_grad = jnp.einsum("td,te->de", hidden2, logit_grad, preferred_element_type=jnp.float32)
    norm2_gain_grad = jnp.sum(hidden2_grad * normed2, axis=0)
    norm2_bias_grad = jnp.sum(hidden2_grad, axis=0)
    middle_grad = grad_out + norm_back(hidden2_grad * norm2_gain, normed2, inverse2)
    proj_bias_grad = jnp.sum(middle_grad, axis=0)
    middle_low = middle_grad.astype(jnp.bfloat16)
    proj_grad = jnp.einsum("tc,td->cd", attended, middle_low, preferred_element_type=jnp.float32)
    attended_grad = jnp.einsum(
        "td,cd->tc", middle_low, proj_weight, preferred_element_type=jnp.float32
    )
    attended_grad = attended_grad.astype(jnp.bfloat16).reshape(images, SEQ, heads_here, HEAD)
    again_scores = (
        jnp.einsum("bqhd,bkhd->bhqk", queries, key_vals, preferred_element_type=jnp.float32)
        * score_scale
    )
    prob_vals = jnp.exp(again_scores - log_total)
    prob_again = prob_vals.astype(jnp.bfloat16)
    value_grad = jnp.einsum(
        "bhqk,bqhd->bkhd", prob_again, attended_grad, preferred_element_type=jnp.float32
    )
    prob_grad = jnp.einsum(
        "bqhd,bkhd->bhqk", attended_grad, values_in, preferred_element_type=jnp.float32
    )
    score_grad = prob_vals * (prob_grad - jnp.sum(prob_vals * prob_grad, axis=-1, keepdims=True))
    score_low = score_grad.astype(jnp.bfloat16)
    query_grad = (
        jnp.einsum("bhqk,bkhd->bqhd", score_low, key_vals, preferred_element_type=jnp.float32)
        * score_scale
    )
    key_grad = (
        jnp.einsum("bhqk,bqhd->bkhd", score_low, queries, preferred_element_type=jnp.float32)
        * score_scale
    )
    proj_low = (
        jnp.stack([query_grad, key_grad, value_grad])
        .reshape(3, tok_count, head_cols)
        .astype(jnp.bfloat16)
    )
    qv_bias_grad = jnp.stack(
        [
            jnp.sum(proj_low[0].astype(jnp.float32), axis=0),
            jnp.sum(proj_low[2].astype(jnp.float32), axis=0),
        ]
    )
    qkv_grad = jnp.einsum("td,jte->jde", hidden1, proj_low, preferred_element_type=jnp.float32)
    hidden1_part = jnp.einsum(
        "jte,jde->td", proj_low, qkv_weight, preferred_element_type=jnp.float32
    )
    hidden1_grad = lax.psum(hidden1_part, "tensor")
    norm1_gain_grad = jnp.sum(hidden1_grad * normed1, axis=0)
    norm1_bias_grad = jnp.sum(hidden1_grad, axis=0)
    input_grad = middle_grad + norm_back(hidden1_grad * norm1_gain, normed1, inverse1)
    summed = lax.psum(
        (
            qkv_grad,
            qv_bias_grad,
            proj_grad,
            proj_bias_grad,
            norm1_gain_grad,
            norm1_bias_grad,
            norm2_gain_grad,
            norm2_bias_grad,
            router_grad,
            out_bias_grad,
        ),
        "dp",
    )
    return (
        output,
        input_grad,
        summed[4],
        summed[5],
        summed[0],
        summed[1],
        summed[2],
        summed[3],
        summed[6],
        summed[7],
        summed[8],
        in_weight_grad[None],
        in_bias_grad[None],
        out_weight_grad[None],
        summed[9],
    )


def solution(mesh):
    return jax.shard_map(
        local,
        mesh=mesh,
        in_specs=(
            P("dp", None),
            P(),
            P(),
            P(None, None, "tensor"),
            P(None, "tensor"),
            P("tensor", None),
            P(),
            P(),
            P(),
            P(),
            P("dp", None, "tensor"),
            P("dp", "tensor"),
            P("dp", "tensor", None),
            P(),
            P("dp", None),
            P("dp", None),
        ),
        out_specs=(
            P("dp", None),
            P("dp", None),
            P(),
            P(),
            P(None, None, "tensor"),
            P(None, "tensor"),
            P("tensor", None),
            P(),
            P(),
            P(),
            P(),
            P("dp", None, "tensor"),
            P("dp", "tensor"),
            P("dp", "tensor", None),
            P(),
        ),
        check_vma=False,
    )
```

profile of v0, /device:TPU:0, one launch (start us, length us, event | category | flops | bytes accessed | tf_op | source)
XLA Modules:
  0.0 652.9 jit_solution(2582611026457275273)
XLA Ops:
  19.0 31.3 %all-reduce.10.cloned.1.call-done = f32[197,768]{1,0:T(8,128)} async-done(((f32[197,768]{1,0:T(8,128)}), f32[197,768]{1,0:T(8,128)}) %all-reduce.10.cloned.1.call-update) | async-done | bytes 605200 | tf_op jit(solution)/shard_map/psum | solution.py:82
  53.9 2.6 reshape.401
  56.5 3.8 scatter_custom_fusion
  62.5 5.7 all-to-all-start
  70.4 3.1 mul.262
  77.9 4.0 scatter_custom_fusion.1
  84.1 9.2 %all-to-all-done = bf16[16,42,768]{2,1,0:T(8,128)(2,1)} async-done(((bf16[16,42,768]{2,1,0:T(8,128)(2,1)}), bf16[16,42,768]{2,1,0:T(8,128)(2,1)}, u32[]{:S(2)}, u32[]{:S(2)}) %all-to-all-start) | async-done | bytes 1032224 | tf_op jit(solution)/shard_map/all_to_all | solution.py:99
  93.3 7.5 %all-to-all-start.2 = ((bf16[16,42,768]{2,1,0:T(8,128)(2,1)}), bf16[16,42,768]{2,1,0:T(8,128)(2,1)}, u32[]{:S(2)}, u32[]{:S(2)}) async-start(bf16[16,42,768]{2,1,0:T(8,128)(2,1)} %reshape_broadcast_in_dim_reshape.7), calls=%async_computation.2 | async-start | bytes 2359296 | tf_op jit(solution)/shard_map/all_to_all | solution.py:131
  104.4 5.1 multiply_convert_fusion
  109.5 16.6 %all-to-all-done.2 = bf16[16,42,768]{2,1,0:T(8,128)(2,1)} async-done(((bf16[16,42,768]{2,1,0:T(8,128)(2,1)}), bf16[16,42,768]{2,1,0:T(8,128)(2,1)}, u32[]{:S(2)}, u32[]{:S(2)}) %all-to-all-start.2) | async-done | bytes 1032224 | tf_op jit(solution)/shard_map/all_to_all | solution.py:131
  128.3 6.7 %fusion.59 = (f32[1536]{0:T(1024)}, bf16[672,1536]{1,0:T(8,128)(2,1)}) fusion(f32[672,1536]{1,0:T(8,128)} %get-tuple-element.111, f32[1536]{0:T(1024)} %reduce.13, bf16[672,768]{1,0:T(8,128)(2,1)} %reshape.375, bf16[1,1536,768]{2,1,0:T(8,128)(2,1)} %param.28), kind=kOutput, calls=%fused_computation.127 | convolution fusion | flops 1597831680 | bytes 9596928 | tf_op jit(solution)/shard_map/rd,fd->rf/dot_general | solution.py:137
  135.0 4.0 dot_general.82
  139.0 5.1 fusion.5
  144.1 7.5 %all-to-all-start.3 = ((f32[16,42,768]{2,1,0:T(8,128)}), f32[16,42,768]{2,1,0:T(8,128)S(1)}, u32[]{:S(2)}, u32[]{:S(2)}) async-start(f32[16,42,768]{2,1,0:T(8,128)} %fusion.5), calls=%async_computation.3 | async-start | bytes 4718592 | tf_op jit(solution)/shard_map/all_to_all | solution.py:147
  151.6 4.0 dot_general.79
  155.7 5.8 fusion.7
  161.4 35.9 %all-to-all-done.3 = f32[16,42,768]{2,1,0:T(8,128)S(1)} async-done(((f32[16,42,768]{2,1,0:T(8,128)}), f32[16,42,768]{2,1,0:T(8,128)S(1)}, u32[]{:S(2)}, u32[]{:S(2)}) %all-to-all-start.3) | async-done | bytes 2064416 | tf_op jit(solution)/shard_map/all_to_all | solution.py:147
  197.3 12.3 %all-to-all-start.1 = ((f32[16,42,768]{2,1,0:T(8,128)}), f32[16,42,768]{2,1,0:T(8,128)}, u32[]{:S(2)}, u32[]{:S(2)}) async-start(f32[16,42,768]{2,1,0:T(8,128)} %fusion.7), calls=%async_computation.1 | async-start | bytes 4718592 | tf_op jit(solution)/shard_map/all_to_all | solution.py:109
  212.1 43.2 %all-to-all-done.1 = f32[16,42,768]{2,1,0:T(8,128)} async-done(((f32[16,42,768]{2,1,0:T(8,128)}), f32[16,42,768]{2,1,0:T(8,128)}, u32[]{:S(2)}, u32[]{:S(2)}) %all-to-all-start.1) | async-done | bytes 2064416 | tf_op jit(solution)/shard_map/all_to_all | solution.py:109
  255.4 91.7 %all-reduce.19 = bf16[16,42,768]{2,1,0:T(8,128)(2,1)} all-reduce(f32[16,42,768]{2,1,0:T(8,128)S(1)} %all-to-all-done.3), channel_id=1, replica_groups=mesh['dp'=16,'tensor'=2] {'tensor'}, use_global_device_ids=true, to_apply=%region_17.18 | all-reduce | flops 516096 | bytes 3096576 | tf_op jit(solution)/shard_map/psum | solution.py:149
  351.5 2.4 reduce_sum.254
  353.9 8.6 %all-reduce.12.cloned.1.call-done = f32[16,42,768]{2,1,0:T(8,128)} async-done(((f32[16,42,768]{2,1,0:T(8,128)}), f32[16,42,768]{2,1,0:T(8,128)}) %all-reduce.12.cloned.1.call-update) | async-done | bytes 2064400 | tf_op jit(solution)/shard_map/psum | solution.py:111
  364.7 2.7 gather_fusion
  369.4 3.5 multiply_reduce_fusion.1
  380.0 3.1 convolution_bitcast_fusion.3
  384.5 2.6 convolution_bitcast_fusion.2
  390.0 6.3 convolution_bitcast_fusion.1
  396.2 4.2 convolution_bitcast_fusion
  402.2 18.3 %all-reduce.14.cloned.1.call-done = f32[197,768]{1,0:T(8,128)} async-done(((f32[197,768]{1,0:T(8,128)}), f32[197,768]{1,0:T(8,128)}) %all-reduce.14.cloned.1.call-update) | async-done | bytes 605200 | tf_op jit(solution)/shard_map/psum | solution.py:206
  424.7 117.8 %all-reduce.18.cloned.1.call-done = (f32[3,768,384]{1,2,0:T(8,128)}, f32[384,768]{1,0:T(8,128)}) async-done(((f32[3,768,384]{1,2,0:T(8,128)}, f32[384,768]{1,0:T(8,128)}), (f32[3,768,384]{1,2,0:T(8,128)}, f32[384,768]{1,0:T(8,128)})) %all-reduce.18.cloned.1.call-update) | async-done | bytes 4718608 | tf_op jit(solution)/shard_map/psum | solution.py:210
  542.5 5.3 copy.104
  547.8 89.3 %all-reduce.16.cloned.1.call-done = (f32[768]{0:T(1024)}, f32[768]{0:T(1024)}, f32[2,384]{1,0:T(2,128)}, f32[768]{0:T(1024)}, f32[768]{0:T(1024)}, /*index=5*/f3...) async-done(((f32[768]{0:T(1024)}, f32[768]{0:T(1024)}, f32[2,384]{1,0:T(2,128)}, f32[768]{0:T(1024)}, f32[768]{0:T(1024)}, /*index=5*/f32[768]{0:T(1024)}, f32[768,16]{0,1:T(8,128)}, ...) | async-done | bytes 116752 | tf_op jit(solution)/shard_map/psum | solution.py:210
  (197 shorter events, 69.2 us)
Async XLA Ops:
  7.2 97.2 %copy-start = (bf16[1,768,1536]{2,1,0:T(8,128)(2,1)S(1)}, bf16[1,768,1536]{2,1,0:T(8,128)(2,1)}, u32[]{:S(2)}) copy-start(bf16[1,768,1536]{2,1,0:T(8,128)(2,1)} %param.26) | copy-start | bytes 7077892
  7.2 43.1 %all-reduce.10.cloned.1.call-start = ((), (), s32[]{:S(2)}) async-start(), calls=%async_computation.4 | async-start | bytes 1228800 | tf_op jit(solution)/shard_map/psum | solution.py:82
  15.2 35.1 %copy-start.5 = (bf16[197,768]{1,0:T(8,128)(2,1)S(1)}, bf16[197,768]{1,0:T(8,128)(2,1)}, u32[]{:S(2)}) copy-start(bf16[197,768]{1,0:T(8,128)(2,1)} %param.16) | copy-start | bytes 907780
  15.2 35.1 %copy-start.39 = (f32[768]{0:T(1024)S(1)}, f32[768]{0:T(1024)}, u32[]{:S(2)}) copy-start(f32[768]{0:T(1024)} %param.22) | copy-start | bytes 9220
  16.9 34.9 %copy-start.26 = (f32[768]{0:T(1024)S(1)}, f32[768]{0:T(1024)}, u32[]{:S(2)}) copy-start(f32[768]{0:T(1024)} %param.23) | copy-start | bytes 9220
  16.9 34.9 %copy-start.40 = (f32[768]{0:T(1024)S(1)}, f32[768]{0:T(1024)}, u32[]{:S(2)}) copy-start(f32[768]{0:T(1024)} %param.24) | copy-start | bytes 9220
  51.8 10.7 %copy-start.32 = (f32[197]{0:T(256)}, f32[197]{0:T(256)S(1)}, u32[]{:S(2)}) copy-start(f32[197]{0:T(256)S(1)} %add_rsqrt_fusion) | copy-start | bytes 2368
  62.5 30.9 %all-to-all-start = ((bf16[16,42,768]{2,1,0:T(8,128)(2,1)}), bf16[16,42,768]{2,1,0:T(8,128)(2,1)}, u32[]{:S(2)}, u32[]{:S(2)}) async-start(bf16[16,42,768]{2,1,0:T(8,128)(2,1)} %reshape_broadcast_in_dim_reshape.6), calls=%async_computation | async-start | bytes 2359296 | tf_op jit(solution)/shard_map/all_to_all | solution.py:99
  68.1 5.4 copy-start.22
  77.9 6.2 copy-start.29
  93.3 32.7 %all-to-all-start.2 = ((bf16[16,42,768]{2,1,0:T(8,128)(2,1)}), bf16[16,42,768]{2,1,0:T(8,128)(2,1)}, u32[]{:S(2)}, u32[]{:S(2)}) async-start(bf16[16,42,768]{2,1,0:T(8,128)(2,1)} %reshape_broadcast_in_dim_reshape.7), calls=%async_computation.2 | async-start | bytes 2359296 | tf_op jit(solution)/shard_map/all_to_all | solution.py:131
  144.1 53.2 %all-to-all-start.3 = ((f32[16,42,768]{2,1,0:T(8,128)}), f32[16,42,768]{2,1,0:T(8,128)S(1)}, u32[]{:S(2)}, u32[]{:S(2)}) async-start(f32[16,42,768]{2,1,0:T(8,128)} %fusion.5), calls=%async_computation.3 | async-start | bytes 4718592 | tf_op jit(solution)/shard_map/all_to_all | solution.py:147
  197.3 58.1 %all-to-all-start.1 = ((f32[16,42,768]{2,1,0:T(8,128)}), f32[16,42,768]{2,1,0:T(8,128)}, u32[]{:S(2)}, u32[]{:S(2)}) async-start(f32[16,42,768]{2,1,0:T(8,128)} %fusion.7), calls=%async_computation.1 | async-start | bytes 4718592 | tf_op jit(solution)/shard_map/all_to_all | solution.py:109
  209.6 152.9 %all-reduce.12.cloned.1.call-start = ((), (), s32[]{:S(2)}) async-start(), calls=%async_computation.5 | async-start | bytes 4718592 | tf_op jit(solution)/shard_map/psum | solution.py:111
  255.4 93.2 %copy-start.31 = (s32[1024]{0:T(1024)S(1)}, s32[1024]{0:T(1024)}, u32[]{:S(2)}) copy-start(s32[1024]{0:T(1024)} %pad_clamp_fusion) | copy-start | bytes 12292
  255.4 165.1 %all-reduce.14.cloned.1.call-start = ((), (), s32[]{:S(2)}) async-start(), calls=%async_computation.6 | async-start | bytes 1228800 | tf_op jit(solution)/shard_map/psum | solution.py:206
  350.7 11.8 %copy-start.23 = (f32[16,768]{1,0:T(8,128)S(1)}, f32[16,768]{1,0:T(8,128)}, u32[]{:S(2)}) copy-start(f32[16,768]{1,0:T(8,128)} %param.29) | copy-start | bytes 147460
  364.7 4.7 copy-start.17
  367.4 5.6 copy-start.35
  367.4 5.7 copy-start.33
  369.4 6.0 copy-start.8
  383.1 159.4 %all-reduce.18.cloned.1.call-start = ((), (), s32[]{:S(2)}) async-start(), calls=%async_computation.8 | async-start | bytes 9437184 | tf_op jit(solution)/shard_map/psum | solution.py:210
  387.2 249.9 %all-reduce.16.cloned.1.call-start = ((), (), s32[]{:S(2)}) async-start(), calls=%async_computation.7 | async-start | bytes 243712 | tf_op jit(solution)/shard_map/psum | solution.py:210
  390.0 6.3 copy-start.13
  390.0 6.3 copy-start.16
  396.2 5.2 copy-start.7
  542.5 103.8 %copy-start.1 = (bf16[1,768,1536]{2,1,0:T(8,128)(2,1)S(1)}, bf16[1,768,1536]{2,1,0:T(8,128)(2,1)}, u32[]{:S(2)}) copy-start(bf16[1,768,1536]{2,1,0:T(8,128)(2,1)} %param.26) | copy-start | bytes 7077892
  637.1 6.2 copy-start.43
  637.1 6.8 %copy-start.42 = (f32[768]{0:T(1024)S(1)}, f32[768]{0:T(1024)}, u32[]{:S(2)}) copy-start(f32[768]{0:T(1024)} %get-tuple-element.125) | copy-start | bytes 9220
  637.1 7.4 %copy-start.41 = (f32[768]{0:T(1024)S(1)}, f32[768]{0:T(1024)}, u32[]{:S(2)}) copy-start(f32[768]{0:T(1024)} %get-tuple-element.126) | copy-start | bytes 9220
  637.1 8.0 %copy-start.25 = (f32[768,16]{0,1:T(8,128)S(1)}, f32[768,16]{0,1:T(8,128)}, u32[]{:S(2)}) copy-start(f32[768,16]{0,1:T(8,128)} %get-tuple-element.127) | copy-start | bytes 147460
  637.1 8.6 %copy-start.24 = (f32[16,768]{1,0:T(8,128)S(1)}, f32[16,768]{1,0:T(8,128)}, u32[]{:S(2)}) copy-start(f32[16,768]{1,0:T(8,128)} %get-tuple-element.131) | copy-start | bytes 147460
  (22 other events, 37.1 us)
Sparse Core Ops, SparseCore 0:
  17.0 33.2 all-reduce.9
  255.5 106.9 all-reduce.11
  383.2 37.2 all-reduce.13
  425.1 117.3 all-reduce.17
  548.5 88.5 all-reduce.15
where the time goes:
time: 656 us; the launch traced here: 653 us
  waiting for transfers between devices  370 us (56%)
  blocking collectives  91.7 us (14%)
  local copies, waits for them, and re-layouts  63 us (10%)
  matrix products  51.2 us (8%)
  starting transfers between devices  33.4 us (5%)
  other arithmetic  28.9 us (4%)
  between operations  14.4 us (2%)
    psum x2, waiting for transfers between devices, local(): lax.psum((qkv_grad, qv_bias_grad, proj_grad, proj_bias_grad, norm1_gain_g...  207 us
    psum x1, blocking collectives, local(): row_back = lax.psum(home_local, 'tensor').astype(jnp.bfloat16)  91.7 us
    all_to_all x1, waiting for transfers between devices, local(): lax.all_to_all(part_out, 'dp', split_axis=0, concat_axis=0, tiled=True)  43.2 us
    all_to_all x1, waiting for transfers between devices, local(): lax.all_to_all(row_part, 'dp', split_axis=0, concat_axis=0, tiled=True)  35.9 us
    psum x1, waiting for transfers between devices, local(): middle = x_in + lax.psum(attn_part, 'tensor') + proj_bias  31.3 us
    psum x1, waiting for transfers between devices, local(): hidden1_grad = lax.psum(hidden1_part, 'tensor')  18.3 us
    unnamed x101, local copies, waits for them, and re-layouts  18.2 us
    all_to_all x1, waiting for transfers between devices, local(): lax.all_to_all(send_grad_all, 'dp', split_axis=0, concat_axis=0, tiled=True)  16.6 us
  transfers between devices with their start and end apart: 9, of which 9 were waited for; matrix products, arithmetic and copies ran while one was open for 11% of the time, Pallas kernels for 0%

commit v1 on v0

v1 whole, which is shorter than its diff:
```python
import jax
import jax.numpy as jnp
from jax import lax
from jax.sharding import PartitionSpec as P

HEAD = 64
SEQ = 197
F32 = jnp.float32
BF16 = jnp.bfloat16

epsilon = 1e-06


def norm_parts(values):
    average = jnp.mean(values, axis=-1, keepdims=True)
    centred = values - average
    inverse = lax.rsqrt(jnp.mean(centred * centred, axis=-1, keepdims=True) + epsilon)
    return (centred * inverse, inverse)


def norm_back(inner_grad, normed, inverse):
    first_mean = jnp.mean(inner_grad, axis=-1, keepdims=True)
    second_mean = jnp.mean(inner_grad * normed, axis=-1, keepdims=True)
    return inverse * (inner_grad - first_mean - normed * second_mean)


def gelu_parts(pre_act):
    normal_cdf = 0.5 * (1.0 + lax.erf(pre_act * 0.7071067811865476))
    density = jnp.exp(-0.5 * pre_act * pre_act) * 0.3989422804014327
    return (pre_act * normal_cdf, normal_cdf + pre_act * density)


def dot(a, b, dims, out=F32):
    return lax.dot_general(a, b, (dims, ((), ())), preferred_element_type=out)


def nn(a, b):
    return dot(a, b, ((1,), (0,)))


def nt(a, b):
    return dot(a, b, ((1,), (1,)))


def tn(a, b):
    return dot(a, b, ((0,), (0,)))


def exact(a, b):
    return lax.dot_general(
        a,
        b,
        (((1,), (0,)), ((), ())),
        precision=lax.Precision.HIGHEST,
        preferred_element_type=F32,
    )


def swap(x):
    return lax.ppermute(x, "tensor", [(0, 1), (1, 0)])


def across(x, bit, count):
    return lax.ppermute(x, "dp", [(i, i ^ bit) for i in range(count)])


def in_order(plane, mine, other, axis):
    first = jnp.where(plane == 0, mine, other)
    second = jnp.where(plane == 0, other, mine)
    return jnp.concatenate([first, second], axis=axis)


def half_of(plane, x, which):
    width = x.shape[-1] // 2
    low, high = x[..., :width], x[..., width:]
    return jnp.where((plane == which), low, high)


def reduce_pieces(total, order, count):
    size = total.shape[0] // count
    live = {r: total[r * size : (r + 1) * size] for r in range(count)}
    for bit in order:
        outgoing = [r for r in sorted(live) if r & bit]
        keep = [r for r in sorted(live) if not r & bit]
        sent = jnp.concatenate([live[r] for r in outgoing], axis=0).astype(BF16)
        got = across(sent, bit, count).astype(F32)
        live = {r: live[r] + got[i * size : (i + 1) * size] for i, r in enumerate(keep)}
    return live[0].astype(BF16)


def spread_pieces(piece, order, count):
    names, held = [0], piece
    for bit in order:
        got = across(held, bit, count)
        held = jnp.concatenate([held, got], axis=0)
        names = names + [r | bit for r in names]
    return held, names


def local(
    inputs,
    norm1_gain,
    norm1_bias,
    qkv_weight,
    qv_bias,
    proj_weight,
    proj_bias,
    norm2_gain,
    norm2_bias,
    router,
    expert_in,
    expert_in_bias,
    expert_out,
    expert_out_bias,
    routes,
    cotangent,
):
    tok_count = inputs.shape[0]
    feat_dim = inputs.shape[1]
    half_dim = feat_dim // 2
    head_cols = qkv_weight.shape[2]
    heads_here = head_cols // HEAD
    images = tok_count // SEQ
    experts = router.shape[1]
    sources = lax.axis_size("dp")
    group_size = sources // experts
    capacity = max(2, (10 * tok_count + 3 * experts - 1) // (3 * experts))
    slots = (capacity + 3 + 15) // 16 * 16
    score_scale = HEAD ** (-0.5)
    plane = lax.axis_index("tensor")
    me = lax.axis_index("dp")
    own_expert = me // group_size
    in_weight, out_weight = expert_in[0], expert_out[0]

    expert_ids = jnp.arange(experts, dtype=jnp.int32)
    slot_ids = jnp.arange(slots, dtype=jnp.int32)
    all_ids = jnp.arange(experts * slots, dtype=jnp.int32)
    pick = [(routes[:, k : k + 1] == expert_ids[None, :]) for k in range(2)]
    named = (pick[0] | pick[1]).astype(BF16)
    before = (
        jnp.arange(tok_count)[:, None] > jnp.arange(tok_count)[None, :]
    ).astype(BF16)
    earlier = nn(before, named)
    rank = [
        jnp.sum(jnp.where(pick[k], earlier, 0.0), axis=1, keepdims=True).astype(jnp.int32)
        for k in range(2)
    ]
    place = [routes[:, k : k + 1] * slots + rank[k] for k in range(2)]
    onehot = ((place[0] == all_ids[None, :]) | (place[1] == all_ids[None, :])).astype(BF16)
    rank_hot = [(rank[k] == slot_ids[None, :]) for k in range(2)]
    pick_low = [pick[k].astype(BF16) for k in range(2)]
    partner = [
        jnp.where(rank_hot[k], routes[:, 1 - k : 2 - k].astype(F32), 0.0).astype(BF16)
        for k in range(2)
    ]
    partner_map = tn(pick_low[0], partner[0]) + tn(pick_low[1], partner[1])

    cot_half = half_of(plane, cotangent, 0)
    cot_send = tn(onehot, cot_half).astype(BF16).reshape(experts, slots, half_dim)
    note = jnp.pad(partner_map.astype(BF16), ((0, 0), (0, half_dim - slots)))[:, None, :]
    cot_send = jnp.where(slot_ids[None, :, None] == slots - 1, note, cot_send)
    cot_send = jnp.repeat(cot_send, group_size, axis=0)
    cot_mine = lax.all_to_all(cot_send, "dp", split_axis=0, concat_axis=0, tiled=True)
    cot_mine = cot_mine.reshape(-1, half_dim)
    cot_other = swap(cot_mine)
    proj_other = swap(proj_weight)
    proj_full = in_order(plane, proj_weight, proj_other, 0)

    x_in = inputs.astype(F32)
    normed1, inverse1 = norm_parts(x_in)
    hidden1 = (normed1 * norm1_gain + norm1_bias).astype(BF16)
    projected = jnp.einsum("td,jde->jte", hidden1, qkv_weight, preferred_element_type=F32)
    bias_rows = jnp.stack([qv_bias[0], jnp.zeros_like(qv_bias[0]), qv_bias[1]])
    projected = (projected + bias_rows[:, None, :]).astype(BF16)
    heads_view = projected.reshape(3, images, SEQ, heads_here, HEAD)
    queries, key_vals, values_in = (heads_view[0], heads_view[1], heads_view[2])
    scores = (
        jnp.einsum("bqhd,bkhd->bhqk", queries, key_vals, preferred_element_type=F32)
        * score_scale
    )
    row_max = jnp.max(scores, axis=-1, keepdims=True)
    exp_scores = jnp.exp(scores - row_max)
    row_total = jnp.sum(exp_scores, axis=-1, keepdims=True)
    prob_vals = exp_scores / row_total
    prob_low = prob_vals.astype(BF16)
    attended = jnp.einsum("bhqk,bkhd->bqhd", prob_low, values_in, preferred_element_type=F32)
    attended = attended.reshape(tok_count, head_cols).astype(BF16)
    attended_all = in_order(plane, attended, swap(attended), 1)
    middle = x_in + nn(attended_all, proj_full) + proj_bias
    normed2, inverse2 = norm_parts(middle)
    hidden2 = (normed2 * norm2_gain + norm2_bias).astype(BF16)

    send = tn(onehot, hidden2).astype(BF16).reshape(experts, slots, feat_dim)
    send = jnp.repeat(send, group_size, axis=0)
    arrived = lax.all_to_all(send, "dp", split_axis=0, concat_axis=0, tiled=True)
    arrived = arrived.reshape(-1, feat_dim)

    logits = nn(hidden2, router)
    chosen = [jnp.sum(jnp.where(pick[k], logits, 0.0), axis=1, keepdims=True) for k in range(2)]
    chosen_max = jnp.maximum(chosen[0], chosen[1])
    chosen_exp = [jnp.exp(chosen[k] - chosen_max) for k in range(2)]
    chosen_sum = chosen_exp[0] + chosen_exp[1]
    gate_vals = [chosen_exp[k] / chosen_sum for k in range(2)]
    gate_map = jnp.where(pick[0], gate_vals[0], 0.0) + jnp.where(pick[1], gate_vals[1], 0.0)
    grad_out = cotangent.astype(F32)
    row_grad = [(gate_vals[k] * grad_out).astype(BF16) for k in range(2)]
    out_bias_grad = tn(pick_low[0], row_grad[0]) + tn(pick_low[1], row_grad[1])

    note_rows = jnp.where(plane == 0, cot_mine, cot_other).reshape(sources, slots, half_dim)
    other_expert = note_rows[:, slots - 1, :slots].reshape(-1, 1).astype(jnp.int32)
    real_slot = (jnp.arange(sources * slots, dtype=jnp.int32)[:, None] % slots) < capacity
    row_logits = nn(arrived, router)
    own_logit = jnp.sum(
        jnp.where(expert_ids[None, :] == own_expert, row_logits, 0.0), axis=1, keepdims=True
    )
    other_logit = jnp.sum(
        jnp.where(expert_ids[None, :] == other_expert, row_logits, 0.0), axis=1, keepdims=True
    )
    top_logit = jnp.maximum(own_logit, other_logit)
    own_exp = jnp.exp(own_logit - top_logit)
    row_gate = own_exp / (own_exp + jnp.exp(other_logit - top_logit))
    row_gate = jnp.where(real_slot, row_gate, 0.0)
    cot_rows = in_order(plane, cot_mine, cot_other, 1)
    grad_rows = (row_gate * cot_rows.astype(F32)).astype(BF16)

    pre_act = nn(arrived, in_weight) + expert_in_bias[0]
    activ_vals, gelu_slope = gelu_parts(pre_act)
    activ_low = activ_vals.astype(BF16)
    act_grad = nt(grad_rows, out_weight) * gelu_slope
    in_bias_grad = jnp.sum(act_grad, axis=0)
    act_low = act_grad.astype(BF16)
    row_part = nt(act_low, in_weight)
    part_out = nn(activ_low, out_weight)

    inner_part = jnp.sum(cot_rows.astype(F32) * part_out, axis=1).reshape(sources, slots)
    inner_all = inner_part + swap(inner_part)
    row_half = half_of(plane, row_part, 0) + swap(half_of(plane, row_part, 1).astype(BF16)).astype(F32)
    gated_out = row_gate * part_out
    out_half = half_of(plane, gated_out, 0) + swap(half_of(plane, gated_out, 1).astype(BF16)).astype(F32)
    inner_high = inner_all.astype(BF16)
    inner_low = (inner_all - inner_high.astype(F32)).astype(BF16)

    def widen(x):
        return jnp.pad(x, ((0, 0), (0, half_dim - slots)))[:, None, :]

    row_send = row_half.astype(BF16).reshape(sources, slots, half_dim)
    row_send = jnp.where(slot_ids[None, :, None] == slots - 1, widen(inner_high), row_send)
    row_send = jnp.where(slot_ids[None, :, None] == slots - 2, widen(inner_low), row_send)
    row_back = lax.all_to_all(row_send, "dp", split_axis=0, concat_axis=0, tiled=True)
    out_send = out_half.astype(BF16).reshape(sources, slots, half_dim)
    out_back = lax.all_to_all(out_send, "dp", split_axis=0, concat_axis=0, tiled=True)
    out_weight_grad = tn(activ_low, grad_rows)
    in_weight_grad = tn(arrived, act_low)

    def over_group(x):
        if group_size == 1:
            return x
        shape = (experts, group_size) + x.shape[1:]
        return jnp.sum(x.reshape(shape).astype(F32), axis=1).astype(BF16)

    inner_high = row_back[:, slots - 1, :slots].reshape(experts, group_size, slots)
    inner_low = row_back[:, slots - 2, :slots].reshape(experts, group_size, slots)
    gate_grad = []
    for k in range(2):
        found = 0.0
        for g in range(group_size):
            found = found + nn(pick_low[k], inner_high[:, g]) + nn(pick_low[k], inner_low[:, g])
        found = jnp.sum(jnp.where(rank_hot[k], found, 0.0), axis=1, keepdims=True)
        bias_row = exact(pick[k].astype(F32), expert_out_bias)
        gate_grad.append(found + jnp.sum(bias_row * grad_out, axis=1, keepdims=True))
    gate_mean = gate_vals[0] * gate_grad[0] + gate_vals[1] * gate_grad[1]
    chosen_grad = [gate_vals[k] * (gate_grad[k] - gate_mean) for k in range(2)]
    logit_grad = (
        jnp.where(pick[0], chosen_grad[0], 0.0) + jnp.where(pick[1], chosen_grad[1], 0.0)
    ).astype(BF16)
    row_home = nn(onehot, over_group(row_back).reshape(-1, half_dim)).astype(BF16)
    row_home = in_order(plane, row_home, swap(row_home), 1).astype(F32)
    hidden2_grad = row_home + nt(logit_grad, router)
    router_grad = tn(logit_grad, hidden2)
    norm2_gain_grad = jnp.sum(hidden2_grad * normed2, axis=0)
    norm2_bias_grad = jnp.sum(hidden2_grad, axis=0)
    middle_grad = grad_out + norm_back(hidden2_grad * norm2_gain, normed2, inverse2)
    proj_bias_grad = jnp.sum(middle_grad, axis=0)
    middle_low = middle_grad.astype(BF16)

    out_home = nn(onehot, over_group(out_back).reshape(-1, half_dim))
    bias_home = exact(gate_map, half_of(plane, expert_out_bias, 0))
    out_own = (half_of(plane, middle, 0) + out_home + bias_home).astype(BF16)
    output = in_order(plane, out_own, swap(out_own), 1)

    def shuffle(width):
        chunk = width // sources
        rows = jnp.arange(width, dtype=jnp.int32)[:, None]
        cols = jnp.arange(width, dtype=jnp.int32)[None, :]
        return (
            ((rows // chunk) == jnp.bitwise_xor(cols // chunk, me)) & (rows % chunk == cols % chunk)
        ).astype(BF16)

    bits = [1 << i for i in range(sources.bit_length() - 1)]
    first_order = bits
    second_order = bits[:1] + bits[2:] + bits[1:2]
    mix_in, mix_proj = shuffle(feat_dim), shuffle(head_cols)
    hidden1_mixed = nn(hidden1, mix_in).astype(BF16)
    attended_mixed = nn(attended, mix_proj).astype(BF16)
    proj_total = tn(attended_mixed, middle_low)
    attended_grad = nt(middle_low, proj_weight).astype(BF16)
    attended_grad = attended_grad.reshape(images, SEQ, heads_here, HEAD)
    value_grad = jnp.einsum("bhqk,bqhd->bkhd", prob_low, attended_grad, preferred_element_type=F32)
    prob_grad = jnp.einsum("bqhd,bkhd->bhqk", attended_grad, values_in, preferred_element_type=F32)
    score_grad = prob_vals * (prob_grad - jnp.sum(prob_vals * prob_grad, axis=-1, keepdims=True))
    score_low = score_grad.astype(BF16)
    query_grad = (
        jnp.einsum("bhqk,bkhd->bqhd", score_low, key_vals, preferred_element_type=F32)
        * score_scale
    )
    key_grad = (
        jnp.einsum("bhqk,bqhd->bkhd", score_low, queries, preferred_element_type=F32)
        * score_scale
    )
    proj_low = [
        g.reshape(tok_count, head_cols).astype(BF16) for g in (query_grad, key_grad, value_grad)
    ]
    proj_low = jnp.concatenate(proj_low, axis=1)
    qkv_total = tn(hidden1_mixed, proj_low)
    qv_sums = jnp.sum(proj_low.astype(F32), axis=0)
    hidden1_part = sum(
        nt(proj_low[:, j * head_cols : (j + 1) * head_cols], qkv_weight[j]) for j in range(3)
    ).astype(BF16)
    hidden1_grad = hidden1_part.astype(F32) + swap(hidden1_part).astype(F32)
    norm1_gain_grad = jnp.sum(hidden1_grad * normed1, axis=0)
    norm1_bias_grad = jnp.sum(hidden1_grad, axis=0)
    input_grad = middle_grad + norm_back(hidden1_grad * norm1_gain, normed1, inverse1)

    early = jnp.concatenate(
        [
            router_grad,
            out_bias_grad,
            norm2_gain_grad[None],
            norm2_bias_grad[None],
            proj_bias_grad[None],
        ],
        axis=0,
    )
    early = lax.psum(early, "dp")
    router_grad, out_bias_grad = early[:experts].T, early[experts : 2 * experts]
    norm2_gain_grad, norm2_bias_grad, proj_bias_grad = (early[2 * experts + i] for i in range(3))
    late = jnp.stack(
        [
            norm1_gain_grad,
            norm1_bias_grad,
            jnp.concatenate([qv_sums[:head_cols], qv_sums[2 * head_cols :]]),
        ]
    )
    for bit in bits:
        late = late + across(late, bit, sources)
    qv_bias_grad = late[2].reshape(2, head_cols)

    def all_sum(total, order, mix):
        held, names = spread_pieces(reduce_pieces(total, order, sources), order[::-1], sources)
        size = held.shape[0] // sources
        back = [names.index(r) for r in range(sources)]
        held = jnp.concatenate([held[i * size : (i + 1) * size] for i in back], axis=0)
        return nn(mix, held)

    proj_grad = all_sum(proj_total, second_order, mix_proj)
    split = (3 * head_cols // 2 + 127) // 128 * 128
    qkv_sum = jnp.concatenate(
        [
            all_sum(qkv_total[:, :split], first_order, mix_in),
            all_sum(qkv_total[:, split:], second_order, mix_in),
        ],
        axis=1,
    )
    qkv_grad = jnp.stack(
        [qkv_sum[:, j * head_cols : (j + 1) * head_cols] for j in range(3)]
    )
    return (
        output,
        input_grad,
        late[0],
        late[1],
        qkv_grad,
        qv_bias_grad,
        proj_grad,
        proj_bias_grad,
        norm2_gain_grad,
        norm2_bias_grad,
        router_grad,
        in_weight_grad[None],
        in_bias_grad[None],
        out_weight_grad[None],
        out_bias_grad,
    )


def solution(mesh):
    return jax.shard_map(
        local,
        mesh=mesh,
        in_specs=(
            P("dp", None),
            P(),
            P(),
            P(None, None, "tensor"),
            P(None, "tensor"),
            P("tensor", None),
            P(),
            P(),
            P(),
            P(),
            P("dp", None, "tensor"),
            P("dp", "tensor"),
            P("dp", "tensor", None),
            P(),
            P("dp", None),
            P("dp", None),
        ),
        out_specs=(
            P("dp", None),
            P("dp", None),
            P(),
            P(),
            P(None, None, "tensor"),
            P(None, "tensor"),
            P("tensor", None),
            P(),
            P(),
            P(),
            P(),
            P("dp", None, "tensor"),
            P("dp", "tensor"),
            P("dp", "tensor", None),
            P(),
        ),
        check_vma=False,
    )
```

time: 656 us -> 407 us (0.62)
  waiting for transfers between devices: 370 us -> 178 us
  blocking collectives: 91.7 us -> 0 us
  starting transfers between devices: 33.4 us -> 67 us
  matrix products: 51.2 us -> 63.7 us
  local copies, waits for them, and re-layouts: 63 us -> 51.7 us
    psum x5 -> x1, waiting for transfers between devices: 265 us -> 84 us  [local(): early = lax.psum(early, 'dp')]
    psum x1 -> x0, blocking collectives: 91.7 us -> none  [local(): row_back = lax.psum(home_local, 'tensor').astype(jnp.bfloat16)]
    all_to_all x4, waiting for transfers between devices: 105 us -> 26.2 us  [the longest x1 13.7 us: local(): lax.all_to_all(cot_send, 'dp', split_axis=0, concat_axis=0, tiled=True)]
    ppermute x0 -> x37, waiting for transfers between devices: none -> 67.9 us  [the longest x9 36.6 us: swap(): return lax.ppermute(x, 'tensor', [(0, 1), (1, 0)])]
    ppermute x0 -> x37, starting transfers between devices: none -> 43.4 us  [the longest x28 31.4 us: across(): return lax.ppermute(x, 'dp', [(i, i ^ bit) for i in range(count)])]
    unnamed x101 -> x224, local copies, waits for them, and re-layouts: 18.2 us -> 34 us
    all_to_all x4, starting transfers between devices: 33 us -> 23.4 us  [the longest x1 7.06 us: local(): lax.all_to_all(row_send, 'dp', split_axis=0, concat_axis=0, tiled=True)]
    select_n x1 -> x10, other arithmetic: 0.01 us -> 8.47 us  [the longest x4 3.29 us: in_order(): first = jnp.where(plane == 0, mine, other)]
  transfers between devices with their start and end apart: 9 -> 42, of which waited for: 9 -> 23; matrix products, arithmetic and copies ran while one was open for 11% -> 27% of each run, Pallas kernels for 0% -> 0%
where the time goes in v1:
time: 407 us; the launch traced here: 405 us
  waiting for transfers between devices  178 us (44%)
  starting transfers between devices  67 us (16%)
  matrix products  63.7 us (16%)
  local copies, waits for them, and re-layouts  51.7 us (13%)
  other arithmetic  28.4 us (7%)
  between operations  15.9 us (4%)
    psum x1, waiting for transfers between devices, local(): early = lax.psum(early, 'dp')  84 us
    dot_general x33, matrix products, dot(): return lax.dot_general(a, b, (dims, ((), ())), preferred_element_type=out)  49.4 us
    ppermute x9, waiting for transfers between devices, swap(): return lax.ppermute(x, 'tensor', [(0, 1), (1, 0)])  36.6 us
    unnamed x224, local copies, waits for them, and re-layouts  34 us
    ppermute x28, starting transfers between devices, across(): return lax.ppermute(x, 'dp', [(i, i ^ bit) for i in range(count)])  31.4 us
    ppermute x28, waiting for transfers between devices, across(): return lax.ppermute(x, 'dp', [(i, i ^ bit) for i in range(count)])  31.3 us
    all_to_all x1, waiting for transfers between devices, local(): lax.all_to_all(cot_send, 'dp', split_axis=0, concat_axis=0, tiled=True)  13.7 us
    ppermute x9, starting transfers between devices, swap(): return lax.ppermute(x, 'tensor', [(0, 1), (1, 0)])  12 us
  transfers between devices with their start and end apart: 42, of which 23 were waited for; matrix products, arithmetic and copies ran while one was open for 27% of the time, Pallas kernels for 0%

profile of v1, /device:TPU:0, one launch (start us, length us, event | category | flops | bytes accessed | tf_op | source)
XLA Modules:
  0.0 404.8 jit_solution(579323102455288849)
XLA Ops:
  7.2 3.0 collective-permute-start.1
  13.5 2.3 fusion.22
  21.4 5.7 %collective-permute-done = bf16[197,384]{1,0:T(8,128)(2,1)} collective-permute-done((bf16[197,384]{1,0:T(8,128)(2,1)}, bf16[197,384]{1,0:T(8,128)(2,1)}, u32[]{:S(2)}, u32[]{:S(2)}) %collective-permute-start) | collective-permute-done | bytes 151328 | tf_op jit(solution)/shard_map/ppermute | solution.py:60
  34.3 6.1 %all-to-all-start.1 = ((bf16[16,48,384]{2,1,0:T(8,128)(2,1)}), bf16[16,48,384]{2,1,0:T(8,128)(2,1)S(1)}, u32[]{:S(2)}, u32[]{:S(2)}) async-start(bf16[16,48,384]{2,1,0:T(8,128)(2,1)} %broadcast_select_fusion), calls=%async_computation.1 | async-start | bytes 1179648 | tf_op jit(solution)/shard_map/all_to_all | solution.py:163
  42.3 13.7 %all-to-all-done.1 = bf16[16,48,384]{2,1,0:T(8,128)(2,1)S(1)} async-done(((bf16[16,48,384]{2,1,0:T(8,128)(2,1)}), bf16[16,48,384]{2,1,0:T(8,128)(2,1)S(1)}, u32[]{:S(2)}, u32[]{:S(2)}) %all-to-all-start.1) | async-done | bytes 589856 | tf_op jit(solution)/shard_map/all_to_all | solution.py:163
  56.8 4.4 %all-to-all-start = ((bf16[16,48,768]{2,1,0:T(8,128)(2,1)}), bf16[16,48,768]{2,1,0:T(8,128)(2,1)S(1)}, u32[]{:S(2)}, u32[]{:S(2)}) async-start(bf16[16,48,768]{2,1,0:T(8,128)(2,1)} %bitcast.139), calls=%async_computation | async-start | bytes 2359296 | tf_op jit(solution)/shard_map/all_to_all | solution.py:195
  70.1 8.3 %collective-permute-done.2 = bf16[768,384]{1,0:T(8,128)(2,1)S(1)} collective-permute-done((bf16[768,384]{1,0:T(8,128)(2,1)}, bf16[768,384]{1,0:T(8,128)(2,1)S(1)}, u32[]{:S(2)}, u32[]{:S(2)}) %collective-permute-start.2) | collective-permute-done | bytes 589856 | tf_op jit(solution)/shard_map/ppermute | solution.py:60
  81.9 4.5 %all-to-all-done = bf16[16,48,768]{2,1,0:T(8,128)(2,1)S(1)} async-done(((bf16[16,48,768]{2,1,0:T(8,128)(2,1)}), bf16[16,48,768]{2,1,0:T(8,128)(2,1)S(1)}, u32[]{:S(2)}, u32[]{:S(2)}) %all-to-all-start) | async-done | bytes 1179680 | tf_op jit(solution)/shard_map/all_to_all | solution.py:195
  87.7 3.4 multiply_convert_fusion
  91.1 4.9 %fusion.244 = (f32[1536]{0:T(1024)}, bf16[768,1536]{1,0:T(8,128)(2,1)S(1)}) fusion(f32[768,1536]{1,0:T(8,128)S(1)} %get-tuple-element.150, f32[1536]{0:T(1024)S(1)} %copy-done.54, bf16[1,1536,768]{2,1,0:T(8,128)(2,1)S(1)} %copy-done.77, f32[768]{0:T(1024)S(1)} %fusion.190, bf16[768,384]{1,0:T(8,128)(2,1)S(1)} %copy-done.27, bf16[768,384]{1,0:T(8,128)(2,1)S(1)} %copy-done.25), kind=kOutput, calls=%fused_computation.487 | convolution fusion | flops 1829632512 | bytes 10632192 | tf_op jit(solution)/shard_map/dot_general | solution.py:34
  100.7 2.8 fusion.6
  104.7 10.8 %collective-permute-done.5 = f32[16,48]{1,0:T(8,128)S(1)} collective-permute-done((f32[16,48]{1,0:T(8,128)S(1)}, f32[16,48]{1,0:T(8,128)S(1)}, u32[]{:S(2)}, u32[]{:S(2)}) %collective-permute-start.5) | collective-permute-done | bytes 3104 | tf_op jit(solution)/shard_map/ppermute | solution.py:60
  118.6 7.1 %all-to-all-start.3 = ((bf16[16,48,384]{2,1,0:T(8,128)(2,1)}), bf16[16,48,384]{2,1,0:T(8,128)(2,1)}, u32[]{:S(2)}, u32[]{:S(2)}) async-start(bf16[16,48,384]{2,1,0:T(8,128)(2,1)} %select_select_fusion), calls=%async_computation.3 | async-start | bytes 1179648 | tf_op jit(solution)/shard_map/all_to_all | solution.py:249
  128.0 5.9 %convolution_bitcast_fusion.1 = f32[1,768,1536]{2,1,0:T(8,128)} fusion(bf16[768,768]{1,0:T(8,128)(2,1)S(1)} %bitcast.138, bf16[768,1536]{1,0:T(8,128)(2,1)} %copy-done.15), kind=kOutput, calls=%fused_computation.10 | convolution fusion | flops 1811939328 | bytes 8257536 | tf_op jit(solution)/shard_map/dot_general | solution.py:34
  133.9 7.6 %collective-permute-done.3 = bf16[768,384]{1,0:T(8,128)(2,1)S(1)} collective-permute-done((bf16[768,384]{1,0:T(8,128)(2,1)S(1)}, bf16[768,384]{1,0:T(8,128)(2,1)S(1)}, u32[]{:S(2)}, u32[]{:S(2)}) %collective-permute-start.3) | collective-permute-done | bytes 589856 | tf_op jit(solution)/shard_map/ppermute | solution.py:60
  142.5 5.8 %all-to-all-start.2 = ((bf16[16,48,384]{2,1,0:T(8,128)(2,1)}), bf16[16,48,384]{2,1,0:T(8,128)(2,1)S(1)}, u32[]{:S(2)}, u32[]{:S(2)}) async-start(bf16[16,48,384]{2,1,0:T(8,128)(2,1)} %bitcast.25), calls=%async_computation.2 | async-start | bytes 1179648 | tf_op jit(solution)/shard_map/all_to_all | solution.py:251
  148.7 6.0 %convolution_bitcast_fusion = f32[1,1536,768]{2,1,0:T(8,128)} fusion(bf16[768,1536]{1,0:T(8,128)(2,1)} %copy-done.79, f32[768]{0:T(1024)S(1)} %copy-done.60, bf16[768,384]{1,0:T(8,128)(2,1)S(1)} %copy-done.28, bf16[768,384]{1,0:T(8,128)(2,1)S(1)} %copy-done.26), kind=kOutput, calls=%fused_computation.9 | convolution fusion | flops 1815478272 | bytes 8260608 | tf_op jit(solution)/shard_map/dot_general | solution.py:34
  155.9 7.9 %all-to-all-done.2 = bf16[16,48,384]{2,1,0:T(8,128)(2,1)S(1)} async-done(((bf16[16,48,384]{2,1,0:T(8,128)(2,1)}), bf16[16,48,384]{2,1,0:T(8,128)(2,1)S(1)}, u32[]{:S(2)}, u32[]{:S(2)}) %all-to-all-start.2) | async-done | bytes 589856 | tf_op jit(solution)/shard_map/all_to_all | solution.py:251
  171.5 4.2 %collective-permute-done.7 = bf16[197,384]{1,0:T(8,128)(2,1)S(1)} collective-permute-done((bf16[197,384]{1,0:T(8,128)(2,1)S(1)}, bf16[197,384]{1,0:T(8,128)(2,1)S(1)}, u32[]{:S(2)}, u32[]{:S(2)}) %collective-permute-start.7) | collective-permute-done | bytes 151328 | tf_op jit(solution)/shard_map/ppermute | solution.py:60
  183.7 4.0 fusion.240
  222.3 3.5 concatenate.134
  227.6 84.0 %all-reduce.5.cloned.1.call-done = f32[35,768]{1,0:T(8,128)} async-done(((f32[35,768]{1,0:T(8,128)}), f32[35,768]{1,0:T(8,128)}) %all-reduce.5.cloned.1.call-update) | async-done | bytes 107536 | tf_op jit(solution)/shard_map/psum | solution.py:344
  317.0 3.8 collective-permute-start.30
  321.5 3.1 collective-permute-done.10
  325.8 2.6 collective-permute-done.11
  338.4 2.6 collective-permute-done.31
  352.2 2.4 collective-permute-start.24
  364.7 4.7 %collective-permute-done.16 = bf16[48,640]{1,0:T(8,128)(2,1)S(1)} collective-permute-done((bf16[48,640]{1,0:T(8,128)(2,1)S(1)}, bf16[48,640]{1,0:T(8,128)(2,1)S(1)}, u32[]{:S(2)}, u32[]{:S(2)}) %collective-permute-start.16) | collective-permute-done | bytes 61472 | tf_op jit(solution)/shard_map/ppermute | solution.py:64
  372.6 3.0 collective-permute-done.17
  377.1 3.4 collective-permute-done.18
  384.4 2.4 collective-permute-done.19
  392.6 5.3 %copy.73 = f32[3,768,384]{2,1,0:T(8,128)} copy(f32[3,768,384]{1,2,0:T(8,128)} %pad_maximum_fusion) | data formatting | bytes 7077888
  (443 shorter events, 149.6 us)
Async XLA Ops:
  7.2 21.0 %collective-permute-start.1 = (bf16[384,768]{1,0:T(8,128)(2,1)}, bf16[384,768]{1,0:T(8,128)(2,1)}, u32[]{:S(2)}, u32[]{:S(2)}) collective-permute-start(bf16[384,768]{1,0:T(8,128)(2,1)} %param.21), channel_id=1, source_target_pairs={{0,1},{1,0},{2,3},{3,2},{4,5},{5,4},{6,7},{7,6},{8,9},{9,8},{10,11... | collective-permute-start | bytes 1769480 | tf_op jit(solution)/shard_map/ppermute | solution.py:60
  21.3 5.9 %collective-permute-start = (bf16[197,384]{1,0:T(8,128)(2,1)}, bf16[197,384]{1,0:T(8,128)(2,1)}, u32[]{:S(2)}, u32[]{:S(2)}) collective-permute-start(bf16[197,384]{1,0:T(8,128)(2,1)} %copy.67), channel_id=1, source_target_pairs={{0,1},{1,0},{2,3},{3,2},{4,5},{5,4},{6,7},{7,6},{8,9},{9,8},{10,11... | collective-permute-start | bytes 453896 | tf_op jit(solution)/shard_map/ppermute | solution.py:60
  34.3 21.7 %all-to-all-start.1 = ((bf16[16,48,384]{2,1,0:T(8,128)(2,1)}), bf16[16,48,384]{2,1,0:T(8,128)(2,1)S(1)}, u32[]{:S(2)}, u32[]{:S(2)}) async-start(bf16[16,48,384]{2,1,0:T(8,128)(2,1)} %broadcast_select_fusion), calls=%async_computation.1 | async-start | bytes 1179648 | tf_op jit(solution)/shard_map/all_to_all | solution.py:163
  56.8 29.6 %all-to-all-start = ((bf16[16,48,768]{2,1,0:T(8,128)(2,1)}), bf16[16,48,768]{2,1,0:T(8,128)(2,1)S(1)}, u32[]{:S(2)}, u32[]{:S(2)}) async-start(bf16[16,48,768]{2,1,0:T(8,128)(2,1)} %bitcast.139), calls=%async_computation | async-start | bytes 2359296 | tf_op jit(solution)/shard_map/all_to_all | solution.py:195
  62.5 15.8 %collective-permute-start.2 = (bf16[768,384]{1,0:T(8,128)(2,1)}, bf16[768,384]{1,0:T(8,128)(2,1)S(1)}, u32[]{:S(2)}, u32[]{:S(2)}) collective-permute-start(bf16[768,384]{1,0:T(8,128)(2,1)} %bitcast.146), channel_id=1, source_target_pairs={{0,1},{1,0},{2,3},{3,2},{4,5},{5,4},{6,7},{7,6},{8,9},{9,8},{10,11... | collective-permute-start | bytes 1769480 | tf_op jit(solution)/shard_map/ppermute | solution.py:60
  99.1 16.5 %collective-permute-start.6 = (bf16[768,384]{1,0:T(8,128)(2,1)}, bf16[768,384]{1,0:T(8,128)(2,1)}, u32[]{:S(2)}, u32[]{:S(2)}) collective-permute-start(bf16[768,384]{1,0:T(8,128)(2,1)} %select_convert_fusion), channel_id=1, source_target_pairs={{0,1},{1,0},{2,3},{3,2},{4,5},{5,4},{6,7},{7,6},{8,9},{9,8},{10,11... | collective-permute-start | bytes 1769480 | tf_op jit(solution)/shard_map/ppermute | solution.py:60
  104.2 11.4 %collective-permute-start.5 = (f32[16,48]{1,0:T(8,128)S(1)}, f32[16,48]{1,0:T(8,128)S(1)}, u32[]{:S(2)}, u32[]{:S(2)}) collective-permute-start(f32[16,48]{1,0:T(8,128)S(1)} %reshape.482), channel_id=1, source_target_pairs={{0,1},{1,0},{2,3},{3,2},{4,5},{5,4},{6,7},{7,6},{8,9},{9,8},{10,11... | collective-permute-start | bytes 9224 | tf_op jit(solution)/shard_map/ppermute | solution.py:60
  118.6 23.9 %all-to-all-start.3 = ((bf16[16,48,384]{2,1,0:T(8,128)(2,1)}), bf16[16,48,384]{2,1,0:T(8,128)(2,1)}, u32[]{:S(2)}, u32[]{:S(2)}) async-start(bf16[16,48,384]{2,1,0:T(8,128)(2,1)} %select_select_fusion), calls=%async_computation.3 | async-start | bytes 1179648 | tf_op jit(solution)/shard_map/all_to_all | solution.py:249
  125.8 15.7 %collective-permute-start.3 = (bf16[768,384]{1,0:T(8,128)(2,1)S(1)}, bf16[768,384]{1,0:T(8,128)(2,1)S(1)}, u32[]{:S(2)}, u32[]{:S(2)}) collective-permute-start(bf16[768,384]{1,0:T(8,128)(2,1)S(1)} %select_convert_fusion.1), channel_id=1, source_target_pairs={{0,1},{1,0},{2,3},{3,2},{4,5},{5,4},{6,7},{7,6},{8,9},{9,8},{10,11... | collective-permute-start | bytes 1769480 | tf_op jit(solution)/shard_map/ppermute | solution.py:60
  142.5 21.3 %all-to-all-start.2 = ((bf16[16,48,384]{2,1,0:T(8,128)(2,1)}), bf16[16,48,384]{2,1,0:T(8,128)(2,1)S(1)}, u32[]{:S(2)}, u32[]{:S(2)}) async-start(bf16[16,48,384]{2,1,0:T(8,128)(2,1)} %bitcast.25), calls=%async_computation.2 | async-start | bytes 1179648 | tf_op jit(solution)/shard_map/all_to_all | solution.py:251
  148.4 163.3 %all-reduce.5.cloned.1.call-start = ((), (), s32[]{:S(2)}) async-start(), calls=%async_computation.4 | async-start | bytes 245760 | tf_op jit(solution)/shard_map/psum | solution.py:344
  166.3 59.5 %collective-permute-start.4 = (bf16[197,384]{1,0:T(8,128)(2,1)}, bf16[197,384]{1,0:T(8,128)(2,1)}, u32[]{:S(2)}, u32[]{:S(2)}) collective-permute-start(bf16[197,384]{1,0:T(8,128)(2,1)} %fusion.52), channel_id=1, source_target_pairs={{0,1},{1,0},{2,3},{3,2},{4,5},{5,4},{6,7},{7,6},{8,9},{9,8},{10,11... | collective-permute-start | bytes 453896 | tf_op jit(solution)/shard_map/ppermute | solution.py:60
  169.2 6.5 %collective-permute-start.7 = (bf16[197,384]{1,0:T(8,128)(2,1)S(1)}, bf16[197,384]{1,0:T(8,128)(2,1)S(1)}, u32[]{:S(2)}, u32[]{:S(2)}) collective-permute-start(bf16[197,384]{1,0:T(8,128)(2,1)S(1)} %convolution_convert_fusion.4), channel_id=1, source_target_pairs={{0,1},{1,0},{2,3},{3,2},{4,5},{5,4},{6,7},{7,6},{8,9},{9,8},{10,11... | collective-permute-start | bytes 453896 | tf_op jit(solution)/shard_map/ppermute | solution.py:60
  193.6 122.0 %collective-permute-start.8 = (bf16[197,768]{1,0:T(8,128)(2,1)S(1)}, bf16[197,768]{1,0:T(8,128)(2,1)S(1)}, u32[]{:S(2)}, u32[]{:S(2)}) collective-permute-start(bf16[197,768]{1,0:T(8,128)(2,1)S(1)} %fusion.23), channel_id=1, source_target_pairs={{0,1},{1,0},{2,3},{3,2},{4,5},{5,4},{6,7},{7,6},{8,9},{9,8},{10,11... | collective-permute-start | bytes 907784 | tf_op jit(solution)/shard_map/ppermute | solution.py:60
  205.4 131.8 %collective-permute-start.13 = (bf16[384,640]{1,0:T(8,128)(2,1)}, bf16[384,640]{1,0:T(8,128)(2,1)}, u32[]{:S(2)}, u32[]{:S(2)}) collective-permute-start(bf16[384,640]{1,0:T(8,128)(2,1)} %constant_dynamic-update-slice_fusion), channel_id=1, source_target_pairs={{0,2},{2,0},{4,6},{6,4},{8,10},{10,8},{12,14},{14,12},{16,18},{18,... | collective-permute-start | bytes 1474568 | tf_op jit(solution)/shard_map/ppermute | solution.py:64
  215.3 117.7 %collective-permute-start.21 = (bf16[384,512]{1,0:T(8,128)(2,1)}, bf16[384,512]{1,0:T(8,128)(2,1)}, u32[]{:S(2)}, u32[]{:S(2)}) collective-permute-start(bf16[384,512]{1,0:T(8,128)(2,1)} %constant_dynamic-update-slice_fusion.24), channel_id=1, source_target_pairs={{0,2},{2,0},{4,6},{6,4},{8,10},{10,8},{12,14},{14,12},{16,18},{18,... | collective-permute-start | bytes 1179656 | tf_op jit(solution)/shard_map/ppermute | solution.py:64
  221.6 93.0 %collective-permute-start.29 = (bf16[192,768]{1,0:T(8,128)(2,1)}, bf16[192,768]{1,0:T(8,128)(2,1)}, u32[]{:S(2)}, u32[]{:S(2)}) collective-permute-start(bf16[192,768]{1,0:T(8,128)(2,1)} %constant_dynamic-update-slice_fusion.48), channel_id=1, source_target_pairs={{0,2},{2,0},{4,6},{6,4},{8,10},{10,8},{12,14},{14,12},{16,18},{18,... | collective-permute-start | bytes 884744 | tf_op jit(solution)/shard_map/ppermute | solution.py:64
  317.0 18.6 %collective-permute-start.30 = (bf16[96,768]{1,0:T(8,128)(2,1)S(1)}, bf16[96,768]{1,0:T(8,128)(2,1)S(1)}, u32[]{:S(2)}, u32[]{:S(2)}) collective-permute-start(bf16[96,768]{1,0:T(8,128)(2,1)S(1)} %pad_maximum_fusion.13), channel_id=1, source_target_pairs={{0,8},{2,10},{4,12},{6,14},{8,0},{10,2},{12,4},{14,6},{16,24},{18,... | collective-permute-start | bytes 442376 | tf_op jit(solution)/shard_map/ppermute | solution.py:64
  334.2 12.1 %collective-permute-start.22 = (bf16[192,512]{1,0:T(8,128)(2,1)S(1)}, bf16[192,512]{1,0:T(8,128)(2,1)S(1)}, u32[]{:S(2)}, u32[]{:S(2)}) collective-permute-start(bf16[192,512]{1,0:T(8,128)(2,1)S(1)} %pad_maximum_fusion.11), channel_id=1, source_target_pairs={{0,8},{2,10},{4,12},{6,14},{8,0},{10,2},{12,4},{14,6},{16,24},{18,... | collective-permute-start | bytes 589832 | tf_op jit(solution)/shard_map/ppermute | solution.py:64
  335.7 5.3 %collective-permute-start.31 = (bf16[48,768]{1,0:T(8,128)(2,1)S(1)}, bf16[48,768]{1,0:T(8,128)(2,1)S(1)}, u32[]{:S(2)}, u32[]{:S(2)}) collective-permute-start(bf16[48,768]{1,0:T(8,128)(2,1)S(1)} %pad_maximum_fusion.19), channel_id=1, source_target_pairs={{0,16},{2,18},{4,20},{6,22},{8,24},{10,26},{12,28},{14,30},{16,0},... | collective-permute-start | bytes 221192 | tf_op jit(solution)/shard_map/ppermute | solution.py:64
  341.7 12.9 %collective-permute-start.14 = (bf16[192,640]{1,0:T(8,128)(2,1)S(1)}, bf16[192,640]{1,0:T(8,128)(2,1)S(1)}, u32[]{:S(2)}, u32[]{:S(2)}) collective-permute-start(bf16[192,640]{1,0:T(8,128)(2,1)S(1)} %pad_maximum_fusion.8), channel_id=1, source_target_pairs={{0,4},{2,6},{4,0},{6,2},{8,12},{10,14},{12,8},{14,10},{16,20},{18,... | collective-permute-start | bytes 737288 | tf_op jit(solution)/shard_map/ppermute | solution.py:64
  346.4 5.8 %collective-permute-start.23 = (bf16[96,512]{1,0:T(8,128)(2,1)S(1)}, bf16[96,512]{1,0:T(8,128)(2,1)S(1)}, u32[]{:S(2)}, u32[]{:S(2)}) collective-permute-start(bf16[96,512]{1,0:T(8,128)(2,1)S(1)} %pad_maximum_fusion.17), channel_id=1, source_target_pairs={{0,16},{2,18},{4,20},{6,22},{8,24},{10,26},{12,28},{14,30},{16,0},... | collective-permute-start | bytes 294920 | tf_op jit(solution)/shard_map/ppermute | solution.py:64
  350.1 9.3 %collective-permute-start.34 = (bf16[48,768]{1,0:T(8,128)(2,1)S(1)}, bf16[48,768]{1,0:T(8,128)(2,1)S(1)}, u32[]{:S(2)}, u32[]{:S(2)}) collective-permute-start(bf16[48,768]{1,0:T(8,128)(2,1)S(1)} %pad_maximum_fusion.20), channel_id=1, source_target_pairs={{0,16},{2,18},{4,20},{6,22},{8,24},{10,26},{12,28},{14,30},{16,0},... | collective-permute-start | bytes 221192 | tf_op jit(solution)/shard_map/ppermute | solution.py:64
  354.7 8.6 %collective-permute-start.15 = (bf16[96,640]{1,0:T(8,128)(2,1)S(1)}, bf16[96,640]{1,0:T(8,128)(2,1)S(1)}, u32[]{:S(2)}, u32[]{:S(2)}) collective-permute-start(bf16[96,640]{1,0:T(8,128)(2,1)S(1)} %pad_maximum_fusion.15), channel_id=1, source_target_pairs={{0,8},{2,10},{4,12},{6,14},{8,0},{10,2},{12,4},{14,6},{16,24},{18,... | collective-permute-start | bytes 368648 | tf_op jit(solution)/shard_map/ppermute | solution.py:64
  359.4 5.2 %collective-permute-start.35 = (bf16[96,768]{1,0:T(8,128)(2,1)S(1)}, bf16[96,768]{1,0:T(8,128)(2,1)S(1)}, u32[]{:S(2)}, u32[]{:S(2)}) collective-permute-start(bf16[96,768]{1,0:T(8,128)(2,1)S(1)} %pad_maximum_fusion.14), channel_id=1, source_target_pairs={{0,8},{2,10},{4,12},{6,14},{8,0},{10,2},{12,4},{14,6},{16,24},{18,... | collective-permute-start | bytes 442376 | tf_op jit(solution)/shard_map/ppermute | solution.py:64
  361.4 8.9 %collective-permute-start.26 = (bf16[96,512]{1,0:T(8,128)(2,1)S(1)}, bf16[96,512]{1,0:T(8,128)(2,1)S(1)}, u32[]{:S(2)}, u32[]{:S(2)}) collective-permute-start(bf16[96,512]{1,0:T(8,128)(2,1)S(1)} %pad_maximum_fusion.18), channel_id=1, source_target_pairs={{0,16},{2,18},{4,20},{6,22},{8,24},{10,26},{12,28},{14,30},{16,0},... | collective-permute-start | bytes 294920 | tf_op jit(solution)/shard_map/ppermute | solution.py:64
  363.4 6.0 %collective-permute-start.16 = (bf16[48,640]{1,0:T(8,128)(2,1)S(1)}, bf16[48,640]{1,0:T(8,128)(2,1)S(1)}, u32[]{:S(2)}, u32[]{:S(2)}) collective-permute-start(bf16[48,640]{1,0:T(8,128)(2,1)S(1)} %fusion.121), channel_id=1, source_target_pairs={{0,16},{2,18},{4,20},{6,22},{8,24},{10,26},{12,28},{14,30},{16,0},... | collective-permute-start | bytes 184328 | tf_op jit(solution)/shard_map/ppermute | solution.py:64
  364.6 18.1 %collective-permute-start.36 = (bf16[192,768]{1,0:T(8,128)(2,1)S(1)}, bf16[192,768]{1,0:T(8,128)(2,1)S(1)}, u32[]{:S(2)}, u32[]{:S(2)}) collective-permute-start(bf16[192,768]{1,0:T(8,128)(2,1)S(1)} %pad_maximum_fusion.7), channel_id=1, source_target_pairs={{0,2},{2,0},{4,6},{6,4},{8,10},{10,8},{12,14},{14,12},{16,18},{18,... | collective-permute-start | bytes 884744 | tf_op jit(solution)/shard_map/ppermute | solution.py:64
  370.0 5.6 %collective-permute-start.17 = (bf16[48,640]{1,0:T(8,128)(2,1)S(1)}, bf16[48,640]{1,0:T(8,128)(2,1)S(1)}, u32[]{:S(2)}, u32[]{:S(2)}) collective-permute-start(bf16[48,640]{1,0:T(8,128)(2,1)S(1)} %get-tuple-element.87), channel_id=1, source_target_pairs={{0,16},{2,18},{4,20},{6,22},{8,24},{10,26},{12,28},{14,30},{16,0},... | collective-permute-start | bytes 184328 | tf_op jit(solution)/shard_map/ppermute | solution.py:64
  370.4 6.6 %collective-permute-start.27 = (bf16[192,512]{1,0:T(8,128)(2,1)S(1)}, bf16[192,512]{1,0:T(8,128)(2,1)S(1)}, u32[]{:S(2)}, u32[]{:S(2)}) collective-permute-start(bf16[192,512]{1,0:T(8,128)(2,1)S(1)} %pad_maximum_fusion.12), channel_id=1, source_target_pairs={{0,8},{2,10},{4,12},{6,14},{8,0},{10,2},{12,4},{14,6},{16,24},{18,... | collective-permute-start | bytes 589832 | tf_op jit(solution)/shard_map/ppermute | solution.py:64
  377.0 9.9 %collective-permute-start.28 = (bf16[384,512]{1,0:T(8,128)(2,1)S(1)}, bf16[384,512]{1,0:T(8,128)(2,1)S(1)}, u32[]{:S(2)}, u32[]{:S(2)}) collective-permute-start(bf16[384,512]{1,0:T(8,128)(2,1)S(1)} %pad_maximum_fusion.5), channel_id=1, source_target_pairs={{0,2},{2,0},{4,6},{6,4},{8,10},{10,8},{12,14},{14,12},{16,18},{18,... | collective-permute-start | bytes 1179656 | tf_op jit(solution)/shard_map/ppermute | solution.py:64
  380.6 6.3 %collective-permute-start.19 = (bf16[192,640]{1,0:T(8,128)(2,1)S(1)}, bf16[192,640]{1,0:T(8,128)(2,1)S(1)}, u32[]{:S(2)}, u32[]{:S(2)}) collective-permute-start(bf16[192,640]{1,0:T(8,128)(2,1)S(1)} %pad_maximum_fusion.9), channel_id=1, source_target_pairs={{0,4},{2,6},{4,0},{6,2},{8,12},{10,14},{12,8},{14,10},{16,20},{18,... | collective-permute-start | bytes 737288 | tf_op jit(solution)/shard_map/ppermute | solution.py:64
  (90 other events, 753.9 us)
Sparse Core Ops, SparseCore 0:
  225.9 85.6 all-reduce.4

commit v2 on v1

--- a/solution.py
+++ b/solution.py
@@ -1,6 +1,8 @@
 import jax
 import jax.numpy as jnp
 from jax import lax
+from jax.experimental import pallas as pl
+from jax.experimental.pallas import tpu as pltpu
 from jax.sharding import PartitionSpec as P
 
 HEAD = 64
@@ -76,25 +78,65 @@
     return jnp.where((plane == which), low, high)
 
 
-def reduce_pieces(total, order, count):
-    size = total.shape[0] // count
-    live = {r: total[r * size : (r + 1) * size] for r in range(count)}
-    for bit in order:
-        outgoing = [r for r in sorted(live) if r & bit]
-        keep = [r for r in sorted(live) if not r & bit]
-        sent = jnp.concatenate([live[r] for r in outgoing], axis=0).astype(BF16)
-        got = across(sent, bit, count).astype(F32)
-        live = {r: live[r] + got[i * size : (i + 1) * size] for i, r in enumerate(keep)}
-    return live[0].astype(BF16)
-
-
-def spread_pieces(piece, order, count):
-    names, held = [0], piece
-    for bit in order:
-        got = across(held, bit, count)
-        held = jnp.concatenate([held, got], axis=0)
-        names = names + [r | bit for r in names]
-    return held, names
+def reduce_rounds(parts, orders, count):
+    def split(part):
+        middle = part.shape[0] // 2
+        return part[:middle], part[middle:]
+
+    both = jnp.concatenate([split(part)[1].astype(BF16) for part in parts], axis=1)
+    both = across(both, orders[0][0], count)
+    place = 0
+    held = []
+    for part in parts:
+        width = part.shape[1]
+        held.append(split(part)[0] + both[:, place : place + width].astype(F32))
+        place += width
+    for turn in range(1, len(orders[0])):
+        held = [
+            split(part)[0] + across(split(part)[1].astype(BF16), order[turn], count).astype(F32)
+            for part, order in zip(held, orders)
+        ]
+    return [part.astype(BF16) for part in held]
+
+
+def spread_rounds(parts, orders, count):
+    for turn in range(len(orders[0]) - 1, 0, -1):
+        parts = [
+            jnp.concatenate([part, across(part, order[turn], count)], axis=0)
+            for part, order in zip(parts, orders)
+        ]
+    mine = jnp.concatenate(parts, axis=1)
+    return mine, across(mine, orders[0][0], count)
+
+
+def finish_kernel(head_cols, width, mix_a, mix_b, mine, got, qkv_ref, proj_ref, small_ref):
+    rows = mine.shape[0]
+
+    def ordered(mix, start, size):
+        low = jnp.dot(mix[:, :rows], mine[:, start : start + size], preferred_element_type=F32)
+        high = jnp.dot(mix[:, rows:], got[:, start : start + size], preferred_element_type=F32)
+        return low + high
+
+    qkv_ref[0] = ordered(mix_a, 0, head_cols)
+    qkv_ref[1] = ordered(mix_a, head_cols, head_cols)
+    small_ref[...] = ordered(mix_a, 2 * head_cols, width)
+    start = 2 * head_cols + width
+    qkv_ref[2] = ordered(mix_b, start, head_cols)
+    proj_ref[...] = ordered(mix_b, start + head_cols, head_cols).T
+
+
+def finish(mix_a, mix_b, mine, got, head_cols, width):
+    feat_dim = mix_a.shape[0]
+    return pl.pallas_call(
+        lambda *refs: finish_kernel(head_cols, width, *refs),
+        out_shape=(
+            jax.ShapeDtypeStruct((3, feat_dim, head_cols), F32),
+            jax.ShapeDtypeStruct((head_cols, feat_dim), F32),
+            jax.ShapeDtypeStruct((feat_dim, width), F32),
+        ),
+        compiler_params=pltpu.CompilerParams(vmem_limit_bytes=48 << 20),
+        name="finish",
+    )(mix_a, mix_b, mine, got)
 
 
 def local(
@@ -160,12 +202,12 @@
     note = jnp.pad(partner_map.astype(BF16), ((0, 0), (0, half_dim - slots)))[:, None, :]
     cot_send = jnp.where(slot_ids[None, :, None] == slots - 1, note, cot_send)
     cot_send = jnp.repeat(cot_send, group_size, axis=0)
+    proj_other = swap(proj_weight)
+    proj_full = in_order(plane, proj_weight, proj_other, 0)
+
+    inputs, cot_send = lax.optimization_barrier((inputs, cot_send))
     cot_mine = lax.all_to_all(cot_send, "dp", split_axis=0, concat_axis=0, tiled=True)
     cot_mine = cot_mine.reshape(-1, half_dim)
-    cot_other = swap(cot_mine)
-    proj_other = swap(proj_weight)
-    proj_full = in_order(plane, proj_weight, proj_other, 0)
-
     x_in = inputs.astype(F32)
     normed1, inverse1 = norm_parts(x_in)
     hidden1 = (normed1 * norm1_gain + norm1_bias).astype(BF16)
@@ -185,13 +227,15 @@
     prob_low = prob_vals.astype(BF16)
     attended = jnp.einsum("bhqk,bkhd->bqhd", prob_low, values_in, preferred_element_type=F32)
     attended = attended.reshape(tok_count, head_cols).astype(BF16)
-    attended_all = in_order(plane, attended, swap(attended), 1)
+    attended_other, cot_mine = lax.optimization_barrier((swap(attended), cot_mine))
+    attended_all = in_order(plane, attended, attended_other, 1)
     middle = x_in + nn(attended_all, proj_full) + proj_bias
     normed2, inverse2 = norm_parts(middle)
     hidden2 = (normed2 * norm2_gain + norm2_bias).astype(BF16)
 
     send = tn(onehot, hidden2).astype(BF16).reshape(experts, slots, feat_dim)
     send = jnp.repeat(send, group_size, axis=0)
+    cot_other = swap(cot_mine)
     arrived = lax.all_to_all(send, "dp", split_axis=0, concat_axis=0, tiled=True)
     arrived = arrived.reshape(-1, feat_dim)
 
@@ -204,7 +248,7 @@
     gate_map = jnp.where(pick[0], gate_vals[0], 0.0) + jnp.where(pick[1], gate_vals[1], 0.0)
     grad_out = cotangent.astype(F32)
     row_grad = [(gate_vals[k] * grad_out).astype(BF16) for k in range(2)]
-    out_bias_grad = tn(pick_low[0], row_grad[0]) + tn(pick_low[1], row_grad[1])
+    out_bias_grad = tn(row_grad[0], pick_low[0]) + tn(row_grad[1], pick_low[1])
 
     note_rows = jnp.where(plane == 0, cot_mine, cot_other).reshape(sources, slots, half_dim)
     other_expert = note_rows[:, slots - 1, :slots].reshape(-1, 1).astype(jnp.int32)
@@ -232,22 +276,19 @@
     row_part = nt(act_low, in_weight)
     part_out = nn(activ_low, out_weight)
 
-    inner_part = jnp.sum(cot_rows.astype(F32) * part_out, axis=1).reshape(sources, slots)
-    inner_all = inner_part + swap(inner_part)
-    row_half = half_of(plane, row_part, 0) + swap(half_of(plane, row_part, 1).astype(BF16)).astype(F32)
-    gated_out = row_gate * part_out
-    out_half = half_of(plane, gated_out, 0) + swap(half_of(plane, gated_out, 1).astype(BF16)).astype(F32)
-    inner_high = inner_all.astype(BF16)
-    inner_low = (inner_all - inner_high.astype(F32)).astype(BF16)
+    inner = jnp.sum(cot_rows.astype(F32) * part_out, axis=1).reshape(sources, slots)
+    inner_high = inner.astype(BF16)
+    inner_low = (inner - inner_high.astype(F32)).astype(BF16)
 
     def widen(x):
-        return jnp.pad(x, ((0, 0), (0, half_dim - slots)))[:, None, :]
-
-    row_send = row_half.astype(BF16).reshape(sources, slots, half_dim)
+        return jnp.pad(x, ((0, 0), (0, feat_dim - slots)))[:, None, :]
+
+    row_send = row_part.astype(BF16).reshape(sources, slots, feat_dim)
     row_send = jnp.where(slot_ids[None, :, None] == slots - 1, widen(inner_high), row_send)
     row_send = jnp.where(slot_ids[None, :, None] == slots - 2, widen(inner_low), row_send)
     row_back = lax.all_to_all(row_send, "dp", split_axis=0, concat_axis=0, tiled=True)
-    out_send = out_half.astype(BF16).reshape(sources, slots, half_dim)
+    out_send = (row_gate * part_out).astype(BF16).reshape(sources, slots, feat_dim)
+    out_send, row_back = lax.optimization_barrier((out_send, row_back))
     out_back = lax.all_to_all(out_send, "dp", split_axis=0, concat_axis=0, tiled=True)
     out_weight_grad = tn(activ_low, grad_rows)
     in_weight_grad = tn(arrived, act_low)
@@ -258,13 +299,12 @@
         shape = (experts, group_size) + x.shape[1:]
         return jnp.sum(x.reshape(shape).astype(F32), axis=1).astype(BF16)
 
-    inner_high = row_back[:, slots - 1, :slots].reshape(experts, group_size, slots)
-    inner_low = row_back[:, slots - 2, :slots].reshape(experts, group_size, slots)
+    inner = row_back[:, slots - 2 :, :slots].astype(F32)
+    inner = jnp.sum(inner.reshape(experts, 2 * group_size, slots), axis=1)
+    inner = inner + swap(inner)
     gate_grad = []
     for k in range(2):
-        found = 0.0
-        for g in range(group_size):
-            found = found + nn(pick_low[k], inner_high[:, g]) + nn(pick_low[k], inner_low[:, g])
+        found = exact(pick[k].astype(F32), inner)
         found = jnp.sum(jnp.where(rank_hot[k], found, 0.0), axis=1, keepdims=True)
         bias_row = exact(pick[k].astype(F32), expert_out_bias)
         gate_grad.append(found + jnp.sum(bias_row * grad_out, axis=1, keepdims=True))
@@ -273,36 +313,32 @@
     logit_grad = (
         jnp.where(pick[0], chosen_grad[0], 0.0) + jnp.where(pick[1], chosen_grad[1], 0.0)
     ).astype(BF16)
-    row_home = nn(onehot, over_group(row_back).reshape(-1, half_dim)).astype(BF16)
-    row_home = in_order(plane, row_home, swap(row_home), 1).astype(F32)
+    row_home = nn(onehot, over_group(row_back).reshape(-1, feat_dim)).astype(BF16)
+    row_home = row_home.astype(F32) + swap(row_home).astype(F32)
     hidden2_grad = row_home + nt(logit_grad, router)
-    router_grad = tn(logit_grad, hidden2)
     norm2_gain_grad = jnp.sum(hidden2_grad * normed2, axis=0)
     norm2_bias_grad = jnp.sum(hidden2_grad, axis=0)
     middle_grad = grad_out + norm_back(hidden2_grad * norm2_gain, normed2, inverse2)
     proj_bias_grad = jnp.sum(middle_grad, axis=0)
     middle_low = middle_grad.astype(BF16)
 
-    out_home = nn(onehot, over_group(out_back).reshape(-1, half_dim))
-    bias_home = exact(gate_map, half_of(plane, expert_out_bias, 0))
-    out_own = (half_of(plane, middle, 0) + out_home + bias_home).astype(BF16)
-    output = in_order(plane, out_own, swap(out_own), 1)
-
-    def shuffle(width):
-        chunk = width // sources
-        rows = jnp.arange(width, dtype=jnp.int32)[:, None]
-        cols = jnp.arange(width, dtype=jnp.int32)[None, :]
-        return (
-            ((rows // chunk) == jnp.bitwise_xor(cols // chunk, me)) & (rows % chunk == cols % chunk)
-        ).astype(BF16)
-
     bits = [1 << i for i in range(sources.bit_length() - 1)]
-    first_order = bits
-    second_order = bits[:1] + bits[2:] + bits[1:2]
-    mix_in, mix_proj = shuffle(feat_dim), shuffle(head_cols)
-    hidden1_mixed = nn(hidden1, mix_in).astype(BF16)
-    attended_mixed = nn(attended, mix_proj).astype(BF16)
-    proj_total = tn(attended_mixed, middle_low)
+    orders = [bits, bits[:1] + bits[2:] + bits[1:2]]
+    chunk = feat_dim // sources
+
+    def mixer(order):
+        rows = jnp.arange(feat_dim, dtype=jnp.int32)[:, None]
+        cols = jnp.arange(feat_dim, dtype=jnp.int32)[None, :]
+        spot = cols // chunk
+        piece = jnp.zeros_like(spot)
+        for i, bit in enumerate(order):
+            piece = piece | jnp.where((spot >> (len(order) - 1 - i)) & 1, bit, 0)
+        return ((rows // chunk == (piece ^ me)) & (rows % chunk == cols % chunk)).astype(BF16)
+
+    mix_a, mix_b = mixer(orders[0]), mixer(orders[1])
+    hidden1_a, hidden1_b = nn(hidden1, mix_a).astype(BF16), nn(hidden1, mix_b).astype(BF16)
+    middle_b = nn(middle_low, mix_b).astype(BF16)
+    proj_total = tn(middle_b, attended)
     attended_grad = nt(middle_low, proj_weight).astype(BF16)
     attended_grad = attended_grad.reshape(images, SEQ, heads_here, HEAD)
     value_grad = jnp.einsum("bhqk,bqhd->bkhd", prob_low, attended_grad, preferred_element_type=F32)
@@ -321,7 +357,8 @@
         g.reshape(tok_count, head_cols).astype(BF16) for g in (query_grad, key_grad, value_grad)
     ]
     proj_low = jnp.concatenate(proj_low, axis=1)
-    qkv_total = tn(hidden1_mixed, proj_low)
+    qk_total = tn(hidden1_a, proj_low[:, : 2 * head_cols])
+    v_total = tn(hidden1_b, proj_low[:, 2 * head_cols :])
     qv_sums = jnp.sum(proj_low.astype(F32), axis=0)
     hidden1_part = sum(
         nt(proj_low[:, j * head_cols : (j + 1) * head_cols], qkv_weight[j]) for j in range(3)
@@ -331,19 +368,19 @@
     norm1_bias_grad = jnp.sum(hidden1_grad, axis=0)
     input_grad = middle_grad + norm_back(hidden1_grad * norm1_gain, normed1, inverse1)
 
-    early = jnp.concatenate(
+    small = jnp.concatenate(
         [
-            router_grad,
+            tn(hidden2, logit_grad),
             out_bias_grad,
-            norm2_gain_grad[None],
-            norm2_bias_grad[None],
-            proj_bias_grad[None],
+            norm2_gain_grad[:, None],
+            norm2_bias_grad[:, None],
+            proj_bias_grad[:, None],
         ],
-        axis=0,
-    )
-    early = lax.psum(early, "dp")
-    router_grad, out_bias_grad = early[:experts].T, early[experts : 2 * experts]
-    norm2_gain_grad, norm2_bias_grad, proj_bias_grad = (early[2 * experts + i] for i in range(3))
+        axis=1,
+    )
+    width = -(-small.shape[1] // 128) * 128
+    small = jnp.pad(small, ((0, 0), (0, width - small.shape[1]))).astype(BF16)
+    small = tn(mix_a, small)
     late = jnp.stack(
         [
             norm1_gain_grad,
@@ -354,25 +391,20 @@
     for bit in bits:
         late = late + across(late, bit, sources)
     qv_bias_grad = late[2].reshape(2, head_cols)
-
-    def all_sum(total, order, mix):
-        held, names = spread_pieces(reduce_pieces(total, order, sources), order[::-1], sources)
-        size = held.shape[0] // sources
-        back = [names.index(r) for r in range(sources)]
-        held = jnp.concatenate([held[i * size : (i + 1) * size] for i in back], axis=0)
-        return nn(mix, held)
-
-    proj_grad = all_sum(proj_total, second_order, mix_proj)
-    split = (3 * head_cols // 2 + 127) // 128 * 128
-    qkv_sum = jnp.concatenate(
-        [
-            all_sum(qkv_total[:, :split], first_order, mix_in),
-            all_sum(qkv_total[:, split:], second_order, mix_in),
-        ],
-        axis=1,
-    )
-    qkv_grad = jnp.stack(
-        [qkv_sum[:, j * head_cols : (j + 1) * head_cols] for j in range(3)]
+    v_total, out_back = lax.optimization_barrier((v_total, out_back))
+    out_home = nn(onehot, over_group(out_back).reshape(-1, feat_dim)).astype(BF16)
+    out_home = out_home.astype(F32) + swap(out_home).astype(F32)
+    output = (middle + (out_home + exact(gate_map, expert_out_bias))).astype(BF16)
+
+    part_a = jnp.concatenate([qk_total, small], axis=1)
+    part_b = jnp.concatenate([v_total, proj_total], axis=1)
+    sums = reduce_rounds([part_a, part_b], orders, sources)
+    mine, got = spread_rounds(sums, orders, sources)
+    qkv_grad, proj_grad, small = finish(mix_a, mix_b, mine, got, head_cols, width)
+    router_grad = small[:, :experts]
+    out_bias_grad = small[:, experts : 2 * experts].T
+    norm2_gain_grad, norm2_bias_grad, proj_bias_grad = (
+        small[:, 2 * experts + i] for i in range(3)
     )
     return (
         output,

time: 407 us -> 247 us (0.61)
  waiting for transfers between devices: 178 us -> 83.5 us
  local copies, waits for them, and re-layouts: 51.7 us -> 12.8 us
  between operations: 15.9 us -> 1.92 us
  starting transfers between devices: 67 us -> 54.8 us
  other arithmetic: 28.4 us -> 21.1 us
  Pallas kernels: 0 us -> 6.7 us
    psum x1 -> x0, waiting for transfers between devices: 84 us -> none  [local(): early = lax.psum(early, 'dp')]
    unnamed x224 -> x164, local copies, waits for them, and re-layouts: 34 us -> 5.11 us
    all_to_all x1, waiting for transfers between devices: 0.01 us -> 15.8 us  [local(): lax.all_to_all(row_send, 'dp', split_axis=0, concat_axis=0, tiled=True)]
    all_to_all x1, waiting for transfers between devices: 13.7 us -> 0.01 us  [local(): lax.all_to_all(cot_send, 'dp', split_axis=0, concat_axis=0, tiled=True)]
    ppermute x28 -> x18, starting transfers between devices: 31.4 us -> 20.1 us  [across(): return lax.ppermute(x, 'dp', [(i, i ^ bit) for i in range(count)])]
    ppermute x9 -> x7, waiting for transfers between devices: 36.6 us -> 26.2 us  [swap(): return lax.ppermute(x, 'tensor', [(0, 1), (1, 0)])]
    concatenate x7 -> x1, local copies, waits for them, and re-layouts: 6.99 us -> 0.03 us  [local(): jnp.concatenate([tn(hidden2, logit_grad), out_bias_grad, norm2_gain_grad[...]
    pallas_call x0 -> x1, Pallas kernels: none -> 6.7 us  [finish(): pl.pallas_call(lambda *refs: finish_kernel(head_cols, width, *refs), out_...]
  transfers between devices with their start and end apart: 42 -> 29, of which waited for: 23 -> 19; matrix products, arithmetic and copies ran while one was open for 27% -> 28% of each run, Pallas kernels for 0% -> 0%
where the time goes in v2:
time: 247 us; the launch traced here: 246 us
  waiting for transfers between devices  83.5 us (34%)
  matrix products  65.4 us (26%)
  starting transfers between devices  54.8 us (22%)
  other arithmetic  21.1 us (9%)
  local copies, waits for them, and re-layouts  12.8 us (5%)
  Pallas kernels  6.7 us (3%)
    dot_general x28, matrix products, dot(): return lax.dot_general(a, b, (dims, ((), ())), preferred_element_type=out)  48.5 us
    ppermute x18, waiting for transfers between devices, across(): return lax.ppermute(x, 'dp', [(i, i ^ bit) for i in range(count)])  34.3 us
    ppermute x7, waiting for transfers between devices, swap(): return lax.ppermute(x, 'tensor', [(0, 1), (1, 0)])  26.2 us
    ppermute x18, starting transfers between devices, across(): return lax.ppermute(x, 'dp', [(i, i ^ bit) for i in range(count)])  20.1 us
    all_to_all x1, waiting for transfers between devices, local(): lax.all_to_all(row_send, 'dp', split_axis=0, concat_axis=0, tiled=True)  15.8 us
    ppermute x7, starting transfers between devices, swap(): return lax.ppermute(x, 'tensor', [(0, 1), (1, 0)])  7.79 us
    all_to_all x1, starting transfers between devices, local(): lax.all_to_all(row_send, 'dp', split_axis=0, concat_axis=0, tiled=True)  7.68 us
    all_to_all x1, starting transfers between devices, local(): lax.all_to_all(out_send, 'dp', split_axis=0, concat_axis=0, tiled=True)  7.53 us
  transfers between devices with their start and end apart: 29, of which 19 were waited for; matrix products, arithmetic and copies ran while one was open for 28% of the time, Pallas kernels for 0%

profile of v2, /device:TPU:0, one launch (start us, length us, event | category | flops | bytes accessed | tf_op | source)
XLA Modules:
  0.0 246.2 jit_solution(7719704281493670917)
XLA Ops:
  0.7 3.0 %collective-permute-start.1 = (bf16[384,768]{1,0:T(8,128)(2,1)}, bf16[384,768]{1,0:T(8,128)(2,1)}, u32[]{:S(2)}, u32[]{:S(2)}) collective-permute-start(bf16[384,768]{1,0:T(8,128)(2,1)} %param.21), channel_id=1, source_target_pairs={{0,1},{1,0},{2,3},{3,2},{4,5},{5,4},{6,7},{7,6},{8,9},{9,8},{10,11... | collective-permute-start | bytes 1769480 | tf_op jit(solution)/shard_map/ppermute | solution.py:62
  8.9 6.0 %all-to-all-start = ((bf16[16,48,384]{2,1,0:T(8,128)(2,1)}), bf16[16,48,384]{2,1,0:T(8,128)(2,1)}, u32[]{:S(2)}, u32[]{:S(2)}) async-start(bf16[16,48,384]{2,1,0:T(8,128)(2,1)} %broadcast_select_fusion), calls=%async_computation | async-start | bytes 1179648 | tf_op jit(solution)/shard_map/all_to_all | solution.py:209
  20.5 2.5 %convolution_convert_fusion.5 = bf16[6,64,197]{2,1,0:T(8,128)(2,1)} fusion(bf16[197,6,64]{0,2,1:T(8,128)(2,1)} %bitcast.146, f32[6,197]{1,0:T(8,128)S(1)} %get-tuple-element.134, bf16[197,6,64]{0,2,1:T(8,128)(2,1)S(1)} %bitcast.132, bf16[197,6,64]{0,2,1:T(8,128)(2,1)} %bitcast.136), kind=kOutput, calls=%fused_computation.100 | convolution fusion | flops 60619064 | bytes 609912 | tf_op jit(solution)/shard_map/bhqk,bkhd->bqhd/dot_general | solution.py:228
  26.9 3.6 %collective-permute-done = bf16[197,384]{1,0:T(8,128)(2,1)} collective-permute-done((bf16[197,384]{1,0:T(8,128)(2,1)S(1)}, bf16[197,384]{1,0:T(8,128)(2,1)}, u32[]{:S(2)}, u32[]{:S(2)}) %collective-permute-start) | collective-permute-done | bytes 151328 | tf_op jit(solution)/shard_map/ppermute | solution.py:62
  36.8 5.7 %all-to-all-start.1 = ((bf16[16,48,768]{2,1,0:T(8,128)(2,1)}), bf16[16,48,768]{2,1,0:T(8,128)(2,1)S(1)}, u32[]{:S(2)}, u32[]{:S(2)}) async-start(bf16[16,48,768]{2,1,0:T(8,128)(2,1)} %bitcast.122), calls=%async_computation.1 | async-start | bytes 2359296 | tf_op jit(solution)/shard_map/all_to_all | solution.py:239
  44.2 14.3 %collective-permute-done.2 = bf16[768,384]{1,0:T(8,128)(2,1)} collective-permute-done((bf16[768,384]{1,0:T(8,128)(2,1)}, bf16[768,384]{1,0:T(8,128)(2,1)}, u32[]{:S(2)}, u32[]{:S(2)}) %collective-permute-start.2) | collective-permute-done | bytes 589856 | tf_op jit(solution)/shard_map/ppermute | solution.py:62
  62.2 5.5 %all-to-all-done.1 = bf16[16,48,768]{2,1,0:T(8,128)(2,1)S(1)} async-done(((bf16[16,48,768]{2,1,0:T(8,128)(2,1)}), bf16[16,48,768]{2,1,0:T(8,128)(2,1)S(1)}, u32[]{:S(2)}, u32[]{:S(2)}) %all-to-all-start.1) | async-done | bytes 1179680 | tf_op jit(solution)/shard_map/all_to_all | solution.py:239
  69.0 3.4 %multiply_convert_fusion = (bf16[768,1536]{1,0:T(8,128)(2,1)S(1)}, f32[768,1536]{1,0:T(8,128)S(1)}) fusion(f32[1536]{0:T(1024)} %reduce.7, bf16[768,768]{1,0:T(8,128)(2,1)S(1)} %bitcast.120, bf16[1,768,1536]{2,1,0:T(8,128)(2,1)S(1)} %copy-done), kind=kOutput, calls=%fused_computation.7 | convolution fusion | flops 1819017216 | bytes 10622976 | tf_op jit(solution)/shard_map/dot_general | solution.py:36
  72.5 3.1 %fusion.6 = (f32[768]{0:T(1024)S(1)}, bf16[768,768]{1,0:T(8,128)(2,1)}) fusion(bf16[768,384]{1,0:T(8,128)(2,1)S(1)} %copy-done.37, bf16[768,384]{1,0:T(8,128)(2,1)S(1)} %copy-done.35, f32[768]{0:T(1024)S(1)} %fusion.184, bf16[768,1536]{1,0:T(8,128)(2,1)S(1)} %get-tuple-element.138, bf16[1,1536,768]{2,1,0:T(8,128)(2,1)S(1)} %copy-done.75), kind=kOutput, calls=%fused_computation.17 | convolution fusion | flops 1816657152 | bytes 7084032 | tf_op jit(solution)/shard_map/dot_general | solution.py:36
  75.6 4.8 %fusion.215 = (f32[1536]{0:T(1024)}, bf16[768,1536]{1,0:T(8,128)(2,1)S(1)}) fusion(f32[768,1536]{1,0:T(8,128)S(1)} %get-tuple-element.139, f32[1536]{0:T(1024)S(1)} %copy-done.60, bf16[1,1536,768]{2,1,0:T(8,128)(2,1)S(1)} %copy-done.75, f32[768]{0:T(1024)S(1)} %fusion.184, bf16[768,384]{1,0:T(8,128)(2,1)S(1)} %copy-done.37, bf16[768,384]{1,0:T(8,128)(2,1)S(1)} %copy-done.35), kind=kOutput, calls=%fused_computation.330 | convolution fusion | flops 1829632512 | bytes 10632192 | tf_op jit(solution)/shard_map/dot_general | solution.py:36
  84.4 7.7 %all-to-all-start.2 = ((bf16[16,48,768]{2,1,0:T(8,128)(2,1)}), bf16[16,48,768]{2,1,0:T(8,128)(2,1)}, u32[]{:S(2)}, u32[]{:S(2)}) async-start(bf16[16,48,768]{2,1,0:T(8,128)(2,1)} %select_select_fusion), calls=%async_computation.2 | async-start | bytes 2359296 | tf_op jit(solution)/shard_map/all_to_all | solution.py:289
  95.6 5.9 %convolution_bitcast_fusion.1 = f32[1,768,1536]{2,1,0:T(8,128)} fusion(bf16[768,768]{1,0:T(8,128)(2,1)S(1)} %bitcast.121, bf16[768,1536]{1,0:T(8,128)(2,1)} %copy-done.19), kind=kOutput, calls=%fused_computation.10 | convolution fusion | flops 1811939328 | bytes 8257536 | tf_op jit(solution)/shard_map/dot_general | solution.py:36
  101.5 15.8 %all-to-all-done.2 = bf16[16,48,768]{2,1,0:T(8,128)(2,1)} async-done(((bf16[16,48,768]{2,1,0:T(8,128)(2,1)}), bf16[16,48,768]{2,1,0:T(8,128)(2,1)}, u32[]{:S(2)}, u32[]{:S(2)}) %all-to-all-start.2) | async-done | bytes 1179680 | tf_op jit(solution)/shard_map/all_to_all | solution.py:289
  122.0 7.5 %all-to-all-start.3 = ((bf16[16,48,768]{2,1,0:T(8,128)(2,1)}), bf16[16,48,768]{2,1,0:T(8,128)(2,1)}, u32[]{:S(2)}, u32[]{:S(2)}) async-start(bf16[16,48,768]{2,1,0:T(8,128)(2,1)} %bitcast.129), calls=%async_computation.3 | async-start | bytes 2359296 | tf_op jit(solution)/shard_map/all_to_all | solution.py:292
  133.3 2.8 %multiply_reduce_fusion = (f32[6,197]{1,0:T(8,128)S(1)}, f32[6,197,197]{1,2,0:T(8,128)}) fusion(f32[6,197,197]{1,2,0:T(8,128)} %get-tuple-element.135, f32[6,197]{1,0:T(8,128)S(1)} %copy-done.58, bf16[197,6,64]{0,2,1:T(8,128)(2,1)S(1)} %bitcast.148, bf16[197,6,64]{0,2,1:T(8,128)(2,1)} %bitcast.147), kind=kOutput, calls=%fused_computation.55 | convolution fusion | flops 30502692 | bytes 2174880 | tf_op jit(solution)/shard_map/bqhd,bkhd->bhqk/dot_general | solution.py:345
  140.7 3.8 %fusion.39 = f32[768,768]{1,0:T(8,128)} fusion(s32[768]{0:T(1024)S(1)} %fusion.181, s32[768]{0:T(1024)S(1)} %get-tuple-element.145, s32[768]{0:T(1024)S(1)} %get-tuple-element.146, bf16[197,384]{0,1:T(8,128)(2,1)} %bitcast.126, bf16[197,384]{0,1:T(8,128)(2,1)} %bitcast.123, bf16[197,768]{1,0:T(8,128)(2,1)S(1)} %copy-done.13, f32[768]{0:T(1024)S(1)} %copy-done.78, ...), kind=kOutput, calls=%fused_computation.72 | convolution fusion | flops 468215040 | bytes 2981416 | tf_op jit(solution)/shard_map/dot_general | solution.py:36
  148.6 2.3 fusion.38
  157.6 4.3 %convolution_bitcast_fusion = f32[1,1536,768]{2,1,0:T(8,128)} fusion(bf16[768,1536]{1,0:T(8,128)(2,1)S(1)} %copy-done.80, f32[768]{0:T(1024)S(1)} %copy-done.64, bf16[768,384]{1,0:T(8,128)(2,1)S(1)} %copy-done.38, bf16[768,384]{1,0:T(8,128)(2,1)S(1)} %copy-done.36), kind=kOutput, calls=%fused_computation.9 | convolution fusion | flops 1815478272 | bytes 8260608 | tf_op jit(solution)/shard_map/dot_general | solution.py:36
  165.0 3.8 %collective-permute-start.18 = (bf16[192,768]{1,0:T(8,128)(2,1)S(1)}, bf16[192,768]{1,0:T(8,128)(2,1)S(1)}, u32[]{:S(2)}, u32[]{:S(2)}) collective-permute-start(bf16[192,768]{1,0:T(8,128)(2,1)S(1)} %slice.282), channel_id=1, source_target_pairs={{0,8},{2,10},{4,12},{6,14},{8,0},{10,2},{12,4},{14,6},{16,24},{18,... | collective-permute-start | bytes 884744 | tf_op jit(solution)/shard_map/ppermute | solution.py:66
  171.1 2.7 %collective-permute-done.6 = bf16[197,768]{1,0:T(8,128)(2,1)S(1)} collective-permute-done((bf16[197,768]{1,0:T(8,128)(2,1)S(1)}, bf16[197,768]{1,0:T(8,128)(2,1)S(1)}, u32[]{:S(2)}, u32[]{:S(2)}) %collective-permute-start.6) | collective-permute-done | bytes 302624 | tf_op jit(solution)/shard_map/ppermute | solution.py:62
  176.6 2.6 %collective-permute-start.19 = (bf16[96,768]{1,0:T(8,128)(2,1)S(1)}, bf16[96,768]{1,0:T(8,128)(2,1)S(1)}, u32[]{:S(2)}, u32[]{:S(2)}) collective-permute-start(bf16[96,768]{1,0:T(8,128)(2,1)S(1)} %slice.284), channel_id=1, source_target_pairs={{0,16},{2,18},{4,20},{6,22},{8,24},{10,26},{12,28},{14,30},{16,0},... | collective-permute-start | bytes 442376 | tf_op jit(solution)/shard_map/ppermute | solution.py:66
  181.3 5.3 %collective-permute-done.19 = bf16[96,768]{1,0:T(8,128)(2,1)S(1)} collective-permute-done((bf16[96,768]{1,0:T(8,128)(2,1)S(1)}, bf16[96,768]{1,0:T(8,128)(2,1)S(1)}, u32[]{:S(2)}, u32[]{:S(2)}) %collective-permute-start.19) | collective-permute-done | bytes 147488 | tf_op jit(solution)/shard_map/ppermute | solution.py:66
  188.8 2.3 collective-permute-done.20
  197.0 6.4 %collective-permute-done.15 = bf16[48,896]{1,0:T(8,128)(2,1)S(1)} collective-permute-done((bf16[48,896]{1,0:T(8,128)(2,1)S(1)}, bf16[48,896]{1,0:T(8,128)(2,1)S(1)}, u32[]{:S(2)}, u32[]{:S(2)}) %collective-permute-start.15) | collective-permute-done | bytes 86048 | tf_op jit(solution)/shard_map/ppermute | solution.py:66
  205.7 5.0 %collective-permute-done.16 = bf16[96,896]{1,0:T(8,128)(2,1)S(1)} collective-permute-done((bf16[96,896]{1,0:T(8,128)(2,1)S(1)}, bf16[96,896]{1,0:T(8,128)(2,1)S(1)}, u32[]{:S(2)}, u32[]{:S(2)}) %collective-permute-start.16) | collective-permute-done | bytes 172064 | tf_op jit(solution)/shard_map/ppermute | solution.py:66
  213.0 2.3 collective-permute-done.23
  215.2 2.9 %collective-permute-done.17 = bf16[192,896]{1,0:T(8,128)(2,1)S(1)} collective-permute-done((bf16[192,896]{1,0:T(8,128)(2,1)S(1)}, bf16[192,896]{1,0:T(8,128)(2,1)S(1)}, u32[]{:S(2)}, u32[]{:S(2)}) %collective-permute-start.17) | collective-permute-done | bytes 344096 | tf_op jit(solution)/shard_map/ppermute | solution.py:66
  218.4 3.7 %collective-permute-done.9 = f32[3,768]{1,0:T(4,128)S(1)} collective-permute-done((f32[3,768]{1,0:T(4,128)S(1)}, f32[3,768]{1,0:T(4,128)S(1)}, u32[]{:S(2)}, u32[]{:S(2)}) %collective-permute-start.9) | collective-permute-done | bytes 9248 | tf_op jit(solution)/shard_map/ppermute | solution.py:66
  222.7 2.5 convolution_convert_fusion.2
  228.4 5.6 %collective-permute-done.5 = bf16[197,768]{1,0:T(8,128)(2,1)} collective-permute-done((bf16[197,768]{1,0:T(8,128)(2,1)}, bf16[197,768]{1,0:T(8,128)(2,1)}, u32[]{:S(2)}, u32[]{:S(2)}) %collective-permute-start.5) | collective-permute-done | bytes 302624 | tf_op jit(solution)/shard_map/ppermute | solution.py:62
  234.0 2.5 %add_convert_fusion = bf16[197,768]{1,0:T(8,128)(2,1)} fusion(f32[197,768]{1,0:T(8,128)S(1)} %copy-done.6, bf16[197,768]{1,0:T(8,128)(2,1)} %collective-permute-done.5, bf16[197,768]{1,0:T(8,128)(2,1)} %convolution_convert_fusion.2, f32[16,768]{1,0:T(8,128)S(1)} %copy-done.43, f32[197]{0:T(256)S(1)} %get-tuple-element.106, f32[197]{0:T(256)S(1)} %get-tuple-element.105, ...), kind=kOutput, calls=%fused_computation.133 | convolution fusion | flops 29972368 | bytes 1565264 | tf_op jit(solution)/shard_map/dot_general | solution.py:52
  236.5 6.7 %finish.1 = (f32[3,768,384]{2,1,0:T(8,128)}, f32[384,768]{1,0:T(8,128)}, f32[768,128]{1,0:T(8,128)S(1)}) custom-call(bf16[768,768]{1,0:T(8,128)(2,1)S(1)} %copy-done.2, bf16[768,768]{1,0:T(8,128)(2,1)S(1)} %get-tuple-element.122.refs_1_, bf16[384,1664]{1,0:T(8,128)(2,1)S(1)} %maximum_maximum_fusion.refs_2_, bf16[384,1664]{1,0:T(8,128)(2,1)} %collective-permute-done.24.refs_3_), custom_call_target="tpu_custom_call" | custom-call | tf_op jit(solution)/shard_map/finish/pallas_call | solution.py:130
  (325 shorter events, 88.0 us)
Async XLA Ops:
  0.6 68.3 %copy-start = (bf16[1,768,1536]{2,1,0:T(8,128)(2,1)S(1)}, bf16[1,768,1536]{2,1,0:T(8,128)(2,1)}, u32[]{:S(2)}) copy-start(bf16[1,768,1536]{2,1,0:T(8,128)(2,1)} %param.26) | copy-start | bytes 7077892
  0.7 24.0 %collective-permute-start.1 = (bf16[384,768]{1,0:T(8,128)(2,1)}, bf16[384,768]{1,0:T(8,128)(2,1)}, u32[]{:S(2)}, u32[]{:S(2)}) collective-permute-start(bf16[384,768]{1,0:T(8,128)(2,1)} %param.21), channel_id=1, source_target_pairs={{0,1},{1,0},{2,3},{3,2},{4,5},{5,4},{6,7},{7,6},{8,9},{9,8},{10,11... | collective-permute-start | bytes 1769480 | tf_op jit(solution)/shard_map/ppermute | solution.py:62
  6.0 28.3 %copy-start.69 = (s32[197,1]{0,1:T(1,128)}, s32[197,1]{0,1:T(1,128)S(1)}, u32[]{:S(2)}) copy-start(s32[197,1]{0,1:T(1,128)S(1)} %get-tuple-element.129) | copy-start | bytes 2368
  6.0 28.3 %copy-start.71 = (s32[197,1]{0,1:T(1,128)}, s32[197,1]{0,1:T(1,128)S(1)}, u32[]{:S(2)}) copy-start(s32[197,1]{0,1:T(1,128)S(1)} %get-tuple-element.131) | copy-start | bytes 2368
  8.9 21.6 %all-to-all-start = ((bf16[16,48,384]{2,1,0:T(8,128)(2,1)}), bf16[16,48,384]{2,1,0:T(8,128)(2,1)}, u32[]{:S(2)}, u32[]{:S(2)}) async-start(bf16[16,48,384]{2,1,0:T(8,128)(2,1)} %broadcast_select_fusion), calls=%async_computation | async-start | bytes 1179648 | tf_op jit(solution)/shard_map/all_to_all | solution.py:209
  24.1 6.4 %collective-permute-start = (bf16[197,384]{1,0:T(8,128)(2,1)S(1)}, bf16[197,384]{1,0:T(8,128)(2,1)}, u32[]{:S(2)}, u32[]{:S(2)}) collective-permute-start(bf16[197,384]{1,0:T(8,128)(2,1)S(1)} %copy.75), channel_id=1, source_target_pairs={{0,1},{1,0},{2,3},{3,2},{4,5},{5,4},{6,7},{7,6},{8,9},{9,8},{10,11... | collective-permute-start | bytes 453896 | tf_op jit(solution)/shard_map/ppermute | solution.py:62
  36.8 30.9 %all-to-all-start.1 = ((bf16[16,48,768]{2,1,0:T(8,128)(2,1)}), bf16[16,48,768]{2,1,0:T(8,128)(2,1)S(1)}, u32[]{:S(2)}, u32[]{:S(2)}) async-start(bf16[16,48,768]{2,1,0:T(8,128)(2,1)} %bitcast.122), calls=%async_computation.1 | async-start | bytes 2359296 | tf_op jit(solution)/shard_map/all_to_all | solution.py:239
  42.5 16.0 %collective-permute-start.2 = (bf16[768,384]{1,0:T(8,128)(2,1)}, bf16[768,384]{1,0:T(8,128)(2,1)}, u32[]{:S(2)}, u32[]{:S(2)}) collective-permute-start(bf16[768,384]{1,0:T(8,128)(2,1)} %bitcast.19), channel_id=1, source_target_pairs={{0,1},{1,0},{2,3},{3,2},{4,5},{5,4},{6,7},{7,6},{8,9},{9,8},{10,11... | collective-permute-start | bytes 1769480 | tf_op jit(solution)/shard_map/ppermute | solution.py:62
  84.4 32.9 %all-to-all-start.2 = ((bf16[16,48,768]{2,1,0:T(8,128)(2,1)}), bf16[16,48,768]{2,1,0:T(8,128)(2,1)}, u32[]{:S(2)}, u32[]{:S(2)}) async-start(bf16[16,48,768]{2,1,0:T(8,128)(2,1)} %select_select_fusion), calls=%async_computation.2 | async-start | bytes 2359296 | tf_op jit(solution)/shard_map/all_to_all | solution.py:289
  118.1 11.5 %collective-permute-start.4 = (f32[16,48]{1,0:T(8,128)S(1)}, f32[16,48]{1,0:T(8,128)S(1)}, u32[]{:S(2)}, u32[]{:S(2)}) collective-permute-start(f32[16,48]{1,0:T(8,128)S(1)} %convert_reduce_fusion.2), channel_id=1, source_target_pairs={{0,1},{1,0},{2,3},{3,2},{4,5},{5,4},{6,7},{7,6},{8,9},{9,8},{10,11... | collective-permute-start | bytes 9224 | tf_op jit(solution)/shard_map/ppermute | solution.py:62
  120.5 10.3 %collective-permute-start.3 = (bf16[197,768]{1,0:T(8,128)(2,1)S(1)}, bf16[197,768]{1,0:T(8,128)(2,1)}, u32[]{:S(2)}, u32[]{:S(2)}) collective-permute-start(bf16[197,768]{1,0:T(8,128)(2,1)S(1)} %convolution_convert_fusion.3), channel_id=1, source_target_pairs={{0,1},{1,0},{2,3},{3,2},{4,5},{5,4},{6,7},{7,6},{8,9},{9,8},{10,11... | collective-permute-start | bytes 907784 | tf_op jit(solution)/shard_map/ppermute | solution.py:62
  122.0 32.7 %all-to-all-start.3 = ((bf16[16,48,768]{2,1,0:T(8,128)(2,1)}), bf16[16,48,768]{2,1,0:T(8,128)(2,1)}, u32[]{:S(2)}, u32[]{:S(2)}) async-start(bf16[16,48,768]{2,1,0:T(8,128)(2,1)} %bitcast.129), calls=%async_computation.3 | async-start | bytes 2359296 | tf_op jit(solution)/shard_map/all_to_all | solution.py:292
  156.4 8.3 %collective-permute-start.11 = (bf16[384,1664]{1,0:T(8,128)(2,1)S(1)}, bf16[384,1664]{1,0:T(8,128)(2,1)S(1)}, u32[]{:S(2)}, u32[]{:S(2)}) collective-permute-start(bf16[384,1664]{1,0:T(8,128)(2,1)S(1)} %pad_maximum_fusion.1), channel_id=1, source_target_pairs={{0,2},{2,0},{4,6},{6,4},{8,10},{10,8},{12,14},{14,12},{16,18},{18,... | collective-permute-start | bytes 3833864 | tf_op jit(solution)/shard_map/ppermute | solution.py:66
  163.9 10.0 %collective-permute-start.6 = (bf16[197,768]{1,0:T(8,128)(2,1)S(1)}, bf16[197,768]{1,0:T(8,128)(2,1)S(1)}, u32[]{:S(2)}, u32[]{:S(2)}) collective-permute-start(bf16[197,768]{1,0:T(8,128)(2,1)S(1)} %fusion.31), channel_id=1, source_target_pairs={{0,1},{1,0},{2,3},{3,2},{4,5},{5,4},{6,7},{7,6},{8,9},{9,8},{10,11... | collective-permute-start | bytes 907784 | tf_op jit(solution)/shard_map/ppermute | solution.py:62
  165.0 11.6 %collective-permute-start.18 = (bf16[192,768]{1,0:T(8,128)(2,1)S(1)}, bf16[192,768]{1,0:T(8,128)(2,1)S(1)}, u32[]{:S(2)}, u32[]{:S(2)}) collective-permute-start(bf16[192,768]{1,0:T(8,128)(2,1)S(1)} %slice.282), channel_id=1, source_target_pairs={{0,8},{2,10},{4,12},{6,14},{8,0},{10,2},{12,4},{14,6},{16,24},{18,... | collective-permute-start | bytes 884744 | tf_op jit(solution)/shard_map/ppermute | solution.py:66
  168.9 10.4 %collective-permute-start.12 = (bf16[192,896]{1,0:T(8,128)(2,1)S(1)}, bf16[192,896]{1,0:T(8,128)(2,1)S(1)}, u32[]{:S(2)}, u32[]{:S(2)}) collective-permute-start(bf16[192,896]{1,0:T(8,128)(2,1)S(1)} %slice.281), channel_id=1, source_target_pairs={{0,4},{2,6},{4,0},{6,2},{8,12},{10,14},{12,8},{14,10},{16,20},{18,... | collective-permute-start | bytes 1032200 | tf_op jit(solution)/shard_map/ppermute | solution.py:66
  176.6 10.0 %collective-permute-start.19 = (bf16[96,768]{1,0:T(8,128)(2,1)S(1)}, bf16[96,768]{1,0:T(8,128)(2,1)S(1)}, u32[]{:S(2)}, u32[]{:S(2)}) collective-permute-start(bf16[96,768]{1,0:T(8,128)(2,1)S(1)} %slice.284), channel_id=1, source_target_pairs={{0,16},{2,18},{4,20},{6,22},{8,24},{10,26},{12,28},{14,30},{16,0},... | collective-permute-start | bytes 442376 | tf_op jit(solution)/shard_map/ppermute | solution.py:66
  179.6 8.3 %collective-permute-start.13 = (bf16[96,896]{1,0:T(8,128)(2,1)S(1)}, bf16[96,896]{1,0:T(8,128)(2,1)S(1)}, u32[]{:S(2)}, u32[]{:S(2)}) collective-permute-start(bf16[96,896]{1,0:T(8,128)(2,1)S(1)} %slice.283), channel_id=1, source_target_pairs={{0,8},{2,10},{4,12},{6,14},{8,0},{10,2},{12,4},{14,6},{16,24},{18,... | collective-permute-start | bytes 516104 | tf_op jit(solution)/shard_map/ppermute | solution.py:66
  186.7 4.4 %collective-permute-start.20 = (bf16[48,768]{1,0:T(8,128)(2,1)S(1)}, bf16[48,768]{1,0:T(8,128)(2,1)S(1)}, u32[]{:S(2)}, u32[]{:S(2)}) collective-permute-start(bf16[48,768]{1,0:T(8,128)(2,1)S(1)} %slice.286), channel_id=1, source_target_pairs={{0,4},{2,6},{4,0},{6,2},{8,12},{10,14},{12,8},{14,10},{16,20},{18,... | collective-permute-start | bytes 221192 | tf_op jit(solution)/shard_map/ppermute | solution.py:66
  188.0 5.9 %collective-permute-start.14 = (bf16[48,896]{1,0:T(8,128)(2,1)S(1)}, bf16[48,896]{1,0:T(8,128)(2,1)S(1)}, u32[]{:S(2)}, u32[]{:S(2)}) collective-permute-start(bf16[48,896]{1,0:T(8,128)(2,1)S(1)} %slice.285), channel_id=1, source_target_pairs={{0,16},{2,18},{4,20},{6,22},{8,24},{10,26},{12,28},{14,30},{16,0},... | collective-permute-start | bytes 258056 | tf_op jit(solution)/shard_map/ppermute | solution.py:66
  191.1 4.4 %collective-permute-start.21 = (bf16[48,768]{1,0:T(8,128)(2,1)S(1)}, bf16[48,768]{1,0:T(8,128)(2,1)S(1)}, u32[]{:S(2)}, u32[]{:S(2)}) collective-permute-start(bf16[48,768]{1,0:T(8,128)(2,1)S(1)} %fusion.134), channel_id=1, source_target_pairs={{0,4},{2,6},{4,0},{6,2},{8,12},{10,14},{12,8},{14,10},{16,20},{18,... | collective-permute-start | bytes 221192 | tf_op jit(solution)/shard_map/ppermute | solution.py:66
  193.9 9.5 %collective-permute-start.15 = (bf16[48,896]{1,0:T(8,128)(2,1)S(1)}, bf16[48,896]{1,0:T(8,128)(2,1)S(1)}, u32[]{:S(2)}, u32[]{:S(2)}) collective-permute-start(bf16[48,896]{1,0:T(8,128)(2,1)S(1)} %fusion.126), channel_id=1, source_target_pairs={{0,16},{2,18},{4,20},{6,22},{8,24},{10,26},{12,28},{14,30},{16,0},... | collective-permute-start | bytes 258056 | tf_op jit(solution)/shard_map/ppermute | solution.py:66
  195.6 9.4 %collective-permute-start.22 = (bf16[96,768]{1,0:T(8,128)(2,1)S(1)}, bf16[96,768]{1,0:T(8,128)(2,1)S(1)}, u32[]{:S(2)}, u32[]{:S(2)}) collective-permute-start(bf16[96,768]{1,0:T(8,128)(2,1)S(1)} %pad_maximum_fusion.7), channel_id=1, source_target_pairs={{0,16},{2,18},{4,20},{6,22},{8,24},{10,26},{12,28},{14,30},{16,0},... | collective-permute-start | bytes 442376 | tf_op jit(solution)/shard_map/ppermute | solution.py:66
  203.4 7.3 %collective-permute-start.16 = (bf16[96,896]{1,0:T(8,128)(2,1)S(1)}, bf16[96,896]{1,0:T(8,128)(2,1)S(1)}, u32[]{:S(2)}, u32[]{:S(2)}) collective-permute-start(bf16[96,896]{1,0:T(8,128)(2,1)S(1)} %pad_maximum_fusion.6), channel_id=1, source_target_pairs={{0,8},{2,10},{4,12},{6,14},{8,0},{10,2},{12,4},{14,6},{16,24},{18,... | collective-permute-start | bytes 516104 | tf_op jit(solution)/shard_map/ppermute | solution.py:66
  203.5 8.8 %collective-permute-start.7 = (f32[3,768]{1,0:T(4,128)S(1)}, f32[3,768]{1,0:T(4,128)S(1)}, u32[]{:S(2)}, u32[]{:S(2)}) collective-permute-start(f32[3,768]{1,0:T(4,128)S(1)} %pad_maximum_fusion.8), channel_id=1, source_target_pairs={{0,2},{2,0},{4,6},{6,4},{8,10},{10,8},{12,14},{14,12},{16,18},{18,... | collective-permute-start | bytes 27656 | tf_op jit(solution)/shard_map/ppermute | solution.py:66
  205.0 10.2 %collective-permute-start.23 = (bf16[192,768]{1,0:T(8,128)(2,1)S(1)}, bf16[192,768]{1,0:T(8,128)(2,1)S(1)}, u32[]{:S(2)}, u32[]{:S(2)}) collective-permute-start(bf16[192,768]{1,0:T(8,128)(2,1)S(1)} %pad_maximum_fusion.5), channel_id=1, source_target_pairs={{0,8},{2,10},{4,12},{6,14},{8,0},{10,2},{12,4},{14,6},{16,24},{18,... | collective-permute-start | bytes 884744 | tf_op jit(solution)/shard_map/ppermute | solution.py:66
  210.8 7.3 %collective-permute-start.17 = (bf16[192,896]{1,0:T(8,128)(2,1)S(1)}, bf16[192,896]{1,0:T(8,128)(2,1)S(1)}, u32[]{:S(2)}, u32[]{:S(2)}) collective-permute-start(bf16[192,896]{1,0:T(8,128)(2,1)S(1)} %pad_maximum_fusion.4), channel_id=1, source_target_pairs={{0,4},{2,6},{4,0},{6,2},{8,12},{10,14},{12,8},{14,10},{16,20},{18,... | collective-permute-start | bytes 1032200 | tf_op jit(solution)/shard_map/ppermute | solution.py:66
  212.4 5.9 %collective-permute-start.8 = (f32[3,768]{1,0:T(4,128)S(1)}, f32[3,768]{1,0:T(4,128)S(1)}, u32[]{:S(2)}, u32[]{:S(2)}) collective-permute-start(f32[3,768]{1,0:T(4,128)S(1)} %fusion.202), channel_id=1, source_target_pairs={{0,4},{2,6},{4,0},{6,2},{8,12},{10,14},{12,8},{14,10},{16,20},{18,... | collective-permute-start | bytes 27656 | tf_op jit(solution)/shard_map/ppermute | solution.py:66
  218.2 18.3 %collective-permute-start.24 = (bf16[384,1664]{1,0:T(8,128)(2,1)S(1)}, bf16[384,1664]{1,0:T(8,128)(2,1)}, u32[]{:S(2)}, u32[]{:S(2)}) collective-permute-start(bf16[384,1664]{1,0:T(8,128)(2,1)S(1)} %maximum_maximum_fusion.refs_2_), channel_id=1, source_target_pairs={{0,2},{2,0},{4,6},{6,4},{8,10},{10,8},{12,14},{14,12},{16,18},{18,... | collective-permute-start | bytes 3833864 | tf_op jit(solution)/shard_map/ppermute | solution.py:66
  218.3 3.8 %collective-permute-start.9 = (f32[3,768]{1,0:T(4,128)S(1)}, f32[3,768]{1,0:T(4,128)S(1)}, u32[]{:S(2)}, u32[]{:S(2)}) collective-permute-start(f32[3,768]{1,0:T(4,128)S(1)} %fusion.255), channel_id=1, source_target_pairs={{0,8},{2,10},{4,12},{6,14},{8,0},{10,2},{12,4},{14,6},{16,24},{18,... | collective-permute-start | bytes 27656 | tf_op jit(solution)/shard_map/ppermute | solution.py:66
  222.1 5.1 %collective-permute-start.10 = (f32[3,768]{1,0:T(4,128)S(1)}, f32[3,768]{1,0:T(4,128)S(1)}, u32[]{:S(2)}, u32[]{:S(2)}) collective-permute-start(f32[3,768]{1,0:T(4,128)S(1)} %add.314), channel_id=1, source_target_pairs={{0,16},{2,18},{4,20},{6,22},{8,24},{10,26},{12,28},{14,30},{16,0},... | collective-permute-start | bytes 27656 | tf_op jit(solution)/shard_map/ppermute | solution.py:66
  225.2 8.8 %collective-permute-start.5 = (bf16[197,768]{1,0:T(8,128)(2,1)}, bf16[197,768]{1,0:T(8,128)(2,1)}, u32[]{:S(2)}, u32[]{:S(2)}) collective-permute-start(bf16[197,768]{1,0:T(8,128)(2,1)} %convolution_convert_fusion.2), channel_id=1, source_target_pairs={{0,1},{1,0},{2,3},{3,2},{4,5},{5,4},{6,7},{7,6},{8,9},{9,8},{10,11... | collective-permute-start | bytes 907784 | tf_op jit(solution)/shard_map/ppermute | solution.py:62
  (78 other events, 368.2 us)

commit v3 on v2

--- a/solution.py
+++ b/solution.py
@@ -78,65 +78,67 @@
     return jnp.where((plane == which), low, high)
 
 
-def reduce_rounds(parts, orders, count):
-    def split(part):
-        middle = part.shape[0] // 2
-        return part[:middle], part[middle:]
-
-    both = jnp.concatenate([split(part)[1].astype(BF16) for part in parts], axis=1)
-    both = across(both, orders[0][0], count)
-    place = 0
-    held = []
-    for part in parts:
-        width = part.shape[1]
-        held.append(split(part)[0] + both[:, place : place + width].astype(F32))
-        place += width
-    for turn in range(1, len(orders[0])):
-        held = [
-            split(part)[0] + across(split(part)[1].astype(BF16), order[turn], count).astype(F32)
-            for part, order in zip(held, orders)
-        ]
-    return [part.astype(BF16) for part in held]
-
-
-def spread_rounds(parts, orders, count):
-    for turn in range(len(orders[0]) - 1, 0, -1):
-        parts = [
-            jnp.concatenate([part, across(part, order[turn], count)], axis=0)
-            for part, order in zip(parts, orders)
-        ]
-    mine = jnp.concatenate(parts, axis=1)
-    return mine, across(mine, orders[0][0], count)
-
-
-def finish_kernel(head_cols, width, mix_a, mix_b, mine, got, qkv_ref, proj_ref, small_ref):
-    rows = mine.shape[0]
-
-    def ordered(mix, start, size):
-        low = jnp.dot(mix[:, :rows], mine[:, start : start + size], preferred_element_type=F32)
-        high = jnp.dot(mix[:, rows:], got[:, start : start + size], preferred_element_type=F32)
-        return low + high
-
-    qkv_ref[0] = ordered(mix_a, 0, head_cols)
-    qkv_ref[1] = ordered(mix_a, head_cols, head_cols)
-    small_ref[...] = ordered(mix_a, 2 * head_cols, width)
-    start = 2 * head_cols + width
-    qkv_ref[2] = ordered(mix_b, start, head_cols)
-    proj_ref[...] = ordered(mix_b, start + head_cols, head_cols).T
-
-
-def finish(mix_a, mix_b, mine, got, head_cols, width):
-    feat_dim = mix_a.shape[0]
+def along(x, orders, turn, count):
+    return lax.ppermute(x, "dp", [(i, i ^ orders[i & 1][turn]) for i in range(count)])
+
+
+def halve(total, orders, turn, count):
+    middle = total.shape[0] // 2
+    return total[:middle] + along(total[middle:].astype(BF16), orders, turn, count).astype(F32)
+
+
+def finish_kernel(head_cols, experts, orders, me_ref, mine, got, qkv_ref, proj_ref, router_ref, bias_ref, norm_ref, held_proj, held_small):
+    me = me_ref[0]
+    count = 1 << len(orders[0])
+    feat_dim = qkv_ref.shape[1]
+    chunk = feat_dim // count
+    half = count // 2
+    odd = me % 2
+    width = held_small.shape[1]
+    for spot in range(count):
+        names = []
+        for order in orders:
+            names.append(sum(bit for i, bit in enumerate(order) if (spot >> (len(order) - 1 - i)) & 1))
+        if spot >= half:
+            names = names[::-1]
+        name = names[0] + odd * (names[1] - names[0])
+        start = pl.multiple_of((name ^ me) * chunk, chunk)
+        source = mine if spot < half else got
+        first = (spot % half) * chunk
+        piece = source[first : first + chunk, :].astype(F32)
+        for j in range(3):
+            qkv_ref[j, pl.ds(start, chunk), :] = piece[:, j * head_cols : (j + 1) * head_cols]
+        held_proj[pl.ds(start, chunk), :] = piece[:, 3 * head_cols : 4 * head_cols]
+        held_small[pl.ds(start, chunk), :] = piece[:, 4 * head_cols :]
+    proj_ref[...] = held_proj[...].T
+    small = held_small[...]
+    router_ref[...] = small[:, :experts]
+    flat = small.T
+    bias_ref[...] = flat[experts : 2 * experts]
+    norm_ref[...] = flat[2 * experts : 2 * experts + 8]
+
+
+def finish(me, mine, got, head_cols, experts, feat_dim, orders):
+    width = mine.shape[1] - 4 * head_cols
+    vmem = pl.BlockSpec(memory_space=pltpu.VMEM)
     return pl.pallas_call(
-        lambda *refs: finish_kernel(head_cols, width, *refs),
+        lambda *refs: finish_kernel(head_cols, experts, orders, *refs),
+        in_specs=[pl.BlockSpec(memory_space=pltpu.SMEM), vmem, vmem],
+        out_specs=[vmem] * 5,
         out_shape=(
             jax.ShapeDtypeStruct((3, feat_dim, head_cols), F32),
             jax.ShapeDtypeStruct((head_cols, feat_dim), F32),
-            jax.ShapeDtypeStruct((feat_dim, width), F32),
+            jax.ShapeDtypeStruct((feat_dim, experts), F32),
+            jax.ShapeDtypeStruct((experts, feat_dim), F32),
+            jax.ShapeDtypeStruct((8, feat_dim), F32),
         ),
-        compiler_params=pltpu.CompilerParams(vmem_limit_bytes=48 << 20),
+        scratch_shapes=[
+            pltpu.VMEM((feat_dim, head_cols), F32),
+            pltpu.VMEM((feat_dim, width), F32),
+        ],
+        compiler_params=pltpu.CompilerParams(vmem_limit_bytes=40 << 20),
         name="finish",
-    )(mix_a, mix_b, mine, got)
+    )(me[None], mine, got)
 
 
 def local(
@@ -287,11 +289,14 @@
     row_send = jnp.where(slot_ids[None, :, None] == slots - 1, widen(inner_high), row_send)
     row_send = jnp.where(slot_ids[None, :, None] == slots - 2, widen(inner_low), row_send)
     row_back = lax.all_to_all(row_send, "dp", split_axis=0, concat_axis=0, tiled=True)
+    out_weight_grad = tn(activ_low, grad_rows)
+    in_weight_grad = tn(arrived, act_low)
+    row_back, out_weight_grad, in_weight_grad = lax.optimization_barrier(
+        (row_back, out_weight_grad, in_weight_grad)
+    )
     out_send = (row_gate * part_out).astype(BF16).reshape(sources, slots, feat_dim)
     out_send, row_back = lax.optimization_barrier((out_send, row_back))
     out_back = lax.all_to_all(out_send, "dp", split_axis=0, concat_axis=0, tiled=True)
-    out_weight_grad = tn(activ_low, grad_rows)
-    in_weight_grad = tn(arrived, act_low)
 
     def over_group(x):
         if group_size == 1:
@@ -326,19 +331,16 @@
     orders = [bits, bits[:1] + bits[2:] + bits[1:2]]
     chunk = feat_dim // sources
 
-    def mixer(order):
-        rows = jnp.arange(feat_dim, dtype=jnp.int32)[:, None]
-        cols = jnp.arange(feat_dim, dtype=jnp.int32)[None, :]
-        spot = cols // chunk
-        piece = jnp.zeros_like(spot)
-        for i, bit in enumerate(order):
-            piece = piece | jnp.where((spot >> (len(order) - 1 - i)) & 1, bit, 0)
-        return ((rows // chunk == (piece ^ me)) & (rows % chunk == cols % chunk)).astype(BF16)
-
-    mix_a, mix_b = mixer(orders[0]), mixer(orders[1])
-    hidden1_a, hidden1_b = nn(hidden1, mix_a).astype(BF16), nn(hidden1, mix_b).astype(BF16)
-    middle_b = nn(middle_low, mix_b).astype(BF16)
-    proj_total = tn(middle_b, attended)
+    rows = jnp.arange(feat_dim, dtype=jnp.int32)[:, None]
+    cols = jnp.arange(feat_dim, dtype=jnp.int32)[None, :]
+    spot = cols // chunk
+    piece = jnp.zeros_like(spot)
+    for i in range(len(bits)):
+        bit = jnp.where((me % 2 == 0) == (spot < sources // 2), orders[0][i], orders[1][i])
+        piece = piece | jnp.where((spot >> (len(bits) - 1 - i)) & 1 == 1, bit, 0)
+    mix = ((rows // chunk == (piece ^ me)) & (rows % chunk == cols % chunk)).astype(BF16)
+    hidden1_mixed = nn(hidden1, mix).astype(BF16)
+    proj_total = tn(nn(middle_low, mix).astype(BF16), attended)
     attended_grad = nt(middle_low, proj_weight).astype(BF16)
     attended_grad = attended_grad.reshape(images, SEQ, heads_here, HEAD)
     value_grad = jnp.einsum("bhqk,bqhd->bkhd", prob_low, attended_grad, preferred_element_type=F32)
@@ -357,8 +359,7 @@
         g.reshape(tok_count, head_cols).astype(BF16) for g in (query_grad, key_grad, value_grad)
     ]
     proj_low = jnp.concatenate(proj_low, axis=1)
-    qk_total = tn(hidden1_a, proj_low[:, : 2 * head_cols])
-    v_total = tn(hidden1_b, proj_low[:, 2 * head_cols :])
+    qkv_total = tn(hidden1_mixed, proj_low)
     qv_sums = jnp.sum(proj_low.astype(F32), axis=0)
     hidden1_part = sum(
         nt(proj_low[:, j * head_cols : (j + 1) * head_cols], qkv_weight[j]) for j in range(3)
@@ -380,7 +381,7 @@
     )
     width = -(-small.shape[1] // 128) * 128
     small = jnp.pad(small, ((0, 0), (0, width - small.shape[1]))).astype(BF16)
-    small = tn(mix_a, small)
+    small = tn(mix, small)
     late = jnp.stack(
         [
             norm1_gain_grad,
@@ -391,21 +392,33 @@
     for bit in bits:
         late = late + across(late, bit, sources)
     qv_bias_grad = late[2].reshape(2, head_cols)
-    v_total, out_back = lax.optimization_barrier((v_total, out_back))
     out_home = nn(onehot, over_group(out_back).reshape(-1, feat_dim)).astype(BF16)
-    out_home = out_home.astype(F32) + swap(out_home).astype(F32)
+    total = jnp.concatenate([qkv_total, proj_total, small], axis=1)
+    total, out_home = lax.optimization_barrier((total, out_home))
+    out_other = swap(out_home)
+    total = halve(total, orders, 0, sources)
+    total = halve(total, orders, 1, sources)
+    total, out_other = lax.optimization_barrier((total, out_other))
+    out_home = out_home.astype(F32) + out_other.astype(F32)
     output = (middle + (out_home + exact(gate_map, expert_out_bias))).astype(BF16)
-
-    part_a = jnp.concatenate([qk_total, small], axis=1)
-    part_b = jnp.concatenate([v_total, proj_total], axis=1)
-    sums = reduce_rounds([part_a, part_b], orders, sources)
-    mine, got = spread_rounds(sums, orders, sources)
-    qkv_grad, proj_grad, small = finish(mix_a, mix_b, mine, got, head_cols, width)
-    router_grad = small[:, :experts]
-    out_bias_grad = small[:, experts : 2 * experts].T
-    norm2_gain_grad, norm2_bias_grad, proj_bias_grad = (
-        small[:, 2 * experts + i] for i in range(3)
-    )
+    for turn in range(2, len(bits)):
+        total = halve(total, orders, turn, sources)
+    mine = total.astype(BF16)
+    for turn in range(len(bits) - 1, 0, -1):
+        mine = jnp.concatenate([mine, along(mine, orders, turn, sources)], axis=0)
+    got = along(mine, orders, 0, sources)
+    if chunk % 16 == 0:
+        qkv_grad, proj_grad, router_grad, out_bias_grad, norm_grads = finish(
+            me, mine, got, head_cols, experts, feat_dim, orders
+        )
+    else:
+        whole = nn(mix, jnp.concatenate([mine, got], axis=0))
+        qkv_grad = jnp.stack([whole[:, j * head_cols : (j + 1) * head_cols] for j in range(3)])
+        proj_grad = whole[:, 3 * head_cols : 4 * head_cols].T
+        router_grad = whole[:, 4 * head_cols : 4 * head_cols + experts]
+        norm_grads = whole[:, 4 * head_cols + experts :].T
+        out_bias_grad, norm_grads = norm_grads[:experts], norm_grads[experts:]
+    norm2_gain_grad, norm2_bias_grad, proj_bias_grad = norm_grads[0], norm_grads[1], norm_grads[2]
     return (
         output,
         input_grad,

time: 247 us -> 249 us (level)
  matrix products: 65.4 us -> 59.5 us
  local copies, waits for them, and re-layouts: 12.8 us -> 17.7 us
  other arithmetic: 21.1 us -> 24.8 us
  starting transfers between devices: 54.8 us -> 57.8 us
    ppermute x0 -> x8, waiting for transfers between devices: none -> 35.7 us  [along(): lax.ppermute(x, 'dp', [(i, i ^ orders[i & 1][turn]) for i in range(count)])]
    ppermute x18 -> x4, waiting for transfers between devices: 34.3 us -> 7.08 us  [across(): return lax.ppermute(x, 'dp', [(i, i ^ bit) for i in range(count)])]
    ppermute x0 -> x8, starting transfers between devices: none -> 21.1 us  [along(): lax.ppermute(x, 'dp', [(i, i ^ orders[i & 1][turn]) for i in range(count)])]
    ppermute x18 -> x4, starting transfers between devices: 20.1 us -> 0.3 us  [across(): return lax.ppermute(x, 'dp', [(i, i ^ bit) for i in range(count)])]
    all_to_all x1, waiting for transfers between devices: 15.8 us -> 8.41 us  [local(): lax.all_to_all(row_send, 'dp', split_axis=0, concat_axis=0, tiled=True)]
    concatenate x6 -> x4, other arithmetic: 0.29 us -> 5.97 us  [the longest x1 4.73 us: local(): total = jnp.concatenate([qkv_total, proj_total, small], axis=1)]
    slice x4, local copies, waits for them, and re-layouts: 1.17 us -> 5.35 us  [local(): queries, key_vals, values_in = (heads_view[0], heads_view[1], heads_view[2])]
    dot_general x28 -> x27, matrix products: 48.5 us -> 44.5 us  [dot(): return lax.dot_general(a, b, (dims, ((), ())), preferred_element_type=out)]
  transfers between devices with their start and end apart: 29 -> 23, of which waited for: 19 -> 16; matrix products, arithmetic and copies ran while one was open for 28% -> 26% of each run, Pallas kernels for 0% -> 0%
where the time goes in v3:
time: 249 us; the launch traced here: 248 us
  waiting for transfers between devices  81.4 us (33%)
  matrix products  59.5 us (24%)
  starting transfers between devices  57.8 us (23%)
  other arithmetic  24.8 us (10%)
  local copies, waits for them, and re-layouts  17.7 us (7%)
  Pallas kernels  4.52 us (2%)
    dot_general x27, matrix products, dot(): return lax.dot_general(a, b, (dims, ((), ())), preferred_element_type=out)  44.5 us
    ppermute x8, waiting for transfers between devices, along(): lax.ppermute(x, 'dp', [(i, i ^ orders[i & 1][turn]) for i in range(count)])  35.7 us
    ppermute x7, waiting for transfers between devices, swap(): return lax.ppermute(x, 'tensor', [(0, 1), (1, 0)])  24.7 us
    ppermute x8, starting transfers between devices, along(): lax.ppermute(x, 'dp', [(i, i ^ orders[i & 1][turn]) for i in range(count)])  21.1 us
    all_to_all x1, waiting for transfers between devices, local(): lax.all_to_all(row_send, 'dp', split_axis=0, concat_axis=0, tiled=True)  8.41 us
    ppermute x7, starting transfers between devices, swap(): return lax.ppermute(x, 'tensor', [(0, 1), (1, 0)])  7.96 us
    all_to_all x1, starting transfers between devices, local(): lax.all_to_all(out_send, 'dp', split_axis=0, concat_axis=0, tiled=True)  7.67 us
    all_to_all x1, starting transfers between devices, local(): lax.all_to_all(row_send, 'dp', split_axis=0, concat_axis=0, tiled=True)  7.64 us
  transfers between devices with their start and end apart: 23, of which 16 were waited for; matrix products, arithmetic and copies ran while one was open for 26% of the time, Pallas kernels for 0%

profile of v3, /device:TPU:0, one launch (start us, length us, event | category | flops | bytes accessed | tf_op | source)
XLA Modules:
  0.0 247.6 jit_solution(13935745768257163836)
XLA Ops:
  6.0 7.4 %all-to-all-start = ((bf16[16,48,384]{2,1,0:T(8,128)(2,1)}), bf16[16,48,384]{2,1,0:T(8,128)(2,1)}, u32[]{:S(2)}, u32[]{:S(2)}) async-start(bf16[16,48,384]{2,1,0:T(8,128)(2,1)} %broadcast_select_fusion), calls=%async_computation | async-start | bytes 1179648 | tf_op jit(solution)/shard_map/all_to_all | solution.py:211
  23.1 2.6 %fusion.187 = (f32[6,197]{1,0:T(8,128)S(1)}, f32[6,197,197]{1,2,0:T(8,128)}) fusion(bf16[197,6,64]{0,2,1:T(8,128)(2,1)} %bitcast.133, bf16[197,6,64]{0,2,1:T(8,128)(2,1)S(1)} %bitcast.129), kind=kOutput, calls=%fused_computation.294 | convolution fusion | flops 30504070 | bytes 1238736 | tf_op jit(solution)/shard_map/sub | solution.py:226
  25.7 2.4 convolution_convert_fusion.5
  29.8 2.2 broadcast_select_fusion.4
  32.0 3.3 %collective-permute-done = bf16[197,384]{1,0:T(8,128)(2,1)} collective-permute-done((bf16[197,384]{1,0:T(8,128)(2,1)S(1)}, bf16[197,384]{1,0:T(8,128)(2,1)}, u32[]{:S(2)}, u32[]{:S(2)}) %collective-permute-start) | collective-permute-done | bytes 151328 | tf_op jit(solution)/shard_map/ppermute | solution.py:62
  41.7 5.7 %all-to-all-start.1 = ((bf16[16,48,768]{2,1,0:T(8,128)(2,1)}), bf16[16,48,768]{2,1,0:T(8,128)(2,1)S(1)}, u32[]{:S(2)}, u32[]{:S(2)}) async-start(bf16[16,48,768]{2,1,0:T(8,128)(2,1)} %bitcast.118), calls=%async_computation.1 | async-start | bytes 2359296 | tf_op jit(solution)/shard_map/all_to_all | solution.py:241
  49.1 14.2 %collective-permute-done.2 = bf16[768,384]{1,0:T(8,128)(2,1)} collective-permute-done((bf16[768,384]{1,0:T(8,128)(2,1)}, bf16[768,384]{1,0:T(8,128)(2,1)}, u32[]{:S(2)}, u32[]{:S(2)}) %collective-permute-start.2) | collective-permute-done | bytes 589856 | tf_op jit(solution)/shard_map/ppermute | solution.py:62
  67.1 5.5 %all-to-all-done.1 = bf16[16,48,768]{2,1,0:T(8,128)(2,1)S(1)} async-done(((bf16[16,48,768]{2,1,0:T(8,128)(2,1)}), bf16[16,48,768]{2,1,0:T(8,128)(2,1)S(1)}, u32[]{:S(2)}, u32[]{:S(2)}) %all-to-all-start.1) | async-done | bytes 1179680 | tf_op jit(solution)/shard_map/all_to_all | solution.py:241
  73.9 3.4 %multiply_convert_fusion = (bf16[768,1536]{1,0:T(8,128)(2,1)S(1)}, f32[768,1536]{1,0:T(8,128)S(1)}) fusion(f32[1536]{0:T(1024)} %reduce.7, bf16[768,768]{1,0:T(8,128)(2,1)S(1)} %bitcast.116, bf16[1,768,1536]{2,1,0:T(8,128)(2,1)S(1)} %copy-done), kind=kOutput, calls=%fused_computation.8 | convolution fusion | flops 1819017216 | bytes 10622976 | tf_op jit(solution)/shard_map/dot_general | solution.py:36
  77.3 4.8 %fusion.189 = (f32[1536]{0:T(1024)}, bf16[768,1536]{1,0:T(8,128)(2,1)S(1)}) fusion(f32[768,1536]{1,0:T(8,128)S(1)} %get-tuple-element.149, f32[1536]{0:T(1024)S(1)} %copy-done.52, bf16[1,1536,768]{2,1,0:T(8,128)(2,1)S(1)} %copy-done.76, f32[768]{0:T(1024)S(1)} %fusion.160, bf16[768,384]{1,0:T(8,128)(2,1)S(1)} %copy-done.24, bf16[768,384]{1,0:T(8,128)(2,1)S(1)} %copy-done.22), kind=kOutput, calls=%fused_computation.296 | convolution fusion | flops 1829632512 | bytes 10632192 | tf_op jit(solution)/shard_map/dot_general | solution.py:36
  82.1 3.1 %fusion.16 = bf16[768,768]{1,0:T(8,128)(2,1)} fusion(bf16[1,768,1536]{2,1,0:T(8,128)(2,1)S(1)} %copy-done, bf16[768,1536]{1,0:T(8,128)(2,1)S(1)} %get-tuple-element.154), kind=kOutput, calls=%fused_computation.27 | convolution fusion | flops 1812529152 | bytes 5898240 | tf_op jit(solution)/shard_map/dot_general | solution.py:36
  85.2 3.1 %fusion.6 = (f32[768]{0:T(1024)S(1)}, bf16[768,768]{1,0:T(8,128)(2,1)}) fusion(bf16[768,384]{1,0:T(8,128)(2,1)S(1)} %copy-done.24, bf16[768,384]{1,0:T(8,128)(2,1)S(1)} %copy-done.22, f32[768]{0:T(1024)S(1)} %fusion.160, bf16[768,1536]{1,0:T(8,128)(2,1)S(1)} %get-tuple-element.148, bf16[1,1536,768]{2,1,0:T(8,128)(2,1)S(1)} %copy-done.76), kind=kOutput, calls=%fused_computation.14 | convolution fusion | flops 1816657152 | bytes 7084032 | tf_op jit(solution)/shard_map/dot_general | solution.py:36
  89.7 7.6 %all-to-all-start.2 = ((bf16[16,48,768]{2,1,0:T(8,128)(2,1)}), bf16[16,48,768]{2,1,0:T(8,128)(2,1)S(1)}, u32[]{:S(2)}, u32[]{:S(2)}) async-start(bf16[16,48,768]{2,1,0:T(8,128)(2,1)} %select_select_fusion), calls=%async_computation.2 | async-start | bytes 2359296 | tf_op jit(solution)/shard_map/all_to_all | solution.py:291
  103.6 6.2 %fusion.119 = f32[1536,768]{1,0:T(8,128)} fusion(bf16[768,1536]{1,0:T(8,128)(2,1)} %copy-done.80, f32[768]{0:T(1024)S(1)} %copy-done.58, bf16[768,384]{1,0:T(8,128)(2,1)} %get-tuple-element.125, bf16[768,384]{1,0:T(8,128)(2,1)S(1)} %copy-done.23), kind=kOutput, calls=%fused_computation.172 | convolution fusion | flops 1815478272 | bytes 8260608 | tf_op jit(solution)/shard_map/dot_general | solution.py:36
  109.9 4.2 %fusion.38 = f32[768,1536]{1,0:T(8,128)} fusion(bf16[768,768]{1,0:T(8,128)(2,1)S(1)} %bitcast.117, bf16[768,1536]{1,0:T(8,128)(2,1)S(1)} %copy-done.11), kind=kOutput, calls=%fused_computation.69 | convolution fusion | flops 1811939328 | bytes 8257536 | tf_op jit(solution)/shard_map/dot_general | solution.py:36
  114.1 8.4 %all-to-all-done.2 = bf16[16,48,768]{2,1,0:T(8,128)(2,1)S(1)} async-done(((bf16[16,48,768]{2,1,0:T(8,128)(2,1)}), bf16[16,48,768]{2,1,0:T(8,128)(2,1)S(1)}, u32[]{:S(2)}, u32[]{:S(2)}) %all-to-all-start.2) | async-done | bytes 1179680 | tf_op jit(solution)/shard_map/all_to_all | solution.py:291
  122.6 7.7 %all-to-all-start.3 = ((bf16[16,48,768]{2,1,0:T(8,128)(2,1)}), bf16[16,48,768]{2,1,0:T(8,128)(2,1)}, u32[]{:S(2)}, u32[]{:S(2)}) async-start(bf16[16,48,768]{2,1,0:T(8,128)(2,1)} %bitcast.127), calls=%async_computation.3 | async-start | bytes 2359296 | tf_op jit(solution)/shard_map/all_to_all | solution.py:299
  135.3 5.4 %collective-permute-done.3 = bf16[197,768]{1,0:T(8,128)(2,1)S(1)} collective-permute-done((bf16[197,768]{1,0:T(8,128)(2,1)S(1)}, bf16[197,768]{1,0:T(8,128)(2,1)S(1)}, u32[]{:S(2)}, u32[]{:S(2)}) %collective-permute-start.3) | collective-permute-done | bytes 302624 | tf_op jit(solution)/shard_map/ppermute | solution.py:62
  149.5 3.4 %fusion.32 = f32[768,1152]{1,0:T(8,128)} fusion(s32[768]{0:T(1024)S(1)} %copy-done.62, s32[768]{0:T(1024)S(1)} %copy-done.61, s32[768]{0:T(1024)S(1)} %copy-done.63, bf16[197,384]{0,1:T(8,128)(2,1)S(1)} %bitcast.137, bf16[197,384]{0,1:T(8,128)(2,1)S(1)} %bitcast.123, bf16[197,384]{0,1:T(8,128)(2,1)S(1)} %bitcast.120, bf16[197,768]{1,0:T(8,128)(2,1)S(1)} %copy-done.7, ...), kind=kOutput, calls=%fused_computation.61 | convolution fusion | flops 585166848 | bytes 4312360 | tf_op jit(solution)/shard_map/dot_general | solution.py:36
  152.9 4.7 %pad_maximum_fusion = f32[768,1664]{1,0:T(8,128)} fusion(f32[768,128]{1,0:T(8,128)} %fusion.33, f32[768,384]{1,0:T(8,128)S(1)} %fusion.31, f32[768,1152]{1,0:T(8,128)} %fusion.32), kind=kLoop, calls=%fused_computation.2 | loop fusion | flops 2555904 | bytes 10223616 | tf_op jit(solution)/shard_map/concatenate | solution.py:396
  161.5 3.0 %collective-permute-done.5 = bf16[384,1664]{1,0:T(8,128)(2,1)S(1)} collective-permute-done((bf16[384,1664]{1,0:T(8,128)(2,1)S(1)}, bf16[384,1664]{1,0:T(8,128)(2,1)S(1)}, u32[]{:S(2)}, u32[]{:S(2)}) %collective-permute-start.5) | collective-permute-done | bytes 1277984 | tf_op jit(solution)/shard_map/ppermute | solution.py:82
  169.8 7.2 %collective-permute-done.6 = bf16[192,1664]{1,0:T(8,128)(2,1)S(1)} collective-permute-done((bf16[192,1664]{1,0:T(8,128)(2,1)S(1)}, bf16[192,1664]{1,0:T(8,128)(2,1)S(1)}, u32[]{:S(2)}, u32[]{:S(2)}) %collective-permute-start.6) | collective-permute-done | bytes 639008 | tf_op jit(solution)/shard_map/ppermute | solution.py:82
  180.3 6.8 %collective-permute-done.13 = bf16[96,1664]{1,0:T(8,128)(2,1)S(1)} collective-permute-done((bf16[96,1664]{1,0:T(8,128)(2,1)S(1)}, bf16[96,1664]{1,0:T(8,128)(2,1)S(1)}, u32[]{:S(2)}, u32[]{:S(2)}) %collective-permute-start.13) | collective-permute-done | bytes 319520 | tf_op jit(solution)/shard_map/ppermute | solution.py:82
  189.8 3.6 %collective-permute-done.14 = bf16[48,1664]{1,0:T(8,128)(2,1)S(1)} collective-permute-done((bf16[48,1664]{1,0:T(8,128)(2,1)S(1)}, bf16[48,1664]{1,0:T(8,128)(2,1)S(1)}, u32[]{:S(2)}, u32[]{:S(2)}) %collective-permute-start.14) | collective-permute-done | bytes 159776 | tf_op jit(solution)/shard_map/ppermute | solution.py:82
  193.4 2.3 collective-permute-start.15
  199.7 7.2 %collective-permute-start.16 = (bf16[96,1664]{1,0:T(8,128)(2,1)S(1)}, bf16[96,1664]{1,0:T(8,128)(2,1)S(1)}, u32[]{:S(2)}, u32[]{:S(2)}) collective-permute-start(bf16[96,1664]{1,0:T(8,128)(2,1)S(1)} %pad_maximum_fusion.5), channel_id=1, source_target_pairs={{0,8},{2,18},{4,12},{6,22},{8,0},{10,26},{12,4},{14,30},{16,24},{1... | collective-permute-start | bytes 958472 | tf_op jit(solution)/shard_map/ppermute | solution.py:82
  207.0 7.1 %collective-permute-done.16 = bf16[96,1664]{1,0:T(8,128)(2,1)S(1)} collective-permute-done((bf16[96,1664]{1,0:T(8,128)(2,1)S(1)}, bf16[96,1664]{1,0:T(8,128)(2,1)S(1)}, u32[]{:S(2)}, u32[]{:S(2)}) %collective-permute-start.16) | collective-permute-done | bytes 319520 | tf_op jit(solution)/shard_map/ppermute | solution.py:82
  214.1 6.2 %collective-permute-start.17 = (bf16[192,1664]{1,0:T(8,128)(2,1)S(1)}, bf16[192,1664]{1,0:T(8,128)(2,1)S(1)}, u32[]{:S(2)}, u32[]{:S(2)}) collective-permute-start(bf16[192,1664]{1,0:T(8,128)(2,1)S(1)} %pad_maximum_fusion.3), channel_id=1, source_target_pairs={{0,4},{2,10},{4,0},{6,14},{8,12},{10,2},{12,8},{14,6},{16,20},{18,... | collective-permute-start | bytes 1916936 | tf_op jit(solution)/shard_map/ppermute | solution.py:82
  222.5 6.3 %collective-permute-done.17 = bf16[192,1664]{1,0:T(8,128)(2,1)S(1)} collective-permute-done((bf16[192,1664]{1,0:T(8,128)(2,1)S(1)}, bf16[192,1664]{1,0:T(8,128)(2,1)S(1)}, u32[]{:S(2)}, u32[]{:S(2)}) %collective-permute-start.17) | collective-permute-done | bytes 639008 | tf_op jit(solution)/shard_map/ppermute | solution.py:82
  230.1 3.7 %collective-permute-done.11 = f32[3,768]{1,0:T(4,128)S(1)} collective-permute-done((f32[3,768]{1,0:T(4,128)S(1)}, f32[3,768]{1,0:T(4,128)S(1)}, u32[]{:S(2)}, u32[]{:S(2)}) %collective-permute-start.11) | collective-permute-done | bytes 9248 | tf_op jit(solution)/shard_map/ppermute | solution.py:66
  235.0 3.4 %collective-permute-done.12 = f32[3,768]{1,0:T(4,128)S(1)} collective-permute-done((f32[3,768]{1,0:T(4,128)S(1)}, f32[3,768]{1,0:T(4,128)S(1)}, u32[]{:S(2)}, u32[]{:S(2)}) %collective-permute-start.12) | collective-permute-done | bytes 9248 | tf_op jit(solution)/shard_map/ppermute | solution.py:66
  241.7 4.5 %finish.1 = (f32[3,768,384]{2,1,0:T(8,128)}, f32[384,768]{1,0:T(8,128)}, f32[768,16]{1,0:T(8,128)S(1)}, f32[16,768]{1,0:T(8,128)}, f32[8,768]{1,0:T(8,128)S(1)}) custom-call(s32[1]{0:T(128)} %bitcast.48.refs_0_, bf16[384,1664]{1,0:T(8,128)(2,1)} %pad_maximum_fusion.1.refs_1_, bf16[384,1664]{1,0:T(8,128)(2,1)} %collective-permute-done.18.refs_2_), custom_call_target="tpu_custom_call" | custom-call | tf_op jit(solution)/shard_map/finish/pallas_call | solution.py:124
  (299 shorter events, 79.0 us)
Async XLA Ops:
  0.6 73.2 %copy-start = (bf16[1,768,1536]{2,1,0:T(8,128)(2,1)S(1)}, bf16[1,768,1536]{2,1,0:T(8,128)(2,1)}, u32[]{:S(2)}) copy-start(bf16[1,768,1536]{2,1,0:T(8,128)(2,1)} %param.26) | copy-start | bytes 7077892
  3.1 36.1 %copy-start.68 = (s32[197,1]{0,1:T(1,128)}, s32[197,1]{0,1:T(1,128)S(1)}, u32[]{:S(2)}) copy-start(s32[197,1]{0,1:T(1,128)S(1)} %get-tuple-element.139) | copy-start | bytes 2368
  3.1 36.1 %copy-start.70 = (s32[197,1]{0,1:T(1,128)}, s32[197,1]{0,1:T(1,128)S(1)}, u32[]{:S(2)}) copy-start(s32[197,1]{0,1:T(1,128)S(1)} %get-tuple-element.141) | copy-start | bytes 2368
  6.0 29.4 %all-to-all-start = ((bf16[16,48,384]{2,1,0:T(8,128)(2,1)}), bf16[16,48,384]{2,1,0:T(8,128)(2,1)}, u32[]{:S(2)}, u32[]{:S(2)}) async-start(bf16[16,48,384]{2,1,0:T(8,128)(2,1)} %broadcast_select_fusion), calls=%async_computation | async-start | bytes 1179648 | tf_op jit(solution)/shard_map/all_to_all | solution.py:211
  13.4 16.4 %collective-permute-start.1 = (bf16[384,768]{1,0:T(8,128)(2,1)S(1)}, bf16[384,768]{1,0:T(8,128)(2,1)}, u32[]{:S(2)}, u32[]{:S(2)}) collective-permute-start(bf16[384,768]{1,0:T(8,128)(2,1)S(1)} %copy-done.8), channel_id=1, source_target_pairs={{0,1},{1,0},{2,3},{3,2},{4,5},{5,4},{6,7},{7,6},{8,9},{9,8},{10,11... | collective-permute-start | bytes 1769480 | tf_op jit(solution)/shard_map/ppermute | solution.py:62
  29.2 6.1 %collective-permute-start = (bf16[197,384]{1,0:T(8,128)(2,1)S(1)}, bf16[197,384]{1,0:T(8,128)(2,1)}, u32[]{:S(2)}, u32[]{:S(2)}) collective-permute-start(bf16[197,384]{1,0:T(8,128)(2,1)S(1)} %copy.71), channel_id=1, source_target_pairs={{0,1},{1,0},{2,3},{3,2},{4,5},{5,4},{6,7},{7,6},{8,9},{9,8},{10,11... | collective-permute-start | bytes 453896 | tf_op jit(solution)/shard_map/ppermute | solution.py:62
  41.7 30.9 %all-to-all-start.1 = ((bf16[16,48,768]{2,1,0:T(8,128)(2,1)}), bf16[16,48,768]{2,1,0:T(8,128)(2,1)S(1)}, u32[]{:S(2)}, u32[]{:S(2)}) async-start(bf16[16,48,768]{2,1,0:T(8,128)(2,1)} %bitcast.118), calls=%async_computation.1 | async-start | bytes 2359296 | tf_op jit(solution)/shard_map/all_to_all | solution.py:241
  47.4 16.0 %collective-permute-start.2 = (bf16[768,384]{1,0:T(8,128)(2,1)}, bf16[768,384]{1,0:T(8,128)(2,1)}, u32[]{:S(2)}, u32[]{:S(2)}) collective-permute-start(bf16[768,384]{1,0:T(8,128)(2,1)} %bitcast.19), channel_id=1, source_target_pairs={{0,1},{1,0},{2,3},{3,2},{4,5},{5,4},{6,7},{7,6},{8,9},{9,8},{10,11... | collective-permute-start | bytes 1769480 | tf_op jit(solution)/shard_map/ppermute | solution.py:62
  89.7 13.9 %copy-start.23 = (bf16[768,384]{1,0:T(8,128)(2,1)S(1)}, bf16[768,384]{1,0:T(8,128)(2,1)}, u32[]{:S(2)}) copy-start(bf16[768,384]{1,0:T(8,128)(2,1)} %copy-done.21) | copy-start | bytes 1769476
  89.7 13.9 %copy-start.58 = (f32[768]{0:T(1024)S(1)}, f32[768]{0:T(1024)}, u32[]{:S(2)}) copy-start(f32[768]{0:T(1024)} %copy-done.57) | copy-start | bytes 9220
  89.7 32.8 %all-to-all-start.2 = ((bf16[16,48,768]{2,1,0:T(8,128)(2,1)}), bf16[16,48,768]{2,1,0:T(8,128)(2,1)S(1)}, u32[]{:S(2)}, u32[]{:S(2)}) async-start(bf16[16,48,768]{2,1,0:T(8,128)(2,1)} %select_select_fusion), calls=%async_computation.2 | async-start | bytes 2359296 | tf_op jit(solution)/shard_map/all_to_all | solution.py:291
  114.1 16.8 %copy-start.69 = (s32[197,1]{0,1:T(1,128)S(1)}, s32[197,1]{0,1:T(1,128)}, u32[]{:S(2)}) copy-start(s32[197,1]{0,1:T(1,128)} %copy-done.68) | copy-start | bytes 2368
  114.1 16.8 %copy-start.71 = (s32[197,1]{0,1:T(1,128)S(1)}, s32[197,1]{0,1:T(1,128)}, u32[]{:S(2)}) copy-start(s32[197,1]{0,1:T(1,128)} %copy-done.70) | copy-start | bytes 2368
  122.6 35.1 %all-to-all-start.3 = ((bf16[16,48,768]{2,1,0:T(8,128)(2,1)}), bf16[16,48,768]{2,1,0:T(8,128)(2,1)}, u32[]{:S(2)}, u32[]{:S(2)}) async-start(bf16[16,48,768]{2,1,0:T(8,128)(2,1)} %bitcast.127), calls=%async_computation.3 | async-start | bytes 2359296 | tf_op jit(solution)/shard_map/all_to_all | solution.py:299
  130.3 3.7 %collective-permute-start.4 = (f32[16,48]{1,0:T(8,128)S(1)}, f32[16,48]{1,0:T(8,128)S(1)}, u32[]{:S(2)}, u32[]{:S(2)}) collective-permute-start(f32[16,48]{1,0:T(8,128)S(1)} %convert_reduce_fusion.2), channel_id=1, source_target_pairs={{0,1},{1,0},{2,3},{3,2},{4,5},{5,4},{6,7},{7,6},{8,9},{9,8},{10,11... | collective-permute-start | bytes 9224 | tf_op jit(solution)/shard_map/ppermute | solution.py:62
  131.4 9.3 %collective-permute-start.3 = (bf16[197,768]{1,0:T(8,128)(2,1)S(1)}, bf16[197,768]{1,0:T(8,128)(2,1)S(1)}, u32[]{:S(2)}, u32[]{:S(2)}) collective-permute-start(bf16[197,768]{1,0:T(8,128)(2,1)S(1)} %convolution_convert_fusion.3), channel_id=1, source_target_pairs={{0,1},{1,0},{2,3},{3,2},{4,5},{5,4},{6,7},{7,6},{8,9},{9,8},{10,11... | collective-permute-start | bytes 907784 | tf_op jit(solution)/shard_map/ppermute | solution.py:62
  161.4 3.1 %collective-permute-start.5 = (bf16[384,1664]{1,0:T(8,128)(2,1)S(1)}, bf16[384,1664]{1,0:T(8,128)(2,1)S(1)}, u32[]{:S(2)}, u32[]{:S(2)}) collective-permute-start(bf16[384,1664]{1,0:T(8,128)(2,1)S(1)} %slice.190), channel_id=1, source_target_pairs={{0,2},{2,0},{4,6},{6,4},{8,10},{10,8},{12,14},{14,12},{16,18},{18,... | collective-permute-start | bytes 3833864 | tf_op jit(solution)/shard_map/ppermute | solution.py:82
  166.5 13.3 %copy-start.12 = (bf16[3,768,384]{2,1,0:T(8,128)(2,1)S(1)}, bf16[3,768,384]{2,1,0:T(8,128)(2,1)}, u32[]{:S(2)}) copy-start(bf16[3,768,384]{2,1,0:T(8,128)(2,1)} %param.19) | copy-start | bytes 5308420
  166.6 10.5 %collective-permute-start.6 = (bf16[192,1664]{1,0:T(8,128)(2,1)S(1)}, bf16[192,1664]{1,0:T(8,128)(2,1)S(1)}, u32[]{:S(2)}, u32[]{:S(2)}) collective-permute-start(bf16[192,1664]{1,0:T(8,128)(2,1)S(1)} %slice.191), channel_id=1, source_target_pairs={{0,4},{2,10},{4,0},{6,14},{8,12},{10,2},{12,8},{14,6},{16,20},{18,... | collective-permute-start | bytes 1916936 | tf_op jit(solution)/shard_map/ppermute | solution.py:82
  168.4 9.4 %collective-permute-start.7 = (bf16[197,768]{1,0:T(8,128)(2,1)S(1)}, bf16[197,768]{1,0:T(8,128)(2,1)S(1)}, u32[]{:S(2)}, u32[]{:S(2)}) collective-permute-start(bf16[197,768]{1,0:T(8,128)(2,1)S(1)} %convolution_convert_fusion.2), channel_id=1, source_target_pairs={{0,1},{1,0},{2,3},{3,2},{4,5},{5,4},{6,7},{7,6},{8,9},{9,8},{10,11... | collective-permute-start | bytes 907784 | tf_op jit(solution)/shard_map/ppermute | solution.py:62
  177.9 9.2 %collective-permute-start.13 = (bf16[96,1664]{1,0:T(8,128)(2,1)S(1)}, bf16[96,1664]{1,0:T(8,128)(2,1)S(1)}, u32[]{:S(2)}, u32[]{:S(2)}) collective-permute-start(bf16[96,1664]{1,0:T(8,128)(2,1)S(1)} %slice.192), channel_id=1, source_target_pairs={{0,8},{2,18},{4,12},{6,22},{8,0},{10,26},{12,4},{14,30},{16,24},{1... | collective-permute-start | bytes 958472 | tf_op jit(solution)/shard_map/ppermute | solution.py:82
  187.2 6.2 %collective-permute-start.14 = (bf16[48,1664]{1,0:T(8,128)(2,1)S(1)}, bf16[48,1664]{1,0:T(8,128)(2,1)S(1)}, u32[]{:S(2)}, u32[]{:S(2)}) collective-permute-start(bf16[48,1664]{1,0:T(8,128)(2,1)S(1)} %slice.193), channel_id=1, source_target_pairs={{0,16},{2,6},{4,20},{6,2},{8,24},{10,14},{12,28},{14,10},{16,0},{1... | collective-permute-start | bytes 479240 | tf_op jit(solution)/shard_map/ppermute | solution.py:82
  193.4 6.2 %collective-permute-start.15 = (bf16[48,1664]{1,0:T(8,128)(2,1)S(1)}, bf16[48,1664]{1,0:T(8,128)(2,1)S(1)}, u32[]{:S(2)}, u32[]{:S(2)}) collective-permute-start(bf16[48,1664]{1,0:T(8,128)(2,1)S(1)} %fusion.94), channel_id=1, source_target_pairs={{0,16},{2,6},{4,20},{6,2},{8,24},{10,14},{12,28},{14,10},{16,0},{1... | collective-permute-start | bytes 479240 | tf_op jit(solution)/shard_map/ppermute | solution.py:82
  196.1 24.7 %copy-start.35 = (f32[16,768]{1,0:T(8,128)S(1)}, f32[16,768]{1,0:T(8,128)}, u32[]{:S(2)}) copy-start(f32[16,768]{1,0:T(8,128)} %param.29) | copy-start | bytes 147460
  196.1 24.1 %collective-permute-start.8 = (bf16[197,768]{1,0:T(8,128)(2,1)S(1)}, bf16[197,768]{1,0:T(8,128)(2,1)S(1)}, u32[]{:S(2)}, u32[]{:S(2)}) collective-permute-start(bf16[197,768]{1,0:T(8,128)(2,1)S(1)} %fusion.26), channel_id=1, source_target_pairs={{0,1},{1,0},{2,3},{3,2},{4,5},{5,4},{6,7},{7,6},{8,9},{9,8},{10,11... | collective-permute-start | bytes 907784 | tf_op jit(solution)/shard_map/ppermute | solution.py:62
  199.7 14.3 %collective-permute-start.16 = (bf16[96,1664]{1,0:T(8,128)(2,1)S(1)}, bf16[96,1664]{1,0:T(8,128)(2,1)S(1)}, u32[]{:S(2)}, u32[]{:S(2)}) collective-permute-start(bf16[96,1664]{1,0:T(8,128)(2,1)S(1)} %pad_maximum_fusion.5), channel_id=1, source_target_pairs={{0,8},{2,18},{4,12},{6,22},{8,0},{10,26},{12,4},{14,30},{16,24},{1... | collective-permute-start | bytes 958472 | tf_op jit(solution)/shard_map/ppermute | solution.py:82
  214.1 14.7 %collective-permute-start.17 = (bf16[192,1664]{1,0:T(8,128)(2,1)S(1)}, bf16[192,1664]{1,0:T(8,128)(2,1)S(1)}, u32[]{:S(2)}, u32[]{:S(2)}) collective-permute-start(bf16[192,1664]{1,0:T(8,128)(2,1)S(1)} %pad_maximum_fusion.3), channel_id=1, source_target_pairs={{0,4},{2,10},{4,0},{6,14},{8,12},{10,2},{12,8},{14,6},{16,20},{18,... | collective-permute-start | bytes 1916936 | tf_op jit(solution)/shard_map/ppermute | solution.py:82
  220.7 1.6 collective-permute-start.9
  222.4 7.6 %collective-permute-start.10 = (f32[3,768]{1,0:T(4,128)S(1)}, f32[3,768]{1,0:T(4,128)S(1)}, u32[]{:S(2)}, u32[]{:S(2)}) collective-permute-start(f32[3,768]{1,0:T(4,128)S(1)} %fusion.178), channel_id=1, source_target_pairs={{0,4},{2,6},{4,0},{6,2},{8,12},{10,14},{12,8},{14,10},{16,20},{18,... | collective-permute-start | bytes 27656 | tf_op jit(solution)/shard_map/ppermute | solution.py:66
  230.0 11.8 %collective-permute-start.18 = (bf16[384,1664]{1,0:T(8,128)(2,1)}, bf16[384,1664]{1,0:T(8,128)(2,1)}, u32[]{:S(2)}, u32[]{:S(2)}) collective-permute-start(bf16[384,1664]{1,0:T(8,128)(2,1)} %pad_maximum_fusion.1.refs_1_), channel_id=1, source_target_pairs={{0,2},{2,0},{4,6},{6,4},{8,10},{10,8},{12,14},{14,12},{16,18},{18,... | collective-permute-start | bytes 3833864 | tf_op jit(solution)/shard_map/ppermute | solution.py:82
  230.0 3.8 %collective-permute-start.11 = (f32[3,768]{1,0:T(4,128)S(1)}, f32[3,768]{1,0:T(4,128)S(1)}, u32[]{:S(2)}, u32[]{:S(2)}) collective-permute-start(f32[3,768]{1,0:T(4,128)S(1)} %fusion.228), channel_id=1, source_target_pairs={{0,8},{2,10},{4,12},{6,14},{8,0},{10,2},{12,4},{14,6},{16,24},{18,... | collective-permute-start | bytes 27656 | tf_op jit(solution)/shard_map/ppermute | solution.py:66
  233.8 4.6 %collective-permute-start.12 = (f32[3,768]{1,0:T(4,128)S(1)}, f32[3,768]{1,0:T(4,128)S(1)}, u32[]{:S(2)}, u32[]{:S(2)}) collective-permute-start(f32[3,768]{1,0:T(4,128)S(1)} %add.304), channel_id=1, source_target_pairs={{0,16},{2,18},{4,20},{6,22},{8,24},{10,26},{12,28},{14,30},{16,0},... | collective-permute-start | bytes 27656 | tf_op jit(solution)/shard_map/ppermute | solution.py:66
  (72 other events, 424.6 us)

commit v4 on v3

--- a/solution.py
+++ b/solution.py
@@ -85,6 +85,143 @@
 def halve(total, orders, turn, count):
     middle = total.shape[0] // 2
     return total[:middle] + along(total[middle:].astype(BF16), orders, turn, count).astype(F32)
+
+
+def home_kernel(back_ref, onehot_ref, routes_ref, rank_ref, gates_ref, bias_dot_ref, home_ref, logit_ref, inner_ref):
+    experts, slots, feat_dim = back_ref.shape
+    tok_count = routes_ref.shape[0]
+    home = nn(onehot_ref[...], back_ref[...].reshape(experts * slots, feat_dim))
+    home_ref[...] = home.astype(BF16)
+    for e in range(experts):
+        inner_ref[0, e : e + 1, :] = back_ref[e, slots - 1 : slots, :slots].astype(F32)
+        inner_ref[1, e : e + 1, :] = back_ref[e, slots - 2 : slots - 1, :slots].astype(F32)
+    expert_ids = lax.broadcasted_iota(jnp.int32, (tok_count, experts), 1)
+    slot_ids = lax.broadcasted_iota(jnp.int32, (tok_count, slots), 1)
+    picks, inner_grads = [], []
+    for k in range(2):
+        pick = routes_ref[:, k : k + 1] == expert_ids
+        hot = jnp.where(pick, 1.0, 0.0).astype(BF16)
+        found = nn(hot, inner_ref[0].astype(BF16)) + nn(hot, inner_ref[1].astype(BF16))
+        found = jnp.where(rank_ref[:, k : k + 1] == slot_ids, found, 0.0)
+        own_bias = jnp.where(pick, bias_dot_ref[...], 0.0)
+        inner_grads.append(
+            jnp.sum(found, axis=1, keepdims=True) + jnp.sum(own_bias, axis=1, keepdims=True)
+        )
+        picks.append(pick)
+    gates = [gates_ref[:, k : k + 1] for k in range(2)]
+    mean = gates[0] * inner_grads[0] + gates[1] * inner_grads[1]
+    logit_grad = 0.0
+    for k in range(2):
+        logit_grad = logit_grad + jnp.where(picks[k], gates[k] * (inner_grads[k] - mean), 0.0)
+    logit_ref[...] = logit_grad.astype(BF16)
+
+
+def home_rows(back, onehot, routes, rank, gates, bias_dot):
+    experts, slots, feat_dim = back.shape
+    tok_count = routes.shape[0]
+    return pl.pallas_call(
+        home_kernel,
+        out_shape=(
+            jax.ShapeDtypeStruct((tok_count, feat_dim), BF16),
+            jax.ShapeDtypeStruct((tok_count, experts), BF16),
+        ),
+        scratch_shapes=[pltpu.VMEM((2, experts, slots), F32)],
+        compiler_params=pltpu.CompilerParams(vmem_limit_bytes=24 << 20),
+        cost_estimate=pl.CostEstimate(
+            flops=2 * tok_count * feat_dim * experts * slots, bytes_accessed=2 << 20, transcendentals=0
+        ),
+        name="home_rows",
+    )(back, onehot, routes, rank, gates, bias_dot)
+
+
+def attention_grads_kernel(
+    home_ref, other_ref, logit_ref, router_ref, cot_ref, normed_ref, inverse_ref, gain_ref, hidden2_ref, bias_grad_ref,
+    proj_ref, projected_ref, lse_ref, attended_ref, hidden_ref, weight_ref, mix_ref,
+    sent_ref, kept_ref, hidden_part_ref, sums_ref, middle_grad_ref, low_ref, back_ref, small_ref,
+):
+    head_cols = attended_ref.shape[1]
+    experts = logit_ref.shape[1]
+    scale = HEAD ** (-0.5)
+    hidden_grad = home_ref[...].astype(F32) + other_ref[...].astype(F32) + nt(logit_ref[...], router_ref[...])
+    normed = normed_ref[...]
+    inner = hidden_grad * gain_ref[...]
+    middle_grad = cot_ref[...].astype(F32) + norm_back(inner, normed, inverse_ref[...])
+    middle_grad_ref[...] = middle_grad
+    middle_low = middle_grad.astype(BF16)
+    small_ref[...] = jnp.zeros_like(small_ref)
+    small_ref[:experts, :] = tn(logit_ref[...], hidden2_ref[...])
+    small_ref[experts : 2 * experts, :] = bias_grad_ref[...]
+    small_ref[2 * experts : 2 * experts + 1, :] = jnp.sum(hidden_grad * normed, axis=0, keepdims=True)
+    small_ref[2 * experts + 1 : 2 * experts + 2, :] = jnp.sum(hidden_grad, axis=0, keepdims=True)
+    small_ref[2 * experts + 2 : 2 * experts + 3, :] = jnp.sum(middle_grad, axis=0, keepdims=True)
+    back_ref[...] = nt(middle_low, proj_ref[...]).astype(BF16)
+    for h in range(head_cols // HEAD):
+        cols = slice(h * HEAD, (h + 1) * HEAD)
+        queries, key_vals, values_in = (projected_ref[j, :, cols] for j in range(3))
+        out_grad = back_ref[:, cols]
+        prob_vals = jnp.exp(nt(queries, key_vals) * scale - lse_ref[:, h : h + 1])
+        prob_low = prob_vals.astype(BF16)
+        prob_grad = nt(out_grad, values_in)
+        row = jnp.sum(prob_vals * prob_grad, axis=-1, keepdims=True)
+        score_low = (prob_vals * (prob_grad - row)).astype(BF16)
+        low_ref[:, h * HEAD : (h + 1) * HEAD] = (nn(score_low, key_vals) * scale).astype(BF16)
+        start = head_cols + h * HEAD
+        low_ref[:, start : start + HEAD] = (tn(score_low, queries) * scale).astype(BF16)
+        start = start + head_cols
+        low_ref[:, start : start + HEAD] = tn(prob_low, out_grad).astype(BF16)
+    low = low_ref[...]
+    half = kept_ref.shape[0]
+    mixed_middle = nt(mix_ref[...], middle_low).astype(BF16)
+    small = small_ref[...].astype(BF16)
+    for part in range(2):
+        rows = slice(part * half, (part + 1) * half)
+        pieces = (
+            nn(hidden_ref[rows, :], low),
+            nn(mixed_middle[rows, :], attended_ref[...]),
+            nt(mix_ref[rows, :], small),
+        )
+        first = 0
+        for piece in pieces:
+            last = first + piece.shape[1]
+            if part == 0:
+                kept_ref[:, first:last] = piece
+            else:
+                sent_ref[:, first:last] = piece.astype(BF16)
+            first = last
+    part = nt(low[:, :head_cols], weight_ref[0])
+    part = part + nt(low[:, head_cols : 2 * head_cols], weight_ref[1])
+    part = part + nt(low[:, 2 * head_cols :], weight_ref[2])
+    hidden_part_ref[...] = part.astype(BF16)
+    sums_ref[...] = jnp.sum(low.astype(F32), axis=0, keepdims=True)
+
+
+def attention_grads(*operands):
+    tok_count, feat_dim = operands[0].shape
+    experts = operands[2].shape[1]
+    head_cols = operands[10].shape[0]
+    small = -(-(2 * experts + 3) // 128) * 128
+    width = 4 * head_cols + small
+    flops = 2 * tok_count * feat_dim * head_cols * 9 + 2 * feat_dim * feat_dim * (tok_count + small)
+    return pl.pallas_call(
+        attention_grads_kernel,
+        out_shape=(
+            jax.ShapeDtypeStruct((feat_dim // 2, width), BF16),
+            jax.ShapeDtypeStruct((feat_dim // 2, width), F32),
+            jax.ShapeDtypeStruct((tok_count, feat_dim), BF16),
+            jax.ShapeDtypeStruct((1, 3 * head_cols), F32),
+            jax.ShapeDtypeStruct((tok_count, feat_dim), F32),
+        ),
+        scratch_shapes=[
+            pltpu.VMEM((tok_count, 3 * head_cols), BF16),
+            pltpu.VMEM((tok_count, head_cols), BF16),
+            pltpu.VMEM((small, feat_dim), F32),
+        ],
+        compiler_params=pltpu.CompilerParams(vmem_limit_bytes=40 << 20),
+        cost_estimate=pl.CostEstimate(
+            flops=flops, bytes_accessed=10 << 20, transcendentals=tok_count * tok_count * 6
+        ),
+        name="attention_grads",
+    )(*operands)
 
 
 def finish_kernel(head_cols, experts, orders, me_ref, mine, got, qkv_ref, proj_ref, router_ref, bias_ref, norm_ref, held_proj, held_small):
@@ -118,7 +255,7 @@
     norm_ref[...] = flat[2 * experts : 2 * experts + 8]
 
 
-def finish(me, mine, got, head_cols, experts, feat_dim, orders):
+def finish(me, mine, came, head_cols, experts, feat_dim, orders):
     width = mine.shape[1] - 4 * head_cols
     vmem = pl.BlockSpec(memory_space=pltpu.VMEM)
     return pl.pallas_call(
@@ -138,7 +275,12 @@
         ],
         compiler_params=pltpu.CompilerParams(vmem_limit_bytes=40 << 20),
         name="finish",
-    )(me[None], mine, got)
+    )(me[None], mine, came)
+
+
+def high_low(values):
+    high = values.astype(BF16)
+    return high, (values - high.astype(F32)).astype(BF16)
 
 
 def local(
@@ -225,8 +367,8 @@
     row_max = jnp.max(scores, axis=-1, keepdims=True)
     exp_scores = jnp.exp(scores - row_max)
     row_total = jnp.sum(exp_scores, axis=-1, keepdims=True)
-    prob_vals = exp_scores / row_total
-    prob_low = prob_vals.astype(BF16)
+    lse = (row_max + jnp.log(row_total)).reshape(heads_here, tok_count).T
+    prob_low = (exp_scores / row_total).astype(BF16)
     attended = jnp.einsum("bhqk,bkhd->bqhd", prob_low, values_in, preferred_element_type=F32)
     attended = attended.reshape(tok_count, head_cols).astype(BF16)
     attended_other, cot_mine = lax.optimization_barrier((swap(attended), cot_mine))
@@ -250,7 +392,7 @@
     gate_map = jnp.where(pick[0], gate_vals[0], 0.0) + jnp.where(pick[1], gate_vals[1], 0.0)
     grad_out = cotangent.astype(F32)
     row_grad = [(gate_vals[k] * grad_out).astype(BF16) for k in range(2)]
-    out_bias_grad = tn(row_grad[0], pick_low[0]) + tn(row_grad[1], pick_low[1])
+    out_bias_grad = tn(pick_low[0], row_grad[0]) + tn(pick_low[1], row_grad[1])
 
     note_rows = jnp.where(plane == 0, cot_mine, cot_other).reshape(sources, slots, half_dim)
     other_expert = note_rows[:, slots - 1, :slots].reshape(-1, 1).astype(jnp.int32)
@@ -272,13 +414,14 @@
     pre_act = nn(arrived, in_weight) + expert_in_bias[0]
     activ_vals, gelu_slope = gelu_parts(pre_act)
     activ_low = activ_vals.astype(BF16)
+    part_out = nn(activ_low, out_weight)
     act_grad = nt(grad_rows, out_weight) * gelu_slope
     in_bias_grad = jnp.sum(act_grad, axis=0)
     act_low = act_grad.astype(BF16)
     row_part = nt(act_low, in_weight)
-    part_out = nn(activ_low, out_weight)
 
     inner = jnp.sum(cot_rows.astype(F32) * part_out, axis=1).reshape(sources, slots)
+    inner = inner + swap(inner)
     inner_high = inner.astype(BF16)
     inner_low = (inner - inner_high.astype(F32)).astype(BF16)
 
@@ -291,12 +434,38 @@
     row_back = lax.all_to_all(row_send, "dp", split_axis=0, concat_axis=0, tiled=True)
     out_weight_grad = tn(activ_low, grad_rows)
     in_weight_grad = tn(arrived, act_low)
-    row_back, out_weight_grad, in_weight_grad = lax.optimization_barrier(
-        (row_back, out_weight_grad, in_weight_grad)
-    )
+    bits = [1 << i for i in range(sources.bit_length() - 1)]
+    orders = [bits, bits[:1] + bits[2:] + bits[1:2]]
+    chunk = feat_dim // sources
+
+    rows = jnp.arange(feat_dim, dtype=jnp.int32)[None, :]
+    cols = jnp.arange(feat_dim, dtype=jnp.int32)[:, None]
+    spot = cols // chunk
+    piece = jnp.zeros_like(spot)
+    for i in range(len(bits)):
+        bit = jnp.where((me % 2 == 0) == (spot < sources // 2), orders[0][i], orders[1][i])
+        piece = piece | jnp.where((spot >> (len(bits) - 1 - i)) & 1 == 1, bit, 0)
+    mix_t = ((rows // chunk == (piece ^ me)) & (rows % chunk == cols % chunk)).astype(BF16)
+    hidden1_t = nt(mix_t, hidden1).astype(BF16)
+    bias_dot = lax.dot_general(
+        grad_out,
+        expert_out_bias,
+        (((1,), (1,)), ((), ())),
+        precision=lax.Precision.HIGHEST,
+        preferred_element_type=F32,
+    )
+    rank_pair = jnp.concatenate(rank, axis=1)
+    gate_pair = jnp.concatenate(gate_vals, axis=1)
     out_send = (row_gate * part_out).astype(BF16).reshape(sources, slots, feat_dim)
-    out_send, row_back = lax.optimization_barrier((out_send, row_back))
-    out_back = lax.all_to_all(out_send, "dp", split_axis=0, concat_axis=0, tiled=True)
+    ready = (
+        out_weight_grad, in_weight_grad, in_bias_grad, out_send, mix_t, hidden1_t, bias_dot, rank_pair,
+        gate_pair, onehot, out_bias_grad, normed2, inverse2, hidden2, lse, projected, gate_map,
+    )
+    row_back, ready = lax.optimization_barrier((row_back, ready))
+    (
+        out_weight_grad, in_weight_grad, in_bias_grad, out_send, mix_t, hidden1_t, bias_dot, rank_pair,
+        gate_pair, onehot, out_bias_grad, normed2, inverse2, hidden2, lse, projected, gate_map,
+    ) = ready
 
     def over_group(x):
         if group_size == 1:
@@ -304,99 +473,46 @@
         shape = (experts, group_size) + x.shape[1:]
         return jnp.sum(x.reshape(shape).astype(F32), axis=1).astype(BF16)
 
-    inner = row_back[:, slots - 2 :, :slots].astype(F32)
-    inner = jnp.sum(inner.reshape(experts, 2 * group_size, slots), axis=1)
-    inner = inner + swap(inner)
-    gate_grad = []
-    for k in range(2):
-        found = exact(pick[k].astype(F32), inner)
-        found = jnp.sum(jnp.where(rank_hot[k], found, 0.0), axis=1, keepdims=True)
-        bias_row = exact(pick[k].astype(F32), expert_out_bias)
-        gate_grad.append(found + jnp.sum(bias_row * grad_out, axis=1, keepdims=True))
-    gate_mean = gate_vals[0] * gate_grad[0] + gate_vals[1] * gate_grad[1]
-    chosen_grad = [gate_vals[k] * (gate_grad[k] - gate_mean) for k in range(2)]
-    logit_grad = (
-        jnp.where(pick[0], chosen_grad[0], 0.0) + jnp.where(pick[1], chosen_grad[1], 0.0)
-    ).astype(BF16)
-    row_home = nn(onehot, over_group(row_back).reshape(-1, feat_dim)).astype(BF16)
-    row_home = row_home.astype(F32) + swap(row_home).astype(F32)
-    hidden2_grad = row_home + nt(logit_grad, router)
-    norm2_gain_grad = jnp.sum(hidden2_grad * normed2, axis=0)
-    norm2_bias_grad = jnp.sum(hidden2_grad, axis=0)
-    middle_grad = grad_out + norm_back(hidden2_grad * norm2_gain, normed2, inverse2)
-    proj_bias_grad = jnp.sum(middle_grad, axis=0)
-    middle_low = middle_grad.astype(BF16)
-
-    bits = [1 << i for i in range(sources.bit_length() - 1)]
-    orders = [bits, bits[:1] + bits[2:] + bits[1:2]]
-    chunk = feat_dim // sources
-
-    rows = jnp.arange(feat_dim, dtype=jnp.int32)[:, None]
-    cols = jnp.arange(feat_dim, dtype=jnp.int32)[None, :]
-    spot = cols // chunk
-    piece = jnp.zeros_like(spot)
-    for i in range(len(bits)):
-        bit = jnp.where((me % 2 == 0) == (spot < sources // 2), orders[0][i], orders[1][i])
-        piece = piece | jnp.where((spot >> (len(bits) - 1 - i)) & 1 == 1, bit, 0)
-    mix = ((rows // chunk == (piece ^ me)) & (rows % chunk == cols % chunk)).astype(BF16)
-    hidden1_mixed = nn(hidden1, mix).astype(BF16)
-    proj_total = tn(nn(middle_low, mix).astype(BF16), attended)
-    attended_grad = nt(middle_low, proj_weight).astype(BF16)
-    attended_grad = attended_grad.reshape(images, SEQ, heads_here, HEAD)
-    value_grad = jnp.einsum("bhqk,bqhd->bkhd", prob_low, attended_grad, preferred_element_type=F32)
-    prob_grad = jnp.einsum("bqhd,bkhd->bhqk", attended_grad, values_in, preferred_element_type=F32)
-    score_grad = prob_vals * (prob_grad - jnp.sum(prob_vals * prob_grad, axis=-1, keepdims=True))
-    score_low = score_grad.astype(BF16)
-    query_grad = (
-        jnp.einsum("bhqk,bkhd->bqhd", score_low, key_vals, preferred_element_type=F32)
-        * score_scale
-    )
-    key_grad = (
-        jnp.einsum("bhqk,bqhd->bkhd", score_low, queries, preferred_element_type=F32)
-        * score_scale
-    )
-    proj_low = [
-        g.reshape(tok_count, head_cols).astype(BF16) for g in (query_grad, key_grad, value_grad)
-    ]
-    proj_low = jnp.concatenate(proj_low, axis=1)
-    qkv_total = tn(hidden1_mixed, proj_low)
-    qv_sums = jnp.sum(proj_low.astype(F32), axis=0)
-    hidden1_part = sum(
-        nt(proj_low[:, j * head_cols : (j + 1) * head_cols], qkv_weight[j]) for j in range(3)
-    ).astype(BF16)
+    row_home, logit_grad = home_rows(
+        over_group(row_back),
+        onehot,
+        routes,
+        rank_pair,
+        gate_pair,
+        bias_dot,
+    )
+    out_send, row_home = lax.optimization_barrier((out_send, row_home))
+    row_other = swap(row_home)
+    out_back = lax.all_to_all(out_send, "dp", split_axis=0, concat_axis=0, tiled=True)
+
+    sent, kept, hidden1_part, qv_sums, middle_grad = attention_grads(
+        row_home,
+        row_other,
+        logit_grad,
+        router,
+        cotangent,
+        normed2,
+        inverse2,
+        norm2_gain[None],
+        hidden2,
+        out_bias_grad,
+        proj_weight,
+        projected,
+        lse,
+        attended,
+        hidden1_t,
+        qkv_weight,
+        mix_t,
+    )
     hidden1_grad = hidden1_part.astype(F32) + swap(hidden1_part).astype(F32)
     norm1_gain_grad = jnp.sum(hidden1_grad * normed1, axis=0)
     norm1_bias_grad = jnp.sum(hidden1_grad, axis=0)
     input_grad = middle_grad + norm_back(hidden1_grad * norm1_gain, normed1, inverse1)
 
-    small = jnp.concatenate(
-        [
-            tn(hidden2, logit_grad),
-            out_bias_grad,
-            norm2_gain_grad[:, None],
-            norm2_bias_grad[:, None],
-            proj_bias_grad[:, None],
-        ],
-        axis=1,
-    )
-    width = -(-small.shape[1] // 128) * 128
-    small = jnp.pad(small, ((0, 0), (0, width - small.shape[1]))).astype(BF16)
-    small = tn(mix, small)
-    late = jnp.stack(
-        [
-            norm1_gain_grad,
-            norm1_bias_grad,
-            jnp.concatenate([qv_sums[:head_cols], qv_sums[2 * head_cols :]]),
-        ]
-    )
-    for bit in bits:
-        late = late + across(late, bit, sources)
-    qv_bias_grad = late[2].reshape(2, head_cols)
     out_home = nn(onehot, over_group(out_back).reshape(-1, feat_dim)).astype(BF16)
-    total = jnp.concatenate([qkv_total, proj_total, small], axis=1)
-    total, out_home = lax.optimization_barrier((total, out_home))
+    sent, out_home = lax.optimization_barrier((sent, out_home))
     out_other = swap(out_home)
-    total = halve(total, orders, 0, sources)
+    total = kept + along(sent, orders, 0, sources).astype(F32)
     total = halve(total, orders, 1, sources)
     total, out_other = lax.optimization_barrier((total, out_other))
     out_home = out_home.astype(F32) + out_other.astype(F32)
@@ -404,15 +520,32 @@
     for turn in range(2, len(bits)):
         total = halve(total, orders, turn, sources)
     mine = total.astype(BF16)
-    for turn in range(len(bits) - 1, 0, -1):
-        mine = jnp.concatenate([mine, along(mine, orders, turn, sources)], axis=0)
-    got = along(mine, orders, 0, sources)
+    full = mine.shape[1]
+    late = jnp.stack(
+        [
+            norm1_gain_grad,
+            norm1_bias_grad,
+            jnp.concatenate([qv_sums[0, :head_cols], qv_sums[0, 2 * head_cols :]]),
+        ]
+    )
+    late = jnp.pad(late, ((0, 5), (0, 0)))
+    for turn in range(len(bits) - 1, -1, -1):
+        high, low = high_low(late)
+        extra = jnp.pad(jnp.concatenate([high, low], axis=0), ((0, 0), (0, full - feat_dim)))
+        came = along(jnp.concatenate([mine, extra], axis=0), orders, turn, sources)
+        size = mine.shape[0]
+        other = came[size : size + 8, :feat_dim].astype(F32) + came[size + 8 :, :feat_dim].astype(F32)
+        late = (high.astype(F32) + low.astype(F32)) + other
+        if turn > 0:
+            mine = jnp.concatenate([mine, came[:size]], axis=0)
+    got = came[:size]
+    qv_bias_grad = late[2].reshape(2, head_cols)
     if chunk % 16 == 0:
         qkv_grad, proj_grad, router_grad, out_bias_grad, norm_grads = finish(
-            me, mine, got, head_cols, experts, feat_dim, orders
+            me, mine, came, head_cols, experts, feat_dim, orders
         )
     else:
-        whole = nn(mix, jnp.concatenate([mine, got], axis=0))
+        whole = tn(mix_t, jnp.concatenate([mine, got], axis=0))
         qkv_grad = jnp.stack([whole[:, j * head_cols : (j + 1) * head_cols] for j in range(3)])
         proj_grad = whole[:, 3 * head_cols : 4 * head_cols].T
         router_grad = whole[:, 4 * head_cols : 4 * head_cols + experts]

time: 249 us -> 260 us (1.044)
  waiting for transfers between devices: 81.4 us -> 107 us
  local copies, waits for them, and re-layouts: 17.7 us -> 36.2 us
  starting transfers between devices: 57.8 us -> 39.6 us
  matrix products: 59.5 us -> 45 us
  other arithmetic: 24.8 us -> 19.2 us
  Pallas kernels: 4.52 us -> 9.92 us
    ppermute x8, waiting for transfers between devices: 35.7 us -> 62.5 us  [along(): lax.ppermute(x, 'dp', [(i, i ^ orders[i & 1][turn]) for i in range(count)])]
    ppermute x8, starting transfers between devices: 21.1 us -> 3.05 us  [along(): lax.ppermute(x, 'dp', [(i, i ^ orders[i & 1][turn]) for i in range(count)])]
    unnamed x163 -> x131, local copies, waits for them, and re-layouts: 4.81 us -> 21.2 us
    pallas_call x0 -> x2, Pallas kernels: none -> 7.11 us  [the longest x1 6.27 us: attention_grads(): pl.pallas_call(attention_grads_kernel, out_shape=(jax.ShapeDtypeStruct((f...]
    ppermute x4 -> x0, waiting for transfers between devices: 7.08 us -> none  [across(): return lax.ppermute(x, 'dp', [(i, i ^ bit) for i in range(count)])]
    dot_general x5 -> x1, matrix products: 6.19 us -> 0.69 us  [exact(): lax.dot_general(a, b, (((1,), (0,)), ((), ())), precision=lax.Precision.H...]
    concatenate x5 -> x11, other arithmetic: 5.98 us -> 1.42 us  [the longest x1 0.59 us: local(): gate_pair = jnp.concatenate(gate_vals, axis=1)]
    dot_general x27 -> x18, matrix products: 44.5 us -> 40.1 us  [dot(): return lax.dot_general(a, b, (dims, ((), ())), preferred_element_type=out)]
  transfers between devices with their start and end apart: 23 -> 19, of which waited for: 16 -> 14; matrix products, arithmetic and copies ran while one was open for 26% -> 17% of each run, Pallas kernels for 0% -> 2%
where the time goes in v4:
time: 260 us; the launch traced here: 259 us
  waiting for transfers between devices  107 us (41%)
  matrix products  45 us (17%)
  starting transfers between devices  39.6 us (15%)
  local copies, waits for them, and re-layouts  36.2 us (14%)
  other arithmetic  19.2 us (7%)
  Pallas kernels  9.92 us (4%)
    ppermute x8, waiting for transfers between devices, along(): lax.ppermute(x, 'dp', [(i, i ^ orders[i & 1][turn]) for i in range(count)])  62.5 us
    dot_general x18, matrix products, dot(): return lax.dot_general(a, b, (dims, ((), ())), preferred_element_type=out)  40.1 us
    ppermute x7, waiting for transfers between devices, swap(): return lax.ppermute(x, 'tensor', [(0, 1), (1, 0)])  29.1 us
    unnamed x131, local copies, waits for them, and re-layouts  21.2 us
    all_to_all x1, waiting for transfers between devices, local(): lax.all_to_all(row_send, 'dp', split_axis=0, concat_axis=0, tiled=True)  11.5 us
    ppermute x7, starting transfers between devices, swap(): return lax.ppermute(x, 'tensor', [(0, 1), (1, 0)])  8 us
    all_to_all x1, starting transfers between devices, local(): lax.all_to_all(out_send, 'dp', split_axis=0, concat_axis=0, tiled=True)  7.88 us
    all_to_all x1, starting transfers between devices, local(): lax.all_to_all(row_send, 'dp', split_axis=0, concat_axis=0, tiled=True)  7.5 us
  transfers between devices with their start and end apart: 19, of which 14 were waited for; matrix products, arithmetic and copies ran while one was open for 17% of the time, Pallas kernels for 2%

profile of v4, /device:TPU:0, one launch (start us, length us, event | category | flops | bytes accessed | tf_op | source)
XLA Modules:
  0.0 258.8 jit_solution(13771264647642998049)
XLA Ops:
  4.4 1.8 copy.84
  9.8 7.4 %all-to-all-start = ((bf16[16,48,384]{2,1,0:T(8,128)(2,1)}), bf16[16,48,384]{2,1,0:T(8,128)(2,1)}, u32[]{:S(2)}, u32[]{:S(2)}) async-start(bf16[16,48,384]{2,1,0:T(8,128)(2,1)} %broadcast_select_fusion), calls=%async_computation | async-start | bytes 1179648 | tf_op jit(solution)/shard_map/all_to_all | solution.py:353
  19.4 2.1 fusion.22.projected_ref
  30.2 3.3 %collective-permute-done.1 = bf16[384,768]{1,0:T(8,128)(2,1)} collective-permute-done((bf16[384,768]{1,0:T(8,128)(2,1)S(1)}, bf16[384,768]{1,0:T(8,128)(2,1)}, u32[]{:S(2)}, u32[]{:S(2)}) %collective-permute-start.1) | collective-permute-done | bytes 589856 | tf_op jit(solution)/shard_map/ppermute | solution.py:62
  33.5 2.2 broadcast_select_fusion.4
  38.2 1.8 fusion.146
  43.6 5.8 %all-to-all-start.1 = ((bf16[16,48,768]{2,1,0:T(8,128)(2,1)}), bf16[16,48,768]{2,1,0:T(8,128)(2,1)}, u32[]{:S(2)}, u32[]{:S(2)}) async-start(bf16[16,48,768]{2,1,0:T(8,128)(2,1)} %bitcast.79), calls=%async_computation.1 | async-start | bytes 2359296 | tf_op jit(solution)/shard_map/all_to_all | solution.py:383
  53.1 2.5 fusion.21.hidden_ref
  57.1 10.3 %collective-permute-done.2 = bf16[768,384]{1,0:T(8,128)(2,1)S(1)} collective-permute-done((bf16[768,384]{1,0:T(8,128)(2,1)}, bf16[768,384]{1,0:T(8,128)(2,1)S(1)}, u32[]{:S(2)}, u32[]{:S(2)}) %collective-permute-start.2) | collective-permute-done | bytes 589856 | tf_op jit(solution)/shard_map/ppermute | solution.py:62
  67.4 2.0 broadcast_select_fusion.1
  70.3 4.3 %all-to-all-done.1 = bf16[16,48,768]{2,1,0:T(8,128)(2,1)} async-done(((bf16[16,48,768]{2,1,0:T(8,128)(2,1)}), bf16[16,48,768]{2,1,0:T(8,128)(2,1)}, u32[]{:S(2)}, u32[]{:S(2)}) %all-to-all-start.1) | async-done | bytes 1179680 | tf_op jit(solution)/shard_map/all_to_all | solution.py:383
  76.4 3.7 %multiply_convert_fusion = (bf16[768,1536]{1,0:T(8,128)(2,1)S(1)}, f32[768,1536]{1,0:T(8,128)S(1)}) fusion(f32[1536]{0:T(1024)S(1)} %reduce.4, bf16[768,768]{1,0:T(8,128)(2,1)} %bitcast.21, bf16[1,768,1536]{2,1,0:T(8,128)(2,1)S(1)} %copy-done), kind=kOutput, calls=%fused_computation.6 | convolution fusion | flops 1819017216 | bytes 10622976 | tf_op jit(solution)/shard_map/dot_general | solution.py:36
  80.1 5.7 %fusion.147 = (f32[1536]{0:T(1024)}, bf16[768,1536]{1,0:T(8,128)(2,1)}) fusion(f32[768,1536]{1,0:T(8,128)S(1)} %get-tuple-element.206, f32[1536]{0:T(1024)S(1)} %reduce.4, bf16[1,1536,768]{2,1,0:T(8,128)(2,1)S(1)} %copy-done.58, f32[768]{0:T(1024)S(1)} %fusion.119, bf16[768,384]{1,0:T(8,128)(2,1)S(1)} %copy-done.35, bf16[768,384]{1,0:T(8,128)(2,1)S(1)} %copy-done.33), kind=kOutput, calls=%fused_computation.262 | convolution fusion | flops 1829632512 | bytes 10632192 | tf_op jit(solution)/shard_map/dot_general | solution.py:36
  85.8 3.1 %multiply_convert_fusion.1 = (bf16[768,768]{1,0:T(8,128)(2,1)}, f32[768]{0:T(1024)S(1)}) fusion(f32[768]{0:T(1024)S(1)} %fusion.119, bf16[768,384]{1,0:T(8,128)(2,1)S(1)} %copy-done.35, bf16[768,384]{1,0:T(8,128)(2,1)S(1)} %copy-done.33, bf16[768,1536]{1,0:T(8,128)(2,1)S(1)} %get-tuple-element.205, bf16[1,1536,768]{2,1,0:T(8,128)(2,1)S(1)} %copy-done.58), kind=kOutput, calls=%fused_computation.20 | convolution fusion | flops 1816657152 | bytes 7084032 | tf_op jit(solution)/shard_map/dot_general | solution.py:36
  90.4 3.7 %fusion.16 = bf16[768,768]{1,0:T(8,128)(2,1)S(1)} fusion(bf16[1,768,1536]{2,1,0:T(8,128)(2,1)S(1)} %copy-done, bf16[768,1536]{1,0:T(8,128)(2,1)} %get-tuple-element.208), kind=kOutput, calls=%fused_computation.25 | convolution fusion | flops 1812529152 | bytes 5898240 | tf_op jit(solution)/shard_map/dot_general | solution.py:36
  95.4 7.5 %all-to-all-start.2 = ((bf16[16,48,768]{2,1,0:T(8,128)(2,1)}), bf16[16,48,768]{2,1,0:T(8,128)(2,1)S(1)}, u32[]{:S(2)}, u32[]{:S(2)}) async-start(bf16[16,48,768]{2,1,0:T(8,128)(2,1)} %select_select_fusion), calls=%async_computation.2 | async-start | bytes 2359296 | tf_op jit(solution)/shard_map/all_to_all | solution.py:434
  105.0 6.1 %fusion.80 = f32[1536,768]{1,0:T(8,128)} fusion(bf16[768,1536]{1,0:T(8,128)(2,1)} %copy-done.61, f32[768]{0:T(1024)S(1)} %fusion.119, bf16[768,384]{1,0:T(8,128)(2,1)S(1)} %copy-done.36, bf16[768,384]{1,0:T(8,128)(2,1)S(1)} %copy-done.34), kind=kOutput, calls=%fused_computation.130 | convolution fusion | flops 1815478272 | bytes 8260608 | tf_op jit(solution)/shard_map/dot_general | solution.py:36
  111.1 5.5 %fusion.28 = f32[768,1536]{1,0:T(8,128)} fusion(bf16[768,768]{1,0:T(8,128)(2,1)} %bitcast.21, bf16[768,1536]{1,0:T(8,128)(2,1)S(1)} %copy-done.30), kind=kOutput, calls=%fused_computation.47 | convolution fusion | flops 1811939328 | bytes 8257536 | tf_op jit(solution)/shard_map/dot_general | solution.py:36
  116.6 11.5 %all-to-all-done.2.back_ref = bf16[16,48,768]{2,1,0:T(8,128)(2,1)S(1)} async-done(((bf16[16,48,768]{2,1,0:T(8,128)(2,1)}), bf16[16,48,768]{2,1,0:T(8,128)(2,1)S(1)}, u32[]{:S(2)}, u32[]{:S(2)}) %all-to-all-start.2) | async-done | bytes 1179680 | tf_op jit(solution)/shard_map/all_to_all | solution.py:434
  133.7 7.9 %all-to-all-start.3 = ((bf16[16,48,768]{2,1,0:T(8,128)(2,1)}), bf16[16,48,768]{2,1,0:T(8,128)(2,1)}, u32[]{:S(2)}, u32[]{:S(2)}) async-start(bf16[16,48,768]{2,1,0:T(8,128)(2,1)} %bitcast.81), calls=%async_computation.3 | async-start | bytes 2359296 | tf_op jit(solution)/shard_map/all_to_all | solution.py:486
  144.9 6.5 %collective-permute-done.4.other_ref = bf16[197,768]{1,0:T(8,128)(2,1)} collective-permute-done((bf16[197,768]{1,0:T(8,128)(2,1)}, bf16[197,768]{1,0:T(8,128)(2,1)}, u32[]{:S(2)}, u32[]{:S(2)}) %collective-permute-start.4) | collective-permute-done | bytes 302624 | tf_op jit(solution)/shard_map/ppermute | solution.py:62
  158.6 6.3 %attention_grads.1 = (bf16[384,1664]{1,0:T(8,128)(2,1)S(1)}, f32[384,1664]{1,0:T(8,128)S(1)}, bf16[197,768]{1,0:T(8,128)(2,1)S(1)}, f32[1,1152]{1,0:T(1,128)S(1)}, f32[197,768]{1,0:T(8,128)S(1)}) custom-call(bf16[197,768]{1,0:T(8,128)(2,1)S(1)} %copy-done.22, bf16[197,768]{1,0:T(8,128)(2,1)} %collective-permute-done.4.other_ref, ...), custom_call_target="tpu_custom_call" | custom-call | flops 1429143552 | bytes 10485760 | tf_op jit(solution)/shard_map/attention_grads/pallas_call | solution.py:205
  170.7 3.2 %collective-permute-done.5 = bf16[384,1664]{1,0:T(8,128)(2,1)S(1)} collective-permute-done((bf16[384,1664]{1,0:T(8,128)(2,1)}, bf16[384,1664]{1,0:T(8,128)(2,1)S(1)}, u32[]{:S(2)}, u32[]{:S(2)}) %collective-permute-start.5) | collective-permute-done | bytes 1277984 | tf_op jit(solution)/shard_map/ppermute | solution.py:82
  173.9 2.0 convert_add_fusion
  179.9 6.6 %collective-permute-done.6 = bf16[192,1664]{1,0:T(8,128)(2,1)S(1)} collective-permute-done((bf16[192,1664]{1,0:T(8,128)(2,1)S(1)}, bf16[192,1664]{1,0:T(8,128)(2,1)S(1)}, u32[]{:S(2)}, u32[]{:S(2)}) %collective-permute-start.6) | collective-permute-done | bytes 639008 | tf_op jit(solution)/shard_map/ppermute | solution.py:82
  186.7 7.4 %collective-permute-done.7 = bf16[197,768]{1,0:T(8,128)(2,1)S(1)} collective-permute-done((bf16[197,768]{1,0:T(8,128)(2,1)S(1)}, bf16[197,768]{1,0:T(8,128)(2,1)S(1)}, u32[]{:S(2)}, u32[]{:S(2)}) %collective-permute-start.7) | collective-permute-done | bytes 302624 | tf_op jit(solution)/shard_map/ppermute | solution.py:62
  195.0 9.5 %collective-permute-done.9 = bf16[96,1664]{1,0:T(8,128)(2,1)S(1)} collective-permute-done((bf16[96,1664]{1,0:T(8,128)(2,1)S(1)}, bf16[96,1664]{1,0:T(8,128)(2,1)S(1)}, u32[]{:S(2)}, u32[]{:S(2)}) %collective-permute-start.9) | collective-permute-done | bytes 319520 | tf_op jit(solution)/shard_map/ppermute | solution.py:82
  205.2 6.9 %collective-permute-done.10 = bf16[48,1664]{1,0:T(8,128)(2,1)S(1)} collective-permute-done((bf16[48,1664]{1,0:T(8,128)(2,1)S(1)}, bf16[48,1664]{1,0:T(8,128)(2,1)S(1)}, u32[]{:S(2)}, u32[]{:S(2)}) %collective-permute-start.10) | collective-permute-done | bytes 159776 | tf_op jit(solution)/shard_map/ppermute | solution.py:82
  212.2 14.3 %collective-permute-done.11 = bf16[64,1664]{1,0:T(8,128)(2,1)S(1)} collective-permute-done((bf16[64,1664]{1,0:T(8,128)(2,1)S(1)}, bf16[64,1664]{1,0:T(8,128)(2,1)S(1)}, u32[]{:S(2)}, u32[]{:S(2)}) %collective-permute-start.11) | collective-permute-done | bytes 213024 | tf_op jit(solution)/shard_map/ppermute | solution.py:82
  226.7 11.0 %collective-permute-done.12 = bf16[112,1664]{1,0:T(8,128)(2,1)S(1)} collective-permute-done((bf16[112,1664]{1,0:T(8,128)(2,1)S(1)}, bf16[112,1664]{1,0:T(8,128)(2,1)S(1)}, u32[]{:S(2)}, u32[]{:S(2)}) %collective-permute-start.12) | collective-permute-done | bytes 372768 | tf_op jit(solution)/shard_map/ppermute | solution.py:82
  238.0 11.0 %collective-permute-done.13 = bf16[208,1664]{1,0:T(8,128)(2,1)S(1)} collective-permute-done((bf16[208,1664]{1,0:T(8,128)(2,1)S(1)}, bf16[208,1664]{1,0:T(8,128)(2,1)S(1)}, u32[]{:S(2)}, u32[]{:S(2)}) %collective-permute-start.13) | collective-permute-done | bytes 692256 | tf_op jit(solution)/shard_map/ppermute | solution.py:82
  252.6 2.8 %finish.1 = (f32[3,768,384]{2,1,0:T(8,128)}, f32[384,768]{1,0:T(8,128)}, f32[768,16]{1,0:T(8,128)S(1)}, f32[16,768]{1,0:T(8,128)}, f32[8,768]{1,0:T(8,128)S(1)}) custom-call(s32[1]{0:T(128)} %bitcast.32.refs_0_, bf16[384,1664]{1,0:T(8,128)(2,1)S(1)} %pad_maximum_fusion.refs_1_, bf16[400,1664]{1,0:T(8,128)(2,1)S(1)} %collective-permute-done.14.refs_2_), custom_call_target="tpu_custom_call" | custom-call | tf_op jit(solution)/shard_map/finish/pallas_call | solution.py:261
  (253 shorter events, 71.7 us)
Async XLA Ops:
  0.6 75.7 %copy-start = (bf16[1,768,1536]{2,1,0:T(8,128)(2,1)S(1)}, bf16[1,768,1536]{2,1,0:T(8,128)(2,1)}, u32[]{:S(2)}) copy-start(bf16[1,768,1536]{2,1,0:T(8,128)(2,1)} %param.26) | copy-start | bytes 7077892
  9.8 27.4 %all-to-all-start = ((bf16[16,48,384]{2,1,0:T(8,128)(2,1)}), bf16[16,48,384]{2,1,0:T(8,128)(2,1)}, u32[]{:S(2)}, u32[]{:S(2)}) async-start(bf16[16,48,384]{2,1,0:T(8,128)(2,1)} %broadcast_select_fusion), calls=%async_computation | async-start | bytes 1179648 | tf_op jit(solution)/shard_map/all_to_all | solution.py:353
  17.2 16.3 %collective-permute-start.1 = (bf16[384,768]{1,0:T(8,128)(2,1)S(1)}, bf16[384,768]{1,0:T(8,128)(2,1)}, u32[]{:S(2)}, u32[]{:S(2)}) collective-permute-start(bf16[384,768]{1,0:T(8,128)(2,1)S(1)} %copy-done.6), channel_id=1, source_target_pairs={{0,1},{1,0},{2,3},{3,2},{4,5},{5,4},{6,7},{7,6},{8,9},{9,8},{10,11... | collective-permute-start | bytes 1769480 | tf_op jit(solution)/shard_map/ppermute | solution.py:62
  18.9 34.2 %copy-start.44 = (f32[197]{0:T(256)}, f32[197]{0:T(256)S(1)}, u32[]{:S(2)}) copy-start(f32[197]{0:T(256)S(1)} %broadcast_multiply_fusion.3) | copy-start | bytes 2368
  19.2 33.9 %copy-start.48 = (f32[197]{0:T(256)}, f32[197]{0:T(256)S(1)}, u32[]{:S(2)}) copy-start(f32[197]{0:T(256)S(1)} %add_rsqrt_fusion.1) | copy-start | bytes 2368
  29.6 7.6 %collective-permute-start = (bf16[197,384]{0,1:T(8,128)(2,1)S(1)}, bf16[197,384]{0,1:T(8,128)(2,1)}, u32[]{:S(2)}, u32[]{:S(2)}) collective-permute-start(bf16[197,384]{0,1:T(8,128)(2,1)S(1)} %bitcast.85), channel_id=1, source_target_pairs={{0,1},{1,0},{2,3},{3,2},{4,5},{5,4},{6,7},{7,6},{8,9},{9,8},{10,11... | collective-permute-start | bytes 453896 | tf_op jit(solution)/shard_map/ppermute | solution.py:62
  43.6 31.0 %all-to-all-start.1 = ((bf16[16,48,768]{2,1,0:T(8,128)(2,1)}), bf16[16,48,768]{2,1,0:T(8,128)(2,1)}, u32[]{:S(2)}, u32[]{:S(2)}) async-start(bf16[16,48,768]{2,1,0:T(8,128)(2,1)} %bitcast.79), calls=%async_computation.1 | async-start | bytes 2359296 | tf_op jit(solution)/shard_map/all_to_all | solution.py:383
  51.5 15.9 %collective-permute-start.2 = (bf16[768,384]{1,0:T(8,128)(2,1)}, bf16[768,384]{1,0:T(8,128)(2,1)S(1)}, u32[]{:S(2)}, u32[]{:S(2)}) collective-permute-start(bf16[768,384]{1,0:T(8,128)(2,1)} %bitcast.19), channel_id=1, source_target_pairs={{0,1},{1,0},{2,3},{3,2},{4,5},{5,4},{6,7},{7,6},{8,9},{9,8},{10,11... | collective-permute-start | bytes 1769480 | tf_op jit(solution)/shard_map/ppermute | solution.py:62
  55.6 19.0 %copy-start.37 = (bf16[768,16]{0,1:T(8,128)(2,1)S(1)}, bf16[768,16]{0,1:T(8,128)(2,1)}, u32[]{:S(2)}) copy-start(bf16[768,16]{0,1:T(8,128)(2,1)} %param.25) | copy-start | bytes 73732
  88.9 5.2 %collective-permute-start.3 = (f32[16,48]{1,0:T(8,128)S(1)}, f32[16,48]{1,0:T(8,128)S(1)}, u32[]{:S(2)}, u32[]{:S(2)}) collective-permute-start(f32[16,48]{1,0:T(8,128)S(1)} %reshape.399), channel_id=1, source_target_pairs={{0,1},{1,0},{2,3},{3,2},{4,5},{5,4},{6,7},{7,6},{8,9},{9,8},{10,11... | collective-permute-start | bytes 9224 | tf_op jit(solution)/shard_map/ppermute | solution.py:62
  95.4 32.6 %all-to-all-start.2 = ((bf16[16,48,768]{2,1,0:T(8,128)(2,1)}), bf16[16,48,768]{2,1,0:T(8,128)(2,1)S(1)}, u32[]{:S(2)}, u32[]{:S(2)}) async-start(bf16[16,48,768]{2,1,0:T(8,128)(2,1)} %select_select_fusion), calls=%async_computation.2 | async-start | bytes 2359296 | tf_op jit(solution)/shard_map/all_to_all | solution.py:434
  111.1 17.1 %copy-start.54 = (f32[197,2]{0,1:T(2,128)S(1)}, f32[197,2]{0,1:T(2,128)}, u32[]{:S(2)}) copy-start(f32[197,2]{0,1:T(2,128)} %pad_maximum_fusion.7) | copy-start | bytes 4732
  131.5 19.9 %copy-start.3 = (bf16[768,768]{1,0:T(8,128)(2,1)S(1)}, bf16[768,768]{1,0:T(8,128)(2,1)}, u32[]{:S(2)}) copy-start(bf16[768,768]{1,0:T(8,128)(2,1)} %fusion.15.mix_ref) | copy-start | bytes 3538948
  133.7 17.8 %copy-start.5 = (f32[197,768]{1,0:T(8,128)S(1)}, f32[197,768]{1,0:T(8,128)}, u32[]{:S(2)}) copy-start(f32[197,768]{1,0:T(8,128)} %get-tuple-element.68.normed_ref) | copy-start | bytes 1815556
  133.7 17.8 %copy-start.9 = (bf16[3,197,384]{2,1,0:T(8,128)(2,1)S(1)}, bf16[3,197,384]{2,1,0:T(8,128)(2,1)}, u32[]{:S(2)}) copy-start(bf16[3,197,384]{2,1,0:T(8,128)(2,1)} %copy-done.8) | copy-start | bytes 1361668
  133.7 35.2 %all-to-all-start.3 = ((bf16[16,48,768]{2,1,0:T(8,128)(2,1)}), bf16[16,48,768]{2,1,0:T(8,128)(2,1)}, u32[]{:S(2)}, u32[]{:S(2)}) async-start(bf16[16,48,768]{2,1,0:T(8,128)(2,1)} %bitcast.81), calls=%async_computation.3 | async-start | bytes 2359296 | tf_op jit(solution)/shard_map/all_to_all | solution.py:486
  141.6 9.9 %collective-permute-start.4 = (bf16[197,768]{1,0:T(8,128)(2,1)}, bf16[197,768]{1,0:T(8,128)(2,1)}, u32[]{:S(2)}, u32[]{:S(2)}) collective-permute-start(bf16[197,768]{1,0:T(8,128)(2,1)} %copy-done.21), channel_id=1, source_target_pairs={{0,1},{1,0},{2,3},{3,2},{4,5},{5,4},{6,7},{7,6},{8,9},{9,8},{10,11... | collective-permute-start | bytes 907784 | tf_op jit(solution)/shard_map/ppermute | solution.py:62
  170.6 3.3 %collective-permute-start.5 = (bf16[384,1664]{1,0:T(8,128)(2,1)}, bf16[384,1664]{1,0:T(8,128)(2,1)S(1)}, u32[]{:S(2)}, u32[]{:S(2)}) collective-permute-start(bf16[384,1664]{1,0:T(8,128)(2,1)} %copy-done.25), channel_id=1, source_target_pairs={{0,2},{2,0},{4,6},{6,4},{8,10},{10,8},{12,14},{14,12},{16,18},{18,... | collective-permute-start | bytes 3833864 | tf_op jit(solution)/shard_map/ppermute | solution.py:82
  175.9 18.5 %copy-start.29 = (bf16[197,768]{1,0:T(8,128)(2,1)S(1)}, bf16[197,768]{1,0:T(8,128)(2,1)}, u32[]{:S(2)}) copy-start(bf16[197,768]{1,0:T(8,128)(2,1)} %param.16) | copy-start | bytes 907780
  175.9 18.5 %copy-start.45 = (f32[197]{0:T(256)S(1)}, f32[197]{0:T(256)}, u32[]{:S(2)}) copy-start(f32[197]{0:T(256)} %copy-done.44) | copy-start | bytes 2368
  176.0 18.5 %copy-start.49 = (f32[197]{0:T(256)S(1)}, f32[197]{0:T(256)}, u32[]{:S(2)}) copy-start(f32[197]{0:T(256)} %copy-done.48) | copy-start | bytes 2368
  176.0 10.5 %collective-permute-start.6 = (bf16[192,1664]{1,0:T(8,128)(2,1)S(1)}, bf16[192,1664]{1,0:T(8,128)(2,1)S(1)}, u32[]{:S(2)}, u32[]{:S(2)}) collective-permute-start(bf16[192,1664]{1,0:T(8,128)(2,1)S(1)} %slice.231), channel_id=1, source_target_pairs={{0,4},{2,10},{4,0},{6,14},{8,12},{10,2},{12,8},{14,6},{16,20},{18,... | collective-permute-start | bytes 1916936 | tf_op jit(solution)/shard_map/ppermute | solution.py:82
  177.8 16.6 %collective-permute-start.8 = (bf16[197,768]{1,0:T(8,128)(2,1)S(1)}, bf16[197,768]{1,0:T(8,128)(2,1)S(1)}, u32[]{:S(2)}, u32[]{:S(2)}) collective-permute-start(bf16[197,768]{1,0:T(8,128)(2,1)S(1)} %copy-done.13), channel_id=1, source_target_pairs={{0,1},{1,0},{2,3},{3,2},{4,5},{5,4},{6,7},{7,6},{8,9},{9,8},{10,11... | collective-permute-start | bytes 907784 | tf_op jit(solution)/shard_map/ppermute | solution.py:62
  178.4 15.6 %collective-permute-start.7 = (bf16[197,768]{1,0:T(8,128)(2,1)S(1)}, bf16[197,768]{1,0:T(8,128)(2,1)S(1)}, u32[]{:S(2)}, u32[]{:S(2)}) collective-permute-start(bf16[197,768]{1,0:T(8,128)(2,1)S(1)} %convolution_convert_fusion.2), channel_id=1, source_target_pairs={{0,1},{1,0},{2,3},{3,2},{4,5},{5,4},{6,7},{7,6},{8,9},{9,8},{10,11... | collective-permute-start | bytes 907784 | tf_op jit(solution)/shard_map/ppermute | solution.py:62
  194.1 10.4 %collective-permute-start.9 = (bf16[96,1664]{1,0:T(8,128)(2,1)S(1)}, bf16[96,1664]{1,0:T(8,128)(2,1)S(1)}, u32[]{:S(2)}, u32[]{:S(2)}) collective-permute-start(bf16[96,1664]{1,0:T(8,128)(2,1)S(1)} %slice.232), channel_id=1, source_target_pairs={{0,8},{2,18},{4,12},{6,22},{8,0},{10,26},{12,4},{14,30},{16,24},{1... | collective-permute-start | bytes 958472 | tf_op jit(solution)/shard_map/ppermute | solution.py:82
  204.6 7.5 %collective-permute-start.10 = (bf16[48,1664]{1,0:T(8,128)(2,1)S(1)}, bf16[48,1664]{1,0:T(8,128)(2,1)S(1)}, u32[]{:S(2)}, u32[]{:S(2)}) collective-permute-start(bf16[48,1664]{1,0:T(8,128)(2,1)S(1)} %slice.233), channel_id=1, source_target_pairs={{0,16},{2,6},{4,20},{6,2},{8,24},{10,14},{12,28},{14,10},{16,0},{1... | collective-permute-start | bytes 479240 | tf_op jit(solution)/shard_map/ppermute | solution.py:82
  212.1 14.4 %collective-permute-start.11 = (bf16[64,1664]{1,0:T(8,128)(2,1)S(1)}, bf16[64,1664]{1,0:T(8,128)(2,1)S(1)}, u32[]{:S(2)}, u32[]{:S(2)}) collective-permute-start(bf16[64,1664]{1,0:T(8,128)(2,1)S(1)} %pad_maximum_fusion.4), channel_id=1, source_target_pairs={{0,16},{2,6},{4,20},{6,2},{8,24},{10,14},{12,28},{14,10},{16,0},{1... | collective-permute-start | bytes 638984 | tf_op jit(solution)/shard_map/ppermute | solution.py:82
  226.6 22.6 %copy-start.40 = (f32[16,768]{1,0:T(8,128)S(1)}, f32[16,768]{1,0:T(8,128)}, u32[]{:S(2)}) copy-start(f32[16,768]{1,0:T(8,128)} %param.29) | copy-start | bytes 147460
  226.6 22.6 %copy-start.41 = (f32[197,16]{0,1:T(8,128)S(1)}, f32[197,16]{0,1:T(8,128)}, u32[]{:S(2)}) copy-start(f32[197,16]{0,1:T(8,128)} %select_add_fusion) | copy-start | bytes 37828
  226.6 11.1 %collective-permute-start.12 = (bf16[112,1664]{1,0:T(8,128)(2,1)S(1)}, bf16[112,1664]{1,0:T(8,128)(2,1)S(1)}, u32[]{:S(2)}, u32[]{:S(2)}) collective-permute-start(bf16[112,1664]{1,0:T(8,128)(2,1)S(1)} %pad_maximum_fusion.3), channel_id=1, source_target_pairs={{0,8},{2,18},{4,12},{6,22},{8,0},{10,26},{12,4},{14,30},{16,24},{1... | collective-permute-start | bytes 1118216 | tf_op jit(solution)/shard_map/ppermute | solution.py:82
  237.9 11.0 %collective-permute-start.13 = (bf16[208,1664]{1,0:T(8,128)(2,1)S(1)}, bf16[208,1664]{1,0:T(8,128)(2,1)S(1)}, u32[]{:S(2)}, u32[]{:S(2)}) collective-permute-start(bf16[208,1664]{1,0:T(8,128)(2,1)S(1)} %pad_maximum_fusion.2), channel_id=1, source_target_pairs={{0,4},{2,10},{4,0},{6,14},{8,12},{10,2},{12,8},{14,6},{16,20},{18,... | collective-permute-start | bytes 2076680 | tf_op jit(solution)/shard_map/ppermute | solution.py:82
  249.1 3.5 %collective-permute-start.14 = (bf16[400,1664]{1,0:T(8,128)(2,1)S(1)}, bf16[400,1664]{1,0:T(8,128)(2,1)S(1)}, u32[]{:S(2)}, u32[]{:S(2)}) collective-permute-start(bf16[400,1664]{1,0:T(8,128)(2,1)S(1)} %fusion.87), channel_id=1, source_target_pairs={{0,2},{2,0},{4,6},{6,4},{8,10},{10,8},{12,14},{14,12},{16,18},{18,... | collective-permute-start | bytes 3993608 | tf_op jit(solution)/shard_map/ppermute | solution.py:82
  (49 other events, 274.7 us)

commit v5 on v4

--- a/solution.py
+++ b/solution.py
@@ -78,37 +78,38 @@
     return jnp.where((plane == which), low, high)
 
 
-def along(x, orders, turn, count):
-    return lax.ppermute(x, "dp", [(i, i ^ orders[i & 1][turn]) for i in range(count)])
-
-
-def halve(total, orders, turn, count):
+def keep_half(total, came):
     middle = total.shape[0] // 2
-    return total[:middle] + along(total[middle:].astype(BF16), orders, turn, count).astype(F32)
-
-
-def home_kernel(back_ref, onehot_ref, routes_ref, rank_ref, gates_ref, bias_dot_ref, home_ref, logit_ref, inner_ref):
+    return total[:middle] + came.astype(F32)
+
+
+def send_half(total, bit, count):
+    return across(total[total.shape[0] // 2 :].astype(BF16), bit, count)
+
+
+def home_kernel(back_ref, onehot_ref, facts_ref, home_ref, logit_ref, inner_ref):
     experts, slots, feat_dim = back_ref.shape
-    tok_count = routes_ref.shape[0]
+    tok_count = facts_ref.shape[0]
     home = nn(onehot_ref[...], back_ref[...].reshape(experts * slots, feat_dim))
     home_ref[...] = home.astype(BF16)
     for e in range(experts):
         inner_ref[0, e : e + 1, :] = back_ref[e, slots - 1 : slots, :slots].astype(F32)
         inner_ref[1, e : e + 1, :] = back_ref[e, slots - 2 : slots - 1, :slots].astype(F32)
-    expert_ids = lax.broadcasted_iota(jnp.int32, (tok_count, experts), 1)
-    slot_ids = lax.broadcasted_iota(jnp.int32, (tok_count, slots), 1)
+    expert_ids = lax.broadcasted_iota(jnp.int32, (tok_count, experts), 1).astype(F32)
+    slot_ids = lax.broadcasted_iota(jnp.int32, (tok_count, slots), 1).astype(F32)
+    bias_dot = facts_ref[:, 16 : 16 + experts]
     picks, inner_grads = [], []
     for k in range(2):
-        pick = routes_ref[:, k : k + 1] == expert_ids
+        pick = facts_ref[:, k : k + 1] == expert_ids
         hot = jnp.where(pick, 1.0, 0.0).astype(BF16)
         found = nn(hot, inner_ref[0].astype(BF16)) + nn(hot, inner_ref[1].astype(BF16))
-        found = jnp.where(rank_ref[:, k : k + 1] == slot_ids, found, 0.0)
-        own_bias = jnp.where(pick, bias_dot_ref[...], 0.0)
+        found = jnp.where(facts_ref[:, k + 2 : k + 3] == slot_ids, found, 0.0)
+        own_bias = jnp.where(pick, bias_dot, 0.0)
         inner_grads.append(
             jnp.sum(found, axis=1, keepdims=True) + jnp.sum(own_bias, axis=1, keepdims=True)
         )
         picks.append(pick)
-    gates = [gates_ref[:, k : k + 1] for k in range(2)]
+    gates = [facts_ref[:, k + 4 : k + 5] for k in range(2)]
     mean = gates[0] * inner_grads[0] + gates[1] * inner_grads[1]
     logit_grad = 0.0
     for k in range(2):
@@ -116,9 +117,9 @@
     logit_ref[...] = logit_grad.astype(BF16)
 
 
-def home_rows(back, onehot, routes, rank, gates, bias_dot):
+def home_rows(back, onehot, facts):
     experts, slots, feat_dim = back.shape
-    tok_count = routes.shape[0]
+    tok_count = facts.shape[0]
     return pl.pallas_call(
         home_kernel,
         out_shape=(
@@ -126,17 +127,17 @@
             jax.ShapeDtypeStruct((tok_count, experts), BF16),
         ),
         scratch_shapes=[pltpu.VMEM((2, experts, slots), F32)],
-        compiler_params=pltpu.CompilerParams(vmem_limit_bytes=24 << 20),
+        compiler_params=pltpu.CompilerParams(vmem_limit_bytes=60 << 20),
         cost_estimate=pl.CostEstimate(
             flops=2 * tok_count * feat_dim * experts * slots, bytes_accessed=2 << 20, transcendentals=0
         ),
         name="home_rows",
-    )(back, onehot, routes, rank, gates, bias_dot)
+    )(back, onehot, facts)
 
 
 def attention_grads_kernel(
-    home_ref, other_ref, logit_ref, router_ref, cot_ref, normed_ref, inverse_ref, gain_ref, hidden2_ref, bias_grad_ref,
-    proj_ref, projected_ref, lse_ref, attended_ref, hidden_ref, weight_ref, mix_ref,
+    home_ref, other_ref, logit_ref, router_ref, cot_ref, normed_ref, facts_ref, gain_ref, hidden2_ref, bias_grad_ref,
+    proj_ref, projected_ref, attended_ref, hidden_ref, weight_ref, mix_ref,
     sent_ref, kept_ref, hidden_part_ref, sums_ref, middle_grad_ref, low_ref, back_ref, small_ref,
 ):
     head_cols = attended_ref.shape[1]
@@ -145,7 +146,7 @@
     hidden_grad = home_ref[...].astype(F32) + other_ref[...].astype(F32) + nt(logit_ref[...], router_ref[...])
     normed = normed_ref[...]
     inner = hidden_grad * gain_ref[...]
-    middle_grad = cot_ref[...].astype(F32) + norm_back(inner, normed, inverse_ref[...])
+    middle_grad = cot_ref[...].astype(F32) + norm_back(inner, normed, facts_ref[:, 6:7])
     middle_grad_ref[...] = middle_grad
     middle_low = middle_grad.astype(BF16)
     small_ref[...] = jnp.zeros_like(small_ref)
@@ -159,7 +160,7 @@
         cols = slice(h * HEAD, (h + 1) * HEAD)
         queries, key_vals, values_in = (projected_ref[j, :, cols] for j in range(3))
         out_grad = back_ref[:, cols]
-        prob_vals = jnp.exp(nt(queries, key_vals) * scale - lse_ref[:, h : h + 1])
+        prob_vals = jnp.exp(nt(queries, key_vals) * scale - facts_ref[:, h + 8 : h + 9])
         prob_low = prob_vals.astype(BF16)
         prob_grad = nt(out_grad, values_in)
         row = jnp.sum(prob_vals * prob_grad, axis=-1, keepdims=True)
@@ -171,14 +172,15 @@
         low_ref[:, start : start + HEAD] = tn(prob_low, out_grad).astype(BF16)
     low = low_ref[...]
     half = kept_ref.shape[0]
-    mixed_middle = nt(mix_ref[...], middle_low).astype(BF16)
+    mixed_middle = nt(mix_ref[1], middle_low).astype(BF16)
     small = small_ref[...].astype(BF16)
     for part in range(2):
         rows = slice(part * half, (part + 1) * half)
         pieces = (
-            nn(hidden_ref[rows, :], low),
+            nn(hidden_ref[0, rows, :], low[:, : 2 * head_cols]),
+            nt(mix_ref[0, rows, :], small),
+            nn(hidden_ref[1, rows, :], low[:, 2 * head_cols :]),
             nn(mixed_middle[rows, :], attended_ref[...]),
-            nt(mix_ref[rows, :], small),
         )
         first = 0
         for piece in pieces:
@@ -216,7 +218,7 @@
             pltpu.VMEM((tok_count, head_cols), BF16),
             pltpu.VMEM((small, feat_dim), F32),
         ],
-        compiler_params=pltpu.CompilerParams(vmem_limit_bytes=40 << 20),
+        compiler_params=pltpu.CompilerParams(vmem_limit_bytes=60 << 20),
         cost_estimate=pl.CostEstimate(
             flops=flops, bytes_accessed=10 << 20, transcendentals=tok_count * tok_count * 6
         ),
@@ -230,23 +232,21 @@
     feat_dim = qkv_ref.shape[1]
     chunk = feat_dim // count
     half = count // 2
-    odd = me % 2
     width = held_small.shape[1]
+    split = 2 * head_cols + width
     for spot in range(count):
-        names = []
+        starts = []
         for order in orders:
-            names.append(sum(bit for i, bit in enumerate(order) if (spot >> (len(order) - 1 - i)) & 1))
-        if spot >= half:
-            names = names[::-1]
-        name = names[0] + odd * (names[1] - names[0])
-        start = pl.multiple_of((name ^ me) * chunk, chunk)
+            name = sum(bit for i, bit in enumerate(order) if (spot >> (len(order) - 1 - i)) & 1)
+            starts.append(pl.ds(pl.multiple_of((name ^ me) * chunk, chunk), chunk))
         source = mine if spot < half else got
         first = (spot % half) * chunk
         piece = source[first : first + chunk, :].astype(F32)
-        for j in range(3):
-            qkv_ref[j, pl.ds(start, chunk), :] = piece[:, j * head_cols : (j + 1) * head_cols]
-        held_proj[pl.ds(start, chunk), :] = piece[:, 3 * head_cols : 4 * head_cols]
-        held_small[pl.ds(start, chunk), :] = piece[:, 4 * head_cols :]
+        qkv_ref[0, starts[0], :] = piece[:, :head_cols]
+        qkv_ref[1, starts[0], :] = piece[:, head_cols : 2 * head_cols]
+        held_small[starts[0], :] = piece[:, 2 * head_cols : split]
+        qkv_ref[2, starts[1], :] = piece[:, split : split + head_cols]
+        held_proj[starts[1], :] = piece[:, split + head_cols :]
     proj_ref[...] = held_proj[...].T
     small = held_small[...]
     router_ref[...] = small[:, :experts]
@@ -273,7 +273,7 @@
             pltpu.VMEM((feat_dim, head_cols), F32),
             pltpu.VMEM((feat_dim, width), F32),
         ],
-        compiler_params=pltpu.CompilerParams(vmem_limit_bytes=40 << 20),
+        compiler_params=pltpu.CompilerParams(vmem_limit_bytes=60 << 20),
         name="finish",
     )(me[None], mine, came)
 
@@ -441,12 +441,16 @@
     rows = jnp.arange(feat_dim, dtype=jnp.int32)[None, :]
     cols = jnp.arange(feat_dim, dtype=jnp.int32)[:, None]
     spot = cols // chunk
-    piece = jnp.zeros_like(spot)
-    for i in range(len(bits)):
-        bit = jnp.where((me % 2 == 0) == (spot < sources // 2), orders[0][i], orders[1][i])
-        piece = piece | jnp.where((spot >> (len(bits) - 1 - i)) & 1 == 1, bit, 0)
-    mix_t = ((rows // chunk == (piece ^ me)) & (rows % chunk == cols % chunk)).astype(BF16)
-    hidden1_t = nt(mix_t, hidden1).astype(BF16)
+    mix_t = []
+    for order in orders:
+        piece = jnp.zeros_like(spot)
+        for i, bit in enumerate(order):
+            piece = piece | jnp.where((spot >> (len(bits) - 1 - i)) & 1 == 1, bit, 0)
+        mix_t.append(
+            ((rows // chunk == (piece ^ me)) & (rows % chunk == cols % chunk)).astype(BF16)
+        )
+    mix_t = jnp.stack(mix_t)
+    hidden1_t = jnp.einsum("jqd,td->jqt", mix_t, hidden1, preferred_element_type=F32).astype(BF16)
     bias_dot = lax.dot_general(
         grad_out,
         expert_out_bias,
@@ -454,17 +458,19 @@
         precision=lax.Precision.HIGHEST,
         preferred_element_type=F32,
     )
-    rank_pair = jnp.concatenate(rank, axis=1)
-    gate_pair = jnp.concatenate(gate_vals, axis=1)
-    out_send = (row_gate * part_out).astype(BF16).reshape(sources, slots, feat_dim)
+    facts = [routes.astype(F32)] + [r.astype(F32) for r in rank] + gate_vals + [inverse2]
+    facts = jnp.concatenate(facts, axis=1)
+    facts = jnp.concatenate([facts, jnp.zeros_like(facts[:, :1]), lse], axis=1)
+    facts = jnp.pad(facts, ((0, 0), (0, 16 - facts.shape[1])))
+    facts = jnp.pad(jnp.concatenate([facts, bias_dot], axis=1), ((0, 0), (0, 112 - experts)))
     ready = (
-        out_weight_grad, in_weight_grad, in_bias_grad, out_send, mix_t, hidden1_t, bias_dot, rank_pair,
-        gate_pair, onehot, out_bias_grad, normed2, inverse2, hidden2, lse, projected, gate_map,
+        out_weight_grad, in_weight_grad, in_bias_grad, mix_t, hidden1_t, facts, onehot,
+        out_bias_grad, normed2, hidden2, projected, attended, router, gate_map,
     )
     row_back, ready = lax.optimization_barrier((row_back, ready))
     (
-        out_weight_grad, in_weight_grad, in_bias_grad, out_send, mix_t, hidden1_t, bias_dot, rank_pair,
-        gate_pair, onehot, out_bias_grad, normed2, inverse2, hidden2, lse, projected, gate_map,
+        out_weight_grad, in_weight_grad, in_bias_grad, mix_t, hidden1_t, facts, onehot,
+        out_bias_grad, normed2, hidden2, projected, attended, router, gate_map,
     ) = ready
 
     def over_group(x):
@@ -476,12 +482,10 @@
     row_home, logit_grad = home_rows(
         over_group(row_back),
         onehot,
-        routes,
-        rank_pair,
-        gate_pair,
-        bias_dot,
-    )
-    out_send, row_home = lax.optimization_barrier((out_send, row_home))
+        facts,
+    )
+    part_out, row_home = lax.optimization_barrier((part_out, row_home))
+    out_send = (row_gate * part_out).astype(BF16).reshape(sources, slots, feat_dim)
     row_other = swap(row_home)
     out_back = lax.all_to_all(out_send, "dp", split_axis=0, concat_axis=0, tiled=True)
 
@@ -492,13 +496,12 @@
         router,
         cotangent,
         normed2,
-        inverse2,
+        facts,
         norm2_gain[None],
         hidden2,
         out_bias_grad,
         proj_weight,
         projected,
-        lse,
         attended,
         hidden1_t,
         qkv_weight,
@@ -509,18 +512,22 @@
     norm1_bias_grad = jnp.sum(hidden1_grad, axis=0)
     input_grad = middle_grad + norm_back(hidden1_grad * norm1_gain, normed1, inverse1)
 
+    split = sent.shape[1] - 2 * head_cols
+    sent, out_back = lax.optimization_barrier((sent, out_back))
+    came = across(sent, bits[0], sources)
+    total = kept + came.astype(F32)
+    totals = [total[:, :split], total[:, split:]]
     out_home = nn(onehot, over_group(out_back).reshape(-1, feat_dim)).astype(BF16)
-    sent, out_home = lax.optimization_barrier((sent, out_home))
-    out_other = swap(out_home)
-    total = kept + along(sent, orders, 0, sources).astype(F32)
-    total = halve(total, orders, 1, sources)
-    total, out_other = lax.optimization_barrier((total, out_other))
+    for turn in range(1, len(bits)):
+        totals, out_home = lax.optimization_barrier((totals, out_home))
+        if turn == 2:
+            out_other = swap(out_home)
+        cames = [send_half(t, order[turn], sources) for t, order in zip(totals, orders)]
+        totals = [keep_half(t, c) for t, c in zip(totals, cames)]
+    totals, out_other = lax.optimization_barrier((totals, out_other))
     out_home = out_home.astype(F32) + out_other.astype(F32)
     output = (middle + (out_home + exact(gate_map, expert_out_bias))).astype(BF16)
-    for turn in range(2, len(bits)):
-        total = halve(total, orders, turn, sources)
-    mine = total.astype(BF16)
-    full = mine.shape[1]
+    mine = [t.astype(BF16) for t in totals]
     late = jnp.stack(
         [
             norm1_gain_grad,
@@ -529,27 +536,49 @@
         ]
     )
     late = jnp.pad(late, ((0, 5), (0, 0)))
-    for turn in range(len(bits) - 1, -1, -1):
+
+    def late_rows(late):
         high, low = high_low(late)
-        extra = jnp.pad(jnp.concatenate([high, low], axis=0), ((0, 0), (0, full - feat_dim)))
-        came = along(jnp.concatenate([mine, extra], axis=0), orders, turn, sources)
-        size = mine.shape[0]
-        other = came[size : size + 8, :feat_dim].astype(F32) + came[size + 8 :, :feat_dim].astype(F32)
-        late = (high.astype(F32) + low.astype(F32)) + other
-        if turn > 0:
-            mine = jnp.concatenate([mine, came[:size]], axis=0)
-    got = came[:size]
+        both = jnp.pad(jnp.concatenate([high, low], axis=0), ((0, 0), (0, split - feat_dim)))
+        return high.astype(F32) + low.astype(F32), both
+
+    def late_sum(own, came):
+        came = came[:, :feat_dim].astype(F32)
+        return own + (came[:8] + came[8:])
+
+    size = chunk
+    for turn in range(len(bits) - 1, 0, -1):
+        own, both = late_rows(late)
+        first, second = lax.optimization_barrier(
+            (jnp.concatenate([mine[0], both], axis=0), mine[1])
+        )
+        came = across(first, orders[0][turn], sources)
+        came_b = across(second, orders[1][turn], sources)
+        late = late_sum(own, came[size:])
+        mine = [
+            jnp.concatenate([mine[0], came[:size]], axis=0),
+            jnp.concatenate([mine[1], came_b], axis=0),
+        ]
+        size = 2 * size
+    own, both = late_rows(late)
+    mine = jnp.concatenate(mine, axis=1)
+    both = jnp.pad(both, ((0, 0), (0, 2 * head_cols)))
+    came = across(jnp.concatenate([mine, both], axis=0), bits[0], sources)
+    late = late_sum(own, came[size:])
     qv_bias_grad = late[2].reshape(2, head_cols)
     if chunk % 16 == 0:
         qkv_grad, proj_grad, router_grad, out_bias_grad, norm_grads = finish(
             me, mine, came, head_cols, experts, feat_dim, orders
         )
     else:
-        whole = tn(mix_t, jnp.concatenate([mine, got], axis=0))
-        qkv_grad = jnp.stack([whole[:, j * head_cols : (j + 1) * head_cols] for j in range(3)])
-        proj_grad = whole[:, 3 * head_cols : 4 * head_cols].T
-        router_grad = whole[:, 4 * head_cols : 4 * head_cols + experts]
-        norm_grads = whole[:, 4 * head_cols + experts :].T
+        whole = jnp.concatenate([mine, came[:size]], axis=0)
+        first, second = tn(mix_t[0], whole[:, :split]), tn(mix_t[1], whole[:, split:])
+        qkv_grad = jnp.stack(
+            [first[:, :head_cols], first[:, head_cols : 2 * head_cols], second[:, :head_cols]]
+        )
+        proj_grad = second[:, head_cols:].T
+        router_grad = first[:, 2 * head_cols : 2 * head_cols + experts]
+        norm_grads = first[:, 2 * head_cols + experts :].T
         out_bias_grad, norm_grads = norm_grads[:experts], norm_grads[experts:]
     norm2_gain_grad, norm2_bias_grad, proj_bias_grad = norm_grads[0], norm_grads[1], norm_grads[2]
     return (

time: 260 us -> 264 us (1.015)
  waiting for transfers between devices: 107 us -> 74.4 us
  other arithmetic: 19.2 us -> 35 us
  starting transfers between devices: 39.6 us -> 53.8 us
  Pallas kernels: 9.92 us -> 17.5 us
    ppermute x8 -> x14, waiting for transfers between devices: 62.5 us -> 37.4 us  [across(): return lax.ppermute(x, 'dp', [(i, i ^ bit) for i in range(count)])]
    ppermute x8 -> x14, starting transfers between devices: 3.05 us -> 20.4 us  [across(): return lax.ppermute(x, 'dp', [(i, i ^ bit) for i in range(count)])]
    unnamed x131 -> x137, local copies, waits for them, and re-layouts: 21.2 us -> 10.5 us
    ppermute x7, waiting for transfers between devices: 29.1 us -> 20.1 us  [swap(): return lax.ppermute(x, 'tensor', [(0, 1), (1, 0)])]
    concatenate x10 -> x12, other arithmetic: 1.41 us -> 9.88 us  [the longest x1 8.59 us: local(): came = across(jnp.concatenate([mine, both], axis=0), bits[0], sources)]
    all_to_all x1, waiting for transfers between devices: 0.01 us -> 4.75 us  [local(): lax.all_to_all(out_send, 'dp', split_axis=0, concat_axis=0, tiled=True)]
    all_to_all x1, waiting for transfers between devices: 4.32 us -> 0.01 us  [local(): lax.all_to_all(send, 'dp', split_axis=0, concat_axis=0, tiled=True)]
    pallas_call x1, Pallas kernels: 6.27 us -> 9.96 us  [attention_grads(): pl.pallas_call(attention_grads_kernel, out_shape=(jax.ShapeDtypeStruct((f...]
  transfers between devices with their start and end apart: 19 -> 25, of which waited for: 14 -> 20; matrix products, arithmetic and copies ran while one was open for 17% -> 25% of each run, Pallas kernels for 2% -> 4%
where the time goes in v5:
time: 264 us; the launch traced here: 263 us
  waiting for transfers between devices  74.4 us (28%)
  starting transfers between devices  53.8 us (20%)
  matrix products  46 us (17%)
  other arithmetic  35 us (13%)
  local copies, waits for them, and re-layouts  34.1 us (13%)
  Pallas kernels  17.5 us (7%)
    ppermute x14, waiting for transfers between devices, across(): return lax.ppermute(x, 'dp', [(i, i ^ bit) for i in range(count)])  37.4 us
    dot_general x17, matrix products, dot(): return lax.dot_general(a, b, (dims, ((), ())), preferred_element_type=out)  36.9 us
    ppermute x14, starting transfers between devices, across(): return lax.ppermute(x, 'dp', [(i, i ^ bit) for i in range(count)])  20.4 us
    ppermute x7, waiting for transfers between devices, swap(): return lax.ppermute(x, 'tensor', [(0, 1), (1, 0)])  20.1 us
    all_to_all x1, waiting for transfers between devices, local(): lax.all_to_all(row_send, 'dp', split_axis=0, concat_axis=0, tiled=True)  12.2 us
    unnamed x137, local copies, waits for them, and re-layouts  10.5 us
    pallas_call x1, Pallas kernels, attention_grads(): pl.pallas_call(attention_grads_kernel, out_shape=(jax.ShapeDtypeStruct((f...  9.96 us
    concatenate x1, other arithmetic, local(): came = across(jnp.concatenate([mine, both], axis=0), bits[0], sources)  8.59 us
  transfers between devices with their start and end apart: 25, of which 20 were waited for; matrix products, arithmetic and copies ran while one was open for 25% of the time, Pallas kernels for 4%

profile of v5, /device:TPU:0, one launch (start us, length us, event | category | flops | bytes accessed | tf_op | source)
XLA Modules:
  0.0 262.6 jit_solution(4662289879181536607)
XLA Ops:
  10.3 7.4 %all-to-all-start = ((bf16[16,48,384]{2,1,0:T(8,128)(2,1)}), bf16[16,48,384]{2,1,0:T(8,128)(2,1)}, u32[]{:S(2)}, u32[]{:S(2)}) async-start(bf16[16,48,384]{2,1,0:T(8,128)(2,1)} %broadcast_select_fusion), calls=%async_computation | async-start | bytes 1179648 | tf_op jit(solution)/shard_map/all_to_all | solution.py:353
  19.9 2.1 fusion.22.projected_ref
  34.0 2.2 broadcast_select_fusion.4
  44.9 5.8 %all-to-all-start.1 = ((bf16[16,48,768]{2,1,0:T(8,128)(2,1)}), bf16[16,48,768]{2,1,0:T(8,128)(2,1)S(1)}, u32[]{:S(2)}, u32[]{:S(2)}) async-start(bf16[16,48,768]{2,1,0:T(8,128)(2,1)} %bitcast.84), calls=%async_computation.1 | async-start | bytes 2359296 | tf_op jit(solution)/shard_map/all_to_all | solution.py:383
  61.6 3.2 %convolution_convert_fusion.1.hidden_ref = bf16[2,768,197]{2,1,0:T(8,128)(2,1)} fusion(pred[1,768,768]{2,1,0:T(32,128)(4,1)} %copy-done.14, pred[1,768,768]{2,1,0:T(32,128)(4,1)} %copy-done.13, bf16[197,768]{1,0:T(8,128)(2,1)} %param.16, f32[768]{0:T(1024)} %param.18, f32[768]{0:T(1024)} %param.17, f32[197]{0:T(256)} %copy-done.45, f32[197]{0:T(256)} %copy-done.35), kind=kOutput, calls=%fused_computation.29 | convolution fusion | flops 467171328 | bytes 2095144 | tf_op jit(solution)/shard_map/jqd,td->jqt/dot_general | solution.py:453
  64.8 9.2 %collective-permute-done.2 = bf16[768,384]{0,1:T(8,128)(2,1)S(1)} collective-permute-done((bf16[768,384]{0,1:T(8,128)(2,1)}, bf16[768,384]{0,1:T(8,128)(2,1)S(1)}, u32[]{:S(2)}, u32[]{:S(2)}) %collective-permute-start.2) | collective-permute-done | bytes 589856 | tf_op jit(solution)/shard_map/ppermute | solution.py:62
  80.1 4.8 %multiply_convert_fusion = (bf16[768,1536]{1,0:T(8,128)(2,1)S(1)}, f32[768,1536]{1,0:T(8,128)}) fusion(f32[1536]{0:T(1024)} %reduce.4, bf16[768,768]{1,0:T(8,128)(2,1)S(1)} %bitcast.80, bf16[1,768,1536]{2,1,0:T(8,128)(2,1)S(1)} %copy-done), kind=kOutput, calls=%fused_computation.6 | convolution fusion | flops 1819017216 | bytes 10622976 | tf_op jit(solution)/shard_map/dot_general | solution.py:36
  84.9 4.1 %fusion.6 = (f32[768]{0:T(1024)}, f32[768,768]{0,1:T(8,128)}) fusion(bf16[768,384]{0,1:T(8,128)(2,1)S(1)} %copy-done.24, bf16[768,384]{0,1:T(8,128)(2,1)S(1)} %copy-done.12, bf16[768,1536]{1,0:T(8,128)(2,1)S(1)} %get-tuple-element.223, bf16[1,1536,768]{2,1,0:T(8,128)(2,1)S(1)} %copy-done.63), kind=kOutput, calls=%fused_computation.16 | convolution fusion | flops 1815477504 | bytes 8260608 | tf_op jit(solution)/shard_map/dot_general | solution.py:36
  93.1 6.7 %fusion.146 = (f32[1536]{0:T(1024)}, bf16[768,1536]{1,0:T(8,128)(2,1)S(1)}) fusion(f32[768,1536]{1,0:T(8,128)} %get-tuple-element.224, f32[1536]{0:T(1024)} %reduce.4, bf16[1,1536,768]{2,1,0:T(8,128)(2,1)} %param.28, f32[768]{0:T(1024)S(1)} %fusion.118, bf16[768,384]{0,1:T(8,128)(2,1)} %get-tuple-element.192, bf16[768,384]{0,1:T(8,128)(2,1)} %get-tuple-element.193), kind=kOutput, calls=%fused_computation.279 | convolution fusion | flops 1829632512 | bytes 10632192 | tf_op jit(solution)/shard_map/dot_general | solution.py:36
  103.3 5.8 %all-to-all-start.2 = ((bf16[16,48,768]{2,1,0:T(8,128)(2,1)}), bf16[16,48,768]{2,1,0:T(8,128)(2,1)S(1)}, u32[]{:S(2)}, u32[]{:S(2)}) async-start(bf16[16,48,768]{2,1,0:T(8,128)(2,1)} %select_select_fusion), calls=%async_computation.2 | async-start | bytes 2359296 | tf_op jit(solution)/shard_map/all_to_all | solution.py:434
  111.5 6.3 %fusion.31 = f32[1536,768]{1,0:T(8,128)} fusion(bf16[768,1536]{1,0:T(8,128)(2,1)} %copy-done.66, f32[768]{0:T(1024)S(1)} %copy-done.44, bf16[768,384]{0,1:T(8,128)(2,1)} %get-tuple-element.192, bf16[768,384]{0,1:T(8,128)(2,1)} %get-tuple-element.193), kind=kOutput, calls=%fused_computation.55 | convolution fusion | flops 1815478272 | bytes 8260608 | tf_op jit(solution)/shard_map/dot_general | solution.py:36
  117.8 4.2 %fusion.26 = f32[768,1536]{1,0:T(8,128)} fusion(bf16[768,768]{1,0:T(8,128)(2,1)S(1)} %bitcast.82, bf16[768,1536]{1,0:T(8,128)(2,1)S(1)} %copy-done.17), kind=kOutput, calls=%fused_computation.47 | convolution fusion | flops 1811939328 | bytes 8257536 | tf_op jit(solution)/shard_map/dot_general | solution.py:36
  122.0 12.2 %all-to-all-done.2.back_ref = bf16[16,48,768]{2,1,0:T(8,128)(2,1)S(1)} async-done(((bf16[16,48,768]{2,1,0:T(8,128)(2,1)}), bf16[16,48,768]{2,1,0:T(8,128)(2,1)S(1)}, u32[]{:S(2)}, u32[]{:S(2)}) %all-to-all-start.2) | async-done | bytes 1179680 | tf_op jit(solution)/shard_map/all_to_all | solution.py:434
  135.3 2.9 %home_rows.1 = (bf16[197,768]{1,0:T(8,128)(2,1)}, bf16[197,16]{1,0:T(8,128)(2,1)}) custom-call(bf16[16,48,768]{2,1,0:T(8,128)(2,1)} %copy-done.9, bf16[197,768]{1,0:T(8,128)(2,1)} %fusion.54.onehot_ref, f32[197,128]{1,0:T(8,128)} %pad.44.facts_ref), custom_call_target="tpu_custom_call" | custom-call | flops 232390656 | bytes 2097152 | tf_op jit(solution)/shard_map/home_rows/pallas_call | solution.py:123
  141.5 7.5 %all-to-all-start.3 = ((bf16[16,48,768]{2,1,0:T(8,128)(2,1)}), bf16[16,48,768]{2,1,0:T(8,128)(2,1)S(1)}, u32[]{:S(2)}, u32[]{:S(2)}) async-start(bf16[16,48,768]{2,1,0:T(8,128)(2,1)} %bitcast.30), calls=%async_computation.3 | async-start | bytes 2359296 | tf_op jit(solution)/shard_map/all_to_all | solution.py:490
  151.7 6.9 %collective-permute-done.4.other_ref = bf16[197,768]{1,0:T(8,128)(2,1)S(1)} collective-permute-done((bf16[197,768]{1,0:T(8,128)(2,1)S(1)}, bf16[197,768]{1,0:T(8,128)(2,1)S(1)}, u32[]{:S(2)}, u32[]{:S(2)}) %collective-permute-start.4) | collective-permute-done | bytes 302624 | tf_op jit(solution)/shard_map/ppermute | solution.py:62
  159.4 10.0 %attention_grads.1 = (bf16[384,1664]{1,0:T(8,128)(2,1)}, f32[384,1664]{1,0:T(8,128)}, bf16[197,768]{1,0:T(8,128)(2,1)}, f32[1,1152]{1,0:T(1,128)}, f32[197,768]{1,0:T(8,128)}) custom-call(bf16[197,768]{1,0:T(8,128)(2,1)} %get-tuple-element.76.home_ref, bf16[197,768]{1,0:T(8,128)(2,1)} %copy-done.26, bf16[197,16]{1,0:T(8,128)(2,1)} %get-tuple-element.77.logit_ref, ...), custom_call_target="tpu_custom_call" | custom-call | flops 1429143552 | bytes 10485760 | tf_op jit(solution)/shard_map/attention_grads/pallas_call | solution.py:207
  169.3 4.8 %all-to-all-done.3 = bf16[16,48,768]{2,1,0:T(8,128)(2,1)S(1)} async-done(((bf16[16,48,768]{2,1,0:T(8,128)(2,1)}), bf16[16,48,768]{2,1,0:T(8,128)(2,1)S(1)}, u32[]{:S(2)}, u32[]{:S(2)}) %all-to-all-start.3) | async-done | bytes 1179680 | tf_op jit(solution)/shard_map/all_to_all | solution.py:490
  180.0 3.8 %collective-permute-start.7 = (bf16[192,768]{1,0:T(8,128)(2,1)S(1)}, bf16[192,768]{1,0:T(8,128)(2,1)S(1)}, u32[]{:S(2)}, u32[]{:S(2)}) collective-permute-start(bf16[192,768]{1,0:T(8,128)(2,1)S(1)} %slice.287), channel_id=1, source_target_pairs={{0,8},{2,10},{4,12},{6,14},{8,0},{10,2},{12,4},{14,6},{16,24},{18,... | collective-permute-start | bytes 884744 | tf_op jit(solution)/shard_map/ppermute | solution.py:66
  186.1 5.2 %collective-permute-done.7 = bf16[192,768]{1,0:T(8,128)(2,1)S(1)} collective-permute-done((bf16[192,768]{1,0:T(8,128)(2,1)S(1)}, bf16[192,768]{1,0:T(8,128)(2,1)S(1)}, u32[]{:S(2)}, u32[]{:S(2)}) %collective-permute-start.7) | collective-permute-done | bytes 294944 | tf_op jit(solution)/shard_map/ppermute | solution.py:66
  191.4 2.6 collective-permute-done.6
  197.6 5.7 %collective-permute-done.9 = bf16[96,768]{1,0:T(8,128)(2,1)S(1)} collective-permute-done((bf16[96,768]{1,0:T(8,128)(2,1)S(1)}, bf16[96,768]{1,0:T(8,128)(2,1)S(1)}, u32[]{:S(2)}, u32[]{:S(2)}) %collective-permute-start.9) | collective-permute-done | bytes 147488 | tf_op jit(solution)/shard_map/ppermute | solution.py:66
  208.7 3.6 %collective-permute-done.10 = bf16[48,896]{1,0:T(8,128)(2,1)S(1)} collective-permute-done((bf16[48,896]{1,0:T(8,128)(2,1)S(1)}, bf16[48,896]{1,0:T(8,128)(2,1)S(1)}, u32[]{:S(2)}, u32[]{:S(2)}) %collective-permute-start.10) | collective-permute-done | bytes 86048 | tf_op jit(solution)/shard_map/ppermute | solution.py:66
  214.3 3.9 %collective-permute-done.15 = bf16[48,768]{1,0:T(8,128)(2,1)S(1)} collective-permute-done((bf16[48,768]{1,0:T(8,128)(2,1)S(1)}, bf16[48,768]{1,0:T(8,128)(2,1)S(1)}, u32[]{:S(2)}, u32[]{:S(2)}) %collective-permute-start.15) | collective-permute-done | bytes 73760 | tf_op jit(solution)/shard_map/ppermute | solution.py:66
  218.3 2.4 collective-permute-done.14
  220.9 2.2 collective-permute-start.16
  223.1 4.9 %collective-permute-done.17 = bf16[96,768]{1,0:T(8,128)(2,1)S(1)} collective-permute-done((bf16[96,768]{1,0:T(8,128)(2,1)S(1)}, bf16[96,768]{1,0:T(8,128)(2,1)S(1)}, u32[]{:S(2)}, u32[]{:S(2)}) %collective-permute-start.17) | collective-permute-done | bytes 147488 | tf_op jit(solution)/shard_map/ppermute | solution.py:66
  228.7 3.3 %collective-permute-start.18 = (bf16[208,896]{1,0:T(8,128)(2,1)S(1)}, bf16[208,896]{1,0:T(8,128)(2,1)S(1)}, u32[]{:S(2)}, u32[]{:S(2)}) collective-permute-start(bf16[208,896]{1,0:T(8,128)(2,1)S(1)} %pad_maximum_fusion.1), channel_id=1, source_target_pairs={{0,4},{2,6},{4,0},{6,2},{8,12},{10,14},{12,8},{14,10},{16,20},{18,... | collective-permute-start | bytes 1118216 | tf_op jit(solution)/shard_map/ppermute | solution.py:66
  232.0 2.5 collective-permute-start.19
  234.5 3.1 %collective-permute-done.18 = bf16[208,896]{1,0:T(8,128)(2,1)S(1)} collective-permute-done((bf16[208,896]{1,0:T(8,128)(2,1)S(1)}, bf16[208,896]{1,0:T(8,128)(2,1)S(1)}, u32[]{:S(2)}, u32[]{:S(2)}) %collective-permute-start.18) | collective-permute-done | bytes 372768 | tf_op jit(solution)/shard_map/ppermute | solution.py:66
  239.2 8.6 %fusion.19 = bf16[400,1664]{1,0:T(8,128)(2,1)S(1)} fusion(bf16[16,896]{1,0:T(8,128)(2,1)S(1)} %fusion.88, bf16[192,768]{1,0:T(8,128)(2,1)S(1)} %collective-permute-done.19, bf16[96,768]{1,0:T(8,128)(2,1)S(1)} %collective-permute-done.17, bf16[48,768]{1,0:T(8,128)(2,1)S(1)} %collective-permute-done.15, bf16[48,768]{1,0:T(8,128)(2,1)S(1)} %convert_add_fusion.7, ...), kind=kLoop, calls=%fused_computation.32 | loop fusion | flops 13312000 | bytes 2637824 | tf_op jit(solution)/shard_map/concatenate | solution.py:566
  254.7 4.6 %finish.1 = (f32[3,768,384]{2,1,0:T(8,128)}, f32[384,768]{1,0:T(8,128)}, f32[768,16]{1,0:T(8,128)}, f32[16,768]{1,0:T(8,128)}, f32[8,768]{1,0:T(8,128)}) custom-call(s32[1]{0:T(128)} %bitcast.32.refs_0_, bf16[384,1664]{1,0:T(8,128)(2,1)} %maximum_maximum_fusion.refs_1_, bf16[400,1664]{1,0:T(8,128)(2,1)} %copy-done.19), custom_call_target="tpu_custom_call" | custom-call | tf_op jit(solution)/shard_map/finish/pallas_call | solution.py:261
  (298 shorter events, 98.3 us)
Async XLA Ops:
  0.6 79.4 %copy-start = (bf16[1,768,1536]{2,1,0:T(8,128)(2,1)S(1)}, bf16[1,768,1536]{2,1,0:T(8,128)(2,1)}, u32[]{:S(2)}) copy-start(bf16[1,768,1536]{2,1,0:T(8,128)(2,1)} %param.26) | copy-start | bytes 7077892
  3.0 39.3 %copy-start.49 = (s32[197,1]{0,1:T(1,128)}, s32[197,1]{0,1:T(1,128)S(1)}, u32[]{:S(2)}) copy-start(s32[197,1]{0,1:T(1,128)S(1)} %get-tuple-element.214) | copy-start | bytes 2368
  3.0 39.3 %copy-start.51 = (s32[197,1]{0,1:T(1,128)}, s32[197,1]{0,1:T(1,128)S(1)}, u32[]{:S(2)}) copy-start(s32[197,1]{0,1:T(1,128)S(1)} %get-tuple-element.216) | copy-start | bytes 2368
  10.3 27.4 %all-to-all-start = ((bf16[16,48,384]{2,1,0:T(8,128)(2,1)}), bf16[16,48,384]{2,1,0:T(8,128)(2,1)}, u32[]{:S(2)}, u32[]{:S(2)}) async-start(bf16[16,48,384]{2,1,0:T(8,128)(2,1)} %broadcast_select_fusion), calls=%async_computation | async-start | bytes 1179648 | tf_op jit(solution)/shard_map/all_to_all | solution.py:353
  17.8 16.2 %collective-permute-start.1 = (bf16[384,768]{1,0:T(8,128)(2,1)S(1)}, bf16[384,768]{1,0:T(8,128)(2,1)}, u32[]{:S(2)}, u32[]{:S(2)}) collective-permute-start(bf16[384,768]{1,0:T(8,128)(2,1)S(1)} %copy-done.11), channel_id=1, source_target_pairs={{0,1},{1,0},{2,3},{3,2},{4,5},{5,4},{6,7},{7,6},{8,9},{9,8},{10,11... | collective-permute-start | bytes 1769480 | tf_op jit(solution)/shard_map/ppermute | solution.py:62
  30.2 7.6 %collective-permute-start = (bf16[197,384]{0,1:T(8,128)(2,1)S(1)}, bf16[197,384]{0,1:T(8,128)(2,1)}, u32[]{:S(2)}, u32[]{:S(2)}) collective-permute-start(bf16[197,384]{0,1:T(8,128)(2,1)S(1)} %bitcast.89), channel_id=1, source_target_pairs={{0,1},{1,0},{2,3},{3,2},{4,5},{5,4},{6,7},{7,6},{8,9},{9,8},{10,11... | collective-permute-start | bytes 453896 | tf_op jit(solution)/shard_map/ppermute | solution.py:62
  44.9 35.2 %all-to-all-start.1 = ((bf16[16,48,768]{2,1,0:T(8,128)(2,1)}), bf16[16,48,768]{2,1,0:T(8,128)(2,1)S(1)}, u32[]{:S(2)}, u32[]{:S(2)}) async-start(bf16[16,48,768]{2,1,0:T(8,128)(2,1)} %bitcast.84), calls=%async_computation.1 | async-start | bytes 2359296 | tf_op jit(solution)/shard_map/all_to_all | solution.py:383
  58.2 15.9 %collective-permute-start.2 = (bf16[768,384]{0,1:T(8,128)(2,1)}, bf16[768,384]{0,1:T(8,128)(2,1)S(1)}, u32[]{:S(2)}, u32[]{:S(2)}) collective-permute-start(bf16[768,384]{0,1:T(8,128)(2,1)} %copy.79), channel_id=1, source_target_pairs={{0,1},{1,0},{2,3},{3,2},{4,5},{5,4},{6,7},{7,6},{8,9},{9,8},{10,11... | collective-permute-start | bytes 1769480 | tf_op jit(solution)/shard_map/ppermute | solution.py:62
  90.3 11.5 %collective-permute-start.3 = (f32[16,48]{1,0:T(8,128)}, f32[16,48]{1,0:T(8,128)S(1)}, u32[]{:S(2)}, u32[]{:S(2)}) collective-permute-start(f32[16,48]{1,0:T(8,128)} %reshape.601), channel_id=1, source_target_pairs={{0,1},{1,0},{2,3},{3,2},{4,5},{5,4},{6,7},{7,6},{8,9},{9,8},{10,11... | collective-permute-start | bytes 9224 | tf_op jit(solution)/shard_map/ppermute | solution.py:62
  103.3 31.0 %all-to-all-start.2 = ((bf16[16,48,768]{2,1,0:T(8,128)(2,1)}), bf16[16,48,768]{2,1,0:T(8,128)(2,1)S(1)}, u32[]{:S(2)}, u32[]{:S(2)}) async-start(bf16[16,48,768]{2,1,0:T(8,128)(2,1)} %select_select_fusion), calls=%async_computation.2 | async-start | bytes 2359296 | tf_op jit(solution)/shard_map/all_to_all | solution.py:434
  141.5 32.6 %all-to-all-start.3 = ((bf16[16,48,768]{2,1,0:T(8,128)(2,1)}), bf16[16,48,768]{2,1,0:T(8,128)(2,1)S(1)}, u32[]{:S(2)}, u32[]{:S(2)}) async-start(bf16[16,48,768]{2,1,0:T(8,128)(2,1)} %bitcast.30), calls=%async_computation.3 | async-start | bytes 2359296 | tf_op jit(solution)/shard_map/all_to_all | solution.py:490
  149.0 9.7 %collective-permute-start.4 = (bf16[197,768]{1,0:T(8,128)(2,1)S(1)}, bf16[197,768]{1,0:T(8,128)(2,1)S(1)}, u32[]{:S(2)}, u32[]{:S(2)}) collective-permute-start(bf16[197,768]{1,0:T(8,128)(2,1)S(1)} %copy-done.25), channel_id=1, source_target_pairs={{0,1},{1,0},{2,3},{3,2},{4,5},{5,4},{6,7},{7,6},{8,9},{9,8},{10,11... | collective-permute-start | bytes 907784 | tf_op jit(solution)/shard_map/ppermute | solution.py:62
  159.4 16.7 %copy-start.10 = (bf16[197,768]{1,0:T(8,128)(2,1)S(1)}, bf16[197,768]{1,0:T(8,128)(2,1)}, u32[]{:S(2)}) copy-start(bf16[197,768]{1,0:T(8,128)(2,1)} %fusion.54.onehot_ref) | copy-start | bytes 907780
  174.1 3.6 %collective-permute-start.5 = (bf16[384,1664]{1,0:T(8,128)(2,1)}, bf16[384,1664]{1,0:T(8,128)(2,1)S(1)}, u32[]{:S(2)}, u32[]{:S(2)}) collective-permute-start(bf16[384,1664]{1,0:T(8,128)(2,1)} %get-tuple-element.89), channel_id=1, source_target_pairs={{0,2},{2,0},{4,6},{6,4},{8,10},{10,8},{12,14},{14,12},{16,18},{18,... | collective-permute-start | bytes 3833864 | tf_op jit(solution)/shard_map/ppermute | solution.py:66
  174.9 10.8 %collective-permute-start.13 = (bf16[197,768]{1,0:T(8,128)(2,1)}, bf16[197,768]{1,0:T(8,128)(2,1)S(1)}, u32[]{:S(2)}, u32[]{:S(2)}) collective-permute-start(bf16[197,768]{1,0:T(8,128)(2,1)} %get-tuple-element.103), channel_id=1, source_target_pairs={{0,1},{1,0},{2,3},{3,2},{4,5},{5,4},{6,7},{7,6},{8,9},{9,8},{10,11... | collective-permute-start | bytes 907784 | tf_op jit(solution)/shard_map/ppermute | solution.py:62
  180.0 11.3 %collective-permute-start.7 = (bf16[192,768]{1,0:T(8,128)(2,1)S(1)}, bf16[192,768]{1,0:T(8,128)(2,1)S(1)}, u32[]{:S(2)}, u32[]{:S(2)}) collective-permute-start(bf16[192,768]{1,0:T(8,128)(2,1)S(1)} %slice.287), channel_id=1, source_target_pairs={{0,8},{2,10},{4,12},{6,14},{8,0},{10,2},{12,4},{14,6},{16,24},{18,... | collective-permute-start | bytes 884744 | tf_op jit(solution)/shard_map/ppermute | solution.py:66
  183.8 10.1 %collective-permute-start.6 = (bf16[192,896]{1,0:T(8,128)(2,1)S(1)}, bf16[192,896]{1,0:T(8,128)(2,1)S(1)}, u32[]{:S(2)}, u32[]{:S(2)}) collective-permute-start(bf16[192,896]{1,0:T(8,128)(2,1)S(1)} %slice.286), channel_id=1, source_target_pairs={{0,4},{2,6},{4,0},{6,2},{8,12},{10,14},{12,8},{14,10},{16,20},{18,... | collective-permute-start | bytes 1032200 | tf_op jit(solution)/shard_map/ppermute | solution.py:66
  194.1 9.2 %collective-permute-start.9 = (bf16[96,768]{1,0:T(8,128)(2,1)S(1)}, bf16[96,768]{1,0:T(8,128)(2,1)S(1)}, u32[]{:S(2)}, u32[]{:S(2)}) collective-permute-start(bf16[96,768]{1,0:T(8,128)(2,1)S(1)} %slice.289), channel_id=1, source_target_pairs={{0,16},{2,18},{4,20},{6,22},{8,24},{10,26},{12,28},{14,30},{16,0},... | collective-permute-start | bytes 442376 | tf_op jit(solution)/shard_map/ppermute | solution.py:66
  195.8 8.4 %collective-permute-start.8 = (bf16[96,896]{1,0:T(8,128)(2,1)S(1)}, bf16[96,896]{1,0:T(8,128)(2,1)S(1)}, u32[]{:S(2)}, u32[]{:S(2)}) collective-permute-start(bf16[96,896]{1,0:T(8,128)(2,1)S(1)} %slice.288), channel_id=1, source_target_pairs={{0,8},{2,10},{4,12},{6,14},{8,0},{10,2},{12,4},{14,6},{16,24},{18,... | collective-permute-start | bytes 516104 | tf_op jit(solution)/shard_map/ppermute | solution.py:66
  204.3 4.4 %collective-permute-start.11 = (bf16[48,768]{1,0:T(8,128)(2,1)S(1)}, bf16[48,768]{1,0:T(8,128)(2,1)S(1)}, u32[]{:S(2)}, u32[]{:S(2)}) collective-permute-start(bf16[48,768]{1,0:T(8,128)(2,1)S(1)} %slice.291), channel_id=1, source_target_pairs={{0,4},{2,6},{4,0},{6,2},{8,12},{10,14},{12,8},{14,10},{16,20},{18,... | collective-permute-start | bytes 221192 | tf_op jit(solution)/shard_map/ppermute | solution.py:66
  205.6 8.2 %collective-permute-start.12 = (bf16[197,768]{1,0:T(8,128)(2,1)S(1)}, bf16[197,768]{1,0:T(8,128)(2,1)S(1)}, u32[]{:S(2)}, u32[]{:S(2)}) collective-permute-start(bf16[197,768]{1,0:T(8,128)(2,1)S(1)} %convolution_convert_fusion.3), channel_id=1, source_target_pairs={{0,1},{1,0},{2,3},{3,2},{4,5},{5,4},{6,7},{7,6},{8,9},{9,8},{10,11... | collective-permute-start | bytes 907784 | tf_op jit(solution)/shard_map/ppermute | solution.py:62
  206.1 6.2 %collective-permute-start.10 = (bf16[48,896]{1,0:T(8,128)(2,1)S(1)}, bf16[48,896]{1,0:T(8,128)(2,1)S(1)}, u32[]{:S(2)}, u32[]{:S(2)}) collective-permute-start(bf16[48,896]{1,0:T(8,128)(2,1)S(1)} %slice.290), channel_id=1, source_target_pairs={{0,16},{2,18},{4,20},{6,22},{8,24},{10,26},{12,28},{14,30},{16,0},... | collective-permute-start | bytes 258056 | tf_op jit(solution)/shard_map/ppermute | solution.py:66
  213.9 4.4 %collective-permute-start.15 = (bf16[48,768]{1,0:T(8,128)(2,1)S(1)}, bf16[48,768]{1,0:T(8,128)(2,1)S(1)}, u32[]{:S(2)}, u32[]{:S(2)}) collective-permute-start(bf16[48,768]{1,0:T(8,128)(2,1)S(1)} %convert_add_fusion.7), channel_id=1, source_target_pairs={{0,4},{2,6},{4,0},{6,2},{8,12},{10,14},{12,8},{14,10},{16,20},{18,... | collective-permute-start | bytes 221192 | tf_op jit(solution)/shard_map/ppermute | solution.py:66
  214.3 6.4 %collective-permute-start.14 = (bf16[64,896]{1,0:T(8,128)(2,1)S(1)}, bf16[64,896]{1,0:T(8,128)(2,1)S(1)}, u32[]{:S(2)}, u32[]{:S(2)}) collective-permute-start(bf16[64,896]{1,0:T(8,128)(2,1)S(1)} %pad_maximum_fusion.7), channel_id=1, source_target_pairs={{0,16},{2,18},{4,20},{6,22},{8,24},{10,26},{12,28},{14,30},{16,0},... | collective-permute-start | bytes 344072 | tf_op jit(solution)/shard_map/ppermute | solution.py:66
  220.8 7.2 %collective-permute-start.17 = (bf16[96,768]{1,0:T(8,128)(2,1)S(1)}, bf16[96,768]{1,0:T(8,128)(2,1)S(1)}, u32[]{:S(2)}, u32[]{:S(2)}) collective-permute-start(bf16[96,768]{1,0:T(8,128)(2,1)S(1)} %pad_maximum_fusion.6), channel_id=1, source_target_pairs={{0,16},{2,18},{4,20},{6,22},{8,24},{10,26},{12,28},{14,30},{16,0},... | collective-permute-start | bytes 442376 | tf_op jit(solution)/shard_map/ppermute | solution.py:66
  220.9 7.7 %collective-permute-start.16 = (bf16[112,896]{1,0:T(8,128)(2,1)S(1)}, bf16[112,896]{1,0:T(8,128)(2,1)S(1)}, u32[]{:S(2)}, u32[]{:S(2)}) collective-permute-start(bf16[112,896]{1,0:T(8,128)(2,1)S(1)} %pad_maximum_fusion.5), channel_id=1, source_target_pairs={{0,8},{2,10},{4,12},{6,14},{8,0},{10,2},{12,4},{14,6},{16,24},{18,... | collective-permute-start | bytes 602120 | tf_op jit(solution)/shard_map/ppermute | solution.py:66
  228.6 19.3 %copy-start.29 = (f32[16,768]{1,0:T(8,128)S(1)}, f32[16,768]{1,0:T(8,128)}, u32[]{:S(2)}) copy-start(f32[16,768]{1,0:T(8,128)} %param.29) | copy-start | bytes 147460
  228.6 20.0 %copy-start.53 = (f32[1536]{0:T(1024)S(1)}, f32[1536]{0:T(1024)}, u32[]{:S(2)}) copy-start(f32[1536]{0:T(1024)} %get-tuple-element.118) | copy-start | bytes 18436
  228.6 20.6 %copy-start.23 = (f32[197,768]{1,0:T(8,128)S(1)}, f32[197,768]{1,0:T(8,128)}, u32[]{:S(2)}) copy-start(f32[197,768]{1,0:T(8,128)} %get-tuple-element.102) | copy-start | bytes 1815556
  228.7 8.9 %collective-permute-start.18 = (bf16[208,896]{1,0:T(8,128)(2,1)S(1)}, bf16[208,896]{1,0:T(8,128)(2,1)S(1)}, u32[]{:S(2)}, u32[]{:S(2)}) collective-permute-start(bf16[208,896]{1,0:T(8,128)(2,1)S(1)} %pad_maximum_fusion.1), channel_id=1, source_target_pairs={{0,4},{2,6},{4,0},{6,2},{8,12},{10,14},{12,8},{14,10},{16,20},{18,... | collective-permute-start | bytes 1118216 | tf_op jit(solution)/shard_map/ppermute | solution.py:66
  232.0 7.2 %collective-permute-start.19 = (bf16[192,768]{1,0:T(8,128)(2,1)S(1)}, bf16[192,768]{1,0:T(8,128)(2,1)S(1)}, u32[]{:S(2)}, u32[]{:S(2)}) collective-permute-start(bf16[192,768]{1,0:T(8,128)(2,1)S(1)} %pad_maximum_fusion.4), channel_id=1, source_target_pairs={{0,8},{2,10},{4,12},{6,14},{8,0},{10,2},{12,4},{14,6},{16,24},{18,... | collective-permute-start | bytes 884744 | tf_op jit(solution)/shard_map/ppermute | solution.py:66
  247.8 4.6 %collective-permute-start.20 = (bf16[400,1664]{1,0:T(8,128)(2,1)S(1)}, bf16[400,1664]{1,0:T(8,128)(2,1)S(1)}, u32[]{:S(2)}, u32[]{:S(2)}) collective-permute-start(bf16[400,1664]{1,0:T(8,128)(2,1)S(1)} %fusion.19), channel_id=1, source_target_pairs={{0,2},{2,0},{4,6},{6,4},{8,10},{10,8},{12,14},{14,12},{16,18},{18,... | collective-permute-start | bytes 3993608 | tf_op jit(solution)/shard_map/ppermute | solution.py:66
  (60 other events, 361.2 us)

commit v6 on v5

--- a/solution.py
+++ b/solution.py
@@ -87,63 +87,193 @@
     return across(total[total.shape[0] // 2 :].astype(BF16), bit, count)
 
 
-def home_kernel(back_ref, onehot_ref, facts_ref, home_ref, logit_ref, inner_ref):
+def expert_kernel(
+    capacity, slots, own_ref, arrived_ref, cot_ref, other_ref, router_ref, in_ref, bias_ref, out_ref,
+    activ_ref, slope_ref, grad_rows_ref, row_ref, out_rows_ref, bias_grad_ref, gate_ref, row_sum, out_sum,
+):
+    step = pl.program_id(0)
+    count = arrived_ref.shape[0]
+    experts = router_ref.shape[1]
+
+    @pl.when(step == 0)
+    def _():
+        logits = nn(arrived_ref[...], router_ref[...])
+        ids = lax.broadcasted_iota(jnp.int32, (count, experts), 1)
+        own = jnp.sum(jnp.where(ids == own_ref[0], logits, 0.0), axis=1, keepdims=True)
+        other = jnp.sum(jnp.where(ids.astype(F32) == other_ref[...], logits, 0.0), axis=1, keepdims=True)
+        top = jnp.maximum(own, other)
+        own, other = jnp.exp(own - top), jnp.exp(other - top)
+        spot = lax.broadcasted_iota(jnp.int32, (count, 1), 0) % slots
+        gate = jnp.where(spot < capacity, own / (own + other), 0.0)
+        gate_ref[...] = jnp.broadcast_to(gate, gate_ref.shape)
+        grad_rows_ref[...] = (gate * cot_ref[...].astype(F32)).astype(BF16)
+        row_sum[...] = jnp.zeros_like(row_sum)
+        out_sum[...] = jnp.zeros_like(out_sum)
+
+    pre_act = nn(arrived_ref[...], in_ref[...]) + bias_ref[...]
+    activ, slope = gelu_parts(pre_act)
+    activ = activ.astype(BF16)
+    activ_ref[...] = activ
+    grad = nt(grad_rows_ref[...], out_ref[...]) * slope
+    bias_grad_ref[...] = jnp.sum(grad, axis=0, keepdims=True)
+    grad = grad.astype(BF16)
+    slope_ref[...] = grad
+    row_sum[...] += nt(grad, in_ref[...])
+    out_sum[...] += nn(activ, out_ref[...])
+
+    @pl.when(step == pl.num_programs(0) - 1)
+    def _():
+        inner = jnp.sum(cot_ref[...].astype(F32) * out_sum[...], axis=1, keepdims=True)
+        inner = jnp.broadcast_to(inner, gate_ref.shape).T
+        out_rows_ref[...] = (gate_ref[:, :1] * out_sum[...]).astype(BF16)
+        spot = lax.broadcasted_iota(jnp.int32, (slots, 128), 0)
+        row_ref[...] = row_sum[...].astype(BF16)
+        for source in range(count // slots):
+            first = source * slots
+            line = inner[:1, first : first + slots]
+            line = jnp.concatenate([line, jnp.zeros((1, 128 - slots), F32)], axis=1)
+            high = line.astype(BF16).astype(F32)
+            tail = row_sum[first + slots - 16 : first + slots, :128]
+            place = lax.broadcasted_iota(jnp.int32, tail.shape, 0)
+            tail = jnp.where(place == 15, high, jnp.where(place == 14, line - high, tail))
+            row_ref[first + slots - 16 : first + slots, :128] = tail.astype(BF16)
+
+
+def expert_rows(own, arrived, cot_rows, other, router, in_weight, in_bias, out_weight, capacity, slots):
+    count, feat_dim = arrived.shape
+    hidden = in_weight.shape[1]
+    block = 512 if hidden % 512 == 0 else hidden
+    whole = lambda shape: pl.BlockSpec(shape, lambda i: (0, 0))
+    return pl.pallas_call(
+        lambda *refs: expert_kernel(capacity, slots, *refs),
+        grid=(hidden // block,),
+        in_specs=[
+            pl.BlockSpec(memory_space=pltpu.SMEM),
+            whole((count, feat_dim)),
+            whole((count, feat_dim)),
+            whole((count, 1)),
+            whole(router.shape),
+            pl.BlockSpec((feat_dim, block), lambda i: (0, i)),
+            pl.BlockSpec((1, block), lambda i: (0, i)),
+            pl.BlockSpec((block, feat_dim), lambda i: (i, 0)),
+        ],
+        out_specs=[
+            pl.BlockSpec((count, block), lambda i: (0, i)),
+            pl.BlockSpec((count, block), lambda i: (0, i)),
+            whole((count, feat_dim)),
+            whole((count, feat_dim)),
+            whole((count, feat_dim)),
+            pl.BlockSpec((1, block), lambda i: (0, i)),
+        ],
+        out_shape=(
+            jax.ShapeDtypeStruct((count, hidden), BF16),
+            jax.ShapeDtypeStruct((count, hidden), BF16),
+            jax.ShapeDtypeStruct((count, feat_dim), BF16),
+            jax.ShapeDtypeStruct((count, feat_dim), BF16),
+            jax.ShapeDtypeStruct((count, feat_dim), BF16),
+            jax.ShapeDtypeStruct((1, hidden), F32),
+        ),
+        scratch_shapes=[
+            pltpu.VMEM((count, 128), F32),
+            pltpu.VMEM((count, feat_dim), F32),
+            pltpu.VMEM((count, feat_dim), F32),
+        ],
+        compiler_params=pltpu.CompilerParams(vmem_limit_bytes=60 << 20),
+        cost_estimate=pl.CostEstimate(
+            flops=8 * count * feat_dim * hidden, bytes_accessed=12 << 20, transcendentals=2 * count * hidden
+        ),
+        name="expert_rows",
+    )(own[None], arrived, cot_rows, other, router, in_weight, in_bias, out_weight)
+
+
+def expert_rows_plain(own, arrived, cot_rows, other, router, in_weight, in_bias, out_weight, capacity, slots):
+    count, feat_dim = arrived.shape
+    logits = nn(arrived, router)
+    ids = jnp.arange(router.shape[1], dtype=jnp.int32)[None, :]
+    own = jnp.sum(jnp.where(ids == own, logits, 0.0), axis=1, keepdims=True)
+    other = jnp.sum(jnp.where(ids.astype(F32) == other, logits, 0.0), axis=1, keepdims=True)
+    top = jnp.maximum(own, other)
+    own, other = jnp.exp(own - top), jnp.exp(other - top)
+    spot = jnp.arange(count, dtype=jnp.int32)[:, None] % slots
+    gate = jnp.where(spot < capacity, own / (own + other), 0.0)
+    grad_rows = (gate * cot_rows.astype(F32)).astype(BF16)
+    activ, slope = gelu_parts(nn(arrived, in_weight) + in_bias)
+    activ = activ.astype(BF16)
+    grad = nt(grad_rows, out_weight) * slope
+    bias_grad = jnp.sum(grad, axis=0, keepdims=True)
+    grad = grad.astype(BF16)
+    part_out = nn(activ, out_weight)
+    inner = jnp.sum(cot_rows.astype(F32) * part_out, axis=1).reshape(-1, slots)
+    high, low = high_low(jnp.pad(inner, ((0, 0), (0, feat_dim - slots)))[:, None, :])
+    rows = nt(grad, in_weight).astype(BF16).reshape(-1, slots, feat_dim)
+    rows = jnp.concatenate([rows[:, : slots - 2], low, high], axis=1).reshape(count, feat_dim)
+    return activ, grad, grad_rows, rows, (gate * part_out).astype(BF16), bias_grad
+
+
+def home_kernel(back_ref, onehot_ref, facts_ref, home_ref, inner_ref):
     experts, slots, feat_dim = back_ref.shape
     tok_count = facts_ref.shape[0]
     home = nn(onehot_ref[...], back_ref[...].reshape(experts * slots, feat_dim))
-    home_ref[...] = home.astype(BF16)
+    home_ref[:tok_count, :] = home.astype(BF16)
     for e in range(experts):
         inner_ref[0, e : e + 1, :] = back_ref[e, slots - 1 : slots, :slots].astype(F32)
         inner_ref[1, e : e + 1, :] = back_ref[e, slots - 2 : slots - 1, :slots].astype(F32)
     expert_ids = lax.broadcasted_iota(jnp.int32, (tok_count, experts), 1).astype(F32)
     slot_ids = lax.broadcasted_iota(jnp.int32, (tok_count, slots), 1).astype(F32)
-    bias_dot = facts_ref[:, 16 : 16 + experts]
-    picks, inner_grads = [], []
+    lanes = lax.broadcasted_iota(jnp.int32, (tok_count, 128), 1)
+    table = jnp.zeros((tok_count, 128), F32)
     for k in range(2):
-        pick = facts_ref[:, k : k + 1] == expert_ids
-        hot = jnp.where(pick, 1.0, 0.0).astype(BF16)
+        hot = jnp.where(facts_ref[:, k : k + 1] == expert_ids, 1.0, 0.0).astype(BF16)
         found = nn(hot, inner_ref[0].astype(BF16)) + nn(hot, inner_ref[1].astype(BF16))
         found = jnp.where(facts_ref[:, k + 2 : k + 3] == slot_ids, found, 0.0)
-        own_bias = jnp.where(pick, bias_dot, 0.0)
-        inner_grads.append(
-            jnp.sum(found, axis=1, keepdims=True) + jnp.sum(own_bias, axis=1, keepdims=True)
-        )
-        picks.append(pick)
+        found = jnp.sum(found, axis=1, keepdims=True)
+        high = found.astype(BF16).astype(F32)
+        table = jnp.where(lanes == 2 * k, high, jnp.where(lanes == 2 * k + 1, found - high, table))
+    home_ref[tok_count + 3 : tok_count + 11, :tok_count] = table.T[:8, :].astype(BF16)
+
+
+def home_rows(back, onehot, facts):
+    experts, slots, feat_dim = back.shape
+    tok_count = facts.shape[0]
+    return pl.pallas_call(
+        home_kernel,
+        out_shape=jax.ShapeDtypeStruct((tok_count + 11, feat_dim), BF16),
+        scratch_shapes=[pltpu.VMEM((2, experts, slots), F32)],
+        compiler_params=pltpu.CompilerParams(vmem_limit_bytes=16 << 20),
+        cost_estimate=pl.CostEstimate(
+            flops=2 * tok_count * feat_dim * experts * slots, bytes_accessed=2 << 20, transcendentals=0
+        ),
+        name="home_rows",
+    )(back, onehot, facts)
+
+
+def attention_grads_kernel(
+    home_ref, other_ref, router_ref, cot_ref, normed_ref, facts_ref, gain_ref, hidden2_ref, bias_grad_ref,
+    proj_ref, projected_ref, attended_ref, hidden_ref, weight_ref, mix_ref,
+    sent_ref, kept_ref, hidden_part_ref, sums_ref, middle_grad_ref, low_ref, back_ref, small_ref, logit_ref,
+):
+    head_cols = attended_ref.shape[1]
+    experts = router_ref.shape[1]
+    tok_count = cot_ref.shape[0]
+    scale = HEAD ** (-0.5)
+    lines = slice(tok_count + 3, tok_count + 11)
+    inner = home_ref[lines, :tok_count].astype(F32) + other_ref[lines, :tok_count].astype(F32)
+    inner = inner.T
+    bias_dot = facts_ref[:, 16 : 16 + experts]
+    expert_ids = lax.broadcasted_iota(jnp.int32, (tok_count, experts), 1).astype(F32)
+    picks = [facts_ref[:, k : k + 1] == expert_ids for k in range(2)]
     gates = [facts_ref[:, k + 4 : k + 5] for k in range(2)]
+    inner_grads = []
+    for k in range(2):
+        own_bias = jnp.sum(jnp.where(picks[k], bias_dot, 0.0), axis=1, keepdims=True)
+        inner_grads.append(inner[:, 2 * k : 2 * k + 1] + inner[:, 2 * k + 1 : 2 * k + 2] + own_bias)
     mean = gates[0] * inner_grads[0] + gates[1] * inner_grads[1]
     logit_grad = 0.0
     for k in range(2):
         logit_grad = logit_grad + jnp.where(picks[k], gates[k] * (inner_grads[k] - mean), 0.0)
     logit_ref[...] = logit_grad.astype(BF16)
-
-
-def home_rows(back, onehot, facts):
-    experts, slots, feat_dim = back.shape
-    tok_count = facts.shape[0]
-    return pl.pallas_call(
-        home_kernel,
-        out_shape=(
-            jax.ShapeDtypeStruct((tok_count, feat_dim), BF16),
-            jax.ShapeDtypeStruct((tok_count, experts), BF16),
-        ),
-        scratch_shapes=[pltpu.VMEM((2, experts, slots), F32)],
-        compiler_params=pltpu.CompilerParams(vmem_limit_bytes=60 << 20),
-        cost_estimate=pl.CostEstimate(
-            flops=2 * tok_count * feat_dim * experts * slots, bytes_accessed=2 << 20, transcendentals=0
-        ),
-        name="home_rows",
-    )(back, onehot, facts)
-
-
-def attention_grads_kernel(
-    home_ref, other_ref, logit_ref, router_ref, cot_ref, normed_ref, facts_ref, gain_ref, hidden2_ref, bias_grad_ref,
-    proj_ref, projected_ref, attended_ref, hidden_ref, weight_ref, mix_ref,
-    sent_ref, kept_ref, hidden_part_ref, sums_ref, middle_grad_ref, low_ref, back_ref, small_ref,
-):
-    head_cols = attended_ref.shape[1]
-    experts = logit_ref.shape[1]
-    scale = HEAD ** (-0.5)
-    hidden_grad = home_ref[...].astype(F32) + other_ref[...].astype(F32) + nt(logit_ref[...], router_ref[...])
+    hidden_grad = home_ref[:tok_count, :].astype(F32) + other_ref[:tok_count, :].astype(F32)
+    hidden_grad = hidden_grad + nt(logit_ref[...], router_ref[...])
     normed = normed_ref[...]
     inner = hidden_grad * gain_ref[...]
     middle_grad = cot_ref[...].astype(F32) + norm_back(inner, normed, facts_ref[:, 6:7])
@@ -198,9 +328,9 @@
 
 
 def attention_grads(*operands):
-    tok_count, feat_dim = operands[0].shape
+    tok_count, feat_dim = operands[3].shape
     experts = operands[2].shape[1]
-    head_cols = operands[10].shape[0]
+    head_cols = operands[9].shape[0]
     small = -(-(2 * experts + 3) // 128) * 128
     width = 4 * head_cols + small
     flops = 2 * tok_count * feat_dim * head_cols * 9 + 2 * feat_dim * feat_dim * (tok_count + small)
@@ -217,6 +347,7 @@
             pltpu.VMEM((tok_count, 3 * head_cols), BF16),
             pltpu.VMEM((tok_count, head_cols), BF16),
             pltpu.VMEM((small, feat_dim), F32),
+            pltpu.VMEM((tok_count, experts), BF16),
         ],
         compiler_params=pltpu.CompilerParams(vmem_limit_bytes=60 << 20),
         cost_estimate=pl.CostEstimate(
@@ -226,46 +357,45 @@
     )(*operands)
 
 
-def finish_kernel(head_cols, experts, orders, me_ref, mine, got, qkv_ref, proj_ref, router_ref, bias_ref, norm_ref, held_proj, held_small):
+def finish_kernel(head_cols, experts, orders, me_ref, mine, mine_b, got, got_b, qkv_ref, proj_ref, router_ref, bias_ref, norm_ref, held_proj, held_small):
     me = me_ref[0]
     count = 1 << len(orders[0])
     feat_dim = qkv_ref.shape[1]
     chunk = feat_dim // count
     half = count // 2
-    width = held_small.shape[1]
-    split = 2 * head_cols + width
     for spot in range(count):
         starts = []
         for order in orders:
             name = sum(bit for i, bit in enumerate(order) if (spot >> (len(order) - 1 - i)) & 1)
             starts.append(pl.ds(pl.multiple_of((name ^ me) * chunk, chunk), chunk))
-        source = mine if spot < half else got
+        source, source_b = (mine, mine_b) if spot < half else (got, got_b)
         first = (spot % half) * chunk
         piece = source[first : first + chunk, :].astype(F32)
         qkv_ref[0, starts[0], :] = piece[:, :head_cols]
         qkv_ref[1, starts[0], :] = piece[:, head_cols : 2 * head_cols]
-        held_small[starts[0], :] = piece[:, 2 * head_cols : split]
-        qkv_ref[2, starts[1], :] = piece[:, split : split + head_cols]
-        held_proj[starts[1], :] = piece[:, split + head_cols :]
+        held_small[starts[0], :] = piece[:, 2 * head_cols :]
+        piece = source_b[first : first + chunk, :].astype(F32)
+        qkv_ref[2, starts[1], :] = piece[:, :head_cols]
+        held_proj[starts[1], :] = piece[:, head_cols:]
     proj_ref[...] = held_proj[...].T
     small = held_small[...]
-    router_ref[...] = small[:, :experts]
     flat = small.T
+    router_ref[...] = flat[:experts]
     bias_ref[...] = flat[experts : 2 * experts]
     norm_ref[...] = flat[2 * experts : 2 * experts + 8]
 
 
-def finish(me, mine, came, head_cols, experts, feat_dim, orders):
-    width = mine.shape[1] - 4 * head_cols
+def finish(me, mine, mine_b, came, came_b, head_cols, experts, feat_dim, orders):
+    width = mine.shape[1] - 2 * head_cols
     vmem = pl.BlockSpec(memory_space=pltpu.VMEM)
     return pl.pallas_call(
         lambda *refs: finish_kernel(head_cols, experts, orders, *refs),
-        in_specs=[pl.BlockSpec(memory_space=pltpu.SMEM), vmem, vmem],
+        in_specs=[pl.BlockSpec(memory_space=pltpu.SMEM)] + [vmem] * 4,
         out_specs=[vmem] * 5,
         out_shape=(
             jax.ShapeDtypeStruct((3, feat_dim, head_cols), F32),
             jax.ShapeDtypeStruct((head_cols, feat_dim), F32),
-            jax.ShapeDtypeStruct((feat_dim, experts), F32),
+            jax.ShapeDtypeStruct((experts, feat_dim), F32),
             jax.ShapeDtypeStruct((experts, feat_dim), F32),
             jax.ShapeDtypeStruct((8, feat_dim), F32),
         ),
@@ -273,9 +403,9 @@
             pltpu.VMEM((feat_dim, head_cols), F32),
             pltpu.VMEM((feat_dim, width), F32),
         ],
-        compiler_params=pltpu.CompilerParams(vmem_limit_bytes=60 << 20),
+        compiler_params=pltpu.CompilerParams(vmem_limit_bytes=40 << 20),
         name="finish",
-    )(me[None], mine, came)
+    )(me[None], mine, mine_b, came, came_b)
 
 
 def high_low(values):
@@ -395,42 +525,14 @@
     out_bias_grad = tn(pick_low[0], row_grad[0]) + tn(pick_low[1], row_grad[1])
 
     note_rows = jnp.where(plane == 0, cot_mine, cot_other).reshape(sources, slots, half_dim)
-    other_expert = note_rows[:, slots - 1, :slots].reshape(-1, 1).astype(jnp.int32)
-    real_slot = (jnp.arange(sources * slots, dtype=jnp.int32)[:, None] % slots) < capacity
-    row_logits = nn(arrived, router)
-    own_logit = jnp.sum(
-        jnp.where(expert_ids[None, :] == own_expert, row_logits, 0.0), axis=1, keepdims=True
-    )
-    other_logit = jnp.sum(
-        jnp.where(expert_ids[None, :] == other_expert, row_logits, 0.0), axis=1, keepdims=True
-    )
-    top_logit = jnp.maximum(own_logit, other_logit)
-    own_exp = jnp.exp(own_logit - top_logit)
-    row_gate = own_exp / (own_exp + jnp.exp(other_logit - top_logit))
-    row_gate = jnp.where(real_slot, row_gate, 0.0)
+    other_expert = note_rows[:, slots - 1, :slots].reshape(-1, 1).astype(F32)
     cot_rows = in_order(plane, cot_mine, cot_other, 1)
-    grad_rows = (row_gate * cot_rows.astype(F32)).astype(BF16)
-
-    pre_act = nn(arrived, in_weight) + expert_in_bias[0]
-    activ_vals, gelu_slope = gelu_parts(pre_act)
-    activ_low = activ_vals.astype(BF16)
-    part_out = nn(activ_low, out_weight)
-    act_grad = nt(grad_rows, out_weight) * gelu_slope
-    in_bias_grad = jnp.sum(act_grad, axis=0)
-    act_low = act_grad.astype(BF16)
-    row_part = nt(act_low, in_weight)
-
-    inner = jnp.sum(cot_rows.astype(F32) * part_out, axis=1).reshape(sources, slots)
-    inner = inner + swap(inner)
-    inner_high = inner.astype(BF16)
-    inner_low = (inner - inner_high.astype(F32)).astype(BF16)
-
-    def widen(x):
-        return jnp.pad(x, ((0, 0), (0, feat_dim - slots)))[:, None, :]
-
-    row_send = row_part.astype(BF16).reshape(sources, slots, feat_dim)
-    row_send = jnp.where(slot_ids[None, :, None] == slots - 1, widen(inner_high), row_send)
-    row_send = jnp.where(slot_ids[None, :, None] == slots - 2, widen(inner_low), row_send)
+    activ_low, act_low, grad_rows, row_send, out_send, in_bias_grad = (
+        expert_rows if sources * slots <= 1024 else expert_rows_plain
+    )(
+        own_expert, arrived, cot_rows, other_expert, router, in_weight, expert_in_bias, out_weight, capacity, slots
+    )
+    row_send = row_send.reshape(sources, slots, feat_dim)
     row_back = lax.all_to_all(row_send, "dp", split_axis=0, concat_axis=0, tiled=True)
     out_weight_grad = tn(activ_low, grad_rows)
     in_weight_grad = tn(arrived, act_low)
@@ -479,20 +581,19 @@
         shape = (experts, group_size) + x.shape[1:]
         return jnp.sum(x.reshape(shape).astype(F32), axis=1).astype(BF16)
 
-    row_home, logit_grad = home_rows(
+    row_home = home_rows(
         over_group(row_back),
         onehot,
         facts,
     )
-    part_out, row_home = lax.optimization_barrier((part_out, row_home))
-    out_send = (row_gate * part_out).astype(BF16).reshape(sources, slots, feat_dim)
+    out_send, row_home = lax.optimization_barrier((out_send, row_home))
+    out_send = out_send.reshape(sources, slots, feat_dim)
     row_other = swap(row_home)
     out_back = lax.all_to_all(out_send, "dp", split_axis=0, concat_axis=0, tiled=True)
 
     sent, kept, hidden1_part, qv_sums, middle_grad = attention_grads(
         row_home,
         row_other,
-        logit_grad,
         router,
         cotangent,
         normed2,
@@ -561,18 +662,21 @@
         ]
         size = 2 * size
     own, both = late_rows(late)
-    mine = jnp.concatenate(mine, axis=1)
-    both = jnp.pad(both, ((0, 0), (0, 2 * head_cols)))
-    came = across(jnp.concatenate([mine, both], axis=0), bits[0], sources)
+    first, second, input_grad, output = lax.optimization_barrier(
+        (jnp.concatenate([mine[0], both], axis=0), mine[1], input_grad, output)
+    )
+    came = across(first, bits[0], sources)
+    came_b = across(second, bits[0], sources)
     late = late_sum(own, came[size:])
     qv_bias_grad = late[2].reshape(2, head_cols)
     if chunk % 16 == 0:
         qkv_grad, proj_grad, router_grad, out_bias_grad, norm_grads = finish(
-            me, mine, came, head_cols, experts, feat_dim, orders
+            me, first, second, came, came_b, head_cols, experts, feat_dim, orders
         )
+        router_grad = router_grad.T
     else:
-        whole = jnp.concatenate([mine, came[:size]], axis=0)
-        first, second = tn(mix_t[0], whole[:, :split]), tn(mix_t[1], whole[:, split:])
+        first = tn(mix_t[0], jnp.concatenate([mine[0], came[:size]], axis=0))
+        second = tn(mix_t[1], jnp.concatenate([mine[1], came_b], axis=0))
         qkv_grad = jnp.stack(
             [first[:, :head_cols], first[:, head_cols : 2 * head_cols], second[:, :head_cols]]
         )
@@ -594,7 +698,7 @@
         norm2_bias_grad,
         router_grad,
         in_weight_grad[None],
-        in_bias_grad[None],
+        in_bias_grad,
         out_weight_grad[None],
         out_bias_grad,
     )

time: 264 us -> 233 us (0.88)
  matrix products: 46 us -> 24.2 us
  local copies, waits for them, and re-layouts: 34.1 us -> 12.8 us
  waiting for transfers between devices: 74.4 us -> 88.2 us
  other arithmetic: 35 us -> 22.3 us
  Pallas kernels: 17.5 us -> 29.4 us
    dot_general x17 -> x12, matrix products: 36.9 us -> 17.9 us  [dot(): return lax.dot_general(a, b, (dims, ((), ())), preferred_element_type=out)]
    pallas_call x1 -> x2, Pallas kernels: 2.88 us -> 15.3 us  [the longest x1 14.7 us: expert_rows(): pl.pallas_call(lambda *refs: expert_kernel(capacity, slots, *refs), grid=...]
    ppermute x14 -> x15, waiting for transfers between devices: 37.4 us -> 46.7 us  [across(): return lax.ppermute(x, 'dp', [(i, i ^ bit) for i in range(count)])]
    concatenate x2 -> x1, other arithmetic: 9.75 us -> 2.18 us  [in_order(): return jnp.concatenate([first, second], axis=axis)]
    unnamed x137 -> x107, local copies, waits for them, and re-layouts: 10.5 us -> 3.56 us
    ppermute x7 -> x6, waiting for transfers between devices: 20.1 us -> 25.2 us  [swap(): return lax.ppermute(x, 'tensor', [(0, 1), (1, 0)])]
    slice x4, local copies, waits for them, and re-layouts: 5.28 us -> 0.48 us  [local(): queries, key_vals, values_in = (heads_view[0], heads_view[1], heads_view[2])]
    ppermute x14 -> x15, starting transfers between devices: 20.4 us -> 17.2 us  [across(): return lax.ppermute(x, 'dp', [(i, i ^ bit) for i in range(count)])]
  transfers between devices with their start and end apart: 25 -> 25, of which waited for: 20 -> 21; matrix products, arithmetic and copies ran while one was open for 25% -> 20% of each run, Pallas kernels for 4% -> 5%
where the time goes in v6:
time: 233 us; the launch traced here: 232 us
  waiting for transfers between devices  88.2 us (38%)
  starting transfers between devices  53.7 us (23%)
  Pallas kernels  29.4 us (13%)
  matrix products  24.2 us (10%)
  other arithmetic  22.3 us (10%)
  local copies, waits for them, and re-layouts  12.8 us (5%)
    ppermute x15, waiting for transfers between devices, across(): return lax.ppermute(x, 'dp', [(i, i ^ bit) for i in range(count)])  46.7 us
    ppermute x6, waiting for transfers between devices, swap(): return lax.ppermute(x, 'tensor', [(0, 1), (1, 0)])  25.2 us
    dot_general x12, matrix products, dot(): return lax.dot_general(a, b, (dims, ((), ())), preferred_element_type=out)  17.9 us
    ppermute x15, starting transfers between devices, across(): return lax.ppermute(x, 'dp', [(i, i ^ bit) for i in range(count)])  17.2 us
    pallas_call x1, Pallas kernels, expert_rows(): pl.pallas_call(lambda *refs: expert_kernel(capacity, slots, *refs), grid=...  14.7 us
    all_to_all x1, waiting for transfers between devices, local(): lax.all_to_all(row_send, 'dp', split_axis=0, concat_axis=0, tiled=True)  13 us
    pallas_call x1, Pallas kernels, attention_grads(): pl.pallas_call(attention_grads_kernel, out_shape=(jax.ShapeDtypeStruct((f...  11.3 us
    ppermute x6, starting transfers between devices, swap(): return lax.ppermute(x, 'tensor', [(0, 1), (1, 0)])  8.43 us
  transfers between devices with their start and end apart: 25, of which 21 were waited for; matrix products, arithmetic and copies ran while one was open for 20% of the time, Pallas kernels for 5%

profile of v6, /device:TPU:0, one launch (start us, length us, event | category | flops | bytes accessed | tf_op | source)
XLA Modules:
  0.0 232.2 jit_solution(11828374020226768203)
XLA Ops:
  5.9 7.4 %all-to-all-start = ((bf16[16,48,384]{2,1,0:T(8,128)(2,1)}), bf16[16,48,384]{2,1,0:T(8,128)(2,1)}, u32[]{:S(2)}, u32[]{:S(2)}) async-start(bf16[16,48,384]{2,1,0:T(8,128)(2,1)} %broadcast_select_fusion), calls=%async_computation | async-start | bytes 1179648 | tf_op jit(solution)/shard_map/all_to_all | solution.py:483
  15.5 2.1 fusion.3.projected_ref
  20.2 9.3 %collective-permute-done.1 = bf16[384,768]{1,0:T(8,128)(2,1)S(1)} collective-permute-done((bf16[384,768]{1,0:T(8,128)(2,1)S(1)}, bf16[384,768]{1,0:T(8,128)(2,1)S(1)}, u32[]{:S(2)}, u32[]{:S(2)}) %collective-permute-start.1) | collective-permute-done | bytes 589856 | tf_op jit(solution)/shard_map/ppermute | solution.py:62
  30.6 2.6 %collective-permute-done = bf16[197,384]{0,1:T(8,128)(2,1)S(1)} collective-permute-done((bf16[197,384]{0,1:T(8,128)(2,1)S(1)}, bf16[197,384]{0,1:T(8,128)(2,1)S(1)}, u32[]{:S(2)}, u32[]{:S(2)}) %collective-permute-start) | collective-permute-done | bytes 151328 | tf_op jit(solution)/shard_map/ppermute | solution.py:62
  38.1 5.9 %all-to-all-start.1 = ((bf16[16,48,768]{2,1,0:T(8,128)(2,1)}), bf16[16,48,768]{2,1,0:T(8,128)(2,1)S(1)}, u32[]{:S(2)}, u32[]{:S(2)}) async-start(bf16[16,48,768]{2,1,0:T(8,128)(2,1)} %bitcast.21), calls=%async_computation.1 | async-start | bytes 2359296 | tf_op jit(solution)/shard_map/all_to_all | solution.py:513
  51.7 3.2 %fusion.mix_ref = bf16[2,768,768]{2,1,0:T(8,128)(2,1)} fusion(pred[1,768,768]{2,1,0:T(32,128)(4,1)} %get-tuple-element.177, pred[1,768,768]{2,1,0:T(32,128)(4,1)} %get-tuple-element.176), kind=kLoop, calls=%fused_computation.7 | loop fusion | flops 2359296 | bytes 3538944 | tf_op jit(solution)/shard_map/stack | solution.py:554
  57.6 5.4 %collective-permute-done.2 = bf16[768,384]{1,0:T(8,128)(2,1)} collective-permute-done((bf16[768,384]{1,0:T(8,128)(2,1)}, bf16[768,384]{1,0:T(8,128)(2,1)}, u32[]{:S(2)}, u32[]{:S(2)}) %collective-permute-start.2) | collective-permute-done | bytes 589856 | tf_op jit(solution)/shard_map/ppermute | solution.py:62
  63.0 2.2 broadcast_select_fusion.2
  67.4 2.2 pad_maximum_fusion.refs_2_
  70.6 14.7 %expert_rows.1 = (bf16[768,1536]{1,0:T(8,128)(2,1)}, bf16[768,1536]{1,0:T(8,128)(2,1)}, bf16[768,768]{1,0:T(8,128)(2,1)}, bf16[768,768]{1,0:T(8,128)(2,1)}, bf16[768,768]{1,0:T(8,128)(2,1)}, /*index=5*/f32[1,1536]{1,0:T(1,128)}) custom-call(s32[1]{0:T(128)} %bitcast.refs_0_, bf16[768,768]{1,0:T(8,128)(2,1)} %bitcast.65, ...), custom_call_target="tpu_custom_call" | custom-call | flops 7247757312 | bytes 12582912 | tf_op jit(solution)/shard_map/expert_rows/pallas_call | solution.py:147
  85.4 7.2 %all-to-all-start.2 = ((bf16[16,48,768]{2,1,0:T(8,128)(2,1)}), bf16[16,48,768]{2,1,0:T(8,128)(2,1)S(1)}, u32[]{:S(2)}, u32[]{:S(2)}) async-start(bf16[16,48,768]{2,1,0:T(8,128)(2,1)} %bitcast.69), calls=%async_computation.2 | async-start | bytes 2359296 | tf_op jit(solution)/shard_map/all_to_all | solution.py:536
  94.1 6.4 %fusion.121 = f32[768,1536]{1,0:T(8,128)} fusion(bf16[768,768]{1,0:T(8,128)(2,1)} %bitcast.66, bf16[768,1536]{1,0:T(8,128)(2,1)} %get-tuple-element.84), kind=kOutput, calls=%fused_computation.243 | convolution fusion | flops 1811939328 | bytes 8257536 | tf_op jit(solution)/shard_map/dot_general | solution.py:36
  100.4 4.3 %fusion.120 = f32[1536,768]{1,0:T(8,128)} fusion(bf16[768,1536]{1,0:T(8,128)(2,1)S(1)} %copy-done.49, bf16[768,768]{1,0:T(8,128)(2,1)S(1)} %copy-done.50), kind=kOutput, calls=%fused_computation.242 | convolution fusion | flops 1811939328 | bytes 8257536 | tf_op jit(solution)/shard_map/dot_general | solution.py:36
  104.7 13.0 %all-to-all-done.2.back_ref = bf16[16,48,768]{2,1,0:T(8,128)(2,1)S(1)} async-done(((bf16[16,48,768]{2,1,0:T(8,128)(2,1)}), bf16[16,48,768]{2,1,0:T(8,128)(2,1)S(1)}, u32[]{:S(2)}, u32[]{:S(2)}) %all-to-all-start.2) | async-done | bytes 1179680 | tf_op jit(solution)/shard_map/all_to_all | solution.py:536
  118.4 7.6 %all-to-all-start.3 = ((bf16[16,48,768]{2,1,0:T(8,128)(2,1)}), bf16[16,48,768]{2,1,0:T(8,128)(2,1)S(1)}, u32[]{:S(2)}, u32[]{:S(2)}) async-start(bf16[16,48,768]{2,1,0:T(8,128)(2,1)} %bitcast.68), calls=%async_computation.3 | async-start | bytes 2359296 | tf_op jit(solution)/shard_map/all_to_all | solution.py:592
  129.8 6.1 %collective-permute-done.3.other_ref = bf16[208,768]{1,0:T(8,128)(2,1)S(1)} collective-permute-done((bf16[208,768]{1,0:T(8,128)(2,1)S(1)}, bf16[208,768]{1,0:T(8,128)(2,1)S(1)}, u32[]{:S(2)}, u32[]{:S(2)}) %collective-permute-start.3) | collective-permute-done | bytes 319520 | tf_op jit(solution)/shard_map/ppermute | solution.py:62
  136.6 11.3 %attention_grads.1 = (bf16[384,1664]{1,0:T(8,128)(2,1)}, f32[384,1664]{1,0:T(8,128)}, bf16[197,768]{1,0:T(8,128)(2,1)}, f32[1,1152]{1,0:T(1,128)}, f32[197,768]{1,0:T(8,128)}) custom-call(bf16[208,768]{1,0:T(8,128)(2,1)} %copy-done.1, bf16[208,768]{1,0:T(8,128)(2,1)} %copy-done.13, bf16[768,16]{1,0:T(8,128)(2,1)} %copy.80.router_ref, ...), custom_call_target="tpu_custom_call" | custom-call | flops 1429143552 | bytes 10485760 | tf_op jit(solution)/shard_map/attention_grads/pallas_call | solution.py:337
  147.9 3.2 %all-to-all-done.3 = bf16[16,48,768]{2,1,0:T(8,128)(2,1)S(1)} async-done(((bf16[16,48,768]{2,1,0:T(8,128)(2,1)}), bf16[16,48,768]{2,1,0:T(8,128)(2,1)S(1)}, u32[]{:S(2)}, u32[]{:S(2)}) %all-to-all-start.3) | async-done | bytes 1179680 | tf_op jit(solution)/shard_map/all_to_all | solution.py:592
  157.6 3.8 %collective-permute-start.6 = (bf16[192,768]{1,0:T(8,128)(2,1)S(1)}, bf16[192,768]{1,0:T(8,128)(2,1)S(1)}, u32[]{:S(2)}, u32[]{:S(2)}) collective-permute-start(bf16[192,768]{1,0:T(8,128)(2,1)S(1)} %slice.287), channel_id=1, source_target_pairs={{0,8},{2,10},{4,12},{6,14},{8,0},{10,2},{12,4},{14,6},{16,24},{18,... | collective-permute-start | bytes 884744 | tf_op jit(solution)/shard_map/ppermute | solution.py:66
  163.3 2.2 collective-permute-start.5
  165.5 2.8 %collective-permute-done.6 = bf16[192,768]{1,0:T(8,128)(2,1)S(1)} collective-permute-done((bf16[192,768]{1,0:T(8,128)(2,1)S(1)}, bf16[192,768]{1,0:T(8,128)(2,1)S(1)}, u32[]{:S(2)}, u32[]{:S(2)}) %collective-permute-start.6) | collective-permute-done | bytes 294944 | tf_op jit(solution)/shard_map/ppermute | solution.py:66
  168.4 4.5 %collective-permute-done.5 = bf16[192,896]{1,0:T(8,128)(2,1)S(1)} collective-permute-done((bf16[192,896]{1,0:T(8,128)(2,1)S(1)}, bf16[192,896]{1,0:T(8,128)(2,1)S(1)}, u32[]{:S(2)}, u32[]{:S(2)}) %collective-permute-start.5) | collective-permute-done | bytes 344096 | tf_op jit(solution)/shard_map/ppermute | solution.py:66
  173.0 5.7 %collective-permute-start.8 = (bf16[96,768]{1,0:T(8,128)(2,1)S(1)}, bf16[96,768]{1,0:T(8,128)(2,1)S(1)}, u32[]{:S(2)}, u32[]{:S(2)}) collective-permute-start(bf16[96,768]{1,0:T(8,128)(2,1)S(1)} %slice.289), channel_id=1, source_target_pairs={{0,16},{2,18},{4,20},{6,22},{8,24},{10,26},{12,28},{14,30},{16,0},... | collective-permute-start | bytes 442376 | tf_op jit(solution)/shard_map/ppermute | solution.py:66
  178.8 5.9 %collective-permute-done.8 = bf16[96,768]{1,0:T(8,128)(2,1)S(1)} collective-permute-done((bf16[96,768]{1,0:T(8,128)(2,1)S(1)}, bf16[96,768]{1,0:T(8,128)(2,1)S(1)}, u32[]{:S(2)}, u32[]{:S(2)}) %collective-permute-start.8) | collective-permute-done | bytes 147488 | tf_op jit(solution)/shard_map/ppermute | solution.py:66
  191.2 3.6 %collective-permute-done.9 = bf16[48,896]{1,0:T(8,128)(2,1)S(1)} collective-permute-done((bf16[48,896]{1,0:T(8,128)(2,1)S(1)}, bf16[48,896]{1,0:T(8,128)(2,1)S(1)}, u32[]{:S(2)}, u32[]{:S(2)}) %collective-permute-start.9) | collective-permute-done | bytes 86048 | tf_op jit(solution)/shard_map/ppermute | solution.py:66
  197.0 2.7 %collective-permute-done.14 = bf16[48,768]{1,0:T(8,128)(2,1)S(1)} collective-permute-done((bf16[48,768]{1,0:T(8,128)(2,1)S(1)}, bf16[48,768]{1,0:T(8,128)(2,1)S(1)}, u32[]{:S(2)}, u32[]{:S(2)}) %collective-permute-start.14) | collective-permute-done | bytes 73760 | tf_op jit(solution)/shard_map/ppermute | solution.py:66
  199.7 6.0 %collective-permute-done.13 = bf16[64,896]{1,0:T(8,128)(2,1)S(1)} collective-permute-done((bf16[64,896]{1,0:T(8,128)(2,1)S(1)}, bf16[64,896]{1,0:T(8,128)(2,1)S(1)}, u32[]{:S(2)}, u32[]{:S(2)}) %collective-permute-start.13) | collective-permute-done | bytes 114720 | tf_op jit(solution)/shard_map/ppermute | solution.py:66
  206.0 6.0 %collective-permute-done.16 = bf16[96,768]{1,0:T(8,128)(2,1)S(1)} collective-permute-done((bf16[96,768]{1,0:T(8,128)(2,1)S(1)}, bf16[96,768]{1,0:T(8,128)(2,1)S(1)}, u32[]{:S(2)}, u32[]{:S(2)}) %collective-permute-start.16) | collective-permute-done | bytes 147488 | tf_op jit(solution)/shard_map/ppermute | solution.py:66
  212.1 3.3 %collective-permute-done.15 = bf16[112,896]{1,0:T(8,128)(2,1)S(1)} collective-permute-done((bf16[112,896]{1,0:T(8,128)(2,1)S(1)}, bf16[112,896]{1,0:T(8,128)(2,1)S(1)}, u32[]{:S(2)}, u32[]{:S(2)}) %collective-permute-start.15) | collective-permute-done | bytes 200736 | tf_op jit(solution)/shard_map/ppermute | solution.py:66
  219.0 3.3 %collective-permute-done.18 = bf16[192,768]{1,0:T(8,128)(2,1)S(1)} collective-permute-done((bf16[192,768]{1,0:T(8,128)(2,1)S(1)}, bf16[192,768]{1,0:T(8,128)(2,1)S(1)}, u32[]{:S(2)}, u32[]{:S(2)}) %collective-permute-start.18) | collective-permute-done | bytes 294944 | tf_op jit(solution)/shard_map/ppermute | solution.py:66
  222.3 2.9 %collective-permute-done.17 = bf16[208,896]{1,0:T(8,128)(2,1)S(1)} collective-permute-done((bf16[208,896]{1,0:T(8,128)(2,1)S(1)}, bf16[208,896]{1,0:T(8,128)(2,1)S(1)}, u32[]{:S(2)}, u32[]{:S(2)}) %collective-permute-start.17) | collective-permute-done | bytes 372768 | tf_op jit(solution)/shard_map/ppermute | solution.py:66
  228.8 2.8 %finish.1 = (f32[3,768,384]{2,1,0:T(8,128)}, f32[384,768]{1,0:T(8,128)}, f32[16,768]{1,0:T(8,128)}, f32[16,768]{1,0:T(8,128)}, f32[8,768]{1,0:T(8,128)S(1)}) custom-call(s32[1]{0:T(128)} %bitcast.refs_0_, bf16[400,896]{1,0:T(8,128)(2,1)S(1)} %fusion.67.refs_1_, bf16[384,768]{1,0:T(8,128)(2,1)S(1)} %pad_maximum_fusion.1.refs_2_, ...), custom_call_target="tpu_custom_call" | custom-call | tf_op jit(solution)/shard_map/finish/pallas_call | solution.py:391
  (251 shorter events, 61.0 us)
Async XLA Ops:
  0.6 43.5 %copy-start = (f32[16,768]{1,0:T(8,128)S(1)}, f32[16,768]{1,0:T(8,128)}, u32[]{:S(2)}) copy-start(f32[16,768]{1,0:T(8,128)} %param.29) | copy-start | bytes 147460
  5.9 27.3 %all-to-all-start = ((bf16[16,48,384]{2,1,0:T(8,128)(2,1)}), bf16[16,48,384]{2,1,0:T(8,128)(2,1)}, u32[]{:S(2)}, u32[]{:S(2)}) async-start(bf16[16,48,384]{2,1,0:T(8,128)(2,1)} %broadcast_select_fusion), calls=%async_computation | async-start | bytes 1179648 | tf_op jit(solution)/shard_map/all_to_all | solution.py:483
  13.3 16.2 %collective-permute-start.1 = (bf16[384,768]{1,0:T(8,128)(2,1)S(1)}, bf16[384,768]{1,0:T(8,128)(2,1)S(1)}, u32[]{:S(2)}, u32[]{:S(2)}) collective-permute-start(bf16[384,768]{1,0:T(8,128)(2,1)S(1)} %copy-done.9), channel_id=1, source_target_pairs={{0,1},{1,0},{2,3},{3,2},{4,5},{5,4},{6,7},{7,6},{8,9},{9,8},{10,11... | collective-permute-start | bytes 1769480 | tf_op jit(solution)/shard_map/ppermute | solution.py:62
  15.1 39.8 %copy-start.20 = (f32[197]{0:T(256)}, f32[197]{0:T(256)S(1)}, u32[]{:S(2)}) copy-start(f32[197]{0:T(256)S(1)} %broadcast_multiply_fusion.3) | copy-start | bytes 2368
  19.5 13.7 %collective-permute-start = (bf16[197,384]{0,1:T(8,128)(2,1)S(1)}, bf16[197,384]{0,1:T(8,128)(2,1)S(1)}, u32[]{:S(2)}, u32[]{:S(2)}) collective-permute-start(bf16[197,384]{0,1:T(8,128)(2,1)S(1)} %bitcast.72), channel_id=1, source_target_pairs={{0,1},{1,0},{2,3},{3,2},{4,5},{5,4},{6,7},{7,6},{8,9},{9,8},{10,11... | collective-permute-start | bytes 453896 | tf_op jit(solution)/shard_map/ppermute | solution.py:62
  20.2 13.0 %copy-start.46 = (f32[768]{0:T(1024)S(1)}, f32[768]{0:T(1024)}, u32[]{:S(2)}) copy-start(f32[768]{0:T(1024)} %param.22) | copy-start | bytes 9220
  36.3 20.4 %copy-start.5 = (bf16[197,768]{1,0:T(8,128)(2,1)}, bf16[197,768]{1,0:T(8,128)(2,1)S(1)}, u32[]{:S(2)}) copy-start(bf16[197,768]{1,0:T(8,128)(2,1)S(1)} %get-tuple-element.92.hidden2_ref) | copy-start | bytes 907780
  38.1 31.5 %all-to-all-start.1 = ((bf16[16,48,768]{2,1,0:T(8,128)(2,1)}), bf16[16,48,768]{2,1,0:T(8,128)(2,1)S(1)}, u32[]{:S(2)}, u32[]{:S(2)}) async-start(bf16[16,48,768]{2,1,0:T(8,128)(2,1)} %bitcast.21), calls=%async_computation.1 | async-start | bytes 2359296 | tf_op jit(solution)/shard_map/all_to_all | solution.py:513
  47.0 16.0 %collective-permute-start.2 = (bf16[768,384]{1,0:T(8,128)(2,1)}, bf16[768,384]{1,0:T(8,128)(2,1)}, u32[]{:S(2)}, u32[]{:S(2)}) collective-permute-start(bf16[768,384]{1,0:T(8,128)(2,1)} %bitcast.20), channel_id=1, source_target_pairs={{0,1},{1,0},{2,3},{3,2},{4,5},{5,4},{6,7},{7,6},{8,9},{9,8},{10,11... | collective-permute-start | bytes 1769480 | tf_op jit(solution)/shard_map/ppermute | solution.py:62
  85.4 32.3 %all-to-all-start.2 = ((bf16[16,48,768]{2,1,0:T(8,128)(2,1)}), bf16[16,48,768]{2,1,0:T(8,128)(2,1)S(1)}, u32[]{:S(2)}, u32[]{:S(2)}) async-start(bf16[16,48,768]{2,1,0:T(8,128)(2,1)} %bitcast.69), calls=%async_computation.2 | async-start | bytes 2359296 | tf_op jit(solution)/shard_map/all_to_all | solution.py:536
  92.8 24.9 %copy-start.2 = (f32[197,128]{1,0:T(8,128)}, f32[197,128]{1,0:T(8,128)S(1)}, u32[]{:S(2)}) copy-start(f32[197,128]{1,0:T(8,128)S(1)} %pad.31.facts_ref) | copy-start | bytes 302596
  118.4 10.6 %copy-start.1 = (bf16[208,768]{1,0:T(8,128)(2,1)}, bf16[208,768]{1,0:T(8,128)(2,1)S(1)}, u32[]{:S(2)}) copy-start(bf16[208,768]{1,0:T(8,128)(2,1)S(1)} %home_rows.1.home_ref) | copy-start | bytes 958468
  118.4 32.8 %all-to-all-start.3 = ((bf16[16,48,768]{2,1,0:T(8,128)(2,1)}), bf16[16,48,768]{2,1,0:T(8,128)(2,1)S(1)}, u32[]{:S(2)}, u32[]{:S(2)}) async-start(bf16[16,48,768]{2,1,0:T(8,128)(2,1)} %bitcast.68), calls=%async_computation.3 | async-start | bytes 2359296 | tf_op jit(solution)/shard_map/all_to_all | solution.py:592
  126.0 9.8 %collective-permute-start.3 = (bf16[208,768]{1,0:T(8,128)(2,1)S(1)}, bf16[208,768]{1,0:T(8,128)(2,1)S(1)}, u32[]{:S(2)}, u32[]{:S(2)}) collective-permute-start(bf16[208,768]{1,0:T(8,128)(2,1)S(1)} %home_rows.1.home_ref), channel_id=1, source_target_pairs={{0,1},{1,0},{2,3},{3,2},{4,5},{5,4},{6,7},{7,6},{8,9},{9,8},{10,11... | collective-permute-start | bytes 958472 | tf_op jit(solution)/shard_map/ppermute | solution.py:62
  151.1 4.2 %collective-permute-start.4 = (bf16[384,1664]{1,0:T(8,128)(2,1)}, bf16[384,1664]{1,0:T(8,128)(2,1)S(1)}, u32[]{:S(2)}, u32[]{:S(2)}) collective-permute-start(bf16[384,1664]{1,0:T(8,128)(2,1)} %get-tuple-element.101), channel_id=1, source_target_pairs={{0,2},{2,0},{4,6},{6,4},{8,10},{10,8},{12,14},{14,12},{16,18},{18,... | collective-permute-start | bytes 3833864 | tf_op jit(solution)/shard_map/ppermute | solution.py:66
  153.3 9.5 %collective-permute-start.12 = (bf16[197,768]{1,0:T(8,128)(2,1)}, bf16[197,768]{1,0:T(8,128)(2,1)S(1)}, u32[]{:S(2)}, u32[]{:S(2)}) collective-permute-start(bf16[197,768]{1,0:T(8,128)(2,1)} %get-tuple-element.112), channel_id=1, source_target_pairs={{0,1},{1,0},{2,3},{3,2},{4,5},{5,4},{6,7},{7,6},{8,9},{9,8},{10,11... | collective-permute-start | bytes 907784 | tf_op jit(solution)/shard_map/ppermute | solution.py:62
  157.6 10.7 %collective-permute-start.6 = (bf16[192,768]{1,0:T(8,128)(2,1)S(1)}, bf16[192,768]{1,0:T(8,128)(2,1)S(1)}, u32[]{:S(2)}, u32[]{:S(2)}) collective-permute-start(bf16[192,768]{1,0:T(8,128)(2,1)S(1)} %slice.287), channel_id=1, source_target_pairs={{0,8},{2,10},{4,12},{6,14},{8,0},{10,2},{12,4},{14,6},{16,24},{18,... | collective-permute-start | bytes 884744 | tf_op jit(solution)/shard_map/ppermute | solution.py:66
  163.3 9.6 %collective-permute-start.5 = (bf16[192,896]{1,0:T(8,128)(2,1)S(1)}, bf16[192,896]{1,0:T(8,128)(2,1)S(1)}, u32[]{:S(2)}, u32[]{:S(2)}) collective-permute-start(bf16[192,896]{1,0:T(8,128)(2,1)S(1)} %slice.286), channel_id=1, source_target_pairs={{0,4},{2,6},{4,0},{6,2},{8,12},{10,14},{12,8},{14,10},{16,20},{18,... | collective-permute-start | bytes 1032200 | tf_op jit(solution)/shard_map/ppermute | solution.py:66
  173.0 11.7 %collective-permute-start.8 = (bf16[96,768]{1,0:T(8,128)(2,1)S(1)}, bf16[96,768]{1,0:T(8,128)(2,1)S(1)}, u32[]{:S(2)}, u32[]{:S(2)}) collective-permute-start(bf16[96,768]{1,0:T(8,128)(2,1)S(1)} %slice.289), channel_id=1, source_target_pairs={{0,16},{2,18},{4,20},{6,22},{8,24},{10,26},{12,28},{14,30},{16,0},... | collective-permute-start | bytes 442376 | tf_op jit(solution)/shard_map/ppermute | solution.py:66
  178.7 8.0 %collective-permute-start.7 = (bf16[96,896]{1,0:T(8,128)(2,1)S(1)}, bf16[96,896]{1,0:T(8,128)(2,1)S(1)}, u32[]{:S(2)}, u32[]{:S(2)}) collective-permute-start(bf16[96,896]{1,0:T(8,128)(2,1)S(1)} %slice.288), channel_id=1, source_target_pairs={{0,8},{2,10},{4,12},{6,14},{8,0},{10,2},{12,4},{14,6},{16,24},{18,... | collective-permute-start | bytes 516104 | tf_op jit(solution)/shard_map/ppermute | solution.py:66
  186.7 4.4 %collective-permute-start.10 = (bf16[48,768]{1,0:T(8,128)(2,1)S(1)}, bf16[48,768]{1,0:T(8,128)(2,1)S(1)}, u32[]{:S(2)}, u32[]{:S(2)}) collective-permute-start(bf16[48,768]{1,0:T(8,128)(2,1)S(1)} %slice.291), channel_id=1, source_target_pairs={{0,4},{2,6},{4,0},{6,2},{8,12},{10,14},{12,8},{14,10},{16,20},{18,... | collective-permute-start | bytes 221192 | tf_op jit(solution)/shard_map/ppermute | solution.py:66
  186.8 8.4 %collective-permute-start.11 = (bf16[197,768]{1,0:T(8,128)(2,1)S(1)}, bf16[197,768]{1,0:T(8,128)(2,1)S(1)}, u32[]{:S(2)}, u32[]{:S(2)}) collective-permute-start(bf16[197,768]{1,0:T(8,128)(2,1)S(1)} %convolution_convert_fusion.3), channel_id=1, source_target_pairs={{0,1},{1,0},{2,3},{3,2},{4,5},{5,4},{6,7},{7,6},{8,9},{9,8},{10,11... | collective-permute-start | bytes 907784 | tf_op jit(solution)/shard_map/ppermute | solution.py:62
  188.4 6.4 %collective-permute-start.9 = (bf16[48,896]{1,0:T(8,128)(2,1)S(1)}, bf16[48,896]{1,0:T(8,128)(2,1)S(1)}, u32[]{:S(2)}, u32[]{:S(2)}) collective-permute-start(bf16[48,896]{1,0:T(8,128)(2,1)S(1)} %slice.290), channel_id=1, source_target_pairs={{0,16},{2,18},{4,20},{6,22},{8,24},{10,26},{12,28},{14,30},{16,0},... | collective-permute-start | bytes 258056 | tf_op jit(solution)/shard_map/ppermute | solution.py:66
  195.3 4.4 %collective-permute-start.14 = (bf16[48,768]{1,0:T(8,128)(2,1)S(1)}, bf16[48,768]{1,0:T(8,128)(2,1)S(1)}, u32[]{:S(2)}, u32[]{:S(2)}) collective-permute-start(bf16[48,768]{1,0:T(8,128)(2,1)S(1)} %convert_add_fusion.7), channel_id=1, source_target_pairs={{0,4},{2,6},{4,0},{6,2},{8,12},{10,14},{12,8},{14,10},{16,20},{18,... | collective-permute-start | bytes 221192 | tf_op jit(solution)/shard_map/ppermute | solution.py:66
  197.0 8.7 %collective-permute-start.13 = (bf16[64,896]{1,0:T(8,128)(2,1)S(1)}, bf16[64,896]{1,0:T(8,128)(2,1)S(1)}, u32[]{:S(2)}, u32[]{:S(2)}) collective-permute-start(bf16[64,896]{1,0:T(8,128)(2,1)S(1)} %pad_maximum_fusion.6), channel_id=1, source_target_pairs={{0,16},{2,18},{4,20},{6,22},{8,24},{10,26},{12,28},{14,30},{16,0},... | collective-permute-start | bytes 344072 | tf_op jit(solution)/shard_map/ppermute | solution.py:66
  205.8 10.8 %copy-start.12 = (f32[197,768]{1,0:T(8,128)S(1)}, f32[197,768]{1,0:T(8,128)}, u32[]{:S(2)}) copy-start(f32[197,768]{1,0:T(8,128)} %get-tuple-element.121) | copy-start | bytes 1815556
  205.8 6.2 %collective-permute-start.16 = (bf16[96,768]{1,0:T(8,128)(2,1)S(1)}, bf16[96,768]{1,0:T(8,128)(2,1)S(1)}, u32[]{:S(2)}, u32[]{:S(2)}) collective-permute-start(bf16[96,768]{1,0:T(8,128)(2,1)S(1)} %pad_maximum_fusion.5), channel_id=1, source_target_pairs={{0,16},{2,18},{4,20},{6,22},{8,24},{10,26},{12,28},{14,30},{16,0},... | collective-permute-start | bytes 442376 | tf_op jit(solution)/shard_map/ppermute | solution.py:66
  205.9 9.4 %collective-permute-start.15 = (bf16[112,896]{1,0:T(8,128)(2,1)S(1)}, bf16[112,896]{1,0:T(8,128)(2,1)S(1)}, u32[]{:S(2)}, u32[]{:S(2)}) collective-permute-start(bf16[112,896]{1,0:T(8,128)(2,1)S(1)} %pad_maximum_fusion.4), channel_id=1, source_target_pairs={{0,8},{2,10},{4,12},{6,14},{8,0},{10,2},{12,4},{14,6},{16,24},{18,... | collective-permute-start | bytes 602120 | tf_op jit(solution)/shard_map/ppermute | solution.py:66
  215.5 6.8 %collective-permute-start.18 = (bf16[192,768]{1,0:T(8,128)(2,1)S(1)}, bf16[192,768]{1,0:T(8,128)(2,1)S(1)}, u32[]{:S(2)}, u32[]{:S(2)}) collective-permute-start(bf16[192,768]{1,0:T(8,128)(2,1)S(1)} %pad_maximum_fusion.3), channel_id=1, source_target_pairs={{0,8},{2,10},{4,12},{6,14},{8,0},{10,2},{12,4},{14,6},{16,24},{18,... | collective-permute-start | bytes 884744 | tf_op jit(solution)/shard_map/ppermute | solution.py:66
  217.7 7.6 %collective-permute-start.17 = (bf16[208,896]{1,0:T(8,128)(2,1)S(1)}, bf16[208,896]{1,0:T(8,128)(2,1)S(1)}, u32[]{:S(2)}, u32[]{:S(2)}) collective-permute-start(bf16[208,896]{1,0:T(8,128)(2,1)S(1)} %pad_maximum_fusion.2), channel_id=1, source_target_pairs={{0,4},{2,6},{4,0},{6,2},{8,12},{10,14},{12,8},{14,10},{16,20},{18,... | collective-permute-start | bytes 1118216 | tf_op jit(solution)/shard_map/ppermute | solution.py:66
  225.3 2.3 collective-permute-start.19
  225.4 3.4 %collective-permute-start.20 = (bf16[384,768]{1,0:T(8,128)(2,1)S(1)}, bf16[384,768]{1,0:T(8,128)(2,1)S(1)}, u32[]{:S(2)}, u32[]{:S(2)}) collective-permute-start(bf16[384,768]{1,0:T(8,128)(2,1)S(1)} %pad_maximum_fusion.1.refs_2_), channel_id=1, source_target_pairs={{0,2},{2,0},{4,6},{6,4},{8,10},{10,8},{12,14},{14,12},{16,18},{18,... | collective-permute-start | bytes 1769480 | tf_op jit(solution)/shard_map/ppermute | solution.py:66
  (44 other events, 239.8 us)

commit v7 on v6

--- a/solution.py
+++ b/solution.py
@@ -471,23 +471,22 @@
     ]
     partner_map = tn(pick_low[0], partner[0]) + tn(pick_low[1], partner[1])
 
-    cot_half = half_of(plane, cotangent, 0)
-    cot_send = tn(onehot, cot_half).astype(BF16).reshape(experts, slots, half_dim)
-    note = jnp.pad(partner_map.astype(BF16), ((0, 0), (0, half_dim - slots)))[:, None, :]
+    cot_send = tn(onehot, cotangent).astype(BF16).reshape(experts, slots, feat_dim)
+    note = jnp.pad(partner_map.astype(BF16), ((0, 0), (0, feat_dim - slots)))[:, None, :]
     cot_send = jnp.where(slot_ids[None, :, None] == slots - 1, note, cot_send)
     cot_send = jnp.repeat(cot_send, group_size, axis=0)
     proj_other = swap(proj_weight)
     proj_full = in_order(plane, proj_weight, proj_other, 0)
 
     inputs, cot_send = lax.optimization_barrier((inputs, cot_send))
-    cot_mine = lax.all_to_all(cot_send, "dp", split_axis=0, concat_axis=0, tiled=True)
-    cot_mine = cot_mine.reshape(-1, half_dim)
+    cot_rows = lax.all_to_all(cot_send, "dp", split_axis=0, concat_axis=0, tiled=True)
     x_in = inputs.astype(F32)
     normed1, inverse1 = norm_parts(x_in)
     hidden1 = (normed1 * norm1_gain + norm1_bias).astype(BF16)
     projected = jnp.einsum("td,jde->jte", hidden1, qkv_weight, preferred_element_type=F32)
     bias_rows = jnp.stack([qv_bias[0], jnp.zeros_like(qv_bias[0]), qv_bias[1]])
     projected = (projected + bias_rows[:, None, :]).astype(BF16)
+    projected, proj_full = lax.optimization_barrier((projected, proj_full))
     heads_view = projected.reshape(3, images, SEQ, heads_here, HEAD)
     queries, key_vals, values_in = (heads_view[0], heads_view[1], heads_view[2])
     scores = (
@@ -501,15 +500,14 @@
     prob_low = (exp_scores / row_total).astype(BF16)
     attended = jnp.einsum("bhqk,bkhd->bqhd", prob_low, values_in, preferred_element_type=F32)
     attended = attended.reshape(tok_count, head_cols).astype(BF16)
-    attended_other, cot_mine = lax.optimization_barrier((swap(attended), cot_mine))
-    attended_all = in_order(plane, attended, attended_other, 1)
+    attended_all = in_order(plane, attended, swap(attended), 1)
+    attended_all, cot_rows = lax.optimization_barrier((attended_all, cot_rows))
     middle = x_in + nn(attended_all, proj_full) + proj_bias
     normed2, inverse2 = norm_parts(middle)
     hidden2 = (normed2 * norm2_gain + norm2_bias).astype(BF16)
 
     send = tn(onehot, hidden2).astype(BF16).reshape(experts, slots, feat_dim)
     send = jnp.repeat(send, group_size, axis=0)
-    cot_other = swap(cot_mine)
     arrived = lax.all_to_all(send, "dp", split_axis=0, concat_axis=0, tiled=True)
     arrived = arrived.reshape(-1, feat_dim)
 
@@ -524,18 +522,8 @@
     row_grad = [(gate_vals[k] * grad_out).astype(BF16) for k in range(2)]
     out_bias_grad = tn(pick_low[0], row_grad[0]) + tn(pick_low[1], row_grad[1])
 
-    note_rows = jnp.where(plane == 0, cot_mine, cot_other).reshape(sources, slots, half_dim)
-    other_expert = note_rows[:, slots - 1, :slots].reshape(-1, 1).astype(F32)
-    cot_rows = in_order(plane, cot_mine, cot_other, 1)
-    activ_low, act_low, grad_rows, row_send, out_send, in_bias_grad = (
-        expert_rows if sources * slots <= 1024 else expert_rows_plain
-    )(
-        own_expert, arrived, cot_rows, other_expert, router, in_weight, expert_in_bias, out_weight, capacity, slots
-    )
-    row_send = row_send.reshape(sources, slots, feat_dim)
-    row_back = lax.all_to_all(row_send, "dp", split_axis=0, concat_axis=0, tiled=True)
-    out_weight_grad = tn(activ_low, grad_rows)
-    in_weight_grad = tn(arrived, act_low)
+    other_expert = cot_rows[:, slots - 1, :slots].reshape(-1, 1).astype(F32)
+    cot_rows = cot_rows.reshape(-1, feat_dim)
     bits = [1 << i for i in range(sources.bit_length() - 1)]
     orders = [bits, bits[:1] + bits[2:] + bits[1:2]]
     chunk = feat_dim // sources
@@ -566,15 +554,26 @@
     facts = jnp.pad(facts, ((0, 0), (0, 16 - facts.shape[1])))
     facts = jnp.pad(jnp.concatenate([facts, bias_dot], axis=1), ((0, 0), (0, 112 - experts)))
     ready = (
-        out_weight_grad, in_weight_grad, in_bias_grad, mix_t, hidden1_t, facts, onehot,
-        out_bias_grad, normed2, hidden2, projected, attended, router, gate_map,
-    )
-    row_back, ready = lax.optimization_barrier((row_back, ready))
+        mix_t, hidden1_t, facts, onehot, out_bias_grad, normed2, hidden2, projected, attended, router, gate_map,
+        other_expert,
+    )
+    arrived, ready = lax.optimization_barrier((arrived, ready))
     (
-        out_weight_grad, in_weight_grad, in_bias_grad, mix_t, hidden1_t, facts, onehot,
-        out_bias_grad, normed2, hidden2, projected, attended, router, gate_map,
+        mix_t, hidden1_t, facts, onehot, out_bias_grad, normed2, hidden2, projected, attended, router, gate_map,
+        other_expert,
     ) = ready
-
+    activ_low, act_low, grad_rows, row_send, out_send, in_bias_grad = (
+        expert_rows if sources * slots <= 1024 else expert_rows_plain
+    )(
+        own_expert, arrived, cot_rows, other_expert, router, in_weight, expert_in_bias, out_weight, capacity, slots
+    )
+    row_send = row_send.reshape(sources, slots, feat_dim)
+    row_back = lax.all_to_all(row_send, "dp", split_axis=0, concat_axis=0, tiled=True)
+    out_weight_grad = tn(activ_low, grad_rows)
+    in_weight_grad = tn(arrived, act_low)
+    out_send, out_weight_grad, in_weight_grad = lax.optimization_barrier(
+        (out_send, out_weight_grad, in_weight_grad)
+    )
     def over_group(x):
         if group_size == 1:
             return x
@@ -586,7 +585,6 @@
         onehot,
         facts,
     )
-    out_send, row_home = lax.optimization_barrier((out_send, row_home))
     out_send = out_send.reshape(sources, slots, feat_dim)
     row_other = swap(row_home)
     out_back = lax.all_to_all(out_send, "dp", split_axis=0, concat_axis=0, tiled=True)
@@ -608,11 +606,7 @@
         qkv_weight,
         mix_t,
     )
-    hidden1_grad = hidden1_part.astype(F32) + swap(hidden1_part).astype(F32)
-    norm1_gain_grad = jnp.sum(hidden1_grad * normed1, axis=0)
-    norm1_bias_grad = jnp.sum(hidden1_grad, axis=0)
-    input_grad = middle_grad + norm_back(hidden1_grad * norm1_gain, normed1, inverse1)
-
+    hidden1_other = swap(hidden1_part)
     split = sent.shape[1] - 2 * head_cols
     sent, out_back = lax.optimization_barrier((sent, out_back))
     came = across(sent, bits[0], sources)
@@ -621,13 +615,17 @@
     out_home = nn(onehot, over_group(out_back).reshape(-1, feat_dim)).astype(BF16)
     for turn in range(1, len(bits)):
         totals, out_home = lax.optimization_barrier((totals, out_home))
+        if turn == len(bits) - 1:
+            out_other = swap(out_home)
         if turn == 2:
-            out_other = swap(out_home)
+            totals, hidden1_other = lax.optimization_barrier((totals, hidden1_other))
         cames = [send_half(t, order[turn], sources) for t, order in zip(totals, orders)]
         totals = [keep_half(t, c) for t, c in zip(totals, cames)]
-    totals, out_other = lax.optimization_barrier((totals, out_other))
-    out_home = out_home.astype(F32) + out_other.astype(F32)
-    output = (middle + (out_home + exact(gate_map, expert_out_bias))).astype(BF16)
+    hidden1_grad = hidden1_part.astype(F32) + hidden1_other.astype(F32)
+    norm1_gain_grad = jnp.sum(hidden1_grad * normed1, axis=0)
+    norm1_bias_grad = jnp.sum(hidden1_grad, axis=0)
+    input_grad = middle_grad + norm_back(hidden1_grad * norm1_gain, normed1, inverse1)
+    bias_home = exact(gate_map, expert_out_bias)
     mine = [t.astype(BF16) for t in totals]
     late = jnp.stack(
         [
@@ -650,9 +648,11 @@
     size = chunk
     for turn in range(len(bits) - 1, 0, -1):
         own, both = late_rows(late)
-        first, second = lax.optimization_barrier(
-            (jnp.concatenate([mine[0], both], axis=0), mine[1])
-        )
+        first, second = jnp.concatenate([mine[0], both], axis=0), mine[1]
+        if turn == 1:
+            first, second, out_other = lax.optimization_barrier((first, second, out_other))
+        else:
+            first, second = lax.optimization_barrier((first, second))
         came = across(first, orders[0][turn], sources)
         came_b = across(second, orders[1][turn], sources)
         late = late_sum(own, came[size:])
@@ -661,6 +661,8 @@
             jnp.concatenate([mine[1], came_b], axis=0),
         ]
         size = 2 * size
+    out_home = out_home.astype(F32) + out_other.astype(F32)
+    output = (middle + (out_home + bias_home)).astype(BF16)
     own, both = late_rows(late)
     first, second, input_grad, output = lax.optimization_barrier(
         (jnp.concatenate([mine[0], both], axis=0), mine[1], input_grad, output)

time: 233 us -> 236 us (1.013)
  waiting for transfers between devices: 88.2 us -> 106 us
  other arithmetic: 22.3 us -> 14 us
  local copies, waits for them, and re-layouts: 12.8 us -> 8.02 us
  starting transfers between devices: 53.7 us -> 50.6 us
    all_to_all x1, waiting for transfers between devices: 0.01 us -> 19.3 us  [local(): lax.all_to_all(send, 'dp', split_axis=0, concat_axis=0, tiled=True)]
    ppermute x6 -> x5, waiting for transfers between devices: 25.2 us -> 13.4 us  [swap(): return lax.ppermute(x, 'tensor', [(0, 1), (1, 0)])]
    all_to_all x1, waiting for transfers between devices: 0.01 us -> 10.6 us  [local(): lax.all_to_all(cot_send, 'dp', split_axis=0, concat_axis=0, tiled=True)]
    ppermute x6 -> x5, starting transfers between devices: 8.43 us -> 5.25 us  [swap(): return lax.ppermute(x, 'tensor', [(0, 1), (1, 0)])]
    select_n x3 -> x2, other arithmetic: 3.3 us -> 0.19 us  [in_order(): first = jnp.where(plane == 0, mine, other)]
    unnamed x107 -> x53, local copies, waits for them, and re-layouts: 3.56 us -> 0.91 us
  transfers between devices with their start and end apart: 25 -> 24, of which waited for: 21 -> 21; matrix products, arithmetic and copies ran while one was open for 20% -> 16% of each run, Pallas kernels for 5% -> 5%
where the time goes in v7:
time: 236 us; the launch traced here: 235 us
  waiting for transfers between devices  106 us (45%)
  starting transfers between devices  50.6 us (21%)
  Pallas kernels  29.5 us (12%)
  matrix products  25.5 us (11%)
  other arithmetic  14 us (6%)
  local copies, waits for them, and re-layouts  8.02 us (3%)
    ppermute x15, waiting for transfers between devices, across(): return lax.ppermute(x, 'dp', [(i, i ^ bit) for i in range(count)])  45.5 us
    all_to_all x1, waiting for transfers between devices, local(): lax.all_to_all(send, 'dp', split_axis=0, concat_axis=0, tiled=True)  19.3 us
    dot_general x12, matrix products, dot(): return lax.dot_general(a, b, (dims, ((), ())), preferred_element_type=out)  18.4 us
    ppermute x15, starting transfers between devices, across(): return lax.ppermute(x, 'dp', [(i, i ^ bit) for i in range(count)])  16.8 us
    pallas_call x1, Pallas kernels, expert_rows(): pl.pallas_call(lambda *refs: expert_kernel(capacity, slots, *refs), grid=...  14.7 us
    all_to_all x1, waiting for transfers between devices, local(): lax.all_to_all(row_send, 'dp', split_axis=0, concat_axis=0, tiled=True)  14.5 us
    ppermute x5, waiting for transfers between devices, swap(): return lax.ppermute(x, 'tensor', [(0, 1), (1, 0)])  13.4 us
    pallas_call x1, Pallas kernels, attention_grads(): pl.pallas_call(attention_grads_kernel, out_shape=(jax.ShapeDtypeStruct((f...  11.3 us
  transfers between devices with their start and end apart: 24, of which 21 were waited for; matrix products, arithmetic and copies ran while one was open for 16% of the time, Pallas kernels for 5%

profile of v7, /device:TPU:0, one launch (start us, length us, event | category | flops | bytes accessed | tf_op | source)
XLA Modules:
  0.0 235.0 jit_solution(884133711127435864)
XLA Ops:
  0.7 3.0 %collective-permute-start = (bf16[384,768]{1,0:T(8,128)(2,1)}, bf16[384,768]{1,0:T(8,128)(2,1)S(1)}, u32[]{:S(2)}, u32[]{:S(2)}) collective-permute-start(bf16[384,768]{1,0:T(8,128)(2,1)} %proj_ref.1), channel_id=1, source_target_pairs={{0,1},{1,0},{2,3},{3,2},{4,5},{5,4},{6,7},{7,6},{8,9},{9,8},{10,11... | collective-permute-start | bytes 1769480 | tf_op jit(solution)/shard_map/ppermute | solution.py:62
  8.8 6.1 %all-to-all-start = ((bf16[16,48,768]{2,1,0:T(8,128)(2,1)}), bf16[16,48,768]{2,1,0:T(8,128)(2,1)}, u32[]{:S(2)}, u32[]{:S(2)}) async-start(bf16[16,48,768]{2,1,0:T(8,128)(2,1)} %broadcast_select_fusion), calls=%async_computation | async-start | bytes 2359296 | tf_op jit(solution)/shard_map/all_to_all | solution.py:482
  17.2 2.2 fusion.3.projected_ref
  24.6 4.8 %collective-permute-done.1 = bf16[197,384]{0,1:T(8,128)(2,1)S(1)} collective-permute-done((bf16[197,384]{0,1:T(8,128)(2,1)S(1)}, bf16[197,384]{0,1:T(8,128)(2,1)S(1)}, u32[]{:S(2)}, u32[]{:S(2)}) %collective-permute-start.1) | collective-permute-done | bytes 151328 | tf_op jit(solution)/shard_map/ppermute | solution.py:62
  29.5 10.6 %all-to-all-done = bf16[16,48,768]{2,1,0:T(8,128)(2,1)} async-done(((bf16[16,48,768]{2,1,0:T(8,128)(2,1)}), bf16[16,48,768]{2,1,0:T(8,128)(2,1)}, u32[]{:S(2)}, u32[]{:S(2)}) %all-to-all-start) | async-done | bytes 1179680 | tf_op jit(solution)/shard_map/all_to_all | solution.py:482
  43.7 7.5 %all-to-all-start.1 = ((bf16[16,48,768]{2,1,0:T(8,128)(2,1)}), bf16[16,48,768]{2,1,0:T(8,128)(2,1)S(1)}, u32[]{:S(2)}, u32[]{:S(2)}) async-start(bf16[16,48,768]{2,1,0:T(8,128)(2,1)} %bitcast.20), calls=%async_computation.1 | async-start | bytes 2359296 | tf_op jit(solution)/shard_map/all_to_all | solution.py:511
  51.4 3.1 %convolution_convert_fusion.2.hidden_ref = bf16[2,768,197]{2,1,0:T(8,128)(2,1)} fusion(pred[1,768,768]{2,1,0:T(32,128)(4,1)} %copy-done.9, pred[1,768,768]{2,1,0:T(32,128)(4,1)} %copy-done.8, bf16[197,768]{1,0:T(8,128)(2,1)S(1)} %copy-done.3, f32[768]{0:T(1024)S(1)} %copy-done.23, f32[768]{0:T(1024)S(1)} %copy-done.17, f32[197]{0:T(256)S(1)} %add_rsqrt_fusion.1, ...), kind=kOutput, calls=%fused_computation.7 | convolution fusion | flops 467171328 | bytes 2095144 | tf_op jit(solution)/shard_map/jqd,td->jqt/dot_general | solution.py:543
  57.0 19.3 %all-to-all-done.1 = bf16[16,48,768]{2,1,0:T(8,128)(2,1)S(1)} async-done(((bf16[16,48,768]{2,1,0:T(8,128)(2,1)}), bf16[16,48,768]{2,1,0:T(8,128)(2,1)S(1)}, u32[]{:S(2)}, u32[]{:S(2)}) %all-to-all-start.1) | async-done | bytes 1179680 | tf_op jit(solution)/shard_map/all_to_all | solution.py:511
  78.2 14.7 %expert_rows.1 = (bf16[768,1536]{1,0:T(8,128)(2,1)}, bf16[768,1536]{1,0:T(8,128)(2,1)}, bf16[768,768]{1,0:T(8,128)(2,1)}, bf16[768,768]{1,0:T(8,128)(2,1)}, bf16[768,768]{1,0:T(8,128)(2,1)}, /*index=5*/f32[1,1536]{1,0:T(1,128)}) custom-call(s32[1]{0:T(128)} %bitcast.refs_0_, bf16[768,768]{1,0:T(8,128)(2,1)} %bitcast.65, bf16[768,768]{1,0:T(8,128)(2,1)} %bitcast.26.refs_2_, ...), custom_call_target="tpu_custom_call" | custom-call | flops 7247757312 | bytes 12582912 | tf_op jit(solution)/shard_map/expert_rows/pallas_call | solution.py:147
  92.9 7.5 %all-to-all-start.2 = ((bf16[16,48,768]{2,1,0:T(8,128)(2,1)}), bf16[16,48,768]{2,1,0:T(8,128)(2,1)S(1)}, u32[]{:S(2)}, u32[]{:S(2)}) async-start(bf16[16,48,768]{2,1,0:T(8,128)(2,1)} %bitcast.68), calls=%async_computation.2 | async-start | bytes 2359296 | tf_op jit(solution)/shard_map/all_to_all | solution.py:571
  100.5 6.4 %fusion.114 = f32[768,1536]{1,0:T(8,128)} fusion(bf16[768,768]{1,0:T(8,128)(2,1)} %bitcast.66, bf16[768,1536]{1,0:T(8,128)(2,1)} %get-tuple-element.102), kind=kOutput, calls=%fused_computation.235 | convolution fusion | flops 1811939328 | bytes 8257536 | tf_op jit(solution)/shard_map/dot_general | solution.py:36
  106.9 4.2 %fusion.113 = f32[1536,768]{1,0:T(8,128)} fusion(bf16[768,1536]{1,0:T(8,128)(2,1)S(1)} %copy-done.24, bf16[768,768]{1,0:T(8,128)(2,1)S(1)} %copy-done.25), kind=kOutput, calls=%fused_computation.234 | convolution fusion | flops 1811939328 | bytes 8257536 | tf_op jit(solution)/shard_map/dot_general | solution.py:36
  111.1 14.5 %all-to-all-done.2.back_ref = bf16[16,48,768]{2,1,0:T(8,128)(2,1)S(1)} async-done(((bf16[16,48,768]{2,1,0:T(8,128)(2,1)}), bf16[16,48,768]{2,1,0:T(8,128)(2,1)S(1)}, u32[]{:S(2)}, u32[]{:S(2)}) %all-to-all-start.2) | async-done | bytes 1179680 | tf_op jit(solution)/shard_map/all_to_all | solution.py:571
  125.6 7.5 %all-to-all-start.3 = ((bf16[16,48,768]{2,1,0:T(8,128)(2,1)}), bf16[16,48,768]{2,1,0:T(8,128)(2,1)}, u32[]{:S(2)}, u32[]{:S(2)}) async-start(bf16[16,48,768]{2,1,0:T(8,128)(2,1)} %bitcast.67), calls=%async_computation.3 | async-start | bytes 2359296 | tf_op jit(solution)/shard_map/all_to_all | solution.py:590
  135.7 7.9 %collective-permute-done.2.other_ref = bf16[208,768]{1,0:T(8,128)(2,1)S(1)} collective-permute-done((bf16[208,768]{1,0:T(8,128)(2,1)S(1)}, bf16[208,768]{1,0:T(8,128)(2,1)S(1)}, u32[]{:S(2)}, u32[]{:S(2)}) %collective-permute-start.2) | collective-permute-done | bytes 319520 | tf_op jit(solution)/shard_map/ppermute | solution.py:62
  144.4 11.3 %attention_grads.1 = (bf16[384,1664]{1,0:T(8,128)(2,1)}, f32[384,1664]{1,0:T(8,128)}, bf16[197,768]{1,0:T(8,128)(2,1)}, f32[1,1152]{1,0:T(1,128)}, f32[197,768]{1,0:T(8,128)}) custom-call(bf16[208,768]{1,0:T(8,128)(2,1)} %copy-done.1, bf16[208,768]{1,0:T(8,128)(2,1)} %copy-done.14, bf16[768,16]{1,0:T(8,128)(2,1)} %copy.76.refs_4_.router_ref, ...), custom_call_target="tpu_custom_call" | custom-call | flops 1429143552 | bytes 10485760 | tf_op jit(solution)/shard_map/attention_grads/pallas_call | solution.py:337
  155.7 2.6 %all-to-all-done.3 = bf16[16,48,768]{2,1,0:T(8,128)(2,1)} async-done(((bf16[16,48,768]{2,1,0:T(8,128)(2,1)}), bf16[16,48,768]{2,1,0:T(8,128)(2,1)}, u32[]{:S(2)}, u32[]{:S(2)}) %all-to-all-start.3) | async-done | bytes 1179680 | tf_op jit(solution)/shard_map/all_to_all | solution.py:590
  161.9 1.9 convert_add_fusion
  164.1 3.8 %collective-permute-start.5 = (bf16[192,768]{1,0:T(8,128)(2,1)S(1)}, bf16[192,768]{1,0:T(8,128)(2,1)S(1)}, u32[]{:S(2)}, u32[]{:S(2)}) collective-permute-start(bf16[192,768]{1,0:T(8,128)(2,1)S(1)} %slice.276), channel_id=1, source_target_pairs={{0,8},{2,10},{4,12},{6,14},{8,0},{10,2},{12,4},{14,6},{16,24},{18,... | collective-permute-start | bytes 884744 | tf_op jit(solution)/shard_map/ppermute | solution.py:66
  171.1 4.4 %collective-permute-done.5 = bf16[192,768]{1,0:T(8,128)(2,1)S(1)} collective-permute-done((bf16[192,768]{1,0:T(8,128)(2,1)S(1)}, bf16[192,768]{1,0:T(8,128)(2,1)S(1)}, u32[]{:S(2)}, u32[]{:S(2)}) %collective-permute-start.5) | collective-permute-done | bytes 294944 | tf_op jit(solution)/shard_map/ppermute | solution.py:66
  175.5 3.3 %collective-permute-done.4 = bf16[192,896]{1,0:T(8,128)(2,1)S(1)} collective-permute-done((bf16[192,896]{1,0:T(8,128)(2,1)S(1)}, bf16[192,896]{1,0:T(8,128)(2,1)S(1)}, u32[]{:S(2)}, u32[]{:S(2)}) %collective-permute-start.4) | collective-permute-done | bytes 344096 | tf_op jit(solution)/shard_map/ppermute | solution.py:66
  180.3 2.5 %collective-permute-start.8 = (bf16[96,768]{1,0:T(8,128)(2,1)S(1)}, bf16[96,768]{1,0:T(8,128)(2,1)S(1)}, u32[]{:S(2)}, u32[]{:S(2)}) collective-permute-start(bf16[96,768]{1,0:T(8,128)(2,1)S(1)} %slice.278), channel_id=1, source_target_pairs={{0,16},{2,18},{4,20},{6,22},{8,24},{10,26},{12,28},{14,30},{16,0},... | collective-permute-start | bytes 442376 | tf_op jit(solution)/shard_map/ppermute | solution.py:66
  182.9 4.7 %collective-permute-done.8 = bf16[96,768]{1,0:T(8,128)(2,1)S(1)} collective-permute-done((bf16[96,768]{1,0:T(8,128)(2,1)S(1)}, bf16[96,768]{1,0:T(8,128)(2,1)S(1)}, u32[]{:S(2)}, u32[]{:S(2)}) %collective-permute-start.8) | collective-permute-done | bytes 147488 | tf_op jit(solution)/shard_map/ppermute | solution.py:66
  188.4 2.3 collective-permute-start.10
  193.1 6.1 %collective-permute-done.9 = bf16[48,896]{1,0:T(8,128)(2,1)S(1)} collective-permute-done((bf16[48,896]{1,0:T(8,128)(2,1)S(1)}, bf16[48,896]{1,0:T(8,128)(2,1)S(1)}, u32[]{:S(2)}, u32[]{:S(2)}) %collective-permute-start.9) | collective-permute-done | bytes 86048 | tf_op jit(solution)/shard_map/ppermute | solution.py:66
  199.4 4.2 %collective-permute-done.12 = bf16[48,768]{1,0:T(8,128)(2,1)S(1)} collective-permute-done((bf16[48,768]{1,0:T(8,128)(2,1)S(1)}, bf16[48,768]{1,0:T(8,128)(2,1)S(1)}, u32[]{:S(2)}, u32[]{:S(2)}) %collective-permute-start.12) | collective-permute-done | bytes 73760 | tf_op jit(solution)/shard_map/ppermute | solution.py:66
  203.7 4.8 %collective-permute-done.11 = bf16[64,896]{1,0:T(8,128)(2,1)S(1)} collective-permute-done((bf16[64,896]{1,0:T(8,128)(2,1)S(1)}, bf16[64,896]{1,0:T(8,128)(2,1)S(1)}, u32[]{:S(2)}, u32[]{:S(2)}) %collective-permute-start.11) | collective-permute-done | bytes 114720 | tf_op jit(solution)/shard_map/ppermute | solution.py:66
  208.7 2.5 %collective-permute-start.14 = (bf16[96,768]{1,0:T(8,128)(2,1)S(1)}, bf16[96,768]{1,0:T(8,128)(2,1)S(1)}, u32[]{:S(2)}, u32[]{:S(2)}) collective-permute-start(bf16[96,768]{1,0:T(8,128)(2,1)S(1)} %pad_maximum_fusion.6), channel_id=1, source_target_pairs={{0,16},{2,18},{4,20},{6,22},{8,24},{10,26},{12,28},{14,30},{16,0},... | collective-permute-start | bytes 442376 | tf_op jit(solution)/shard_map/ppermute | solution.py:66
  211.6 4.5 %collective-permute-done.14 = bf16[96,768]{1,0:T(8,128)(2,1)S(1)} collective-permute-done((bf16[96,768]{1,0:T(8,128)(2,1)S(1)}, bf16[96,768]{1,0:T(8,128)(2,1)S(1)}, u32[]{:S(2)}, u32[]{:S(2)}) %collective-permute-start.14) | collective-permute-done | bytes 147488 | tf_op jit(solution)/shard_map/ppermute | solution.py:66
  221.3 3.7 %collective-permute-done.17 = bf16[192,768]{1,0:T(8,128)(2,1)S(1)} collective-permute-done((bf16[192,768]{1,0:T(8,128)(2,1)S(1)}, bf16[192,768]{1,0:T(8,128)(2,1)S(1)}, u32[]{:S(2)}, u32[]{:S(2)}) %collective-permute-start.17) | collective-permute-done | bytes 294944 | tf_op jit(solution)/shard_map/ppermute | solution.py:66
  225.0 2.9 %collective-permute-done.16 = bf16[208,896]{1,0:T(8,128)(2,1)S(1)} collective-permute-done((bf16[208,896]{1,0:T(8,128)(2,1)S(1)}, bf16[208,896]{1,0:T(8,128)(2,1)S(1)}, u32[]{:S(2)}, u32[]{:S(2)}) %collective-permute-start.16) | collective-permute-done | bytes 372768 | tf_op jit(solution)/shard_map/ppermute | solution.py:66
  231.5 2.8 %finish.1 = (f32[3,768,384]{2,1,0:T(8,128)}, f32[384,768]{1,0:T(8,128)}, f32[16,768]{1,0:T(8,128)}, f32[16,768]{1,0:T(8,128)}, f32[8,768]{1,0:T(8,128)S(1)}) custom-call(s32[1]{0:T(128)} %bitcast.refs_0_, bf16[400,896]{1,0:T(8,128)(2,1)S(1)} %fusion.61.refs_1_, bf16[384,768]{1,0:T(8,128)(2,1)S(1)} %pad_maximum_fusion.1.refs_2_, ...), custom_call_target="tpu_custom_call" | custom-call | tf_op jit(solution)/shard_map/finish/pallas_call | solution.py:391
  (194 shorter events, 45.6 us)
Async XLA Ops:
  0.6 14.5 %copy-start = (f32[16,768]{1,0:T(8,128)S(1)}, f32[16,768]{1,0:T(8,128)}, u32[]{:S(2)}) copy-start(f32[16,768]{1,0:T(8,128)} %param.29) | copy-start | bytes 147460
  0.7 18.8 %collective-permute-start = (bf16[384,768]{1,0:T(8,128)(2,1)}, bf16[384,768]{1,0:T(8,128)(2,1)S(1)}, u32[]{:S(2)}, u32[]{:S(2)}) collective-permute-start(bf16[384,768]{1,0:T(8,128)(2,1)} %proj_ref.1), channel_id=1, source_target_pairs={{0,1},{1,0},{2,3},{3,2},{4,5},{5,4},{6,7},{7,6},{8,9},{9,8},{10,11... | collective-permute-start | bytes 1769480 | tf_op jit(solution)/shard_map/ppermute | solution.py:62
  8.8 31.3 %all-to-all-start = ((bf16[16,48,768]{2,1,0:T(8,128)(2,1)}), bf16[16,48,768]{2,1,0:T(8,128)(2,1)}, u32[]{:S(2)}, u32[]{:S(2)}) async-start(bf16[16,48,768]{2,1,0:T(8,128)(2,1)} %broadcast_select_fusion), calls=%async_computation | async-start | bytes 2359296 | tf_op jit(solution)/shard_map/all_to_all | solution.py:482
  22.2 7.2 %collective-permute-start.1 = (bf16[197,384]{0,1:T(8,128)(2,1)S(1)}, bf16[197,384]{0,1:T(8,128)(2,1)S(1)}, u32[]{:S(2)}, u32[]{:S(2)}) collective-permute-start(bf16[197,384]{0,1:T(8,128)(2,1)S(1)} %bitcast.71), channel_id=1, source_target_pairs={{0,1},{1,0},{2,3},{3,2},{4,5},{5,4},{6,7},{7,6},{8,9},{9,8},{10,11... | collective-permute-start | bytes 453896 | tf_op jit(solution)/shard_map/ppermute | solution.py:62
  24.6 15.5 %copy-start.6 = (bf16[768,768]{1,0:T(8,128)(2,1)S(1)}, bf16[768,768]{1,0:T(8,128)(2,1)}, u32[]{:S(2)}) copy-start(bf16[768,768]{1,0:T(8,128)(2,1)} %pad_maximum_fusion) | copy-start | bytes 3538948
  24.6 15.6 %copy-start.19 = (f32[768]{0:T(1024)S(1)}, f32[768]{0:T(1024)}, u32[]{:S(2)}) copy-start(f32[768]{0:T(1024)} %param.22) | copy-start | bytes 9220
  29.5 11.4 %copy-start.18 = (f32[768]{0:T(1024)S(1)}, f32[768]{0:T(1024)}, u32[]{:S(2)}) copy-start(f32[768]{0:T(1024)} %param.23) | copy-start | bytes 9220
  29.5 11.4 %copy-start.20 = (f32[768]{0:T(1024)S(1)}, f32[768]{0:T(1024)}, u32[]{:S(2)}) copy-start(f32[768]{0:T(1024)} %param.24) | copy-start | bytes 9220
  41.9 12.5 %copy-start.5 = (bf16[197,768]{1,0:T(8,128)(2,1)}, bf16[197,768]{1,0:T(8,128)(2,1)S(1)}, u32[]{:S(2)}) copy-start(bf16[197,768]{1,0:T(8,128)(2,1)S(1)} %get-tuple-element.91.hidden2_ref) | copy-start | bytes 907780
  43.7 32.6 %all-to-all-start.1 = ((bf16[16,48,768]{2,1,0:T(8,128)(2,1)}), bf16[16,48,768]{2,1,0:T(8,128)(2,1)S(1)}, u32[]{:S(2)}, u32[]{:S(2)}) async-start(bf16[16,48,768]{2,1,0:T(8,128)(2,1)} %bitcast.20), calls=%async_computation.1 | async-start | bytes 2359296 | tf_op jit(solution)/shard_map/all_to_all | solution.py:511
  54.9 78.2 %copy-start.2 = (f32[197,128]{1,0:T(8,128)}, f32[197,128]{1,0:T(8,128)S(1)}, u32[]{:S(2)}) copy-start(f32[197,128]{1,0:T(8,128)S(1)} %pad.31.facts_ref) | copy-start | bytes 302596
  92.9 32.6 %all-to-all-start.2 = ((bf16[16,48,768]{2,1,0:T(8,128)(2,1)}), bf16[16,48,768]{2,1,0:T(8,128)(2,1)S(1)}, u32[]{:S(2)}, u32[]{:S(2)}) async-start(bf16[16,48,768]{2,1,0:T(8,128)(2,1)} %bitcast.68), calls=%async_computation.2 | async-start | bytes 2359296 | tf_op jit(solution)/shard_map/all_to_all | solution.py:571
  125.6 32.7 %all-to-all-start.3 = ((bf16[16,48,768]{2,1,0:T(8,128)(2,1)}), bf16[16,48,768]{2,1,0:T(8,128)(2,1)}, u32[]{:S(2)}, u32[]{:S(2)}) async-start(bf16[16,48,768]{2,1,0:T(8,128)(2,1)} %bitcast.67), calls=%async_computation.3 | async-start | bytes 2359296 | tf_op jit(solution)/shard_map/all_to_all | solution.py:590
  133.8 9.8 %collective-permute-start.2 = (bf16[208,768]{1,0:T(8,128)(2,1)S(1)}, bf16[208,768]{1,0:T(8,128)(2,1)S(1)}, u32[]{:S(2)}, u32[]{:S(2)}) collective-permute-start(bf16[208,768]{1,0:T(8,128)(2,1)S(1)} %home_rows.1.home_ref), channel_id=1, source_target_pairs={{0,1},{1,0},{2,3},{3,2},{4,5},{5,4},{6,7},{7,6},{8,9},{9,8},{10,11... | collective-permute-start | bytes 958472 | tf_op jit(solution)/shard_map/ppermute | solution.py:62
  158.3 3.6 %collective-permute-start.3 = (bf16[384,1664]{1,0:T(8,128)(2,1)}, bf16[384,1664]{1,0:T(8,128)(2,1)S(1)}, u32[]{:S(2)}, u32[]{:S(2)}) collective-permute-start(bf16[384,1664]{1,0:T(8,128)(2,1)} %get-tuple-element.104), channel_id=1, source_target_pairs={{0,2},{2,0},{4,6},{6,4},{8,10},{10,8},{12,14},{14,12},{16,18},{18,... | collective-permute-start | bytes 3833864 | tf_op jit(solution)/shard_map/ppermute | solution.py:66
  164.1 11.3 %collective-permute-start.5 = (bf16[192,768]{1,0:T(8,128)(2,1)S(1)}, bf16[192,768]{1,0:T(8,128)(2,1)S(1)}, u32[]{:S(2)}, u32[]{:S(2)}) collective-permute-start(bf16[192,768]{1,0:T(8,128)(2,1)S(1)} %slice.276), channel_id=1, source_target_pairs={{0,8},{2,10},{4,12},{6,14},{8,0},{10,2},{12,4},{14,6},{16,24},{18,... | collective-permute-start | bytes 884744 | tf_op jit(solution)/shard_map/ppermute | solution.py:66
  168.7 10.1 %collective-permute-start.4 = (bf16[192,896]{1,0:T(8,128)(2,1)S(1)}, bf16[192,896]{1,0:T(8,128)(2,1)S(1)}, u32[]{:S(2)}, u32[]{:S(2)}) collective-permute-start(bf16[192,896]{1,0:T(8,128)(2,1)S(1)} %slice.275), channel_id=1, source_target_pairs={{0,4},{2,6},{4,0},{6,2},{8,12},{10,14},{12,8},{14,10},{16,20},{18,... | collective-permute-start | bytes 1032200 | tf_op jit(solution)/shard_map/ppermute | solution.py:66
  170.5 9.0 %collective-permute-start.6 = (bf16[197,768]{1,0:T(8,128)(2,1)S(1)}, bf16[197,768]{1,0:T(8,128)(2,1)S(1)}, u32[]{:S(2)}, u32[]{:S(2)}) collective-permute-start(bf16[197,768]{1,0:T(8,128)(2,1)S(1)} %copy-done.12), channel_id=1, source_target_pairs={{0,1},{1,0},{2,3},{3,2},{4,5},{5,4},{6,7},{7,6},{8,9},{9,8},{10,11... | collective-permute-start | bytes 907784 | tf_op jit(solution)/shard_map/ppermute | solution.py:62
  179.9 8.4 %collective-permute-start.7 = (bf16[96,896]{1,0:T(8,128)(2,1)S(1)}, bf16[96,896]{1,0:T(8,128)(2,1)S(1)}, u32[]{:S(2)}, u32[]{:S(2)}) collective-permute-start(bf16[96,896]{1,0:T(8,128)(2,1)S(1)} %slice.277), channel_id=1, source_target_pairs={{0,8},{2,10},{4,12},{6,14},{8,0},{10,2},{12,4},{14,6},{16,24},{18,... | collective-permute-start | bytes 516104 | tf_op jit(solution)/shard_map/ppermute | solution.py:66
  180.3 7.3 %collective-permute-start.8 = (bf16[96,768]{1,0:T(8,128)(2,1)S(1)}, bf16[96,768]{1,0:T(8,128)(2,1)S(1)}, u32[]{:S(2)}, u32[]{:S(2)}) collective-permute-start(bf16[96,768]{1,0:T(8,128)(2,1)S(1)} %slice.278), channel_id=1, source_target_pairs={{0,16},{2,18},{4,20},{6,22},{8,24},{10,26},{12,28},{14,30},{16,0},... | collective-permute-start | bytes 442376 | tf_op jit(solution)/shard_map/ppermute | solution.py:66
  188.4 4.7 %collective-permute-start.10 = (bf16[48,768]{1,0:T(8,128)(2,1)S(1)}, bf16[48,768]{1,0:T(8,128)(2,1)S(1)}, u32[]{:S(2)}, u32[]{:S(2)}) collective-permute-start(bf16[48,768]{1,0:T(8,128)(2,1)S(1)} %slice.280), channel_id=1, source_target_pairs={{0,4},{2,6},{4,0},{6,2},{8,12},{10,14},{12,8},{14,10},{16,20},{18,... | collective-permute-start | bytes 221192 | tf_op jit(solution)/shard_map/ppermute | solution.py:66
  190.7 8.5 %collective-permute-start.9 = (bf16[48,896]{1,0:T(8,128)(2,1)S(1)}, bf16[48,896]{1,0:T(8,128)(2,1)S(1)}, u32[]{:S(2)}, u32[]{:S(2)}) collective-permute-start(bf16[48,896]{1,0:T(8,128)(2,1)S(1)} %slice.279), channel_id=1, source_target_pairs={{0,16},{2,18},{4,20},{6,22},{8,24},{10,26},{12,28},{14,30},{16,0},... | collective-permute-start | bytes 258056 | tf_op jit(solution)/shard_map/ppermute | solution.py:66
  199.2 4.4 %collective-permute-start.12 = (bf16[48,768]{1,0:T(8,128)(2,1)S(1)}, bf16[48,768]{1,0:T(8,128)(2,1)S(1)}, u32[]{:S(2)}, u32[]{:S(2)}) collective-permute-start(bf16[48,768]{1,0:T(8,128)(2,1)S(1)} %add_convert_fusion.3), channel_id=1, source_target_pairs={{0,4},{2,6},{4,0},{6,2},{8,12},{10,14},{12,8},{14,10},{16,20},{18,... | collective-permute-start | bytes 221192 | tf_op jit(solution)/shard_map/ppermute | solution.py:66
  199.3 9.1 %collective-permute-start.11 = (bf16[64,896]{1,0:T(8,128)(2,1)S(1)}, bf16[64,896]{1,0:T(8,128)(2,1)S(1)}, u32[]{:S(2)}, u32[]{:S(2)}) collective-permute-start(bf16[64,896]{1,0:T(8,128)(2,1)S(1)} %pad_maximum_fusion.7), channel_id=1, source_target_pairs={{0,16},{2,18},{4,20},{6,22},{8,24},{10,26},{12,28},{14,30},{16,0},... | collective-permute-start | bytes 344072 | tf_op jit(solution)/shard_map/ppermute | solution.py:66
  208.6 10.7 %copy-start.13 = (f32[197,768]{1,0:T(8,128)S(1)}, f32[197,768]{1,0:T(8,128)}, u32[]{:S(2)}) copy-start(f32[197,768]{1,0:T(8,128)} %get-tuple-element.126) | copy-start | bytes 1815556
  208.6 9.5 %collective-permute-start.13 = (bf16[112,896]{1,0:T(8,128)(2,1)S(1)}, bf16[112,896]{1,0:T(8,128)(2,1)S(1)}, u32[]{:S(2)}, u32[]{:S(2)}) collective-permute-start(bf16[112,896]{1,0:T(8,128)(2,1)S(1)} %pad_maximum_fusion.5), channel_id=1, source_target_pairs={{0,8},{2,10},{4,12},{6,14},{8,0},{10,2},{12,4},{14,6},{16,24},{18,... | collective-permute-start | bytes 602120 | tf_op jit(solution)/shard_map/ppermute | solution.py:66
  208.7 7.4 %collective-permute-start.14 = (bf16[96,768]{1,0:T(8,128)(2,1)S(1)}, bf16[96,768]{1,0:T(8,128)(2,1)S(1)}, u32[]{:S(2)}, u32[]{:S(2)}) collective-permute-start(bf16[96,768]{1,0:T(8,128)(2,1)S(1)} %pad_maximum_fusion.6), channel_id=1, source_target_pairs={{0,16},{2,18},{4,20},{6,22},{8,24},{10,26},{12,28},{14,30},{16,0},... | collective-permute-start | bytes 442376 | tf_op jit(solution)/shard_map/ppermute | solution.py:66
  211.1 7.1 %collective-permute-start.15 = (bf16[197,768]{1,0:T(8,128)(2,1)S(1)}, bf16[197,768]{1,0:T(8,128)(2,1)S(1)}, u32[]{:S(2)}, u32[]{:S(2)}) collective-permute-start(bf16[197,768]{1,0:T(8,128)(2,1)S(1)} %convolution_convert_fusion.3), channel_id=1, source_target_pairs={{0,1},{1,0},{2,3},{3,2},{4,5},{5,4},{6,7},{7,6},{8,9},{9,8},{10,11... | collective-permute-start | bytes 907784 | tf_op jit(solution)/shard_map/ppermute | solution.py:62
  218.2 6.8 %collective-permute-start.17 = (bf16[192,768]{1,0:T(8,128)(2,1)S(1)}, bf16[192,768]{1,0:T(8,128)(2,1)S(1)}, u32[]{:S(2)}, u32[]{:S(2)}) collective-permute-start(bf16[192,768]{1,0:T(8,128)(2,1)S(1)} %pad_maximum_fusion.4), channel_id=1, source_target_pairs={{0,8},{2,10},{4,12},{6,14},{8,0},{10,2},{12,4},{14,6},{16,24},{18,... | collective-permute-start | bytes 884744 | tf_op jit(solution)/shard_map/ppermute | solution.py:66
  220.4 7.6 %collective-permute-start.16 = (bf16[208,896]{1,0:T(8,128)(2,1)S(1)}, bf16[208,896]{1,0:T(8,128)(2,1)S(1)}, u32[]{:S(2)}, u32[]{:S(2)}) collective-permute-start(bf16[208,896]{1,0:T(8,128)(2,1)S(1)} %pad_maximum_fusion.3), channel_id=1, source_target_pairs={{0,4},{2,6},{4,0},{6,2},{8,12},{10,14},{12,8},{14,10},{16,20},{18,... | collective-permute-start | bytes 1118216 | tf_op jit(solution)/shard_map/ppermute | solution.py:66
  228.1 2.3 collective-permute-start.18
  228.1 3.4 %collective-permute-start.19 = (bf16[384,768]{1,0:T(8,128)(2,1)S(1)}, bf16[384,768]{1,0:T(8,128)(2,1)S(1)}, u32[]{:S(2)}, u32[]{:S(2)}) collective-permute-start(bf16[384,768]{1,0:T(8,128)(2,1)S(1)} %pad_maximum_fusion.1.refs_2_), channel_id=1, source_target_pairs={{0,2},{2,0},{4,6},{6,4},{8,10},{10,8},{12,14},{14,12},{16,18},{18,... | collective-permute-start | bytes 1769480 | tf_op jit(solution)/shard_map/ppermute | solution.py:66
  (18 other events, 80.2 us)

commit v8 on v7

--- a/solution.py
+++ b/solution.py
@@ -81,10 +81,6 @@
 def keep_half(total, came):
     middle = total.shape[0] // 2
     return total[:middle] + came.astype(F32)
-
-
-def send_half(total, bit, count):
-    return across(total[total.shape[0] // 2 :].astype(BF16), bit, count)
 
 
 def expert_kernel(
@@ -471,15 +467,16 @@
     ]
     partner_map = tn(pick_low[0], partner[0]) + tn(pick_low[1], partner[1])
 
-    cot_send = tn(onehot, cotangent).astype(BF16).reshape(experts, slots, feat_dim)
-    note = jnp.pad(partner_map.astype(BF16), ((0, 0), (0, feat_dim - slots)))[:, None, :]
+    cot_half = half_of(plane, cotangent, 0)
+    cot_send = tn(onehot, cot_half).astype(BF16).reshape(experts, slots, half_dim)
+    note = jnp.pad(partner_map.astype(BF16), ((0, 0), (0, half_dim - slots)))[:, None, :]
     cot_send = jnp.where(slot_ids[None, :, None] == slots - 1, note, cot_send)
     cot_send = jnp.repeat(cot_send, group_size, axis=0)
     proj_other = swap(proj_weight)
     proj_full = in_order(plane, proj_weight, proj_other, 0)
 
     inputs, cot_send = lax.optimization_barrier((inputs, cot_send))
-    cot_rows = lax.all_to_all(cot_send, "dp", split_axis=0, concat_axis=0, tiled=True)
+    cot_mine = lax.all_to_all(cot_send, "dp", split_axis=0, concat_axis=0, tiled=True)
     x_in = inputs.astype(F32)
     normed1, inverse1 = norm_parts(x_in)
     hidden1 = (normed1 * norm1_gain + norm1_bias).astype(BF16)
@@ -501,7 +498,8 @@
     attended = jnp.einsum("bhqk,bkhd->bqhd", prob_low, values_in, preferred_element_type=F32)
     attended = attended.reshape(tok_count, head_cols).astype(BF16)
     attended_all = in_order(plane, attended, swap(attended), 1)
-    attended_all, cot_rows = lax.optimization_barrier((attended_all, cot_rows))
+    attended_all, cot_mine = lax.optimization_barrier((attended_all, cot_mine))
+    cot_other = swap(cot_mine)
     middle = x_in + nn(attended_all, proj_full) + proj_bias
     normed2, inverse2 = norm_parts(middle)
     hidden2 = (normed2 * norm2_gain + norm2_bias).astype(BF16)
@@ -522,8 +520,8 @@
     row_grad = [(gate_vals[k] * grad_out).astype(BF16) for k in range(2)]
     out_bias_grad = tn(pick_low[0], row_grad[0]) + tn(pick_low[1], row_grad[1])
 
-    other_expert = cot_rows[:, slots - 1, :slots].reshape(-1, 1).astype(F32)
-    cot_rows = cot_rows.reshape(-1, feat_dim)
+    other_expert = cot_mine[:, slots - 1, :slots].reshape(-1, 1).astype(F32)
+    cot_rows = in_order(plane, cot_mine, cot_other, 2).reshape(-1, feat_dim)
     bits = [1 << i for i in range(sources.bit_length() - 1)]
     orders = [bits, bits[:1] + bits[2:] + bits[1:2]]
     chunk = feat_dim // sources
@@ -554,13 +552,13 @@
     facts = jnp.pad(facts, ((0, 0), (0, 16 - facts.shape[1])))
     facts = jnp.pad(jnp.concatenate([facts, bias_dot], axis=1), ((0, 0), (0, 112 - experts)))
     ready = (
-        mix_t, hidden1_t, facts, onehot, out_bias_grad, normed2, hidden2, projected, attended, router, gate_map,
-        other_expert,
+        mix_t, hidden1_t, facts, onehot, out_bias_grad, normed2, hidden2, projected, attended, gate_map,
+        cot_rows,
     )
     arrived, ready = lax.optimization_barrier((arrived, ready))
     (
-        mix_t, hidden1_t, facts, onehot, out_bias_grad, normed2, hidden2, projected, attended, router, gate_map,
-        other_expert,
+        mix_t, hidden1_t, facts, onehot, out_bias_grad, normed2, hidden2, projected, attended, gate_map,
+        cot_rows,
     ) = ready
     activ_low, act_low, grad_rows, row_send, out_send, in_bias_grad = (
         expert_rows if sources * slots <= 1024 else expert_rows_plain
@@ -619,7 +617,8 @@
             out_other = swap(out_home)
         if turn == 2:
             totals, hidden1_other = lax.optimization_barrier((totals, hidden1_other))
-        cames = [send_half(t, order[turn], sources) for t, order in zip(totals, orders)]
+        sends = lax.optimization_barrier([t[t.shape[0] // 2 :].astype(BF16) for t in totals])
+        cames = [across(t, order[turn], sources) for t, order in zip(sends, orders)]
         totals = [keep_half(t, c) for t, c in zip(totals, cames)]
     hidden1_grad = hidden1_part.astype(F32) + hidden1_other.astype(F32)
     norm1_gain_grad = jnp.sum(hidden1_grad * normed1, axis=0)

time: 236 us -> 221 us (0.936)
  waiting for transfers between devices: 106 us -> 83.6 us
  starting transfers between devices: 50.6 us -> 57.2 us
  matrix products: 25.5 us -> 21.5 us
  other arithmetic: 14 us -> 16.8 us
    all_to_all x1, waiting for transfers between devices: 19.3 us -> 2.22 us  [local(): lax.all_to_all(send, 'dp', split_axis=0, concat_axis=0, tiled=True)]
    ppermute x5 -> x6, waiting for transfers between devices: 13.4 us -> 29.8 us  [swap(): return lax.ppermute(x, 'tensor', [(0, 1), (1, 0)])]
    ppermute x15, waiting for transfers between devices: 45.5 us -> 34 us  [across(): return lax.ppermute(x, 'dp', [(i, i ^ bit) for i in range(count)])]
    all_to_all x1, waiting for transfers between devices: 10.6 us -> 0.46 us  [local(): lax.all_to_all(cot_send, 'dp', split_axis=0, concat_axis=0, tiled=True)]
    ppermute x15, starting transfers between devices: 16.8 us -> 25 us  [across(): return lax.ppermute(x, 'dp', [(i, i ^ bit) for i in range(count)])]
    unnamed x53 -> x58, local copies, waits for them, and re-layouts: 0.91 us -> 3.45 us
    ppermute x5 -> x6, starting transfers between devices: 5.25 us -> 5.87 us  [swap(): return lax.ppermute(x, 'tensor', [(0, 1), (1, 0)])]
  transfers between devices with their start and end apart: 24 -> 25, of which waited for: 21 -> 22; matrix products, arithmetic and copies ran while one was open for 16% -> 18% of each run, Pallas kernels for 5% -> 5%
where the time goes in v8:
time: 221 us; the launch traced here: 220 us
  waiting for transfers between devices  83.6 us (38%)
  starting transfers between devices  57.2 us (26%)
  Pallas kernels  29.5 us (13%)
  matrix products  21.5 us (10%)
  other arithmetic  16.8 us (8%)
  local copies, waits for them, and re-layouts  9.74 us (4%)
    ppermute x15, waiting for transfers between devices, across(): return lax.ppermute(x, 'dp', [(i, i ^ bit) for i in range(count)])  34 us
    ppermute x6, waiting for transfers between devices, swap(): return lax.ppermute(x, 'tensor', [(0, 1), (1, 0)])  29.8 us
    ppermute x15, starting transfers between devices, across(): return lax.ppermute(x, 'dp', [(i, i ^ bit) for i in range(count)])  25 us
    dot_general x12, matrix products, dot(): return lax.dot_general(a, b, (dims, ((), ())), preferred_element_type=out)  17.3 us
    pallas_call x1, Pallas kernels, expert_rows(): pl.pallas_call(lambda *refs: expert_kernel(capacity, slots, *refs), grid=...  14.7 us
    all_to_all x1, waiting for transfers between devices, local(): lax.all_to_all(row_send, 'dp', split_axis=0, concat_axis=0, tiled=True)  14.5 us
    pallas_call x1, Pallas kernels, attention_grads(): pl.pallas_call(attention_grads_kernel, out_shape=(jax.ShapeDtypeStruct((f...  11.3 us
    all_to_all x1, starting transfers between devices, local(): lax.all_to_all(out_send, 'dp', split_axis=0, concat_axis=0, tiled=True)  7.54 us
  transfers between devices with their start and end apart: 25, of which 22 were waited for; matrix products, arithmetic and copies ran while one was open for 18% of the time, Pallas kernels for 5%

profile of v8, /device:TPU:0, one launch (start us, length us, event | category | flops | bytes accessed | tf_op | source)
XLA Modules:
  0.0 219.8 jit_solution(11838604110173101899)
XLA Ops:
  0.7 3.0 %collective-permute-start = (bf16[384,768]{1,0:T(8,128)(2,1)}, bf16[384,768]{1,0:T(8,128)(2,1)S(1)}, u32[]{:S(2)}, u32[]{:S(2)}) collective-permute-start(bf16[384,768]{1,0:T(8,128)(2,1)} %proj_ref.1), channel_id=1, source_target_pairs={{0,1},{1,0},{2,3},{3,2},{4,5},{5,4},{6,7},{7,6},{8,9},{9,8},{10,11... | collective-permute-start | bytes 1769480 | tf_op jit(solution)/shard_map/ppermute | solution.py:62
  7.3 6.0 %all-to-all-start = ((bf16[16,48,384]{2,1,0:T(8,128)(2,1)}), bf16[16,48,384]{2,1,0:T(8,128)(2,1)}, u32[]{:S(2)}, u32[]{:S(2)}) async-start(bf16[16,48,384]{2,1,0:T(8,128)(2,1)} %broadcast_select_fusion), calls=%async_computation | async-start | bytes 1179648 | tf_op jit(solution)/shard_map/all_to_all | solution.py:479
  21.9 6.5 %collective-permute-done.1 = bf16[197,384]{0,1:T(8,128)(2,1)S(1)} collective-permute-done((bf16[197,384]{0,1:T(8,128)(2,1)S(1)}, bf16[197,384]{0,1:T(8,128)(2,1)S(1)}, u32[]{:S(2)}, u32[]{:S(2)}) %collective-permute-start.1) | collective-permute-done | bytes 151328 | tf_op jit(solution)/shard_map/ppermute | solution.py:62
  32.5 5.3 %all-to-all-start.1 = ((bf16[16,48,768]{2,1,0:T(8,128)(2,1)}), bf16[16,48,768]{2,1,0:T(8,128)(2,1)S(1)}, u32[]{:S(2)}, u32[]{:S(2)}) async-start(bf16[16,48,768]{2,1,0:T(8,128)(2,1)} %bitcast.20), calls=%async_computation.1 | async-start | bytes 2359296 | tf_op jit(solution)/shard_map/all_to_all | solution.py:509
  37.9 3.1 %fusion.mix_ref = bf16[2,768,768]{2,1,0:T(8,128)(2,1)} fusion(pred[1,768,768]{2,1,0:T(32,128)(4,1)} %copy-done.9, pred[1,768,768]{2,1,0:T(32,128)(4,1)} %copy-done.8), kind=kLoop, calls=%fused_computation.7 | loop fusion | flops 2359296 | bytes 3538944 | tf_op jit(solution)/shard_map/stack | solution.py:540
  45.7 12.6 %collective-permute-done.2 = bf16[16,48,384]{2,1,0:T(8,128)(2,1)} collective-permute-done((bf16[16,48,384]{2,1,0:T(8,128)(2,1)}, bf16[16,48,384]{2,1,0:T(8,128)(2,1)}, u32[]{:S(2)}, u32[]{:S(2)}) %collective-permute-start.2) | collective-permute-done | bytes 589856 | tf_op jit(solution)/shard_map/ppermute | solution.py:62
  60.8 2.2 %all-to-all-done.1 = bf16[16,48,768]{2,1,0:T(8,128)(2,1)S(1)} async-done(((bf16[16,48,768]{2,1,0:T(8,128)(2,1)}), bf16[16,48,768]{2,1,0:T(8,128)(2,1)S(1)}, u32[]{:S(2)}, u32[]{:S(2)}) %all-to-all-start.1) | async-done | bytes 1179680 | tf_op jit(solution)/shard_map/all_to_all | solution.py:509
  64.0 14.7 %expert_rows.1 = (bf16[768,1536]{1,0:T(8,128)(2,1)}, bf16[768,1536]{1,0:T(8,128)(2,1)}, bf16[768,768]{1,0:T(8,128)(2,1)}, bf16[768,768]{1,0:T(8,128)(2,1)}, bf16[768,768]{1,0:T(8,128)(2,1)}, /*index=5*/f32[1,1536]{1,0:T(1,128)}) custom-call(s32[1]{0:T(128)} %bitcast.refs_0_, bf16[768,768]{1,0:T(8,128)(2,1)} %bitcast.63, bf16[768,768]{1,0:T(8,128)(2,1)} %bitcast.66, ...), custom_call_target="tpu_custom_call" | custom-call | flops 7247757312 | bytes 12582912 | tf_op jit(solution)/shard_map/expert_rows/pallas_call | solution.py:143
  78.7 7.5 %all-to-all-start.2 = ((bf16[16,48,768]{2,1,0:T(8,128)(2,1)}), bf16[16,48,768]{2,1,0:T(8,128)(2,1)S(1)}, u32[]{:S(2)}, u32[]{:S(2)}) async-start(bf16[16,48,768]{2,1,0:T(8,128)(2,1)} %bitcast.67), calls=%async_computation.2 | async-start | bytes 2359296 | tf_op jit(solution)/shard_map/all_to_all | solution.py:569
  86.2 6.4 %fusion.115 = f32[768,1536]{1,0:T(8,128)} fusion(bf16[768,768]{1,0:T(8,128)(2,1)} %bitcast.64, bf16[768,1536]{1,0:T(8,128)(2,1)} %get-tuple-element.106), kind=kOutput, calls=%fused_computation.239 | convolution fusion | flops 1811939328 | bytes 8257536 | tf_op jit(solution)/shard_map/dot_general | solution.py:36
  92.6 4.2 %fusion.114 = f32[1536,768]{1,0:T(8,128)} fusion(bf16[768,1536]{1,0:T(8,128)(2,1)S(1)} %copy-done.25, bf16[768,768]{1,0:T(8,128)(2,1)S(1)} %copy-done.26), kind=kOutput, calls=%fused_computation.238 | convolution fusion | flops 1811939328 | bytes 8257536 | tf_op jit(solution)/shard_map/dot_general | solution.py:36
  96.8 14.5 %all-to-all-done.2.back_ref = bf16[16,48,768]{2,1,0:T(8,128)(2,1)S(1)} async-done(((bf16[16,48,768]{2,1,0:T(8,128)(2,1)}), bf16[16,48,768]{2,1,0:T(8,128)(2,1)S(1)}, u32[]{:S(2)}, u32[]{:S(2)}) %all-to-all-start.2) | async-done | bytes 1179680 | tf_op jit(solution)/shard_map/all_to_all | solution.py:569
  111.3 7.5 %all-to-all-start.3 = ((bf16[16,48,768]{2,1,0:T(8,128)(2,1)}), bf16[16,48,768]{2,1,0:T(8,128)(2,1)}, u32[]{:S(2)}, u32[]{:S(2)}) async-start(bf16[16,48,768]{2,1,0:T(8,128)(2,1)} %bitcast.65), calls=%async_computation.3 | async-start | bytes 2359296 | tf_op jit(solution)/shard_map/all_to_all | solution.py:588
  121.4 7.9 %collective-permute-done.3.other_ref = bf16[208,768]{1,0:T(8,128)(2,1)S(1)} collective-permute-done((bf16[208,768]{1,0:T(8,128)(2,1)S(1)}, bf16[208,768]{1,0:T(8,128)(2,1)S(1)}, u32[]{:S(2)}, u32[]{:S(2)}) %collective-permute-start.3) | collective-permute-done | bytes 319520 | tf_op jit(solution)/shard_map/ppermute | solution.py:62
  130.1 11.3 %attention_grads.1 = (bf16[384,1664]{1,0:T(8,128)(2,1)}, f32[384,1664]{1,0:T(8,128)}, bf16[197,768]{1,0:T(8,128)(2,1)}, f32[1,1152]{1,0:T(1,128)}, f32[197,768]{1,0:T(8,128)}) custom-call(bf16[208,768]{1,0:T(8,128)(2,1)} %copy-done.1, bf16[208,768]{1,0:T(8,128)(2,1)} %copy-done.15, bf16[768,16]{1,0:T(8,128)(2,1)} %copy.80.refs_4_.router_ref, ...), custom_call_target="tpu_custom_call" | custom-call | flops 1429143552 | bytes 10485760 | tf_op jit(solution)/shard_map/attention_grads/pallas_call | solution.py:333
  141.4 2.6 %all-to-all-done.3 = bf16[16,48,768]{2,1,0:T(8,128)(2,1)} async-done(((bf16[16,48,768]{2,1,0:T(8,128)(2,1)}), bf16[16,48,768]{2,1,0:T(8,128)(2,1)}, u32[]{:S(2)}, u32[]{:S(2)}) %all-to-all-start.3) | async-done | bytes 1179680 | tf_op jit(solution)/shard_map/all_to_all | solution.py:588
  147.6 2.0 convert_add_fusion
  149.9 3.8 %collective-permute-start.6 = (bf16[192,768]{1,0:T(8,128)(2,1)S(1)}, bf16[192,768]{1,0:T(8,128)(2,1)S(1)}, u32[]{:S(2)}, u32[]{:S(2)}) collective-permute-start(bf16[192,768]{1,0:T(8,128)(2,1)S(1)} %slice.284), channel_id=1, source_target_pairs={{0,8},{2,10},{4,12},{6,14},{8,0},{10,2},{12,4},{14,6},{16,24},{18,... | collective-permute-start | bytes 884744 | tf_op jit(solution)/shard_map/ppermute | solution.py:66
  156.8 4.4 %collective-permute-done.6 = bf16[192,768]{1,0:T(8,128)(2,1)S(1)} collective-permute-done((bf16[192,768]{1,0:T(8,128)(2,1)S(1)}, bf16[192,768]{1,0:T(8,128)(2,1)S(1)}, u32[]{:S(2)}, u32[]{:S(2)}) %collective-permute-start.6) | collective-permute-done | bytes 294944 | tf_op jit(solution)/shard_map/ppermute | solution.py:66
  161.3 3.3 %collective-permute-done.5 = bf16[192,896]{1,0:T(8,128)(2,1)S(1)} collective-permute-done((bf16[192,896]{1,0:T(8,128)(2,1)S(1)}, bf16[192,896]{1,0:T(8,128)(2,1)S(1)}, u32[]{:S(2)}, u32[]{:S(2)}) %collective-permute-start.5) | collective-permute-done | bytes 344096 | tf_op jit(solution)/shard_map/ppermute | solution.py:66
  166.1 2.4 %collective-permute-start.9 = (bf16[96,768]{1,0:T(8,128)(2,1)S(1)}, bf16[96,768]{1,0:T(8,128)(2,1)S(1)}, u32[]{:S(2)}, u32[]{:S(2)}) collective-permute-start(bf16[96,768]{1,0:T(8,128)(2,1)S(1)} %slice.286), channel_id=1, source_target_pairs={{0,16},{2,18},{4,20},{6,22},{8,24},{10,26},{12,28},{14,30},{16,0},... | collective-permute-start | bytes 442376 | tf_op jit(solution)/shard_map/ppermute | solution.py:66
  168.6 4.8 %collective-permute-done.9 = bf16[96,768]{1,0:T(8,128)(2,1)S(1)} collective-permute-done((bf16[96,768]{1,0:T(8,128)(2,1)S(1)}, bf16[96,768]{1,0:T(8,128)(2,1)S(1)}, u32[]{:S(2)}, u32[]{:S(2)}) %collective-permute-start.9) | collective-permute-done | bytes 147488 | tf_op jit(solution)/shard_map/ppermute | solution.py:66
  178.6 2.4 %collective-permute-done.10 = bf16[48,896]{1,0:T(8,128)(2,1)S(1)} collective-permute-done((bf16[48,896]{1,0:T(8,128)(2,1)S(1)}, bf16[48,896]{1,0:T(8,128)(2,1)S(1)}, u32[]{:S(2)}, u32[]{:S(2)}) %collective-permute-start.10) | collective-permute-done | bytes 86048 | tf_op jit(solution)/shard_map/ppermute | solution.py:66
  183.5 2.0 collective-permute-done.13
  185.5 2.0 collective-permute-done.12
  187.6 5.0 %collective-permute-start.14 = (bf16[112,896]{1,0:T(8,128)(2,1)S(1)}, bf16[112,896]{1,0:T(8,128)(2,1)S(1)}, u32[]{:S(2)}, u32[]{:S(2)}) collective-permute-start(bf16[112,896]{1,0:T(8,128)(2,1)S(1)} %pad_maximum_fusion.6), channel_id=1, source_target_pairs={{0,8},{2,10},{4,12},{6,14},{8,0},{10,2},{12,4},{14,6},{16,24},{18,... | collective-permute-start | bytes 602120 | tf_op jit(solution)/shard_map/ppermute | solution.py:66
  192.6 3.4 %collective-permute-start.15 = (bf16[96,768]{1,0:T(8,128)(2,1)S(1)}, bf16[96,768]{1,0:T(8,128)(2,1)S(1)}, u32[]{:S(2)}, u32[]{:S(2)}) collective-permute-start(bf16[96,768]{1,0:T(8,128)(2,1)S(1)} %pad_maximum_fusion.7), channel_id=1, source_target_pairs={{0,16},{2,18},{4,20},{6,22},{8,24},{10,26},{12,28},{14,30},{16,0},... | collective-permute-start | bytes 442376 | tf_op jit(solution)/shard_map/ppermute | solution.py:66
  196.5 3.9 %collective-permute-done.15 = bf16[96,768]{1,0:T(8,128)(2,1)S(1)} collective-permute-done((bf16[96,768]{1,0:T(8,128)(2,1)S(1)}, bf16[96,768]{1,0:T(8,128)(2,1)S(1)}, u32[]{:S(2)}, u32[]{:S(2)}) %collective-permute-start.15) | collective-permute-done | bytes 147488 | tf_op jit(solution)/shard_map/ppermute | solution.py:66
  200.6 2.3 %collective-permute-done.16 = bf16[197,768]{1,0:T(8,128)(2,1)S(1)} collective-permute-done((bf16[197,768]{1,0:T(8,128)(2,1)S(1)}, bf16[197,768]{1,0:T(8,128)(2,1)S(1)}, u32[]{:S(2)}, u32[]{:S(2)}) %collective-permute-start.16) | collective-permute-done | bytes 302624 | tf_op jit(solution)/shard_map/ppermute | solution.py:62
  206.2 3.3 %collective-permute-done.18 = bf16[192,768]{1,0:T(8,128)(2,1)S(1)} collective-permute-done((bf16[192,768]{1,0:T(8,128)(2,1)S(1)}, bf16[192,768]{1,0:T(8,128)(2,1)S(1)}, u32[]{:S(2)}, u32[]{:S(2)}) %collective-permute-start.18) | collective-permute-done | bytes 294944 | tf_op jit(solution)/shard_map/ppermute | solution.py:66
  209.6 3.1 %collective-permute-done.17 = bf16[208,896]{1,0:T(8,128)(2,1)S(1)} collective-permute-done((bf16[208,896]{1,0:T(8,128)(2,1)S(1)}, bf16[208,896]{1,0:T(8,128)(2,1)S(1)}, u32[]{:S(2)}, u32[]{:S(2)}) %collective-permute-start.17) | collective-permute-done | bytes 372768 | tf_op jit(solution)/shard_map/ppermute | solution.py:66
  216.3 2.8 %finish.1 = (f32[3,768,384]{2,1,0:T(8,128)}, f32[384,768]{1,0:T(8,128)}, f32[16,768]{1,0:T(8,128)}, f32[16,768]{1,0:T(8,128)}, f32[8,768]{1,0:T(8,128)S(1)}) custom-call(s32[1]{0:T(128)} %bitcast.refs_0_, bf16[400,896]{1,0:T(8,128)(2,1)S(1)} %fusion.61.refs_1_, bf16[384,768]{1,0:T(8,128)(2,1)S(1)} %pad_maximum_fusion.2.refs_2_, ...), custom_call_target="tpu_custom_call" | custom-call | tf_op jit(solution)/shard_map/finish/pallas_call | solution.py:387
  (202 shorter events, 52.1 us)
Async XLA Ops:
  0.6 13.1 %copy-start = (f32[16,768]{1,0:T(8,128)S(1)}, f32[16,768]{1,0:T(8,128)}, u32[]{:S(2)}) copy-start(f32[16,768]{1,0:T(8,128)} %param.29) | copy-start | bytes 147460
  0.7 17.4 %collective-permute-start = (bf16[384,768]{1,0:T(8,128)(2,1)}, bf16[384,768]{1,0:T(8,128)(2,1)S(1)}, u32[]{:S(2)}, u32[]{:S(2)}) collective-permute-start(bf16[384,768]{1,0:T(8,128)(2,1)} %proj_ref.1), channel_id=1, source_target_pairs={{0,1},{1,0},{2,3},{3,2},{4,5},{5,4},{6,7},{7,6},{8,9},{9,8},{10,11... | collective-permute-start | bytes 1769480 | tf_op jit(solution)/shard_map/ppermute | solution.py:62
  7.3 21.6 %all-to-all-start = ((bf16[16,48,384]{2,1,0:T(8,128)(2,1)}), bf16[16,48,384]{2,1,0:T(8,128)(2,1)}, u32[]{:S(2)}, u32[]{:S(2)}) async-start(bf16[16,48,384]{2,1,0:T(8,128)(2,1)} %broadcast_select_fusion), calls=%async_computation | async-start | bytes 1179648 | tf_op jit(solution)/shard_map/all_to_all | solution.py:479
  21.1 7.9 %copy-start.6 = (bf16[768,768]{1,0:T(8,128)(2,1)S(1)}, bf16[768,768]{1,0:T(8,128)(2,1)}, u32[]{:S(2)}) copy-start(bf16[768,768]{1,0:T(8,128)(2,1)} %pad_maximum_fusion) | copy-start | bytes 3538948
  21.1 7.9 %copy-start.20 = (f32[768]{0:T(1024)S(1)}, f32[768]{0:T(1024)}, u32[]{:S(2)}) copy-start(f32[768]{0:T(1024)} %param.22) | copy-start | bytes 9220
  21.1 7.2 %collective-permute-start.1 = (bf16[197,384]{0,1:T(8,128)(2,1)S(1)}, bf16[197,384]{0,1:T(8,128)(2,1)S(1)}, u32[]{:S(2)}, u32[]{:S(2)}) collective-permute-start(bf16[197,384]{0,1:T(8,128)(2,1)S(1)} %bitcast.70), channel_id=1, source_target_pairs={{0,1},{1,0},{2,3},{3,2},{4,5},{5,4},{6,7},{7,6},{8,9},{9,8},{10,11... | collective-permute-start | bytes 453896 | tf_op jit(solution)/shard_map/ppermute | solution.py:62
  30.7 11.1 %copy-start.5 = (bf16[197,768]{1,0:T(8,128)(2,1)}, bf16[197,768]{1,0:T(8,128)(2,1)S(1)}, u32[]{:S(2)}) copy-start(bf16[197,768]{1,0:T(8,128)(2,1)S(1)} %get-tuple-element.95.hidden2_ref) | copy-start | bytes 907780
  32.5 30.5 %all-to-all-start.1 = ((bf16[16,48,768]{2,1,0:T(8,128)(2,1)}), bf16[16,48,768]{2,1,0:T(8,128)(2,1)S(1)}, u32[]{:S(2)}, u32[]{:S(2)}) async-start(bf16[16,48,768]{2,1,0:T(8,128)(2,1)} %bitcast.20), calls=%async_computation.1 | async-start | bytes 2359296 | tf_op jit(solution)/shard_map/all_to_all | solution.py:509
  42.2 76.6 %copy-start.2 = (f32[197,128]{1,0:T(8,128)}, f32[197,128]{1,0:T(8,128)S(1)}, u32[]{:S(2)}) copy-start(f32[197,128]{1,0:T(8,128)S(1)} %pad.31.facts_ref) | copy-start | bytes 302596
  42.2 16.0 %collective-permute-start.2 = (bf16[16,48,384]{2,1,0:T(8,128)(2,1)}, bf16[16,48,384]{2,1,0:T(8,128)(2,1)}, u32[]{:S(2)}, u32[]{:S(2)}) collective-permute-start(bf16[16,48,384]{2,1,0:T(8,128)(2,1)} %all-to-all-done), channel_id=1, source_target_pairs={{0,1},{1,0},{2,3},{3,2},{4,5},{5,4},{6,7},{7,6},{8,9},{9,8},{10,11... | collective-permute-start | bytes 1769480 | tf_op jit(solution)/shard_map/ppermute | solution.py:62
  78.7 32.6 %all-to-all-start.2 = ((bf16[16,48,768]{2,1,0:T(8,128)(2,1)}), bf16[16,48,768]{2,1,0:T(8,128)(2,1)S(1)}, u32[]{:S(2)}, u32[]{:S(2)}) async-start(bf16[16,48,768]{2,1,0:T(8,128)(2,1)} %bitcast.67), calls=%async_computation.2 | async-start | bytes 2359296 | tf_op jit(solution)/shard_map/all_to_all | solution.py:569
  111.3 32.7 %all-to-all-start.3 = ((bf16[16,48,768]{2,1,0:T(8,128)(2,1)}), bf16[16,48,768]{2,1,0:T(8,128)(2,1)}, u32[]{:S(2)}, u32[]{:S(2)}) async-start(bf16[16,48,768]{2,1,0:T(8,128)(2,1)} %bitcast.65), calls=%async_computation.3 | async-start | bytes 2359296 | tf_op jit(solution)/shard_map/all_to_all | solution.py:588
  119.5 9.8 %copy-start.1 = (bf16[208,768]{1,0:T(8,128)(2,1)}, bf16[208,768]{1,0:T(8,128)(2,1)S(1)}, u32[]{:S(2)}) copy-start(bf16[208,768]{1,0:T(8,128)(2,1)S(1)} %home_rows.1.home_ref) | copy-start | bytes 958468
  119.5 9.8 %collective-permute-start.3 = (bf16[208,768]{1,0:T(8,128)(2,1)S(1)}, bf16[208,768]{1,0:T(8,128)(2,1)S(1)}, u32[]{:S(2)}, u32[]{:S(2)}) collective-permute-start(bf16[208,768]{1,0:T(8,128)(2,1)S(1)} %home_rows.1.home_ref), channel_id=1, source_target_pairs={{0,1},{1,0},{2,3},{3,2},{4,5},{5,4},{6,7},{7,6},{8,9},{9,8},{10,11... | collective-permute-start | bytes 958472 | tf_op jit(solution)/shard_map/ppermute | solution.py:62
  144.0 3.6 %collective-permute-start.4 = (bf16[384,1664]{1,0:T(8,128)(2,1)}, bf16[384,1664]{1,0:T(8,128)(2,1)S(1)}, u32[]{:S(2)}, u32[]{:S(2)}) collective-permute-start(bf16[384,1664]{1,0:T(8,128)(2,1)} %get-tuple-element.108), channel_id=1, source_target_pairs={{0,2},{2,0},{4,6},{6,4},{8,10},{10,8},{12,14},{14,12},{16,18},{18,... | collective-permute-start | bytes 3833864 | tf_op jit(solution)/shard_map/ppermute | solution.py:66
  149.9 11.3 %collective-permute-start.6 = (bf16[192,768]{1,0:T(8,128)(2,1)S(1)}, bf16[192,768]{1,0:T(8,128)(2,1)S(1)}, u32[]{:S(2)}, u32[]{:S(2)}) collective-permute-start(bf16[192,768]{1,0:T(8,128)(2,1)S(1)} %slice.284), channel_id=1, source_target_pairs={{0,8},{2,10},{4,12},{6,14},{8,0},{10,2},{12,4},{14,6},{16,24},{18,... | collective-permute-start | bytes 884744 | tf_op jit(solution)/shard_map/ppermute | solution.py:66
  154.5 10.1 %collective-permute-start.5 = (bf16[192,896]{1,0:T(8,128)(2,1)S(1)}, bf16[192,896]{1,0:T(8,128)(2,1)S(1)}, u32[]{:S(2)}, u32[]{:S(2)}) collective-permute-start(bf16[192,896]{1,0:T(8,128)(2,1)S(1)} %slice.283), channel_id=1, source_target_pairs={{0,4},{2,6},{4,0},{6,2},{8,12},{10,14},{12,8},{14,10},{16,20},{18,... | collective-permute-start | bytes 1032200 | tf_op jit(solution)/shard_map/ppermute | solution.py:66
  156.3 9.0 %collective-permute-start.7 = (bf16[197,768]{1,0:T(8,128)(2,1)S(1)}, bf16[197,768]{1,0:T(8,128)(2,1)S(1)}, u32[]{:S(2)}, u32[]{:S(2)}) collective-permute-start(bf16[197,768]{1,0:T(8,128)(2,1)S(1)} %copy-done.13), channel_id=1, source_target_pairs={{0,1},{1,0},{2,3},{3,2},{4,5},{5,4},{6,7},{7,6},{8,9},{9,8},{10,11... | collective-permute-start | bytes 907784 | tf_op jit(solution)/shard_map/ppermute | solution.py:62
  165.7 8.4 %collective-permute-start.8 = (bf16[96,896]{1,0:T(8,128)(2,1)S(1)}, bf16[96,896]{1,0:T(8,128)(2,1)S(1)}, u32[]{:S(2)}, u32[]{:S(2)}) collective-permute-start(bf16[96,896]{1,0:T(8,128)(2,1)S(1)} %slice.285), channel_id=1, source_target_pairs={{0,8},{2,10},{4,12},{6,14},{8,0},{10,2},{12,4},{14,6},{16,24},{18,... | collective-permute-start | bytes 516104 | tf_op jit(solution)/shard_map/ppermute | solution.py:66
  166.1 7.3 %collective-permute-start.9 = (bf16[96,768]{1,0:T(8,128)(2,1)S(1)}, bf16[96,768]{1,0:T(8,128)(2,1)S(1)}, u32[]{:S(2)}, u32[]{:S(2)}) collective-permute-start(bf16[96,768]{1,0:T(8,128)(2,1)S(1)} %slice.286), channel_id=1, source_target_pairs={{0,16},{2,18},{4,20},{6,22},{8,24},{10,26},{12,28},{14,30},{16,0},... | collective-permute-start | bytes 442376 | tf_op jit(solution)/shard_map/ppermute | solution.py:66
  174.2 4.4 %collective-permute-start.11 = (bf16[48,768]{1,0:T(8,128)(2,1)S(1)}, bf16[48,768]{1,0:T(8,128)(2,1)S(1)}, u32[]{:S(2)}, u32[]{:S(2)}) collective-permute-start(bf16[48,768]{1,0:T(8,128)(2,1)S(1)} %slice.288), channel_id=1, source_target_pairs={{0,4},{2,6},{4,0},{6,2},{8,12},{10,14},{12,8},{14,10},{16,20},{18,... | collective-permute-start | bytes 221192 | tf_op jit(solution)/shard_map/ppermute | solution.py:66
  175.6 5.4 %collective-permute-start.10 = (bf16[48,896]{1,0:T(8,128)(2,1)S(1)}, bf16[48,896]{1,0:T(8,128)(2,1)S(1)}, u32[]{:S(2)}, u32[]{:S(2)}) collective-permute-start(bf16[48,896]{1,0:T(8,128)(2,1)S(1)} %slice.287), channel_id=1, source_target_pairs={{0,16},{2,18},{4,20},{6,22},{8,24},{10,26},{12,28},{14,30},{16,0},... | collective-permute-start | bytes 258056 | tf_op jit(solution)/shard_map/ppermute | solution.py:66
  181.1 4.4 %collective-permute-start.13 = (bf16[48,768]{1,0:T(8,128)(2,1)S(1)}, bf16[48,768]{1,0:T(8,128)(2,1)S(1)}, u32[]{:S(2)}, u32[]{:S(2)}) collective-permute-start(bf16[48,768]{1,0:T(8,128)(2,1)S(1)} %add_convert_fusion.3), channel_id=1, source_target_pairs={{0,4},{2,6},{4,0},{6,2},{8,12},{10,14},{12,8},{14,10},{16,20},{18,... | collective-permute-start | bytes 221192 | tf_op jit(solution)/shard_map/ppermute | solution.py:66
  181.8 5.7 %collective-permute-start.12 = (bf16[64,896]{1,0:T(8,128)(2,1)S(1)}, bf16[64,896]{1,0:T(8,128)(2,1)S(1)}, u32[]{:S(2)}, u32[]{:S(2)}) collective-permute-start(bf16[64,896]{1,0:T(8,128)(2,1)S(1)} %pad_maximum_fusion.8), channel_id=1, source_target_pairs={{0,16},{2,18},{4,20},{6,22},{8,24},{10,26},{12,28},{14,30},{16,0},... | collective-permute-start | bytes 344072 | tf_op jit(solution)/shard_map/ppermute | solution.py:66
  187.6 16.5 %copy-start.14 = (f32[197,768]{1,0:T(8,128)S(1)}, f32[197,768]{1,0:T(8,128)}, u32[]{:S(2)}) copy-start(f32[197,768]{1,0:T(8,128)} %get-tuple-element.136) | copy-start | bytes 1815556
  187.6 12.8 %collective-permute-start.14 = (bf16[112,896]{1,0:T(8,128)(2,1)S(1)}, bf16[112,896]{1,0:T(8,128)(2,1)S(1)}, u32[]{:S(2)}, u32[]{:S(2)}) collective-permute-start(bf16[112,896]{1,0:T(8,128)(2,1)S(1)} %pad_maximum_fusion.6), channel_id=1, source_target_pairs={{0,8},{2,10},{4,12},{6,14},{8,0},{10,2},{12,4},{14,6},{16,24},{18,... | collective-permute-start | bytes 602120 | tf_op jit(solution)/shard_map/ppermute | solution.py:66
  192.6 7.8 %collective-permute-start.15 = (bf16[96,768]{1,0:T(8,128)(2,1)S(1)}, bf16[96,768]{1,0:T(8,128)(2,1)S(1)}, u32[]{:S(2)}, u32[]{:S(2)}) collective-permute-start(bf16[96,768]{1,0:T(8,128)(2,1)S(1)} %pad_maximum_fusion.7), channel_id=1, source_target_pairs={{0,16},{2,18},{4,20},{6,22},{8,24},{10,26},{12,28},{14,30},{16,0},... | collective-permute-start | bytes 442376 | tf_op jit(solution)/shard_map/ppermute | solution.py:66
  196.0 6.9 %collective-permute-start.16 = (bf16[197,768]{1,0:T(8,128)(2,1)S(1)}, bf16[197,768]{1,0:T(8,128)(2,1)S(1)}, u32[]{:S(2)}, u32[]{:S(2)}) collective-permute-start(bf16[197,768]{1,0:T(8,128)(2,1)S(1)} %convolution_convert_fusion.3), channel_id=1, source_target_pairs={{0,1},{1,0},{2,3},{3,2},{4,5},{5,4},{6,7},{7,6},{8,9},{9,8},{10,11... | collective-permute-start | bytes 907784 | tf_op jit(solution)/shard_map/ppermute | solution.py:62
  202.8 6.7 %collective-permute-start.18 = (bf16[192,768]{1,0:T(8,128)(2,1)S(1)}, bf16[192,768]{1,0:T(8,128)(2,1)S(1)}, u32[]{:S(2)}, u32[]{:S(2)}) collective-permute-start(bf16[192,768]{1,0:T(8,128)(2,1)S(1)} %pad_maximum_fusion.5), channel_id=1, source_target_pairs={{0,8},{2,10},{4,12},{6,14},{8,0},{10,2},{12,4},{14,6},{16,24},{18,... | collective-permute-start | bytes 884744 | tf_op jit(solution)/shard_map/ppermute | solution.py:66
  205.2 7.6 %collective-permute-start.17 = (bf16[208,896]{1,0:T(8,128)(2,1)S(1)}, bf16[208,896]{1,0:T(8,128)(2,1)S(1)}, u32[]{:S(2)}, u32[]{:S(2)}) collective-permute-start(bf16[208,896]{1,0:T(8,128)(2,1)S(1)} %pad_maximum_fusion.4), channel_id=1, source_target_pairs={{0,4},{2,6},{4,0},{6,2},{8,12},{10,14},{12,8},{14,10},{16,20},{18,... | collective-permute-start | bytes 1118216 | tf_op jit(solution)/shard_map/ppermute | solution.py:66
  212.8 2.3 %collective-permute-start.19 = (bf16[400,896]{1,0:T(8,128)(2,1)S(1)}, bf16[400,896]{1,0:T(8,128)(2,1)S(1)}, u32[]{:S(2)}, u32[]{:S(2)}) collective-permute-start(bf16[400,896]{1,0:T(8,128)(2,1)S(1)} %fusion.61.refs_1_), channel_id=1, source_target_pairs={{0,2},{2,0},{4,6},{6,4},{8,10},{10,8},{12,14},{14,12},{16,18},{18,... | collective-permute-start | bytes 2150408 | tf_op jit(solution)/shard_map/ppermute | solution.py:66
  212.9 3.4 %collective-permute-start.20 = (bf16[384,768]{1,0:T(8,128)(2,1)S(1)}, bf16[384,768]{1,0:T(8,128)(2,1)S(1)}, u32[]{:S(2)}, u32[]{:S(2)}) collective-permute-start(bf16[384,768]{1,0:T(8,128)(2,1)S(1)} %pad_maximum_fusion.2.refs_2_), channel_id=1, source_target_pairs={{0,2},{2,0},{4,6},{6,4},{8,10},{10,8},{12,14},{14,12},{16,18},{18,... | collective-permute-start | bytes 1769480 | tf_op jit(solution)/shard_map/ppermute | solution.py:66
  (20 other events, 69.6 us)

commit v9 on v8

--- a/solution.py
+++ b/solution.py
@@ -347,7 +347,7 @@
         ],
         compiler_params=pltpu.CompilerParams(vmem_limit_bytes=60 << 20),
         cost_estimate=pl.CostEstimate(
-            flops=flops, bytes_accessed=10 << 20, transcendentals=tok_count * tok_count * 6
+            flops=30 * flops, bytes_accessed=10 << 20, transcendentals=tok_count * tok_count * 6
         ),
         name="attention_grads",
     )(*operands)
@@ -606,17 +606,16 @@
     )
     hidden1_other = swap(hidden1_part)
     split = sent.shape[1] - 2 * head_cols
-    sent, out_back = lax.optimization_barrier((sent, out_back))
     came = across(sent, bits[0], sources)
     total = kept + came.astype(F32)
     totals = [total[:, :split], total[:, split:]]
-    out_home = nn(onehot, over_group(out_back).reshape(-1, feat_dim)).astype(BF16)
     for turn in range(1, len(bits)):
-        totals, out_home = lax.optimization_barrier((totals, out_home))
+        if turn == 2:
+            totals, hidden1_other, out_back = lax.optimization_barrier((totals, hidden1_other, out_back))
+            out_home = nn(onehot, over_group(out_back).reshape(-1, feat_dim)).astype(BF16)
         if turn == len(bits) - 1:
+            totals, out_home = lax.optimization_barrier((totals, out_home))
             out_other = swap(out_home)
-        if turn == 2:
-            totals, hidden1_other = lax.optimization_barrier((totals, hidden1_other))
         sends = lax.optimization_barrier([t[t.shape[0] // 2 :].astype(BF16) for t in totals])
         cames = [across(t, order[turn], sources) for t, order in zip(sends, orders)]
         totals = [keep_half(t, c) for t, c in zip(totals, cames)]

time: 221 us -> 237 us (1.072)
  blocking collectives: 0 us -> 37 us
  starting transfers between devices: 57.2 us -> 38.9 us
  waiting for transfers between devices: 83.6 us -> 77.9 us
  other arithmetic: 16.8 us -> 20.7 us
    all_to_all x0 -> x1, blocking collectives: none -> 37 us  [local(): lax.all_to_all(row_send, 'dp', split_axis=0, concat_axis=0, tiled=True)]
    all_to_all x1 -> x0, waiting for transfers between devices: 14.5 us -> none  [local(): lax.all_to_all(row_send, 'dp', split_axis=0, concat_axis=0, tiled=True)]
    ppermute x15, waiting for transfers between devices: 34 us -> 47.2 us  [across(): return lax.ppermute(x, 'dp', [(i, i ^ bit) for i in range(count)])]
    all_to_all x1 -> x0, starting transfers between devices: 7.5 us -> none  [local(): lax.all_to_all(row_send, 'dp', split_axis=0, concat_axis=0, tiled=True)]
    ppermute x15, starting transfers between devices: 25 us -> 17.7 us  [across(): return lax.ppermute(x, 'dp', [(i, i ^ bit) for i in range(count)])]
    all_to_all x1, starting transfers between devices: 7.54 us -> 3.96 us  [local(): lax.all_to_all(out_send, 'dp', split_axis=0, concat_axis=0, tiled=True)]
    all_to_all x1, waiting for transfers between devices: 2.59 us -> 0.01 us  [local(): lax.all_to_all(out_send, 'dp', split_axis=0, concat_axis=0, tiled=True)]
  transfers between devices with their start and end apart: 25 -> 24, of which waited for: 22 -> 17; matrix products, arithmetic and copies ran while one was open for 18% -> 18% of each run, Pallas kernels for 5% -> 0%
where the time goes in v9:
time: 237 us; the launch traced here: 236 us
  waiting for transfers between devices  77.9 us (33%)
  starting transfers between devices  38.9 us (16%)
  blocking collectives  37 us (16%)
  Pallas kernels  29.5 us (12%)
  other arithmetic  20.7 us (9%)
  matrix products  19.9 us (8%)
  local copies, waits for them, and re-layouts  10.6 us (4%)
    ppermute x15, waiting for transfers between devices, across(): return lax.ppermute(x, 'dp', [(i, i ^ bit) for i in range(count)])  47.2 us
    all_to_all x1, blocking collectives, local(): lax.all_to_all(row_send, 'dp', split_axis=0, concat_axis=0, tiled=True)  37 us
    ppermute x6, waiting for transfers between devices, swap(): return lax.ppermute(x, 'tensor', [(0, 1), (1, 0)])  28 us
    ppermute x15, starting transfers between devices, across(): return lax.ppermute(x, 'dp', [(i, i ^ bit) for i in range(count)])  17.7 us
    dot_general x12, matrix products, dot(): return lax.dot_general(a, b, (dims, ((), ())), preferred_element_type=out)  15.7 us
    pallas_call x1, Pallas kernels, expert_rows(): pl.pallas_call(lambda *refs: expert_kernel(capacity, slots, *refs), grid=...  14.7 us
    pallas_call x1, Pallas kernels, attention_grads(): pl.pallas_call(attention_grads_kernel, out_shape=(jax.ShapeDtypeStruct((f...  11.3 us
    all_to_all x1, starting transfers between devices, local(): lax.all_to_all(cot_send, 'dp', split_axis=0, concat_axis=0, tiled=True)  5.95 us
  transfers between devices with their start and end apart: 24, of which 17 were waited for; matrix products, arithmetic and copies ran while one was open for 18% of the time, Pallas kernels for 0%

profile of v9, /device:TPU:0, one launch (start us, length us, event | category | flops | bytes accessed | tf_op | source)
XLA Modules:
  0.0 235.9 jit_solution(16496720809886034599)
XLA Ops:
  0.7 3.0 %collective-permute-start = (bf16[384,768]{1,0:T(8,128)(2,1)}, bf16[384,768]{1,0:T(8,128)(2,1)S(1)}, u32[]{:S(2)}, u32[]{:S(2)}) collective-permute-start(bf16[384,768]{1,0:T(8,128)(2,1)} %proj_ref.1), channel_id=1, source_target_pairs={{0,1},{1,0},{2,3},{3,2},{4,5},{5,4},{6,7},{7,6},{8,9},{9,8},{10,11... | collective-permute-start | bytes 1769480 | tf_op jit(solution)/shard_map/ppermute | solution.py:62
  7.3 6.0 %all-to-all-start = ((bf16[16,48,384]{2,1,0:T(8,128)(2,1)}), bf16[16,48,384]{2,1,0:T(8,128)(2,1)}, u32[]{:S(2)}, u32[]{:S(2)}) async-start(bf16[16,48,384]{2,1,0:T(8,128)(2,1)} %broadcast_select_fusion), calls=%async_computation | async-start | bytes 1179648 | tf_op jit(solution)/shard_map/all_to_all | solution.py:479
  15.5 1.8 convolution_convert_fusion.1.hidden_ref
  21.9 6.5 %collective-permute-done.1 = bf16[197,384]{0,1:T(8,128)(2,1)S(1)} collective-permute-done((bf16[197,384]{0,1:T(8,128)(2,1)S(1)}, bf16[197,384]{0,1:T(8,128)(2,1)S(1)}, u32[]{:S(2)}, u32[]{:S(2)}) %collective-permute-start.1) | collective-permute-done | bytes 151328 | tf_op jit(solution)/shard_map/ppermute | solution.py:62
  30.7 1.8 convolution_convert_fusion
  32.5 5.3 %all-to-all-start.1 = ((bf16[16,48,768]{2,1,0:T(8,128)(2,1)}), bf16[16,48,768]{2,1,0:T(8,128)(2,1)S(1)}, u32[]{:S(2)}, u32[]{:S(2)}) async-start(bf16[16,48,768]{2,1,0:T(8,128)(2,1)} %bitcast.20), calls=%async_computation.1 | async-start | bytes 2359296 | tf_op jit(solution)/shard_map/all_to_all | solution.py:509
  37.9 3.1 %fusion.mix_ref = bf16[2,768,768]{2,1,0:T(8,128)(2,1)} fusion(pred[1,768,768]{2,1,0:T(32,128)(4,1)} %copy-done.10, pred[1,768,768]{2,1,0:T(32,128)(4,1)} %copy-done.9), kind=kLoop, calls=%fused_computation.7 | loop fusion | flops 2359296 | bytes 3538944 | tf_op jit(solution)/shard_map/stack | solution.py:540
  45.7 12.5 %collective-permute-done.2 = bf16[16,48,384]{2,1,0:T(8,128)(2,1)} collective-permute-done((bf16[16,48,384]{2,1,0:T(8,128)(2,1)}, bf16[16,48,384]{2,1,0:T(8,128)(2,1)}, u32[]{:S(2)}, u32[]{:S(2)}) %collective-permute-start.2) | collective-permute-done | bytes 589856 | tf_op jit(solution)/shard_map/ppermute | solution.py:62
  60.7 2.3 all-to-all-done.1
  64.0 14.7 %expert_rows.1 = (bf16[768,1536]{1,0:T(8,128)(2,1)}, bf16[768,1536]{1,0:T(8,128)(2,1)}, bf16[768,768]{1,0:T(8,128)(2,1)}, bf16[768,768]{1,0:T(8,128)(2,1)}, bf16[768,768]{1,0:T(8,128)(2,1)}, /*index=5*/f32[1,1536]{1,0:T(1,128)}) custom-call(s32[1]{0:T(128)} %bitcast.refs_0_, bf16[768,768]{1,0:T(8,128)(2,1)} %bitcast.64, bf16[768,768]{1,0:T(8,128)(2,1)} %bitcast.67, ...), custom_call_target="tpu_custom_call" | custom-call | flops 7247757312 | bytes 12582912 | tf_op jit(solution)/shard_map/expert_rows/pallas_call | solution.py:143
  78.7 37.0 %all_to_all.20.back_ref = bf16[16,48,768]{2,1,0:T(8,128)(2,1)S(1)} all-to-all(bf16[16,48,768]{2,1,0:T(8,128)(2,1)} %bitcast.68), channel_id=1, replica_groups=mesh['dp'=16,'tensor'=2] {'dp'}, dimensions={0} | all-to-all | bytes 2359296 | tf_op jit(solution)/shard_map/all_to_all | solution.py:569
  118.2 7.9 %collective-permute-done.3.other_ref = bf16[208,768]{1,0:T(8,128)(2,1)S(1)} collective-permute-done((bf16[208,768]{1,0:T(8,128)(2,1)S(1)}, bf16[208,768]{1,0:T(8,128)(2,1)S(1)}, u32[]{:S(2)}, u32[]{:S(2)}) %collective-permute-start.3) | collective-permute-done | bytes 319520 | tf_op jit(solution)/shard_map/ppermute | solution.py:62
  126.9 11.3 %attention_grads.1 = (bf16[384,1664]{1,0:T(8,128)(2,1)}, f32[384,1664]{1,0:T(8,128)}, bf16[197,768]{1,0:T(8,128)(2,1)}, f32[1,1152]{1,0:T(1,128)}, f32[197,768]{1,0:T(8,128)}) custom-call(bf16[208,768]{1,0:T(8,128)(2,1)} %copy-done.2, bf16[208,768]{1,0:T(8,128)(2,1)} %copy-done.28, bf16[768,16]{1,0:T(8,128)(2,1)} %copy.80.refs_4_.router_ref, ...), custom_call_target="tpu_custom_call" | custom-call | flops 42874306560 | bytes 10485760 | tf_op jit(solution)/shard_map/attention_grads/pallas_call | solution.py:333
  138.2 6.0 %fusion.116 = f32[768,1536]{1,0:T(8,128)} fusion(bf16[768,768]{1,0:T(8,128)(2,1)S(1)} %bitcast.65, bf16[768,1536]{1,0:T(8,128)(2,1)} %get-tuple-element.102), kind=kOutput, calls=%fused_computation.238 | convolution fusion | flops 1811939328 | bytes 8257536 | tf_op jit(solution)/shard_map/dot_general | solution.py:36
  144.3 4.3 %fusion.115 = f32[1536,768]{1,0:T(8,128)} fusion(bf16[768,1536]{1,0:T(8,128)(2,1)S(1)} %copy-done.30, bf16[768,768]{1,0:T(8,128)(2,1)S(1)} %copy-done.31), kind=kOutput, calls=%fused_computation.237 | convolution fusion | flops 1811939328 | bytes 8257536 | tf_op jit(solution)/shard_map/dot_general | solution.py:36
  148.6 4.0 %all-to-all-start.3 = ((bf16[16,48,768]{2,1,0:T(8,128)(2,1)}), bf16[16,48,768]{2,1,0:T(8,128)(2,1)S(1)}, u32[]{:S(2)}, u32[]{:S(2)}) async-start(bf16[16,48,768]{2,1,0:T(8,128)(2,1)} %bitcast.66), calls=%async_computation.3 | async-start | bytes 2359296 | tf_op jit(solution)/shard_map/all_to_all | solution.py:588
  152.5 2.3 fusion.105
  159.5 21.1 %collective-permute-done.6 = bf16[192,768]{1,0:T(8,128)(2,1)S(1)} collective-permute-done((bf16[192,768]{1,0:T(8,128)(2,1)S(1)}, bf16[192,768]{1,0:T(8,128)(2,1)S(1)}, u32[]{:S(2)}, u32[]{:S(2)}) %collective-permute-start.6) | collective-permute-done | bytes 294944 | tf_op jit(solution)/shard_map/ppermute | solution.py:66
  185.8 1.8 collective-permute-start.9
  188.1 4.5 %collective-permute-done.9 = bf16[96,768]{1,0:T(8,128)(2,1)S(1)} collective-permute-done((bf16[96,768]{1,0:T(8,128)(2,1)S(1)}, bf16[96,768]{1,0:T(8,128)(2,1)S(1)}, u32[]{:S(2)}, u32[]{:S(2)}) %collective-permute-start.9) | collective-permute-done | bytes 147488 | tf_op jit(solution)/shard_map/ppermute | solution.py:66
  195.7 1.7 collective-permute-start.10
  198.6 2.9 %collective-permute-done.10 = bf16[48,896]{1,0:T(8,128)(2,1)S(1)} collective-permute-done((bf16[48,896]{1,0:T(8,128)(2,1)S(1)}, bf16[48,896]{1,0:T(8,128)(2,1)S(1)}, u32[]{:S(2)}, u32[]{:S(2)}) %collective-permute-start.10) | collective-permute-done | bytes 86048 | tf_op jit(solution)/shard_map/ppermute | solution.py:66
  203.7 2.3 collective-permute-done.13
  206.0 1.9 collective-permute-done.12
  208.0 2.2 collective-permute-start.14
  210.2 2.1 collective-permute-start.15
  212.8 5.0 %collective-permute-done.15 = bf16[96,768]{1,0:T(8,128)(2,1)S(1)} collective-permute-done((bf16[96,768]{1,0:T(8,128)(2,1)S(1)}, bf16[96,768]{1,0:T(8,128)(2,1)S(1)}, u32[]{:S(2)}, u32[]{:S(2)}) %collective-permute-start.15) | collective-permute-done | bytes 147488 | tf_op jit(solution)/shard_map/ppermute | solution.py:66
  219.3 2.1 fusion.18
  223.7 2.2 collective-permute-done.18
  225.9 3.0 %collective-permute-done.17 = bf16[208,896]{1,0:T(8,128)(2,1)S(1)} collective-permute-done((bf16[208,896]{1,0:T(8,128)(2,1)S(1)}, bf16[208,896]{1,0:T(8,128)(2,1)S(1)}, u32[]{:S(2)}, u32[]{:S(2)}) %collective-permute-start.17) | collective-permute-done | bytes 372768 | tf_op jit(solution)/shard_map/ppermute | solution.py:66
  229.6 1.7 collective-permute-done.19.refs_3_
  232.5 2.8 %finish.1 = (f32[3,768,384]{2,1,0:T(8,128)}, f32[384,768]{1,0:T(8,128)}, f32[16,768]{1,0:T(8,128)}, f32[16,768]{1,0:T(8,128)}, f32[8,768]{1,0:T(8,128)S(1)}) custom-call(s32[1]{0:T(128)} %bitcast.refs_0_, bf16[400,896]{1,0:T(8,128)(2,1)S(1)} %fusion.61.refs_1_, bf16[384,768]{1,0:T(8,128)(2,1)S(1)} %pad_maximum_fusion.2.refs_2_, ...), custom_call_target="tpu_custom_call" | custom-call | tf_op jit(solution)/shard_map/finish/pallas_call | solution.py:387
  (209 shorter events, 47.5 us)
Async XLA Ops:
  0.6 13.1 %copy-start = (f32[16,768]{1,0:T(8,128)S(1)}, f32[16,768]{1,0:T(8,128)}, u32[]{:S(2)}) copy-start(f32[16,768]{1,0:T(8,128)} %param.29) | copy-start | bytes 147460
  0.7 17.4 %collective-permute-start = (bf16[384,768]{1,0:T(8,128)(2,1)}, bf16[384,768]{1,0:T(8,128)(2,1)S(1)}, u32[]{:S(2)}, u32[]{:S(2)}) collective-permute-start(bf16[384,768]{1,0:T(8,128)(2,1)} %proj_ref.1), channel_id=1, source_target_pairs={{0,1},{1,0},{2,3},{3,2},{4,5},{5,4},{6,7},{7,6},{8,9},{9,8},{10,11... | collective-permute-start | bytes 1769480 | tf_op jit(solution)/shard_map/ppermute | solution.py:62
  7.3 21.6 %all-to-all-start = ((bf16[16,48,384]{2,1,0:T(8,128)(2,1)}), bf16[16,48,384]{2,1,0:T(8,128)(2,1)}, u32[]{:S(2)}, u32[]{:S(2)}) async-start(bf16[16,48,384]{2,1,0:T(8,128)(2,1)} %broadcast_select_fusion), calls=%async_computation | async-start | bytes 1179648 | tf_op jit(solution)/shard_map/all_to_all | solution.py:479
  21.1 8.4 %copy-start.14 = (bf16[6,64,197]{2,1,0:T(8,128)(2,1)}, bf16[6,64,197]{2,1,0:T(8,128)(2,1)S(1)}, u32[]{:S(2)}) copy-start(bf16[6,64,197]{2,1,0:T(8,128)(2,1)S(1)} %convolution_convert_fusion.4) | copy-start | bytes 453892
  21.1 7.9 %copy-start.5 = (bf16[768,768]{1,0:T(8,128)(2,1)S(1)}, bf16[768,768]{1,0:T(8,128)(2,1)}, u32[]{:S(2)}) copy-start(bf16[768,768]{1,0:T(8,128)(2,1)} %pad_maximum_fusion) | copy-start | bytes 3538948
  21.1 7.2 %collective-permute-start.1 = (bf16[197,384]{0,1:T(8,128)(2,1)S(1)}, bf16[197,384]{0,1:T(8,128)(2,1)S(1)}, u32[]{:S(2)}, u32[]{:S(2)}) collective-permute-start(bf16[197,384]{0,1:T(8,128)(2,1)S(1)} %bitcast.71), channel_id=1, source_target_pairs={{0,1},{1,0},{2,3},{3,2},{4,5},{5,4},{6,7},{7,6},{8,9},{9,8},{10,11... | collective-permute-start | bytes 453896 | tf_op jit(solution)/shard_map/ppermute | solution.py:62
  30.7 11.0 %copy-start.8 = (bf16[197,768]{1,0:T(8,128)(2,1)}, bf16[197,768]{1,0:T(8,128)(2,1)S(1)}, u32[]{:S(2)}) copy-start(bf16[197,768]{1,0:T(8,128)(2,1)S(1)} %get-tuple-element.88.hidden2_ref) | copy-start | bytes 907780
  32.5 30.4 %all-to-all-start.1 = ((bf16[16,48,768]{2,1,0:T(8,128)(2,1)}), bf16[16,48,768]{2,1,0:T(8,128)(2,1)S(1)}, u32[]{:S(2)}, u32[]{:S(2)}) async-start(bf16[16,48,768]{2,1,0:T(8,128)(2,1)} %bitcast.20), calls=%async_computation.1 | async-start | bytes 2359296 | tf_op jit(solution)/shard_map/all_to_all | solution.py:509
  42.2 73.5 %copy-start.1 = (f32[197,128]{1,0:T(8,128)}, f32[197,128]{1,0:T(8,128)S(1)}, u32[]{:S(2)}) copy-start(f32[197,128]{1,0:T(8,128)S(1)} %pad.31.facts_ref) | copy-start | bytes 302596
  42.2 16.0 %collective-permute-start.2 = (bf16[16,48,384]{2,1,0:T(8,128)(2,1)}, bf16[16,48,384]{2,1,0:T(8,128)(2,1)}, u32[]{:S(2)}, u32[]{:S(2)}) collective-permute-start(bf16[16,48,384]{2,1,0:T(8,128)(2,1)} %all-to-all-done), channel_id=1, source_target_pairs={{0,1},{1,0},{2,3},{3,2},{4,5},{5,4},{6,7},{7,6},{8,9},{9,8},{10,11... | collective-permute-start | bytes 1769480 | tf_op jit(solution)/shard_map/ppermute | solution.py:62
  116.3 9.8 %copy-start.2 = (bf16[208,768]{1,0:T(8,128)(2,1)}, bf16[208,768]{1,0:T(8,128)(2,1)S(1)}, u32[]{:S(2)}) copy-start(bf16[208,768]{1,0:T(8,128)(2,1)S(1)} %home_rows.1.home_ref) | copy-start | bytes 958468
  116.3 9.8 %collective-permute-start.3 = (bf16[208,768]{1,0:T(8,128)(2,1)S(1)}, bf16[208,768]{1,0:T(8,128)(2,1)S(1)}, u32[]{:S(2)}, u32[]{:S(2)}) collective-permute-start(bf16[208,768]{1,0:T(8,128)(2,1)S(1)} %home_rows.1.home_ref), channel_id=1, source_target_pairs={{0,1},{1,0},{2,3},{3,2},{4,5},{5,4},{6,7},{7,6},{8,9},{9,8},{10,11... | collective-permute-start | bytes 958472 | tf_op jit(solution)/shard_map/ppermute | solution.py:62
  118.2 20.0 %copy-start.7 = (bf16[16,48,768]{2,1,0:T(8,128)(2,1)S(1)}, bf16[16,48,768]{2,1,0:T(8,128)(2,1)}, u32[]{:S(2)}) copy-start(bf16[16,48,768]{2,1,0:T(8,128)(2,1)} %copy-done.6) | copy-start | bytes 3538948
  138.2 14.3 %collective-permute-start.4 = (bf16[384,1664]{1,0:T(8,128)(2,1)}, bf16[384,1664]{1,0:T(8,128)(2,1)}, u32[]{:S(2)}, u32[]{:S(2)}) collective-permute-start(bf16[384,1664]{1,0:T(8,128)(2,1)} %get-tuple-element.95), channel_id=1, source_target_pairs={{0,2},{2,0},{4,6},{6,4},{8,10},{10,8},{12,14},{14,12},{16,18},{18,... | collective-permute-start | bytes 3833864 | tf_op jit(solution)/shard_map/ppermute | solution.py:66
  148.6 33.8 %all-to-all-start.3 = ((bf16[16,48,768]{2,1,0:T(8,128)(2,1)}), bf16[16,48,768]{2,1,0:T(8,128)(2,1)S(1)}, u32[]{:S(2)}, u32[]{:S(2)}) async-start(bf16[16,48,768]{2,1,0:T(8,128)(2,1)} %bitcast.66), calls=%async_computation.3 | async-start | bytes 2359296 | tf_op jit(solution)/shard_map/all_to_all | solution.py:588
  155.0 25.6 %collective-permute-start.6 = (bf16[192,768]{1,0:T(8,128)(2,1)S(1)}, bf16[192,768]{1,0:T(8,128)(2,1)S(1)}, u32[]{:S(2)}, u32[]{:S(2)}) collective-permute-start(bf16[192,768]{1,0:T(8,128)(2,1)S(1)} %slice.209), channel_id=1, source_target_pairs={{0,8},{2,10},{4,12},{6,14},{8,0},{10,2},{12,4},{14,6},{16,24},{18,... | collective-permute-start | bytes 884744 | tf_op jit(solution)/shard_map/ppermute | solution.py:66
  157.3 24.2 %collective-permute-start.5 = (bf16[192,896]{1,0:T(8,128)(2,1)S(1)}, bf16[192,896]{1,0:T(8,128)(2,1)S(1)}, u32[]{:S(2)}, u32[]{:S(2)}) collective-permute-start(bf16[192,896]{1,0:T(8,128)(2,1)S(1)} %slice.208), channel_id=1, source_target_pairs={{0,4},{2,6},{4,0},{6,2},{8,12},{10,14},{12,8},{14,10},{16,20},{18,... | collective-permute-start | bytes 1032200 | tf_op jit(solution)/shard_map/ppermute | solution.py:66
  158.9 23.5 %collective-permute-start.7 = (bf16[197,768]{1,0:T(8,128)(2,1)S(1)}, bf16[197,768]{1,0:T(8,128)(2,1)}, u32[]{:S(2)}, u32[]{:S(2)}) collective-permute-start(bf16[197,768]{1,0:T(8,128)(2,1)S(1)} %copy-done.13), channel_id=1, source_target_pairs={{0,1},{1,0},{2,3},{3,2},{4,5},{5,4},{6,7},{7,6},{8,9},{9,8},{10,11... | collective-permute-start | bytes 907784 | tf_op jit(solution)/shard_map/ppermute | solution.py:62
  184.9 9.1 %collective-permute-start.8 = (bf16[96,896]{1,0:T(8,128)(2,1)S(1)}, bf16[96,896]{1,0:T(8,128)(2,1)S(1)}, u32[]{:S(2)}, u32[]{:S(2)}) collective-permute-start(bf16[96,896]{1,0:T(8,128)(2,1)S(1)} %slice.279), channel_id=1, source_target_pairs={{0,8},{2,10},{4,12},{6,14},{8,0},{10,2},{12,4},{14,6},{16,24},{18,... | collective-permute-start | bytes 516104 | tf_op jit(solution)/shard_map/ppermute | solution.py:66
  185.8 6.8 %collective-permute-start.9 = (bf16[96,768]{1,0:T(8,128)(2,1)S(1)}, bf16[96,768]{1,0:T(8,128)(2,1)S(1)}, u32[]{:S(2)}, u32[]{:S(2)}) collective-permute-start(bf16[96,768]{1,0:T(8,128)(2,1)S(1)} %slice.280), channel_id=1, source_target_pairs={{0,16},{2,18},{4,20},{6,22},{8,24},{10,26},{12,28},{14,30},{16,0},... | collective-permute-start | bytes 442376 | tf_op jit(solution)/shard_map/ppermute | solution.py:66
  194.2 4.4 %collective-permute-start.11 = (bf16[48,768]{1,0:T(8,128)(2,1)S(1)}, bf16[48,768]{1,0:T(8,128)(2,1)S(1)}, u32[]{:S(2)}, u32[]{:S(2)}) collective-permute-start(bf16[48,768]{1,0:T(8,128)(2,1)S(1)} %slice.282), channel_id=1, source_target_pairs={{0,4},{2,6},{4,0},{6,2},{8,12},{10,14},{12,8},{14,10},{16,20},{18,... | collective-permute-start | bytes 221192 | tf_op jit(solution)/shard_map/ppermute | solution.py:66
  195.7 5.8 %collective-permute-start.10 = (bf16[48,896]{1,0:T(8,128)(2,1)S(1)}, bf16[48,896]{1,0:T(8,128)(2,1)S(1)}, u32[]{:S(2)}, u32[]{:S(2)}) collective-permute-start(bf16[48,896]{1,0:T(8,128)(2,1)S(1)} %slice.281), channel_id=1, source_target_pairs={{0,16},{2,18},{4,20},{6,22},{8,24},{10,26},{12,28},{14,30},{16,0},... | collective-permute-start | bytes 258056 | tf_op jit(solution)/shard_map/ppermute | solution.py:66
  201.6 4.4 %collective-permute-start.13 = (bf16[48,768]{1,0:T(8,128)(2,1)S(1)}, bf16[48,768]{1,0:T(8,128)(2,1)S(1)}, u32[]{:S(2)}, u32[]{:S(2)}) collective-permute-start(bf16[48,768]{1,0:T(8,128)(2,1)S(1)} %add_convert_fusion.3), channel_id=1, source_target_pairs={{0,4},{2,6},{4,0},{6,2},{8,12},{10,14},{12,8},{14,10},{16,20},{18,... | collective-permute-start | bytes 221192 | tf_op jit(solution)/shard_map/ppermute | solution.py:66
  202.2 5.7 %collective-permute-start.12 = (bf16[64,896]{1,0:T(8,128)(2,1)S(1)}, bf16[64,896]{1,0:T(8,128)(2,1)S(1)}, u32[]{:S(2)}, u32[]{:S(2)}) collective-permute-start(bf16[64,896]{1,0:T(8,128)(2,1)S(1)} %pad_maximum_fusion.8), channel_id=1, source_target_pairs={{0,16},{2,18},{4,20},{6,22},{8,24},{10,26},{12,28},{14,30},{16,0},... | collective-permute-start | bytes 344072 | tf_op jit(solution)/shard_map/ppermute | solution.py:66
  208.0 11.3 %copy-start.16 = (f32[197,768]{1,0:T(8,128)S(1)}, f32[197,768]{1,0:T(8,128)}, u32[]{:S(2)}) copy-start(f32[197,768]{1,0:T(8,128)} %get-tuple-element.122) | copy-start | bytes 1815556
  208.0 9.9 %collective-permute-start.14 = (bf16[112,896]{1,0:T(8,128)(2,1)S(1)}, bf16[112,896]{1,0:T(8,128)(2,1)S(1)}, u32[]{:S(2)}, u32[]{:S(2)}) collective-permute-start(bf16[112,896]{1,0:T(8,128)(2,1)S(1)} %pad_maximum_fusion.6), channel_id=1, source_target_pairs={{0,8},{2,10},{4,12},{6,14},{8,0},{10,2},{12,4},{14,6},{16,24},{18,... | collective-permute-start | bytes 602120 | tf_op jit(solution)/shard_map/ppermute | solution.py:66
  210.2 7.7 %collective-permute-start.15 = (bf16[96,768]{1,0:T(8,128)(2,1)S(1)}, bf16[96,768]{1,0:T(8,128)(2,1)S(1)}, u32[]{:S(2)}, u32[]{:S(2)}) collective-permute-start(bf16[96,768]{1,0:T(8,128)(2,1)S(1)} %pad_maximum_fusion.7), channel_id=1, source_target_pairs={{0,16},{2,18},{4,20},{6,22},{8,24},{10,26},{12,28},{14,30},{16,0},... | collective-permute-start | bytes 442376 | tf_op jit(solution)/shard_map/ppermute | solution.py:66
  212.3 6.9 %collective-permute-start.16 = (bf16[197,768]{1,0:T(8,128)(2,1)S(1)}, bf16[197,768]{1,0:T(8,128)(2,1)S(1)}, u32[]{:S(2)}, u32[]{:S(2)}) collective-permute-start(bf16[197,768]{1,0:T(8,128)(2,1)S(1)} %convolution_convert_fusion.3), channel_id=1, source_target_pairs={{0,1},{1,0},{2,3},{3,2},{4,5},{5,4},{6,7},{7,6},{8,9},{9,8},{10,11... | collective-permute-start | bytes 907784 | tf_op jit(solution)/shard_map/ppermute | solution.py:62
  219.2 6.7 %collective-permute-start.18 = (bf16[192,768]{1,0:T(8,128)(2,1)S(1)}, bf16[192,768]{1,0:T(8,128)(2,1)S(1)}, u32[]{:S(2)}, u32[]{:S(2)}) collective-permute-start(bf16[192,768]{1,0:T(8,128)(2,1)S(1)} %pad_maximum_fusion.5), channel_id=1, source_target_pairs={{0,8},{2,10},{4,12},{6,14},{8,0},{10,2},{12,4},{14,6},{16,24},{18,... | collective-permute-start | bytes 884744 | tf_op jit(solution)/shard_map/ppermute | solution.py:66
  221.3 7.6 %collective-permute-start.17 = (bf16[208,896]{1,0:T(8,128)(2,1)S(1)}, bf16[208,896]{1,0:T(8,128)(2,1)S(1)}, u32[]{:S(2)}, u32[]{:S(2)}) collective-permute-start(bf16[208,896]{1,0:T(8,128)(2,1)S(1)} %pad_maximum_fusion.4), channel_id=1, source_target_pairs={{0,4},{2,6},{4,0},{6,2},{8,12},{10,14},{12,8},{14,10},{16,20},{18,... | collective-permute-start | bytes 1118216 | tf_op jit(solution)/shard_map/ppermute | solution.py:66
  229.0 2.3 collective-permute-start.19
  229.1 3.4 %collective-permute-start.20 = (bf16[384,768]{1,0:T(8,128)(2,1)S(1)}, bf16[384,768]{1,0:T(8,128)(2,1)S(1)}, u32[]{:S(2)}, u32[]{:S(2)}) collective-permute-start(bf16[384,768]{1,0:T(8,128)(2,1)S(1)} %pad_maximum_fusion.2.refs_2_), channel_id=1, source_target_pairs={{0,2},{2,0},{4,6},{6,4},{8,10},{10,8},{12,14},{14,12},{16,18},{18,... | collective-permute-start | bytes 1769480 | tf_op jit(solution)/shard_map/ppermute | solution.py:66
  (24 other events, 82.8 us)

commit v10 on v8

--- a/solution.py
+++ b/solution.py
@@ -347,7 +347,7 @@
         ],
         compiler_params=pltpu.CompilerParams(vmem_limit_bytes=60 << 20),
         cost_estimate=pl.CostEstimate(
-            flops=flops, bytes_accessed=10 << 20, transcendentals=tok_count * tok_count * 6
+            flops=30 * flops, bytes_accessed=10 << 20, transcendentals=tok_count * tok_count * 6
         ),
         name="attention_grads",
     )(*operands)
@@ -606,13 +606,13 @@
     )
     hidden1_other = swap(hidden1_part)
     split = sent.shape[1] - 2 * head_cols
-    sent, out_back = lax.optimization_barrier((sent, out_back))
     came = across(sent, bits[0], sources)
     total = kept + came.astype(F32)
     totals = [total[:, :split], total[:, split:]]
     out_home = nn(onehot, over_group(out_back).reshape(-1, feat_dim)).astype(BF16)
     for turn in range(1, len(bits)):
-        totals, out_home = lax.optimization_barrier((totals, out_home))
+        if turn >= 2:
+            totals, out_home = lax.optimization_barrier((totals, out_home))
         if turn == len(bits) - 1:
             out_other = swap(out_home)
         if turn == 2:

time: 221 us -> 218 us (0.986)
  starting transfers between devices: 57.2 us -> 50.8 us
  other arithmetic: 16.8 us -> 19.1 us
    ppermute x6, waiting for transfers between devices: 29.8 us -> 18.9 us  [swap(): return lax.ppermute(x, 'tensor', [(0, 1), (1, 0)])]
    ppermute x15, starting transfers between devices: 25 us -> 16.6 us  [across(): return lax.ppermute(x, 'dp', [(i, i ^ bit) for i in range(count)])]
    ppermute x15, waiting for transfers between devices: 34 us -> 40.5 us  [across(): return lax.ppermute(x, 'dp', [(i, i ^ bit) for i in range(count)])]
    another operation x0 -> x1, other arithmetic: none -> 3.53 us
    all_to_all x1, waiting for transfers between devices: 14.5 us -> 17.5 us  [local(): lax.all_to_all(row_send, 'dp', split_axis=0, concat_axis=0, tiled=True)]
    add x4, other arithmetic: 0.17 us -> 2.42 us  [keep_half(): return total[:middle] + came.astype(F32)]
  transfers between devices with their start and end apart: 25 -> 25, of which waited for: 22 -> 19; matrix products, arithmetic and copies ran while one was open for 18% -> 21% of each run, Pallas kernels for 5% -> 5%
where the time goes in v10:
time: 218 us; the launch traced here: 217 us
  waiting for transfers between devices  84.9 us (39%)
  starting transfers between devices  50.8 us (23%)
  Pallas kernels  29.5 us (14%)
  matrix products  21.7 us (10%)
  other arithmetic  19.1 us (9%)
  local copies, waits for them, and re-layouts  9.85 us (5%)
    ppermute x15, waiting for transfers between devices, across(): return lax.ppermute(x, 'dp', [(i, i ^ bit) for i in range(count)])  40.5 us
    ppermute x6, waiting for transfers between devices, swap(): return lax.ppermute(x, 'tensor', [(0, 1), (1, 0)])  18.9 us
    all_to_all x1, waiting for transfers between devices, local(): lax.all_to_all(row_send, 'dp', split_axis=0, concat_axis=0, tiled=True)  17.5 us
    dot_general x12, matrix products, dot(): return lax.dot_general(a, b, (dims, ((), ())), preferred_element_type=out)  17.5 us
    ppermute x15, starting transfers between devices, across(): return lax.ppermute(x, 'dp', [(i, i ^ bit) for i in range(count)])  16.6 us
    pallas_call x1, Pallas kernels, expert_rows(): pl.pallas_call(lambda *refs: expert_kernel(capacity, slots, *refs), grid=...  14.7 us
    pallas_call x1, Pallas kernels, attention_grads(): pl.pallas_call(attention_grads_kernel, out_shape=(jax.ShapeDtypeStruct((f...  11.3 us
    ppermute x6, starting transfers between devices, swap(): return lax.ppermute(x, 'tensor', [(0, 1), (1, 0)])  7.79 us
  transfers between devices with their start and end apart: 25, of which 19 were waited for; matrix products, arithmetic and copies ran while one was open for 21% of the time, Pallas kernels for 5%

profile of v10, /device:TPU:0, one launch (start us, length us, event | category | flops | bytes accessed | tf_op | source)
XLA Modules:
  0.0 217.4 jit_solution(11601952894017732517)
XLA Ops:
  0.7 3.0 %collective-permute-start = (bf16[384,768]{1,0:T(8,128)(2,1)}, bf16[384,768]{1,0:T(8,128)(2,1)S(1)}, u32[]{:S(2)}, u32[]{:S(2)}) collective-permute-start(bf16[384,768]{1,0:T(8,128)(2,1)} %proj_ref.1), channel_id=1, source_target_pairs={{0,1},{1,0},{2,3},{3,2},{4,5},{5,4},{6,7},{7,6},{8,9},{9,8},{10,11... | collective-permute-start | bytes 1769480 | tf_op jit(solution)/shard_map/ppermute | solution.py:62
  7.3 6.0 %all-to-all-start = ((bf16[16,48,384]{2,1,0:T(8,128)(2,1)}), bf16[16,48,384]{2,1,0:T(8,128)(2,1)}, u32[]{:S(2)}, u32[]{:S(2)}) async-start(bf16[16,48,384]{2,1,0:T(8,128)(2,1)} %broadcast_select_fusion), calls=%async_computation | async-start | bytes 1179648 | tf_op jit(solution)/shard_map/all_to_all | solution.py:479
  15.5 1.8 convolution_convert_fusion.1.hidden_ref
  21.9 6.5 %collective-permute-done.1 = bf16[197,384]{0,1:T(8,128)(2,1)S(1)} collective-permute-done((bf16[197,384]{0,1:T(8,128)(2,1)S(1)}, bf16[197,384]{0,1:T(8,128)(2,1)S(1)}, u32[]{:S(2)}, u32[]{:S(2)}) %collective-permute-start.1) | collective-permute-done | bytes 151328 | tf_op jit(solution)/shard_map/ppermute | solution.py:62
  32.5 5.5 %all-to-all-start.1 = ((bf16[16,48,768]{2,1,0:T(8,128)(2,1)}), bf16[16,48,768]{2,1,0:T(8,128)(2,1)}, u32[]{:S(2)}, u32[]{:S(2)}) async-start(bf16[16,48,768]{2,1,0:T(8,128)(2,1)} %bitcast.20), calls=%async_computation.1 | async-start | bytes 2359296 | tf_op jit(solution)/shard_map/all_to_all | solution.py:509
  38.1 1.9 fusion.mix_ref
  44.7 12.3 %collective-permute-done.2 = bf16[16,48,384]{2,1,0:T(8,128)(2,1)S(1)} collective-permute-done((bf16[16,48,384]{2,1,0:T(8,128)(2,1)}, bf16[16,48,384]{2,1,0:T(8,128)(2,1)S(1)}, u32[]{:S(2)}, u32[]{:S(2)}) %collective-permute-start.2) | collective-permute-done | bytes 589856 | tf_op jit(solution)/shard_map/ppermute | solution.py:62
  59.4 3.8 %all-to-all-done.1 = bf16[16,48,768]{2,1,0:T(8,128)(2,1)} async-done(((bf16[16,48,768]{2,1,0:T(8,128)(2,1)}), bf16[16,48,768]{2,1,0:T(8,128)(2,1)}, u32[]{:S(2)}, u32[]{:S(2)}) %all-to-all-start.1) | async-done | bytes 1179680 | tf_op jit(solution)/shard_map/all_to_all | solution.py:509
  63.2 14.7 %expert_rows.1 = (bf16[768,1536]{1,0:T(8,128)(2,1)}, bf16[768,1536]{1,0:T(8,128)(2,1)}, bf16[768,768]{1,0:T(8,128)(2,1)}, bf16[768,768]{1,0:T(8,128)(2,1)}, bf16[768,768]{1,0:T(8,128)(2,1)}, /*index=5*/f32[1,1536]{1,0:T(1,128)}) custom-call(s32[1]{0:T(128)} %bitcast.refs_0_, bf16[768,768]{1,0:T(8,128)(2,1)} %bitcast.21.refs_1_, bf16[768,768]{1,0:T(8,128)(2,1)} %bitcast.66, ...), custom_call_target="tpu_custom_call" | custom-call | flops 7247757312 | bytes 12582912 | tf_op jit(solution)/shard_map/expert_rows/pallas_call | solution.py:143
  77.9 7.5 %all-to-all-start.2 = ((bf16[16,48,768]{2,1,0:T(8,128)(2,1)}), bf16[16,48,768]{2,1,0:T(8,128)(2,1)S(1)}, u32[]{:S(2)}, u32[]{:S(2)}) async-start(bf16[16,48,768]{2,1,0:T(8,128)(2,1)} %bitcast.65), calls=%async_computation.2 | async-start | bytes 2359296 | tf_op jit(solution)/shard_map/all_to_all | solution.py:569
  86.8 6.2 %fusion.116 = f32[768,1536]{1,0:T(8,128)} fusion(bf16[768,768]{1,0:T(8,128)(2,1)} %bitcast.21.refs_1_, bf16[768,1536]{1,0:T(8,128)(2,1)} %get-tuple-element.103), kind=kOutput, calls=%fused_computation.238 | convolution fusion | flops 1811939328 | bytes 8257536 | tf_op jit(solution)/shard_map/dot_general | solution.py:36
  93.0 17.5 %all-to-all-done.2.back_ref = bf16[16,48,768]{2,1,0:T(8,128)(2,1)S(1)} async-done(((bf16[16,48,768]{2,1,0:T(8,128)(2,1)}), bf16[16,48,768]{2,1,0:T(8,128)(2,1)S(1)}, u32[]{:S(2)}, u32[]{:S(2)}) %all-to-all-start.2) | async-done | bytes 1179680 | tf_op jit(solution)/shard_map/all_to_all | solution.py:569
  111.8 5.9 %fusion.115 = f32[1536,768]{1,0:T(8,128)} fusion(bf16[768,1536]{1,0:T(8,128)(2,1)} %get-tuple-element.101, bf16[768,768]{1,0:T(8,128)(2,1)S(1)} %copy-done.27), kind=kOutput, calls=%fused_computation.237 | convolution fusion | flops 1811939328 | bytes 8257536 | tf_op jit(solution)/shard_map/dot_general | solution.py:36
  117.7 7.5 %all-to-all-start.3 = ((bf16[16,48,768]{2,1,0:T(8,128)(2,1)}), bf16[16,48,768]{2,1,0:T(8,128)(2,1)S(1)}, u32[]{:S(2)}, u32[]{:S(2)}) async-start(bf16[16,48,768]{2,1,0:T(8,128)(2,1)} %bitcast.64), calls=%async_computation.3 | async-start | bytes 2359296 | tf_op jit(solution)/shard_map/all_to_all | solution.py:588
  125.2 11.3 %attention_grads.1 = (bf16[384,1664]{1,0:T(8,128)(2,1)}, f32[384,1664]{1,0:T(8,128)}, bf16[197,768]{1,0:T(8,128)(2,1)}, f32[1,1152]{1,0:T(1,128)}, f32[197,768]{1,0:T(8,128)}) custom-call(bf16[208,768]{1,0:T(8,128)(2,1)} %copy-done.2, bf16[208,768]{1,0:T(8,128)(2,1)} %collective-permute-done.3.other_ref, bf16[768,16]{1,0:T(8,128)(2,1)} %copy.80.refs_4_.router_ref, ...), custom_call_target="tpu_custom_call" | custom-call | flops 42874306560 | bytes 10485760 | tf_op jit(solution)/shard_map/attention_grads/pallas_call | solution.py:333
  137.7 2.1 collective-permute-done.4
  139.8 3.5 %fusion.105 = (bf16[384,1664]{1,0:T(8,128)(2,1)S(1)}, f32[384,1664]{1,0:T(8,128)}) fusion(f32[384,1664]{1,0:T(8,128)} %get-tuple-element.96, bf16[384,1664]{1,0:T(8,128)(2,1)S(1)} %collective-permute-done.4), kind=kLoop, calls=%fused_computation.227 | loop fusion | flops 1916928 | bytes 7667712 | tf_op jit(solution)/shard_map/convert.7
  144.8 1.9 collective-permute-start.6
  146.7 3.7 %all-to-all-done.3 = bf16[16,48,768]{2,1,0:T(8,128)(2,1)S(1)} async-done(((bf16[16,48,768]{2,1,0:T(8,128)(2,1)}), bf16[16,48,768]{2,1,0:T(8,128)(2,1)S(1)}, u32[]{:S(2)}, u32[]{:S(2)}) %all-to-all-start.3) | async-done | bytes 1179680 | tf_op jit(solution)/shard_map/all_to_all | solution.py:588
  151.4 2.1 collective-permute-start.5
  155.1 2.4 %collective-permute-done.6 = bf16[192,768]{1,0:T(8,128)(2,1)} collective-permute-done((bf16[192,768]{1,0:T(8,128)(2,1)}, bf16[192,768]{1,0:T(8,128)(2,1)}, u32[]{:S(2)}, u32[]{:S(2)}) %collective-permute-start.6) | collective-permute-done | bytes 294944 | tf_op jit(solution)/shard_map/ppermute | solution.py:66
  158.7 3.8 %collective-permute-done.5 = bf16[192,896]{1,0:T(8,128)(2,1)S(1)} collective-permute-done((bf16[192,896]{1,0:T(8,128)(2,1)S(1)}, bf16[192,896]{1,0:T(8,128)(2,1)S(1)}, u32[]{:S(2)}, u32[]{:S(2)}) %collective-permute-start.5) | collective-permute-done | bytes 344096 | tf_op jit(solution)/shard_map/ppermute | solution.py:66
  164.1 3.7 %collective-permute-start.8 = (bf16[96,896]{1,0:T(8,128)(2,1)S(1)}, bf16[96,896]{1,0:T(8,128)(2,1)S(1)}, u32[]{:S(2)}, u32[]{:S(2)}) collective-permute-start(bf16[96,896]{1,0:T(8,128)(2,1)S(1)} %slice.279), channel_id=1, source_target_pairs={{0,8},{2,10},{4,12},{6,14},{8,0},{10,2},{12,4},{14,6},{16,24},{18,... | collective-permute-start | bytes 516104 | tf_op jit(solution)/shard_map/ppermute | solution.py:66
  168.9 8.4 %collective-permute-done.9 = bf16[96,768]{1,0:T(8,128)(2,1)S(1)} collective-permute-done((bf16[96,768]{1,0:T(8,128)(2,1)S(1)}, bf16[96,768]{1,0:T(8,128)(2,1)S(1)}, u32[]{:S(2)}, u32[]{:S(2)}) %collective-permute-start.9) | collective-permute-done | bytes 147488 | tf_op jit(solution)/shard_map/ppermute | solution.py:66
  180.0 1.9 collective-permute-done.11
  181.9 3.9 %collective-permute-done.10 = bf16[48,896]{1,0:T(8,128)(2,1)S(1)} collective-permute-done((bf16[48,896]{1,0:T(8,128)(2,1)S(1)}, bf16[48,896]{1,0:T(8,128)(2,1)S(1)}, u32[]{:S(2)}, u32[]{:S(2)}) %collective-permute-start.10) | collective-permute-done | bytes 86048 | tf_op jit(solution)/shard_map/ppermute | solution.py:66
  186.0 4.2 %collective-permute-done.13 = bf16[48,768]{1,0:T(8,128)(2,1)S(1)} collective-permute-done((bf16[48,768]{1,0:T(8,128)(2,1)S(1)}, bf16[48,768]{1,0:T(8,128)(2,1)S(1)}, u32[]{:S(2)}, u32[]{:S(2)}) %collective-permute-start.13) | collective-permute-done | bytes 73760 | tf_op jit(solution)/shard_map/ppermute | solution.py:66
  191.9 1.8 collective-permute-start.15
  195.2 5.1 %collective-permute-done.15 = bf16[96,768]{1,0:T(8,128)(2,1)S(1)} collective-permute-done((bf16[96,768]{1,0:T(8,128)(2,1)S(1)}, bf16[96,768]{1,0:T(8,128)(2,1)S(1)}, u32[]{:S(2)}, u32[]{:S(2)}) %collective-permute-start.15) | collective-permute-done | bytes 147488 | tf_op jit(solution)/shard_map/ppermute | solution.py:66
  204.7 2.8 %collective-permute-done.18 = bf16[192,768]{1,0:T(8,128)(2,1)S(1)} collective-permute-done((bf16[192,768]{1,0:T(8,128)(2,1)S(1)}, bf16[192,768]{1,0:T(8,128)(2,1)S(1)}, u32[]{:S(2)}, u32[]{:S(2)}) %collective-permute-start.18) | collective-permute-done | bytes 294944 | tf_op jit(solution)/shard_map/ppermute | solution.py:66
  207.6 2.8 %collective-permute-done.17 = bf16[208,896]{1,0:T(8,128)(2,1)S(1)} collective-permute-done((bf16[208,896]{1,0:T(8,128)(2,1)S(1)}, bf16[208,896]{1,0:T(8,128)(2,1)S(1)}, u32[]{:S(2)}, u32[]{:S(2)}) %collective-permute-start.17) | collective-permute-done | bytes 372768 | tf_op jit(solution)/shard_map/ppermute | solution.py:66
  213.9 2.8 %finish.1 = (f32[3,768,384]{2,1,0:T(8,128)}, f32[384,768]{1,0:T(8,128)}, f32[16,768]{1,0:T(8,128)}, f32[16,768]{1,0:T(8,128)}, f32[8,768]{1,0:T(8,128)S(1)}) custom-call(s32[1]{0:T(128)} %bitcast.refs_0_, bf16[400,896]{1,0:T(8,128)(2,1)S(1)} %fusion.61.refs_1_, bf16[384,768]{1,0:T(8,128)(2,1)S(1)} %pad_maximum_fusion.2.refs_2_, ...), custom_call_target="tpu_custom_call" | custom-call | tf_op jit(solution)/shard_map/finish/pallas_call | solution.py:387
  (202 shorter events, 47.4 us)
Async XLA Ops:
  0.6 13.1 %copy-start = (f32[16,768]{1,0:T(8,128)S(1)}, f32[16,768]{1,0:T(8,128)}, u32[]{:S(2)}) copy-start(f32[16,768]{1,0:T(8,128)} %param.29) | copy-start | bytes 147460
  0.7 17.4 %collective-permute-start = (bf16[384,768]{1,0:T(8,128)(2,1)}, bf16[384,768]{1,0:T(8,128)(2,1)S(1)}, u32[]{:S(2)}, u32[]{:S(2)}) collective-permute-start(bf16[384,768]{1,0:T(8,128)(2,1)} %proj_ref.1), channel_id=1, source_target_pairs={{0,1},{1,0},{2,3},{3,2},{4,5},{5,4},{6,7},{7,6},{8,9},{9,8},{10,11... | collective-permute-start | bytes 1769480 | tf_op jit(solution)/shard_map/ppermute | solution.py:62
  7.3 21.6 %all-to-all-start = ((bf16[16,48,384]{2,1,0:T(8,128)(2,1)}), bf16[16,48,384]{2,1,0:T(8,128)(2,1)}, u32[]{:S(2)}, u32[]{:S(2)}) async-start(bf16[16,48,384]{2,1,0:T(8,128)(2,1)} %broadcast_select_fusion), calls=%async_computation | async-start | bytes 1179648 | tf_op jit(solution)/shard_map/all_to_all | solution.py:479
  21.1 7.9 %copy-start.5 = (bf16[768,768]{1,0:T(8,128)(2,1)S(1)}, bf16[768,768]{1,0:T(8,128)(2,1)}, u32[]{:S(2)}) copy-start(bf16[768,768]{1,0:T(8,128)(2,1)} %pad_maximum_fusion) | copy-start | bytes 3538948
  21.1 7.2 %collective-permute-start.1 = (bf16[197,384]{0,1:T(8,128)(2,1)S(1)}, bf16[197,384]{0,1:T(8,128)(2,1)S(1)}, u32[]{:S(2)}, u32[]{:S(2)}) collective-permute-start(bf16[197,384]{0,1:T(8,128)(2,1)S(1)} %bitcast.69), channel_id=1, source_target_pairs={{0,1},{1,0},{2,3},{3,2},{4,5},{5,4},{6,7},{7,6},{8,9},{9,8},{10,11... | collective-permute-start | bytes 453896 | tf_op jit(solution)/shard_map/ppermute | solution.py:62
  30.7 10.0 %copy-start.6 = (bf16[197,768]{1,0:T(8,128)(2,1)}, bf16[197,768]{1,0:T(8,128)(2,1)S(1)}, u32[]{:S(2)}) copy-start(bf16[197,768]{1,0:T(8,128)(2,1)S(1)} %get-tuple-element.90.hidden2_ref) | copy-start | bytes 907780
  32.5 30.7 %all-to-all-start.1 = ((bf16[16,48,768]{2,1,0:T(8,128)(2,1)}), bf16[16,48,768]{2,1,0:T(8,128)(2,1)}, u32[]{:S(2)}, u32[]{:S(2)}) async-start(bf16[16,48,768]{2,1,0:T(8,128)(2,1)} %bitcast.20), calls=%async_computation.1 | async-start | bytes 2359296 | tf_op jit(solution)/shard_map/all_to_all | solution.py:509
  41.2 69.3 %copy-start.1 = (f32[197,128]{1,0:T(8,128)}, f32[197,128]{1,0:T(8,128)S(1)}, u32[]{:S(2)}) copy-start(f32[197,128]{1,0:T(8,128)S(1)} %pad.31.facts_ref) | copy-start | bytes 302596
  41.2 15.9 %collective-permute-start.2 = (bf16[16,48,384]{2,1,0:T(8,128)(2,1)}, bf16[16,48,384]{2,1,0:T(8,128)(2,1)S(1)}, u32[]{:S(2)}, u32[]{:S(2)}) collective-permute-start(bf16[16,48,384]{2,1,0:T(8,128)(2,1)} %all-to-all-done), channel_id=1, source_target_pairs={{0,1},{1,0},{2,3},{3,2},{4,5},{5,4},{6,7},{7,6},{8,9},{9,8},{10,11... | collective-permute-start | bytes 1769480 | tf_op jit(solution)/shard_map/ppermute | solution.py:62
  77.9 32.6 %all-to-all-start.2 = ((bf16[16,48,768]{2,1,0:T(8,128)(2,1)}), bf16[16,48,768]{2,1,0:T(8,128)(2,1)S(1)}, u32[]{:S(2)}, u32[]{:S(2)}) async-start(bf16[16,48,768]{2,1,0:T(8,128)(2,1)} %bitcast.65), calls=%async_computation.2 | async-start | bytes 2359296 | tf_op jit(solution)/shard_map/all_to_all | solution.py:569
  111.2 14.0 %collective-permute-start.3 = (bf16[208,768]{1,0:T(8,128)(2,1)S(1)}, bf16[208,768]{1,0:T(8,128)(2,1)}, u32[]{:S(2)}, u32[]{:S(2)}) collective-permute-start(bf16[208,768]{1,0:T(8,128)(2,1)S(1)} %home_rows.1.home_ref), channel_id=1, source_target_pairs={{0,1},{1,0},{2,3},{3,2},{4,5},{5,4},{6,7},{7,6},{8,9},{9,8},{10,11... | collective-permute-start | bytes 958472 | tf_op jit(solution)/shard_map/ppermute | solution.py:62
  117.7 32.7 %all-to-all-start.3 = ((bf16[16,48,768]{2,1,0:T(8,128)(2,1)}), bf16[16,48,768]{2,1,0:T(8,128)(2,1)S(1)}, u32[]{:S(2)}, u32[]{:S(2)}) async-start(bf16[16,48,768]{2,1,0:T(8,128)(2,1)} %bitcast.64), calls=%async_computation.3 | async-start | bytes 2359296 | tf_op jit(solution)/shard_map/all_to_all | solution.py:588
  136.6 3.2 %collective-permute-start.4 = (bf16[384,1664]{1,0:T(8,128)(2,1)}, bf16[384,1664]{1,0:T(8,128)(2,1)S(1)}, u32[]{:S(2)}, u32[]{:S(2)}) collective-permute-start(bf16[384,1664]{1,0:T(8,128)(2,1)} %get-tuple-element.97), channel_id=1, source_target_pairs={{0,2},{2,0},{4,6},{6,4},{8,10},{10,8},{12,14},{14,12},{16,18},{18,... | collective-permute-start | bytes 3833864 | tf_op jit(solution)/shard_map/ppermute | solution.py:66
  144.1 9.5 %copy-start.11 = (bf16[197,768]{1,0:T(8,128)(2,1)S(1)}, bf16[197,768]{1,0:T(8,128)(2,1)}, u32[]{:S(2)}) copy-start(bf16[197,768]{1,0:T(8,128)(2,1)} %get-tuple-element.107) | copy-start | bytes 907780
  144.8 12.7 %collective-permute-start.6 = (bf16[192,768]{1,0:T(8,128)(2,1)}, bf16[192,768]{1,0:T(8,128)(2,1)}, u32[]{:S(2)}, u32[]{:S(2)}) collective-permute-start(bf16[192,768]{1,0:T(8,128)(2,1)} %slice.209), channel_id=1, source_target_pairs={{0,8},{2,10},{4,12},{6,14},{8,0},{10,2},{12,4},{14,6},{16,24},{18,... | collective-permute-start | bytes 884744 | tf_op jit(solution)/shard_map/ppermute | solution.py:66
  151.4 11.0 %collective-permute-start.5 = (bf16[192,896]{1,0:T(8,128)(2,1)S(1)}, bf16[192,896]{1,0:T(8,128)(2,1)S(1)}, u32[]{:S(2)}, u32[]{:S(2)}) collective-permute-start(bf16[192,896]{1,0:T(8,128)(2,1)S(1)} %copy-done.16), channel_id=1, source_target_pairs={{0,4},{2,6},{4,0},{6,2},{8,12},{10,14},{12,8},{14,10},{16,20},{18,... | collective-permute-start | bytes 1032200 | tf_op jit(solution)/shard_map/ppermute | solution.py:66
  153.6 10.0 %collective-permute-start.7 = (bf16[197,768]{1,0:T(8,128)(2,1)S(1)}, bf16[197,768]{1,0:T(8,128)(2,1)S(1)}, u32[]{:S(2)}, u32[]{:S(2)}) collective-permute-start(bf16[197,768]{1,0:T(8,128)(2,1)S(1)} %copy-done.11), channel_id=1, source_target_pairs={{0,1},{1,0},{2,3},{3,2},{4,5},{5,4},{6,7},{7,6},{8,9},{9,8},{10,11... | collective-permute-start | bytes 907784 | tf_op jit(solution)/shard_map/ppermute | solution.py:62
  164.1 13.2 %collective-permute-start.8 = (bf16[96,896]{1,0:T(8,128)(2,1)S(1)}, bf16[96,896]{1,0:T(8,128)(2,1)S(1)}, u32[]{:S(2)}, u32[]{:S(2)}) collective-permute-start(bf16[96,896]{1,0:T(8,128)(2,1)S(1)} %slice.279), channel_id=1, source_target_pairs={{0,8},{2,10},{4,12},{6,14},{8,0},{10,2},{12,4},{14,6},{16,24},{18,... | collective-permute-start | bytes 516104 | tf_op jit(solution)/shard_map/ppermute | solution.py:66
  167.9 9.5 %collective-permute-start.9 = (bf16[96,768]{1,0:T(8,128)(2,1)S(1)}, bf16[96,768]{1,0:T(8,128)(2,1)S(1)}, u32[]{:S(2)}, u32[]{:S(2)}) collective-permute-start(bf16[96,768]{1,0:T(8,128)(2,1)S(1)} %slice.280), channel_id=1, source_target_pairs={{0,16},{2,18},{4,20},{6,22},{8,24},{10,26},{12,28},{14,30},{16,0},... | collective-permute-start | bytes 442376 | tf_op jit(solution)/shard_map/ppermute | solution.py:66
  177.4 4.4 %collective-permute-start.11 = (bf16[48,768]{1,0:T(8,128)(2,1)S(1)}, bf16[48,768]{1,0:T(8,128)(2,1)S(1)}, u32[]{:S(2)}, u32[]{:S(2)}) collective-permute-start(bf16[48,768]{1,0:T(8,128)(2,1)S(1)} %slice.282), channel_id=1, source_target_pairs={{0,4},{2,6},{4,0},{6,2},{8,12},{10,14},{12,8},{14,10},{16,20},{18,... | collective-permute-start | bytes 221192 | tf_op jit(solution)/shard_map/ppermute | solution.py:66
  179.2 6.6 %collective-permute-start.10 = (bf16[48,896]{1,0:T(8,128)(2,1)S(1)}, bf16[48,896]{1,0:T(8,128)(2,1)S(1)}, u32[]{:S(2)}, u32[]{:S(2)}) collective-permute-start(bf16[48,896]{1,0:T(8,128)(2,1)S(1)} %slice.281), channel_id=1, source_target_pairs={{0,16},{2,18},{4,20},{6,22},{8,24},{10,26},{12,28},{14,30},{16,0},... | collective-permute-start | bytes 258056 | tf_op jit(solution)/shard_map/ppermute | solution.py:66
  185.8 4.4 %collective-permute-start.13 = (bf16[48,768]{1,0:T(8,128)(2,1)S(1)}, bf16[48,768]{1,0:T(8,128)(2,1)S(1)}, u32[]{:S(2)}, u32[]{:S(2)}) collective-permute-start(bf16[48,768]{1,0:T(8,128)(2,1)S(1)} %add_convert_fusion.3), channel_id=1, source_target_pairs={{0,4},{2,6},{4,0},{6,2},{8,12},{10,14},{12,8},{14,10},{16,20},{18,... | collective-permute-start | bytes 221192 | tf_op jit(solution)/shard_map/ppermute | solution.py:66
  185.9 5.8 %collective-permute-start.12 = (bf16[64,896]{1,0:T(8,128)(2,1)S(1)}, bf16[64,896]{1,0:T(8,128)(2,1)S(1)}, u32[]{:S(2)}, u32[]{:S(2)}) collective-permute-start(bf16[64,896]{1,0:T(8,128)(2,1)S(1)} %pad_maximum_fusion.8), channel_id=1, source_target_pairs={{0,16},{2,18},{4,20},{6,22},{8,24},{10,26},{12,28},{14,30},{16,0},... | collective-permute-start | bytes 344072 | tf_op jit(solution)/shard_map/ppermute | solution.py:66
  191.8 9.3 %copy-start.12 = (bf16[197,768]{1,0:T(8,128)(2,1)S(1)}, bf16[197,768]{1,0:T(8,128)(2,1)}, u32[]{:S(2)}) copy-start(bf16[197,768]{1,0:T(8,128)(2,1)} %get-tuple-element.107) | copy-start | bytes 907780
  191.8 9.3 %copy-start.13 = (f32[197,768]{1,0:T(8,128)S(1)}, f32[197,768]{1,0:T(8,128)}, u32[]{:S(2)}) copy-start(f32[197,768]{1,0:T(8,128)} %get-tuple-element.126) | copy-start | bytes 1815556
  191.8 8.5 %collective-permute-start.14 = (bf16[112,896]{1,0:T(8,128)(2,1)S(1)}, bf16[112,896]{1,0:T(8,128)(2,1)S(1)}, u32[]{:S(2)}, u32[]{:S(2)}) collective-permute-start(bf16[112,896]{1,0:T(8,128)(2,1)S(1)} %pad_maximum_fusion.6), channel_id=1, source_target_pairs={{0,8},{2,10},{4,12},{6,14},{8,0},{10,2},{12,4},{14,6},{16,24},{18,... | collective-permute-start | bytes 602120 | tf_op jit(solution)/shard_map/ppermute | solution.py:66
  191.9 8.4 %collective-permute-start.15 = (bf16[96,768]{1,0:T(8,128)(2,1)S(1)}, bf16[96,768]{1,0:T(8,128)(2,1)S(1)}, u32[]{:S(2)}, u32[]{:S(2)}) collective-permute-start(bf16[96,768]{1,0:T(8,128)(2,1)S(1)} %pad_maximum_fusion.7), channel_id=1, source_target_pairs={{0,16},{2,18},{4,20},{6,22},{8,24},{10,26},{12,28},{14,30},{16,0},... | collective-permute-start | bytes 442376 | tf_op jit(solution)/shard_map/ppermute | solution.py:66
  193.7 6.9 %collective-permute-start.16 = (bf16[197,768]{1,0:T(8,128)(2,1)S(1)}, bf16[197,768]{1,0:T(8,128)(2,1)S(1)}, u32[]{:S(2)}, u32[]{:S(2)}) collective-permute-start(bf16[197,768]{1,0:T(8,128)(2,1)S(1)} %convolution_convert_fusion.3), channel_id=1, source_target_pairs={{0,1},{1,0},{2,3},{3,2},{4,5},{5,4},{6,7},{7,6},{8,9},{9,8},{10,11... | collective-permute-start | bytes 907784 | tf_op jit(solution)/shard_map/ppermute | solution.py:62
  200.6 7.0 %collective-permute-start.18 = (bf16[192,768]{1,0:T(8,128)(2,1)S(1)}, bf16[192,768]{1,0:T(8,128)(2,1)S(1)}, u32[]{:S(2)}, u32[]{:S(2)}) collective-permute-start(bf16[192,768]{1,0:T(8,128)(2,1)S(1)} %pad_maximum_fusion.5), channel_id=1, source_target_pairs={{0,8},{2,10},{4,12},{6,14},{8,0},{10,2},{12,4},{14,6},{16,24},{18,... | collective-permute-start | bytes 884744 | tf_op jit(solution)/shard_map/ppermute | solution.py:66
  202.2 8.1 %collective-permute-start.17 = (bf16[208,896]{1,0:T(8,128)(2,1)S(1)}, bf16[208,896]{1,0:T(8,128)(2,1)S(1)}, u32[]{:S(2)}, u32[]{:S(2)}) collective-permute-start(bf16[208,896]{1,0:T(8,128)(2,1)S(1)} %pad_maximum_fusion.4), channel_id=1, source_target_pairs={{0,4},{2,6},{4,0},{6,2},{8,12},{10,14},{12,8},{14,10},{16,20},{18,... | collective-permute-start | bytes 1118216 | tf_op jit(solution)/shard_map/ppermute | solution.py:66
  210.4 2.3 %collective-permute-start.19 = (bf16[400,896]{1,0:T(8,128)(2,1)S(1)}, bf16[400,896]{1,0:T(8,128)(2,1)S(1)}, u32[]{:S(2)}, u32[]{:S(2)}) collective-permute-start(bf16[400,896]{1,0:T(8,128)(2,1)S(1)} %fusion.61.refs_1_), channel_id=1, source_target_pairs={{0,2},{2,0},{4,6},{6,4},{8,10},{10,8},{12,14},{14,12},{16,18},{18,... | collective-permute-start | bytes 2150408 | tf_op jit(solution)/shard_map/ppermute | solution.py:66
  210.5 3.4 %collective-permute-start.20 = (bf16[384,768]{1,0:T(8,128)(2,1)S(1)}, bf16[384,768]{1,0:T(8,128)(2,1)S(1)}, u32[]{:S(2)}, u32[]{:S(2)}) collective-permute-start(bf16[384,768]{1,0:T(8,128)(2,1)S(1)} %pad_maximum_fusion.2.refs_2_), channel_id=1, source_target_pairs={{0,2},{2,0},{4,6},{6,4},{8,10},{10,8},{12,14},{14,12},{16,18},{18,... | collective-permute-start | bytes 1769480 | tf_op jit(solution)/shard_map/ppermute | solution.py:66
  (21 other events, 77.2 us)
